TPU v7x, 32 devices: a whole 2x2x4 slice. The times are simulated.
32 devices in a mesh: dp: 2 (over x), ctx: 4 (over y, core), tp: 4 (over z).
Axes of the slice: x: 2, y: 2, z: 4, core: 2. Of those that a mesh axis runs over, the one named last changes fastest.
Arguments:
- layer_input: bfloat16 [8192, 2048], P(('dp', 'ctx'), 'tp'), may hold values from -6 to 6
- gain_attn: float32 [2048], P('tp'), may hold values from 0.5 to 1.5
- w_query: bfloat16 [2048, 2048], P(('dp', 'ctx'), 'tp'), may hold values from -0.125 to 0.125
- w_key: bfloat16 [2048, 2048], P(('dp', 'ctx'), 'tp'), may hold values from -0.125 to 0.125
- w_value: bfloat16 [2048, 4096], P(('dp', 'ctx'), 'tp'), may hold values from -0.125 to 0.125
- w_retgate: bfloat16 [2048, 4096], P(('dp', 'ctx'), 'tp'), may hold values from -0.125 to 0.125
- w_out: bfloat16 [2048, 4096], P(('dp', 'ctx'), 'tp'), may hold values from -0.125 to 0.125
- gain_mlp: float32 [2048], P('tp'), may hold values from 0.5 to 1.5
- w_gate: bfloat16 [2048, 4096], P(('dp', 'ctx'), 'tp'), may hold values from -0.125 to 0.125
- w_up: bfloat16 [2048, 4096], P(('dp', 'ctx'), 'tp'), may hold values from -0.125 to 0.125
- w_down: bfloat16 [2048, 4096], P(('dp', 'ctx'), 'tp'), may hold values from -0.09375 to 0.09375
- cotangent: bfloat16 [8192, 2048], P(('dp', 'ctx'), 'tp'), may hold values from -6 to 6
Outputs:
- layer_output: bfloat16 [8192, 2048], P(('dp', 'ctx'), 'tp')
- grad_input: bfloat16 [8192, 2048], P(('dp', 'ctx'), 'tp')
- grad_gain_attn: float32 [2048], P('tp')
- grad_w_query: float32 [2048, 2048], P(('dp', 'ctx'), 'tp')
- grad_w_key: float32 [2048, 2048], P(('dp', 'ctx'), 'tp')
- grad_w_value: float32 [2048, 4096], P(('dp', 'ctx'), 'tp')
- grad_w_retgate: float32 [2048, 4096], P(('dp', 'ctx'), 'tp')
- grad_w_out: float32 [2048, 4096], P(('dp', 'ctx'), 'tp')
- grad_gain_mlp: float32 [2048], P('tp')
- grad_w_gate: float32 [2048, 4096], P(('dp', 'ctx'), 'tp')
- grad_w_up: float32 [2048, 4096], P(('dp', 'ctx'), 'tp')
- grad_w_down: float32 [2048, 4096], P(('dp', 'ctx'), 'tp')
All inputs are finite; a program needn't handle non-finite values.
Results may differ from a plain program's by a relative error of at most 0.019.
Values may be sent and summed in bfloat16 or wider, within the bound.
No kernel may reach another device: no remote copies, remote signals or barrier semaphores. Data moves between devices by JAX's collectives and lax.ppermute only.
A program may use at most 192 MiB of HBM per device.

v0:
```python
import math

import jax
import jax.numpy as jnp
from jax import lax
from jax.experimental import pallas as pl
from jax.experimental.pallas import tpu as pltpu
from jax.sharding import PartitionSpec as P


HK = 256
HV = 512
EPSILON = 1e-06
BLOCK = 256
F32 = jnp.float32
BF16 = jnp.bfloat16


def nn(a, b):
    return lax.dot_general(a, b, (((1,), (0,)), ((), ())), preferred_element_type=F32)


def tn(a, b):
    return lax.dot_general(a, b, (((0,), (0,)), ((), ())), preferred_element_type=F32)


def nt(a, b):
    return lax.dot_general(a, b, (((1,), (1,)), ((), ())), preferred_element_type=F32)


def right(lo, hi):
    return [(i, i + 1) for i in range(lo, hi)]


def left(lo, hi):
    return [(i, i - 1) for i in range(hi, lo, -1)]


def line_gather(x, axis):
    n, i = lax.axis_size(axis), lax.axis_index(axis)
    rights, lefts = [x], [x]
    for k in range(1, n):
        r_pairs = right(k - 1, n - 1)
        l_pairs = left(0, n - k)
        if 2 * k > n + 1:
            both = lax.ppermute(jnp.where(i >= k - 1, rights[-1], lefts[-1]), axis, r_pairs + l_pairs)
            rights.append(both)
            lefts.append(both)
        else:
            rights.append(lax.ppermute(rights[-1], axis, r_pairs))
            lefts.append(lax.ppermute(lefts[-1], axis, l_pairs))
    return [x] + [jnp.where(i >= k, rights[k], lefts[n - k]) for k in range(1, n)]


def place(blocks, axis, dtype):
    n, i = lax.axis_size(axis), lax.axis_index(axis)
    rows, width = blocks[0].shape
    full = jnp.zeros((rows, n * width), dtype)
    for k, block in enumerate(blocks):
        at = ((i - k) % n) * width
        full = lax.dynamic_update_slice(full, block.astype(dtype), (0, at))
    return full


def line_scatter(parts, axis):
    n, i = lax.axis_size(axis), lax.axis_index(axis)
    width = parts.shape[1] // n

    def block(j):
        return lax.dynamic_slice(parts, (0, jnp.clip(j, 0, n - 1) * width), (parts.shape[0], width))

    from_left = from_right = None
    early = []
    for k in range(1, n):
        r_pairs = right(0, k)
        l_pairs = left(n - 1 - k, n - 1)
        if 2 * k < n - 1:
            data = block(jnp.where(i < k, i + n - k, i - n + k))
            if from_left is not None:
                data = (data.astype(F32) + jnp.where(i < k, from_left, from_right).astype(F32)).astype(BF16)
            from_left = from_right = lax.ppermute(data, axis, r_pairs + l_pairs)
            from_left = jnp.where(i <= k, from_left, jnp.zeros_like(from_left))
            from_right = jnp.where(i >= n - 1 - k, from_right, jnp.zeros_like(from_right))
        else:
            r_data, l_data = block(i + n - k), block(i - n + k)
            if from_left is not None:
                r_data = (r_data.astype(F32) + from_left.astype(F32)).astype(BF16)
                l_data = (l_data.astype(F32) + from_right.astype(F32)).astype(BF16)
            from_left = lax.ppermute(r_data, axis, r_pairs)
            from_right = lax.ppermute(l_data, axis, l_pairs)
        if k < n - 1:
            early.append((from_left, from_right))
    return block(i).astype(F32) + from_left.astype(F32) + from_right.astype(F32), early


def small_gather(x, axis):
    n = lax.axis_size(axis)
    blocks = [x] + [lax.ppermute(x, axis, [(j, (j + s) % n) for j in range(n)]) for s in range(1, n)]
    return place(blocks, axis, x.dtype)


def swap_sum(x, axis):
    n = lax.axis_size(axis)
    g = 1
    while g < n:
        x = x + lax.ppermute(x, axis, [(j, j ^ g) for j in range(n)])
        g *= 2
    return x


def states_before(local, log_block, axis):
    n, b = lax.axis_size(axis), lax.axis_index(axis)
    total, prefix, g = local, jnp.zeros_like(local), 1
    while g < n:
        got = lax.ppermute(total.astype(BF16), axis, [(j, j ^ g) for j in range(n)]).astype(F32)
        upper = (b // g) % 2 == 1
        mine = jnp.exp((b % g).astype(F32) * log_block)[:, None, None]
        whole = jnp.exp(g * log_block)[:, None, None]
        prefix = jnp.where(upper, prefix + mine * got, prefix)
        total = jnp.where(upper, whole * got + total, whole * total + got)
        g *= 2
    return prefix


def states_after(local, log_block, axis):
    first = None
    n, b = lax.axis_size(axis), lax.axis_index(axis)
    total, suffix, g = local, jnp.zeros_like(local), 1
    while g < n:
        got = lax.ppermute(total.astype(BF16), axis, [(j, j ^ g) for j in range(n)]).astype(F32)
        first = got if first is None else first
        upper = (b // g) % 2 == 1
        mine = jnp.exp((g - 1 - b % g).astype(F32) * log_block)[:, None, None]
        whole = jnp.exp(g * log_block)[:, None, None]
        suffix = jnp.where(upper, suffix, suffix + mine * got)
        total = jnp.where(upper, got + whole * total, total + whole * got)
        g *= 2
    return suffix, first


def pair_swap(x):
    lane = lax.broadcasted_iota(jnp.int32, x.shape, 1)
    width = x.shape[1]
    return jnp.where(lane % 2 == 0, pltpu.roll(x, width - 1, 1), pltpu.roll(x, 1, 1))


def project_kernel(heads, x_ref, w_ref, cos_ref, sin_ref, q_ref, k_ref):
    out = nn(x_ref[...], w_ref[...])
    c, s = cos_ref[...], sin_ref[...]
    for h in range(2 * heads):
        one = out[:, h * HK : (h + 1) * HK]
        turned = one * c + pair_swap(one) * s
        if h < heads:
            q_ref[:, h * HK : (h + 1) * HK] = turned.astype(BF16)
        else:
            k_ref[:, (h - heads) * HK : (h - heads + 1) * HK] = (turned * (1.0 / math.sqrt(HK))).astype(BF16)


def project(x, w, heads, cosine, sine):
    rows, features = x.shape
    out = pl.BlockSpec((BLOCK, heads * HK), lambda r: (r, 0))
    table = pl.BlockSpec((BLOCK, HK), lambda r: (r, 0))
    return pl.pallas_call(
        lambda *refs: project_kernel(heads, *refs),
        grid=(rows // BLOCK,),
        in_specs=[
            pl.BlockSpec((BLOCK, features), lambda r: (r, 0)),
            pl.BlockSpec((features, 2 * heads * HK), lambda r: (0, 0)),
            table,
            table,
        ],
        out_specs=[out, out],
        out_shape=[jax.ShapeDtypeStruct((rows, heads * HK), BF16)] * 2,
        cost_estimate=pl.CostEstimate(
            flops=4 * rows * features * heads * HK,
            bytes_accessed=2 * rows * features + 4 * features * heads * HK + 4 * rows * heads * HK,
            transcendentals=0,
        ),
        name="project",
    )(x, w, cosine, sine)


def decay_vectors(log_gamma):
    down = lax.broadcasted_iota(jnp.int32, (BLOCK, 1), 0).astype(F32)
    across = lax.broadcasted_iota(jnp.int32, (1, BLOCK), 1).astype(F32)
    return jnp.exp(down * log_gamma), jnp.exp(-across * log_gamma)


def block_decay(scores, r, j, log_gamma, down, across):
    out = scores * (down * jnp.exp(log_gamma * (BLOCK * (r - j)))) * across
    if r == j:
        n = lax.broadcasted_iota(jnp.int32, scores.shape, 0)
        m = lax.broadcasted_iota(jnp.int32, scores.shape, 1)
        out = jnp.where(n >= m, out, 0.0)
    return out.astype(BF16)


def cut(r):
    return slice(r * BLOCK, (r + 1) * BLOCK)


def forward_kernel(first, count, lg_ref, q_ref, k_ref, v_ref, gate_ref, state_ref, gated_ref, ret_ref):
    log_gamma = lg_ref[pl.program_id(0)]
    down, across = decay_vectors(log_gamma)
    state = state_ref[0]
    for at in range(count):
        r = first + at
        q = q_ref[cut(at), :]
        ret = nn(q, state) * (down * jnp.exp(log_gamma * (BLOCK * r)))
        for j in range(r + 1):
            weights = block_decay(nt(q, k_ref[cut(j), :]), r, j, log_gamma, down, across)
            ret = ret + nn(weights, v_ref[cut(j), :])
        ret_ref[cut(at), :] = ret
        scale = lax.rsqrt(jnp.mean(ret * ret, axis=1, keepdims=True) + EPSILON)
        gate = gate_ref[cut(at), :]
        gated_ref[cut(at), :] = (gate / (1.0 + jnp.exp(-gate)) * (ret * scale)).astype(BF16)


def retention_forward(part, parts, log_gamma, q, k, v, gate, state):
    rows = q.shape[0]
    heads = q.shape[1] // HK
    own = rows // parts
    seen = own * (part + 1)
    count = own // BLOCK
    pairs = sum(part * count + at + 1 for at in range(count))
    flops = heads * (pairs * 2 * BLOCK * BLOCK * (HK + HV) + 2 * own * HK * HV)
    return pl.pallas_call(
        lambda *refs: forward_kernel(part * count, count, *refs),
        grid=(heads,),
        in_specs=[
            pl.BlockSpec(memory_space=pltpu.SMEM),
            pl.BlockSpec((own, HK), lambda h: (part, h)),
            pl.BlockSpec((seen, HK), lambda h: (0, h)),
            pl.BlockSpec((seen, HV), lambda h: (0, h)),
            pl.BlockSpec((own, HV), lambda h: (part, h)),
            pl.BlockSpec((1, HK, HV), lambda h: (h, 0, 0)),
        ],
        out_specs=[pl.BlockSpec((own, HV), lambda h: (0, h)), pl.BlockSpec((own, HV), lambda h: (0, h))],
        out_shape=[
            jax.ShapeDtypeStruct((own, heads * HV), BF16),
            jax.ShapeDtypeStruct((own, heads * HV), F32),
        ],
        cost_estimate=pl.CostEstimate(flops=flops, bytes_accessed=16 * own * heads * HV, transcendentals=own * heads * HV),
        name="retention_forward",
    )(log_gamma, q, k, v, gate, state)


def gate_backward_kernel(first, count, lg_ref, q_ref, grad_ref, gate_ref, ret_ref, g_gate_ref, g_ret_ref, state_ref, inner_ref):
    log_gamma = lg_ref[pl.program_id(0)]
    down, _ = decay_vectors(log_gamma)
    state = None
    for at in range(count):
        r = first + at
        ret = ret_ref[cut(at), :]
        gate = gate_ref[cut(at), :]
        grad = grad_ref[cut(at), :]
        scale = lax.rsqrt(jnp.mean(ret * ret, axis=1, keepdims=True) + EPSILON)
        grouped = ret * scale
        sig = 1.0 / (1.0 + jnp.exp(-gate))
        g_gate = (grad * grouped * (sig * (1.0 + gate * (1.0 - sig)))).astype(BF16)
        g = grad * (gate * sig)
        g_ret = (scale * (g - grouped * jnp.mean(g * grouped, axis=1, keepdims=True))).astype(BF16)
        g_gate_ref[cut(at), :] = g_gate
        g_ret_ref[cut(at), :] = g_ret
        inner_ref[0, cut(at), :] = jnp.sum(g_gate.astype(F32) * gate, axis=1, keepdims=True)
        q = (q_ref[cut(at), :].astype(F32) * (down * jnp.exp(log_gamma * (BLOCK * r)))).astype(BF16)
        add = tn(q, g_ret)
        state = add if state is None else state + add
    state_ref[0] = state


def gate_backward(part, parts, log_gamma, q, grad, gate, ret):
    rows = q.shape[0]
    heads = q.shape[1] // HK
    own = rows // parts
    count = own // BLOCK
    return pl.pallas_call(
        lambda *refs: gate_backward_kernel(part * count, count, *refs),
        grid=(heads,),
        in_specs=[
            pl.BlockSpec(memory_space=pltpu.SMEM),
            pl.BlockSpec((own, HK), lambda h: (part, h)),
            pl.BlockSpec((own, HV), lambda h: (0, h)),
            pl.BlockSpec((own, HV), lambda h: (part, h)),
            pl.BlockSpec((own, HV), lambda h: (0, h)),
        ],
        out_specs=[
            pl.BlockSpec((own, HV), lambda h: (0, h)),
            pl.BlockSpec((own, HV), lambda h: (0, h)),
            pl.BlockSpec((1, HK, HV), lambda h: (h, 0, 0)),
            pl.BlockSpec((1, own, 1), lambda h: (h, 0, 0)),
        ],
        out_shape=[
            jax.ShapeDtypeStruct((own, heads * HV), BF16),
            jax.ShapeDtypeStruct((own, heads * HV), BF16),
            jax.ShapeDtypeStruct((heads, HK, HV), F32),
            jax.ShapeDtypeStruct((heads, own, 1), F32),
        ],
        cost_estimate=pl.CostEstimate(
            flops=heads * 2 * own * HK * HV, bytes_accessed=16 * own * heads * HV, transcendentals=own * heads * HV
        ),
        name="gate_backward",
    )(log_gamma, q, grad, gate, ret)


def backward_kernel(parts, per, lg_ref, q_ref, k_ref, v_ref, state_in_ref, state_grad_ref, cos_ref, sin_ref, *refs):
    g_refs, (g_q_ref, g_k_ref, g_v_ref, inner_ref, acc_k, acc_v) = refs[:parts], refs[parts:]
    log_gamma = lg_ref[pl.program_id(0)]
    down, across = decay_vectors(log_gamma)
    state_in, state_grad = state_in_ref[0], state_grad_ref[0]
    key_scale = 1.0 / math.sqrt(HK)
    total = parts * per

    def put(ref, r, x, factor):
        turned = x * cos_ref[cut(r), :] - pair_swap(x) * sin_ref[cut(r), :]
        ref[cut(r), :] = (turned * factor).astype(BF16)

    for r in range(total):
        g = g_refs[r // per][cut(r % per), :]
        q, k, v = q_ref[cut(r), :], k_ref[cut(r), :], v_ref[cut(r), :]
        tail = down_tail(log_gamma, total * BLOCK - r * BLOCK)
        acc_v[cut(r), :] = nn((k.astype(F32) * tail).astype(BF16), state_grad)
        acc_k[cut(r), :] = nt(v, state_grad) * tail
        g_q = nt(g, state_in) * (down * jnp.exp(log_gamma * (BLOCK * r)))
        for j in range(r + 1):
            kj, vj = k_ref[cut(j), :], v_ref[cut(j), :]
            weights = block_decay(nt(q, kj), r, j, log_gamma, down, across)
            g_scores = block_decay(nt(g, vj), r, j, log_gamma, down, across)
            acc_v[cut(j), :] += tn(weights, g)
            acc_k[cut(j), :] += tn(g_scores, q)
            g_q = g_q + nn(g_scores, kj)
        inner_ref[0, cut(r), :] = jnp.sum(g_q * q.astype(F32), axis=1, keepdims=True)
        put(g_q_ref, r, g_q, 1.0)
    for r in range(total):
        g_k = acc_k[cut(r), :]
        g_v = acc_v[cut(r), :].astype(BF16)
        g_v_ref[cut(r), :] = g_v
        inner_ref[0, cut(r), :] += jnp.sum(g_k * k_ref[cut(r), :].astype(F32), axis=1, keepdims=True) + jnp.sum(
            g_v.astype(F32) * v_ref[cut(r), :].astype(F32), axis=1, keepdims=True
        )
        put(g_k_ref, r, g_k, key_scale)


def down_tail(log_gamma, start):
    m = lax.broadcasted_iota(jnp.int32, (BLOCK, 1), 0).astype(F32)
    return jnp.exp((start - m) * log_gamma)


def retention_backward(log_gamma, q, k, v, state_in, state_grad, cosine, sine, g_ret):
    rows = q.shape[0]
    heads = q.shape[1] // HK
    parts = len(g_ret)
    own = rows // parts
    blocks = rows // BLOCK
    pairs = blocks * (blocks + 1) // 2
    flops = heads * 2 * (pairs * BLOCK * BLOCK * (3 * HK + 2 * HV) + 3 * rows * HK * HV)
    head_keys = pl.BlockSpec((rows, HK), lambda h: (0, h))
    head_values = pl.BlockSpec((rows, HV), lambda h: (0, h))
    head_state = pl.BlockSpec((1, HK, HV), lambda h: (h, 0, 0))
    table = pl.BlockSpec((rows, HK), lambda h: (0, 0))
    return pl.pallas_call(
        lambda *refs: backward_kernel(parts, own // BLOCK, *refs),
        grid=(heads,),
        in_specs=[
            pl.BlockSpec(memory_space=pltpu.SMEM),
            head_keys,
            head_keys,
            head_values,
            head_state,
            head_state,
            table,
            table,
            *[pl.BlockSpec((own, HV), lambda h: (0, h))] * parts,
        ],
        out_specs=[head_keys, head_keys, head_values, pl.BlockSpec((1, rows, 1), lambda h: (h, 0, 0))],
        out_shape=[
            jax.ShapeDtypeStruct((rows, heads * HK), BF16),
            jax.ShapeDtypeStruct((rows, heads * HK), BF16),
            jax.ShapeDtypeStruct((rows, heads * HV), BF16),
            jax.ShapeDtypeStruct((heads, rows, 1), F32),
        ],
        scratch_shapes=[pltpu.VMEM((rows, HK), F32), pltpu.VMEM((rows, HV), F32)],
        cost_estimate=pl.CostEstimate(flops=flops, bytes_accessed=16 * rows * heads * HK, transcendentals=0),
        name="retention_backward",
    )(log_gamma, q, k, v, state_in, state_grad, cosine, sine, *g_ret)


def after(x, *before):
    return lax.optimization_barrier((x, *before))[0]


def on_device(
    layer_input,
    gain_attn,
    w_query,
    w_key,
    w_value,
    w_retgate,
    w_out,
    gain_mlp,
    w_gate,
    w_up,
    w_down,
    cotangent,
):
    data = ("dp", "ctx")
    rows, width = layer_input.shape
    n_tp, at_tp = lax.axis_size("tp"), lax.axis_index("tp")
    features = width * n_tp
    heads = w_query.shape[1] // HK
    units = w_gate.shape[1]

    parts = 2
    own = rows // parts
    cuts = [slice(c * own, (c + 1) * own) for c in range(parts)]

    qk = heads * HK
    vw = heads * HV
    attn_shard = jnp.concatenate([w_query, w_key, w_value, w_retgate, w_out], axis=1)
    attn_full = lax.all_gather(attn_shard, data, axis=0, tiled=True)
    in_full, out_full = attn_full[:, : 2 * qk + 2 * vw], attn_full[:, 2 * qk + 2 * vw :]

    gains = small_gather(jnp.stack([gain_attn, gain_mlp]), "tp")

    def normed_full(blocks, gain_all):
        squares = sum(jnp.sum(jnp.square(b.astype(F32)), axis=1, keepdims=True) for b in blocks)
        scale = lax.rsqrt(squares / features + EPSILON)
        done = []
        for k, b in enumerate(blocks):
            gain = lax.dynamic_slice(gain_all, (0, ((at_tp - k) % n_tp) * width), (1, width))
            done.append((b.astype(F32) * scale * gain).astype(BF16))
        return place(done, "tp", BF16), scale

    log_gamma = jnp.log1p(-jnp.exp2(-5.0 - (at_tp * heads + jnp.arange(heads)).astype(F32)))
    log_block = rows * log_gamma
    positions = lax.axis_index("ctx") * rows + jnp.arange(rows)
    frequencies = jnp.exp(-math.log(10000.0) * jnp.linspace(0.0, 1.0, HK // 2, dtype=F32))
    angles = positions.astype(F32)[:, None] * frequencies[None, :]
    cosine = jnp.repeat(jnp.cos(angles), 2, axis=1)
    sine = jnp.stack([-jnp.sin(angles), jnp.sin(angles)], axis=2).reshape(rows, HK)
    steps = jnp.arange(rows).astype(F32)
    tail_decay = [jnp.exp((rows - steps) * log_gamma[h])[:, None] for h in range(heads)]

    x_blocks = line_gather(layer_input, "tp")
    normed, scale_attn = normed_full(x_blocks, gains[0:1])
    grad_full = lax.all_gather(after(cotangent, x_blocks[1]), "tp", axis=1, tiled=True)
    mlp_shard = jnp.concatenate([after(w_gate, normed), w_up, w_down], axis=1)
    mlp_full = lax.all_gather(mlp_shard, data, axis=0, tiled=True)
    gate_up_full, down_full = mlp_full[:, : 2 * units], mlp_full[:, 2 * units :]
    q, k = project(normed, attn_full, heads, cosine, sine)
    v = nn(normed, in_full[:, 2 * qk : 2 * qk + vw]).astype(BF16)
    keyed = [
        (k[:, h * HK : (h + 1) * HK].astype(F32) * tail_decay[h]).astype(BF16) for h in range(heads)
    ]
    local_state = jnp.stack([tn(keyed[h], v[:, h * HV : (h + 1) * HV]) for h in range(heads)])
    gate_pre = nn(after(normed, local_state), in_full[:, 2 * qk + vw :])
    state_in = states_before(local_state, log_block, "ctx").astype(BF16)
    gated, retained = [], []
    for c in range(parts):
        one, other = retention_forward(c, parts, log_gamma, q, k, v, gate_pre, state_in)
        gated.append(one)
        retained.append(other)

    x_own = layer_input.astype(F32)
    middle, normed_mlp, scale_mlp, hidden, grad_acts, inner_mlp, grad_middle, grad_attn = ([] for _ in range(8))
    gain_mlp_sum = 0.0

    def norm_back(own_rows, scale, gain, inner, partial):
        grad_normed, _ = line_scatter(partial, "tp")
        hat = own_rows * scale
        grad = scale * (grad_normed * gain[None, :] - hat * (inner[:, None] / features))
        return grad, jnp.sum(grad_normed * hat, axis=0)

    def row_total(inner):
        lanes = 128
        return swap_sum(inner.reshape(-1, lanes), "tp").reshape(-1)

    branch = [line_scatter(nt(gated[c], out_full).astype(BF16), "tp")[0] for c in range(parts)]
    for c in range(parts):
        middle.append(x_own[cuts[c]] + branch[c])
        blocks = line_gather(middle[c].astype(BF16), "tp")
        one, other = normed_full(blocks, gains[1:2])
        normed_mlp.append(one)
        scale_mlp.append(other)
    for c in range(parts):
        gate_up = nn(normed_mlp[c], gate_up_full)
        gate_act, up_act = gate_up[:, :units], gate_up[:, units:]
        grad_hidden = nn(grad_full[cuts[c]], down_full)
        cdf = 0.5 * (1.0 + lax.erf(gate_act * math.sqrt(0.5)))
        gelu = gate_act * cdf
        density = jnp.exp(-0.5 * gate_act * gate_act) * (1.0 / math.sqrt(2.0 * math.pi))
        hidden.append((gelu * up_act).astype(BF16))
        grad_gate_act = (grad_hidden * up_act * (cdf + gate_act * density)).astype(BF16)
        grad_up_act = (grad_hidden * gelu).astype(BF16)
        inner_mlp.append(
            jnp.sum(grad_gate_act.astype(F32) * gate_act + grad_up_act.astype(F32) * up_act, axis=1)
        )
        grad_acts.append(jnp.concatenate([grad_gate_act, grad_up_act], axis=1))
    for c in range(parts):
        back = nt(grad_acts[c], gate_up_full).astype(BF16)
        grad_mid, gain_sum = norm_back(middle[c], scale_mlp[c], gain_mlp, row_total(inner_mlp[c]), back)
        gain_mlp_sum = gain_mlp_sum + gain_sum
        grad_middle.append(cotangent[cuts[c]].astype(F32) + grad_mid)
    for c in range(parts):
        grad_attn.append(place(line_gather(grad_middle[c].astype(BF16), "tp"), "tp", BF16))
    hidden_all = jnp.concatenate(hidden)
    mlp_parts = nt(hidden_all, down_full).astype(BF16)
    grad_down = tn(grad_full, hidden_all).astype(BF16)
    grad_gate_up = tn(jnp.concatenate(normed_mlp), jnp.concatenate(grad_acts)).astype(BF16)

    grad_attn[0] = after(grad_attn[0], grad_gate_up, grad_down, mlp_parts)
    mlp_parts = after(mlp_parts, grad_attn[0])
    mlp_out, mlp_early = line_scatter(mlp_parts, "tp")
    layer_output = (jnp.concatenate(middle) + mlp_out).astype(BF16)
    g_gate, g_ret = [], []
    partial_state = 0.0
    inner_attn = []
    for c in range(parts):
        grad_gated = nn(grad_attn[c], out_full)
        gg, gr, ps, inner = gate_backward(c, parts, log_gamma, q, grad_gated, gate_pre, retained[c])
        g_gate.append(gg)
        g_ret.append(gr)
        partial_state = partial_state + ps
        inner_attn.append(jnp.sum(inner[:, :, 0], axis=0))
    state_grad, got = states_after(partial_state, log_block, "ctx")
    state_grad = state_grad.astype(BF16)
    g_gate = jnp.concatenate(g_gate)
    grad_out = tn(after(jnp.concatenate(grad_attn), got, mlp_early[0]), jnp.concatenate(gated)).astype(BF16)
    grad_retgate = tn(normed, after(g_gate, got, mlp_early[0])).astype(BF16)
    g_q, g_k, g_v, inner = retention_backward(
        log_gamma, q, k, v, state_in, after(state_grad, grad_out, grad_retgate, mlp_early[-1]), cosine, sine, g_ret
    )
    inner_attn = jnp.concatenate(inner_attn) + jnp.sum(inner[:, :, 0], axis=0)
    grads_attn = jnp.concatenate([g_q, g_k, g_v, g_gate], axis=1)
    back = []
    for c in range(parts):
        back.append(nt(after(grads_attn[cuts[c]], *back), in_full).astype(BF16))
    grad_qkv_w = tn(normed, after(grads_attn[:, : 2 * qk + vw], *back, mlp_out)).astype(BF16)
    inner_attn = row_total(inner_attn)
    grad_input, gain_attn_sum = [], 0.0
    for c in range(parts):
        grad_in, gain_sum = norm_back(x_own[cuts[c]], scale_attn[cuts[c]], gain_attn, inner_attn[cuts[c]], back[c])
        grad_input.append((grad_middle[c] + grad_in).astype(BF16))
        gain_attn_sum = gain_attn_sum + gain_sum
    grad_input = jnp.concatenate(grad_input)

    def shard(grad):
        return lax.psum_scatter(grad, data, scatter_dimension=0, tiled=True).astype(F32)

    s_down = shard(grad_down)
    s_gate_up = shard(grad_gate_up)
    s_out = shard(grad_out)
    s_retgate = shard(grad_retgate)
    s_qkv = shard(grad_qkv_w)
    s_query, s_key, s_value = s_qkv[:, :qk], s_qkv[:, qk : 2 * qk], s_qkv[:, 2 * qk :]
    gain_sums = swap_sum(swap_sum(jnp.stack([gain_attn_sum, gain_mlp_sum]), "ctx"), "dp")
    return (
        layer_output,
        grad_input,
        gain_sums[0],
        s_query,
        s_key,
        s_value,
        s_retgate,
        s_out,
        gain_sums[1],
        s_gate_up[:, :units],
        s_gate_up[:, units:],
        s_down,
    )


def solution(mesh):
    tokens = P(("dp", "ctx"), "tp")
    gain = P("tp")
    weight = P(("dp", "ctx"), "tp")

    return jax.shard_map(
        on_device,
        mesh=mesh,
        in_specs=(tokens, gain, weight, weight, weight, weight, weight, gain, weight, weight, weight, tokens),
        out_specs=(tokens, tokens, gain, weight, weight, weight, weight, weight, gain, weight, weight, weight),
        check_vma=False,
    )
```

profile of v0, /device:TPU:0, one launch (start us, length us, event | category | flops | bytes accessed | tf_op | source)
XLA Modules:
  0.0 903.5 jit_solution(2858535728260957788)
XLA Ops:
  13.3 5.7 collective-permute-start
  19.0 21.2 %collective-permute-done.2 = bf16[1024,512]{1,0:T(8,128)(2,1)S(1)} collective-permute-done((bf16[1024,512]{1,0:T(8,128)(2,1)S(1)}, bf16[1024,512]{1,0:T(8,128)(2,1)S(1)}, u32[]{:S(2)}, u32[]{:S(2)}) %collective-permute-start.2) | collective-permute-done | bytes 1048608 | tf_op jit(solution)/shard_map/ppermute | solution.py:51
  43.1 5.5 collective-permute-start.6
  52.5 14.2 %collective-permute-done.3 = bf16[1024,512]{1,0:T(8,128)(2,1)} collective-permute-done((bf16[1024,512]{1,0:T(8,128)(2,1)S(1)}, bf16[1024,512]{1,0:T(8,128)(2,1)}, u32[]{:S(2)}, u32[]{:S(2)}) %collective-permute-start.3) | collective-permute-done | bytes 1048608 | tf_op jit(solution)/shard_map/ppermute | solution.py:51
  71.1 24.5 %collective-permute-done.4 = bf16[1024,512]{1,0:T(8,128)(2,1)S(1)} collective-permute-done((bf16[1024,512]{1,0:T(8,128)(2,1)}, bf16[1024,512]{1,0:T(8,128)(2,1)S(1)}, u32[]{:S(2)}, u32[]{:S(2)}) %collective-permute-start.4) | collective-permute-done | bytes 1048608 | tf_op jit(solution)/shard_map/ppermute | solution.py:46
  122.9 9.7 %project.1 = (bf16[1024,512]{1,0:T(8,128)(2,1)}, bf16[1024,512]{1,0:T(8,128)(2,1)}) custom-call(bf16[1024,2048]{1,0:T(8,128)(2,1)} %fusion.116.refs_0_, bf16[2048,4096]{1,0:T(8,128)(2,1)} %all-gather.4.cloned.1.call-done.refs_1_, f32[1024,256]{1,0:T(8,128)} %copy.29.refs_2_.refs_6_, f32[1024,256]{1,0:T(8,128)} %copy.30.refs_3_.refs_7_), custom_call_target="tpu_custom_call" | custom-call | flops 4294967296 | bytes 10485760 | tf_op jit(solution)/shard_map/project/pallas_call | solution.py:163
  132.6 8.0 fusion.82.refs_3_
  148.4 9.9 %fusion.12.refs_4_.refs_3_ = f32[1024,1024]{1,0:T(8,128)} fusion(bf16[1024,2048]{1,0:T(8,128)(2,1)} %fusion.116.refs_0_, bf16[2048,4096]{1,0:T(8,128)(2,1)} %all-gather.4.cloned.1.call-done.refs_1_), kind=kOutput, calls=%fused_computation.15 | convolution fusion | flops 4294967296 | bytes 12582912 | tf_op jit(solution)/shard_map/dot_general | solution.py:20
  158.3 14.4 %collective-permute-done.9 = bf16[2,256,512]{2,1,0:T(8,128)(2,1)S(1)} collective-permute-done((bf16[2,256,512]{2,1,0:T(8,128)(2,1)S(1)}, bf16[2,256,512]{2,1,0:T(8,128)(2,1)S(1)}, u32[]{:S(2)}, u32[]{:S(2)}) %collective-permute-start.9) | collective-permute-done | bytes 524320 | tf_op jit(solution)/shard_map/ppermute | solution.py:115
  173.8 7.3 retention_forward.3
  230.1 5.2 collective-permute-start.17
  248.3 14.6 %collective-permute-done.17 = bf16[512,512]{1,0:T(8,128)(2,1)} collective-permute-done((bf16[512,512]{1,0:T(8,128)(2,1)}, bf16[512,512]{1,0:T(8,128)(2,1)}, u32[]{:S(2)}, u32[]{:S(2)}) %collective-permute-start.17) | collective-permute-done | bytes 524320 | tf_op jit(solution)/shard_map/ppermute | solution.py:89
  262.9 15.1 %collective-permute-done.19 = bf16[512,512]{1,0:T(8,128)(2,1)} collective-permute-done((bf16[512,512]{1,0:T(8,128)(2,1)}, bf16[512,512]{1,0:T(8,128)(2,1)}, u32[]{:S(2)}, u32[]{:S(2)}) %collective-permute-start.19) | collective-permute-done | bytes 524320 | tf_op jit(solution)/shard_map/ppermute | solution.py:90
  278.0 5.9 collective-permute-done.12
  283.9 27.1 %collective-permute-done.14 = bf16[512,512]{1,0:T(8,128)(2,1)} collective-permute-done((bf16[512,512]{1,0:T(8,128)(2,1)S(1)}, bf16[512,512]{1,0:T(8,128)(2,1)}, u32[]{:S(2)}, u32[]{:S(2)}) %collective-permute-start.14) | collective-permute-done | bytes 524320 | tf_op jit(solution)/shard_map/ppermute | solution.py:90
  323.5 17.2 %collective-permute-done.22 = bf16[512,512]{1,0:T(8,128)(2,1)S(1)} collective-permute-done((bf16[512,512]{1,0:T(8,128)(2,1)S(1)}, bf16[512,512]{1,0:T(8,128)(2,1)S(1)}, u32[]{:S(2)}, u32[]{:S(2)}) %collective-permute-start.22) | collective-permute-done | bytes 524320 | tf_op jit(solution)/shard_map/ppermute | solution.py:51
  342.7 6.8 collective-permute-done.25
  353.2 9.9 %collective-permute-done.23 = bf16[512,512]{1,0:T(8,128)(2,1)S(1)} collective-permute-done((bf16[512,512]{1,0:T(8,128)(2,1)S(1)}, bf16[512,512]{1,0:T(8,128)(2,1)S(1)}, u32[]{:S(2)}, u32[]{:S(2)}) %collective-permute-start.23) | collective-permute-done | bytes 524320 | tf_op jit(solution)/shard_map/ppermute | solution.py:51
  364.7 9.7 %collective-permute-done.28 = bf16[512,512]{1,0:T(8,128)(2,1)S(1)} collective-permute-done((bf16[512,512]{1,0:T(8,128)(2,1)S(1)}, bf16[512,512]{1,0:T(8,128)(2,1)S(1)}, u32[]{:S(2)}, u32[]{:S(2)}) %collective-permute-start.28) | collective-permute-done | bytes 524320 | tf_op jit(solution)/shard_map/ppermute | solution.py:51
  376.1 9.5 %collective-permute-done.24 = bf16[512,512]{1,0:T(8,128)(2,1)S(1)} collective-permute-done((bf16[512,512]{1,0:T(8,128)(2,1)S(1)}, bf16[512,512]{1,0:T(8,128)(2,1)S(1)}, u32[]{:S(2)}, u32[]{:S(2)}) %collective-permute-start.24) | collective-permute-done | bytes 524320 | tf_op jit(solution)/shard_map/ppermute | solution.py:46
  386.1 9.8 %collective-permute-done.29 = bf16[512,512]{1,0:T(8,128)(2,1)S(1)} collective-permute-done((bf16[512,512]{1,0:T(8,128)(2,1)S(1)}, bf16[512,512]{1,0:T(8,128)(2,1)S(1)}, u32[]{:S(2)}, u32[]{:S(2)}) %collective-permute-start.29) | collective-permute-done | bytes 524320 | tf_op jit(solution)/shard_map/ppermute | solution.py:46
  403.1 11.3 %fusion.10 = f32[512,2048]{1,0:T(8,128)} fusion(bf16[512,2048]{1,0:T(8,128)(2,1)} %get-tuple-element.172, bf16[2048,3072]{1,0:T(8,128)(2,1)} %all-gather.6.cloned.1.call-done), kind=kOutput, calls=%fused_computation.13 | convolution fusion | flops 4294967296 | bytes 14680064 | tf_op jit(solution)/shard_map/dot_general | solution.py:20
  414.4 9.0 add_reduce_fusion.1
  424.4 6.0 fusion.37
  443.3 6.3 fusion.40
  457.7 8.4 convolution_convert_fusion.4
  489.7 6.9 collective-permute-start.49
  500.2 9.9 %collective-permute-start.37 = (bf16[512,512]{1,0:T(8,128)(2,1)S(1)}, bf16[512,512]{1,0:T(8,128)(2,1)}, u32[]{:S(2)}, u32[]{:S(2)}) collective-permute-start(bf16[512,512]{1,0:T(8,128)(2,1)S(1)} %get-tuple-element.89), channel_id=1, source_target_pairs={{0,1},{1,2},{2,3},{4,5},{5,6},{6,7},{8,9},{9,10},{10,11},{12,13},{... | collective-permute-start | bytes 1572872 | tf_op jit(solution)/shard_map/ppermute | solution.py:50
  514.7 8.2 collective-permute-start.54
  526.3 25.4 %convolution_convert_fusion.1 = bf16[2048,2048]{1,0:T(8,128)(2,1)} fusion(bf16[512,2048]{1,0:T(8,128)(2,1)S(1)} %copy-done.38, bf16[512,2048]{1,0:T(8,128)(2,1)} %get-tuple-element.172, bf16[512,1024]{1,0:T(8,128)(2,1)S(1)} %copy-done.76, bf16[512,1024]{1,0:T(8,128)(2,1)S(1)} %copy-done.75, bf16[512,1024]{1,0:T(8,128)(2,1)S(1)} %copy-done.74, ...), kind=kOutput, calls=%fused_computation.5 | convolution fusion | flops 8619294720 | bytes 16777216 | tf_op jit(solution)/shard_map/dot_general | solution.py:24
  556.6 7.4 convolution_convert_fusion.5
  564.0 11.2 %collective-permute-done.57 = bf16[512,512]{1,0:T(8,128)(2,1)S(1)} collective-permute-done((bf16[512,512]{1,0:T(8,128)(2,1)}, bf16[512,512]{1,0:T(8,128)(2,1)S(1)}, u32[]{:S(2)}, u32[]{:S(2)}) %collective-permute-start.57) | collective-permute-done | bytes 524320 | tf_op jit(solution)/shard_map/ppermute | solution.py:51
  576.6 6.0 collective-permute-done.41
  592.6 6.5 fusion.43.refs_2_
  599.1 5.4 gate_backward.3
  604.5 6.5 fusion.45.refs_2_
  611.0 5.4 gate_backward.2
  624.6 6.2 convolution_convert_fusion.3
  634.0 8.8 convolution_convert_fusion.2
  650.4 24.5 %collective-permute-done.60 = bf16[2,256,512]{2,1,0:T(8,128)(2,1)S(1)} collective-permute-done((bf16[2,256,512]{2,1,0:T(8,128)(2,1)}, bf16[2,256,512]{2,1,0:T(8,128)(2,1)S(1)}, u32[]{:S(2)}, u32[]{:S(2)}) %collective-permute-start.60) | collective-permute-done | bytes 524320 | tf_op jit(solution)/shard_map/ppermute | solution.py:130
  684.8 21.2 %retention_backward.1 = (bf16[1024,512]{1,0:T(8,128)(2,1)}, bf16[1024,512]{1,0:T(8,128)(2,1)}, bf16[1024,1024]{1,0:T(8,128)(2,1)}, f32[2,1024,1]{2,1,0:T(8,128)}) custom-call(f32[2]{0:T(128)} %copy-done.61, bf16[1024,512]{1,0:T(8,128)(2,1)} %get-tuple-element.40.refs_1_, bf16[1024,512]{1,0:T(8,128)(2,1)} %get-tuple-element.41.refs_2_, ...), custom_call_target="tpu_custom_call" | custom-call | flops 6308233216 | bytes 8388608 | tf_op jit(solution)/shard_map/retention_backward/pallas_call | solution.py:361
  713.1 12.4 %fusion.31 = bf16[512,2048]{1,0:T(8,128)(2,1)} fusion(bf16[512,3072]{1,0:T(8,128)(2,1)} %get-tuple-element.108, bf16[2048,4096]{1,0:T(8,128)(2,1)} %all-gather.4.cloned.1.call-done.refs_1_), kind=kOutput, calls=%fused_computation.42 | convolution fusion | flops 6443499520 | bytes 17825792 | tf_op jit(solution)/shard_map/dot_general | solution.py:28
  727.8 10.0 %fusion.34 = bf16[512,2048]{1,0:T(8,128)(2,1)} fusion(bf16[512,3072]{1,0:T(8,128)(2,1)} %get-tuple-element.66, bf16[2048,4096]{1,0:T(8,128)(2,1)S(1)} %bitcast.61), kind=kOutput, calls=%fused_computation.43 | convolution fusion | flops 6443499520 | bytes 17825792 | tf_op jit(solution)/shard_map/dot_general | solution.py:28
  741.5 13.6 %convolution_convert_fusion = bf16[2048,2048]{1,0:T(8,128)(2,1)} fusion(bf16[1024,2048]{1,0:T(8,128)(2,1)} %fusion.116.refs_0_, bf16[1024,2048]{1,0:T(8,128)(2,1)S(1)} %copy-done.30), kind=kOutput, calls=%fused_computation.4 | convolution fusion | flops 8594128896 | bytes 16777216 | tf_op jit(solution)/shard_map/dot_general | solution.py:24
  763.8 9.7 %collective-permute-done.61 = bf16[512,512]{1,0:T(8,128)(2,1)S(1)} collective-permute-done((bf16[512,512]{1,0:T(8,128)(2,1)S(1)}, bf16[512,512]{1,0:T(8,128)(2,1)S(1)}, u32[]{:S(2)}, u32[]{:S(2)}) %collective-permute-start.61) | collective-permute-done | bytes 524320 | tf_op jit(solution)/shard_map/ppermute | solution.py:81
  774.9 5.3 collective-permute-start.62
  820.3 8.1 collective-permute-done.67
  847.0 45.9 %reduce-scatter.6.cloned.1.call-done = bf16[256,2048]{1,0:T(8,128)(2,1)} async-done(((bf16[2048,2048]{1,0:T(8,128)(2,1)}), bf16[256,2048]{1,0:T(8,128)(2,1)}) %reduce-scatter.6.cloned.1.call-update) | async-done | bytes 1048592 | tf_op jit(solution)/shard_map/reduce_scatter | solution.py:548
  (453 shorter events, 330.1 us)
Async XLA Ops:
  7.2 115.8 %all-gather.4.cloned.1.call-start = ((), (), s32[]{:S(2)}) async-start(), calls=%async_computation.5 | async-start | bytes 18874368 | tf_op jit(solution)/shard_map/all_gather | solution.py:420
  11.9 391.1 %all-gather.6.cloned.1.call-start = ((), (), s32[]{:S(2)}) async-start(), calls=%async_computation.6 | async-start | bytes 14155776 | tf_op jit(solution)/shard_map/all_gather | solution.py:448
  12.0 28.1 %collective-permute-start.2 = (bf16[1024,512]{1,0:T(8,128)(2,1)S(1)}, bf16[1024,512]{1,0:T(8,128)(2,1)S(1)}, u32[]{:S(2)}, u32[]{:S(2)}) collective-permute-start(bf16[1024,512]{1,0:T(8,128)(2,1)S(1)} %copy-done.24), channel_id=1, source_target_pairs={{3,2},{2,1},{1,0},{7,6},{6,5},{5,4},{11,10},{10,9},{9,8},{15,14},{... | collective-permute-start | bytes 3145736 | tf_op jit(solution)/shard_map/ppermute | solution.py:51
  13.3 28.1 %collective-permute-start = (bf16[1024,512]{1,0:T(8,128)(2,1)S(1)}, bf16[1024,512]{1,0:T(8,128)(2,1)S(1)}, u32[]{:S(2)}, u32[]{:S(2)}) collective-permute-start(bf16[1024,512]{1,0:T(8,128)(2,1)S(1)} %copy-done.24), channel_id=1, source_target_pairs={{0,1},{1,2},{2,3},{4,5},{5,6},{6,7},{8,9},{9,10},{10,11},{12,13},{... | collective-permute-start | bytes 3145736 | tf_op jit(solution)/shard_map/ppermute | solution.py:50
  40.1 26.6 %collective-permute-start.3 = (bf16[1024,512]{1,0:T(8,128)(2,1)S(1)}, bf16[1024,512]{1,0:T(8,128)(2,1)}, u32[]{:S(2)}, u32[]{:S(2)}) collective-permute-start(bf16[1024,512]{1,0:T(8,128)(2,1)S(1)} %collective-permute-done.2), channel_id=1, source_target_pairs={{2,1},{1,0},{6,5},{5,4},{10,9},{9,8},{14,13},{13,12},{18,17},{17,1... | collective-permute-start | bytes 3145736 | tf_op jit(solution)/shard_map/ppermute | solution.py:51
  41.4 25.3 %collective-permute-start.1 = (bf16[1024,512]{1,0:T(8,128)(2,1)S(1)}, bf16[1024,512]{1,0:T(8,128)(2,1)}, u32[]{:S(2)}, u32[]{:S(2)}) collective-permute-start(bf16[1024,512]{1,0:T(8,128)(2,1)S(1)} %collective-permute-done), channel_id=1, source_target_pairs={{1,2},{2,3},{5,6},{6,7},{9,10},{10,11},{13,14},{14,15},{17,18},{18... | collective-permute-start | bytes 3145736 | tf_op jit(solution)/shard_map/ppermute | solution.py:50
  43.1 27.8 %collective-permute-start.6 = (f32[2,512]{1,0:T(2,128)S(1)}, f32[2,512]{1,0:T(2,128)S(1)}, u32[]{:S(2)}, u32[]{:S(2)}) collective-permute-start(f32[2,512]{1,0:T(2,128)S(1)} %get-tuple-element.170), channel_id=1, source_target_pairs={{0,2},{1,3},{2,0},{3,1},{4,6},{5,7},{6,4},{7,5},{8,10},{9,11},{10,... | collective-permute-start | bytes 12296 | tf_op jit(solution)/shard_map/ppermute | solution.py:98
  48.6 22.3 %collective-permute-start.5 = (f32[2,512]{1,0:T(2,128)S(1)}, f32[2,512]{1,0:T(2,128)S(1)}, u32[]{:S(2)}, u32[]{:S(2)}) collective-permute-start(f32[2,512]{1,0:T(2,128)S(1)} %get-tuple-element.170), channel_id=1, source_target_pairs={{0,1},{1,2},{2,3},{3,0},{4,5},{5,6},{6,7},{7,4},{8,9},{9,10},{10,1... | collective-permute-start | bytes 12296 | tf_op jit(solution)/shard_map/ppermute | solution.py:98
  69.3 26.3 %collective-permute-start.4 = (bf16[1024,512]{1,0:T(8,128)(2,1)}, bf16[1024,512]{1,0:T(8,128)(2,1)S(1)}, u32[]{:S(2)}, u32[]{:S(2)}) collective-permute-start(bf16[1024,512]{1,0:T(8,128)(2,1)} %get-tuple-element.107), channel_id=1, source_target_pairs={{2,3},{1,0},{6,7},{5,4},{10,11},{9,8},{14,15},{13,12},{18,19},{17,... | collective-permute-start | bytes 3145736 | tf_op jit(solution)/shard_map/ppermute | solution.py:46
  107.7 306.7 %all-gather.8.cloned.1.call-start = ((), (), s32[]{:S(2)}) async-start(), calls=%async_computation.7 | async-start | bytes 5242880 | tf_op jit(solution)/shard_map/all_gather | solution.py:446
  146.8 25.9 %collective-permute-start.9 = (bf16[2,256,512]{2,1,0:T(8,128)(2,1)S(1)}, bf16[2,256,512]{2,1,0:T(8,128)(2,1)S(1)}, u32[]{:S(2)}, u32[]{:S(2)}) collective-permute-start(bf16[2,256,512]{2,1,0:T(8,128)(2,1)S(1)} %fusion.112), channel_id=1, source_target_pairs={{0,8},{4,12},{8,0},{12,4},{1,9},{5,13},{9,1},{13,5},{2,10},{6,14},... | collective-permute-start | bytes 1572872 | tf_op jit(solution)/shard_map/ppermute | solution.py:115
  218.1 22.3 %collective-permute-start.11 = (bf16[512,512]{1,0:T(8,128)(2,1)}, bf16[512,512]{1,0:T(8,128)(2,1)S(1)}, u32[]{:S(2)}, u32[]{:S(2)}) collective-permute-start(bf16[512,512]{1,0:T(8,128)(2,1)} %get-tuple-element.126), channel_id=1, source_target_pairs={{0,1},{1,2},{4,5},{5,6},{8,9},{9,10},{12,13},{13,14},{16,17},{17,1... | collective-permute-start | bytes 1572872 | tf_op jit(solution)/shard_map/ppermute | solution.py:89
  224.1 608.3 %reduce-scatter.14.cloned.1.call-start = ((), (), s32[]{:S(2)}) async-start(), calls=%async_computation.12 | async-start | bytes 4718592 | tf_op jit(solution)/shard_map/reduce_scatter | solution.py:548
  230.1 32.8 %collective-permute-start.17 = (bf16[512,512]{1,0:T(8,128)(2,1)}, bf16[512,512]{1,0:T(8,128)(2,1)}, u32[]{:S(2)}, u32[]{:S(2)}) collective-permute-start(bf16[512,512]{1,0:T(8,128)(2,1)} %get-tuple-element.143), channel_id=1, source_target_pairs={{0,1},{1,2},{2,3},{4,5},{5,6},{6,7},{8,9},{9,10},{10,11},{12,13},{... | collective-permute-start | bytes 1572872 | tf_op jit(solution)/shard_map/ppermute | solution.py:89
  235.3 42.8 %collective-permute-start.19 = (bf16[512,512]{1,0:T(8,128)(2,1)}, bf16[512,512]{1,0:T(8,128)(2,1)}, u32[]{:S(2)}, u32[]{:S(2)}) collective-permute-start(bf16[512,512]{1,0:T(8,128)(2,1)} %get-tuple-element.144), channel_id=1, source_target_pairs={{3,2},{2,1},{1,0},{7,6},{6,5},{5,4},{11,10},{10,9},{9,8},{15,14},{... | collective-permute-start | bytes 1572872 | tf_op jit(solution)/shard_map/ppermute | solution.py:90
  242.7 41.2 %collective-permute-start.12 = (bf16[512,512]{1,0:T(8,128)(2,1)}, bf16[512,512]{1,0:T(8,128)(2,1)S(1)}, u32[]{:S(2)}, u32[]{:S(2)}) collective-permute-start(bf16[512,512]{1,0:T(8,128)(2,1)} %get-tuple-element.141), channel_id=1, source_target_pairs={{0,1},{1,2},{2,3},{4,5},{5,6},{6,7},{8,9},{9,10},{10,11},{12,13},{... | collective-permute-start | bytes 1572872 | tf_op jit(solution)/shard_map/ppermute | solution.py:89
  247.0 64.0 %collective-permute-start.14 = (bf16[512,512]{1,0:T(8,128)(2,1)S(1)}, bf16[512,512]{1,0:T(8,128)(2,1)}, u32[]{:S(2)}, u32[]{:S(2)}) collective-permute-start(bf16[512,512]{1,0:T(8,128)(2,1)S(1)} %get-tuple-element.142), channel_id=1, source_target_pairs={{3,2},{2,1},{1,0},{7,6},{6,5},{5,4},{11,10},{10,9},{9,8},{15,14},{... | collective-permute-start | bytes 1572872 | tf_op jit(solution)/shard_map/ppermute | solution.py:90
  314.4 26.3 %collective-permute-start.22 = (bf16[512,512]{1,0:T(8,128)(2,1)S(1)}, bf16[512,512]{1,0:T(8,128)(2,1)S(1)}, u32[]{:S(2)}, u32[]{:S(2)}) collective-permute-start(bf16[512,512]{1,0:T(8,128)(2,1)S(1)} %get-tuple-element.95), channel_id=1, source_target_pairs={{3,2},{2,1},{1,0},{7,6},{6,5},{5,4},{11,10},{10,9},{9,8},{15,14},{... | collective-permute-start | bytes 1572872 | tf_op jit(solution)/shard_map/ppermute | solution.py:51
  315.6 26.4 %collective-permute-start.20 = (bf16[512,512]{1,0:T(8,128)(2,1)S(1)}, bf16[512,512]{1,0:T(8,128)(2,1)S(1)}, u32[]{:S(2)}, u32[]{:S(2)}) collective-permute-start(bf16[512,512]{1,0:T(8,128)(2,1)S(1)} %get-tuple-element.95), channel_id=1, source_target_pairs={{0,1},{1,2},{2,3},{4,5},{5,6},{6,7},{8,9},{9,10},{10,11},{12,13},{... | collective-permute-start | bytes 1572872 | tf_op jit(solution)/shard_map/ppermute | solution.py:50
  320.2 29.3 %collective-permute-start.25 = (bf16[512,512]{1,0:T(8,128)(2,1)S(1)}, bf16[512,512]{1,0:T(8,128)(2,1)S(1)}, u32[]{:S(2)}, u32[]{:S(2)}) collective-permute-start(bf16[512,512]{1,0:T(8,128)(2,1)S(1)} %get-tuple-element.139), channel_id=1, source_target_pairs={{0,1},{1,2},{2,3},{4,5},{5,6},{6,7},{8,9},{9,10},{10,11},{12,13},{... | collective-permute-start | bytes 1572872 | tf_op jit(solution)/shard_map/ppermute | solution.py:50
  322.2 29.8 %collective-permute-start.27 = (bf16[512,512]{1,0:T(8,128)(2,1)S(1)}, bf16[512,512]{1,0:T(8,128)(2,1)S(1)}, u32[]{:S(2)}, u32[]{:S(2)}) collective-permute-start(bf16[512,512]{1,0:T(8,128)(2,1)S(1)} %get-tuple-element.139), channel_id=1, source_target_pairs={{3,2},{2,1},{1,0},{7,6},{6,5},{5,4},{11,10},{10,9},{9,8},{15,14},{... | collective-permute-start | bytes 1572872 | tf_op jit(solution)/shard_map/ppermute | solution.py:51
  340.7 22.5 %collective-permute-start.23 = (bf16[512,512]{1,0:T(8,128)(2,1)S(1)}, bf16[512,512]{1,0:T(8,128)(2,1)S(1)}, u32[]{:S(2)}, u32[]{:S(2)}) collective-permute-start(bf16[512,512]{1,0:T(8,128)(2,1)S(1)} %collective-permute-done.22), channel_id=1, source_target_pairs={{2,1},{1,0},{6,5},{5,4},{10,9},{9,8},{14,13},{13,12},{18,17},{17,1... | collective-permute-start | bytes 1572872 | tf_op jit(solution)/shard_map/ppermute | solution.py:51
  351.9 22.5 %collective-permute-start.28 = (bf16[512,512]{1,0:T(8,128)(2,1)S(1)}, bf16[512,512]{1,0:T(8,128)(2,1)S(1)}, u32[]{:S(2)}, u32[]{:S(2)}) collective-permute-start(bf16[512,512]{1,0:T(8,128)(2,1)S(1)} %collective-permute-done.27), channel_id=1, source_target_pairs={{2,1},{1,0},{6,5},{5,4},{10,9},{9,8},{14,13},{13,12},{18,17},{17,1... | collective-permute-start | bytes 1572872 | tf_op jit(solution)/shard_map/ppermute | solution.py:51
  363.4 22.2 %collective-permute-start.24 = (bf16[512,512]{1,0:T(8,128)(2,1)S(1)}, bf16[512,512]{1,0:T(8,128)(2,1)S(1)}, u32[]{:S(2)}, u32[]{:S(2)}) collective-permute-start(bf16[512,512]{1,0:T(8,128)(2,1)S(1)} %get-tuple-element.98), channel_id=1, source_target_pairs={{2,3},{1,0},{6,7},{5,4},{10,11},{9,8},{14,15},{13,12},{18,19},{17,... | collective-permute-start | bytes 1572872 | tf_op jit(solution)/shard_map/ppermute | solution.py:46
  423.4 42.9 %collective-permute-start.35 = (f32[4,128]{1,0:T(4,128)S(1)}, f32[4,128]{1,0:T(4,128)S(1)}, u32[]{:S(2)}, u32[]{:S(2)}) collective-permute-start(f32[4,128]{1,0:T(4,128)S(1)} %bitcast.79), channel_id=1, source_target_pairs={{0,1},{1,0},{2,3},{3,2},{4,5},{5,4},{6,7},{7,6},{8,9},{9,8},{10,11... | collective-permute-start | bytes 6152 | tf_op jit(solution)/shard_map/ppermute | solution.py:106
  430.5 22.3 %collective-permute-start.30 = (bf16[512,512]{1,0:T(8,128)(2,1)S(1)}, bf16[512,512]{1,0:T(8,128)(2,1)S(1)}, u32[]{:S(2)}, u32[]{:S(2)}) collective-permute-start(bf16[512,512]{1,0:T(8,128)(2,1)S(1)} %constant_dynamic-slice_fusion.4), channel_id=1, source_target_pairs={{0,1},{3,2},{4,5},{7,6},{8,9},{11,10},{12,13},{15,14},{16,17},{19,... | collective-permute-start | bytes 1572872 | tf_op jit(solution)/shard_map/ppermute | solution.py:81
  454.1 21.7 %collective-permute-start.31 = (bf16[512,512]{1,0:T(8,128)(2,1)}, bf16[512,512]{1,0:T(8,128)(2,1)}, u32[]{:S(2)}, u32[]{:S(2)}) collective-permute-start(bf16[512,512]{1,0:T(8,128)(2,1)} %get-tuple-element.124), channel_id=1, source_target_pairs={{0,1},{1,2},{4,5},{5,6},{8,9},{9,10},{12,13},{13,14},{16,17},{17,1... | collective-permute-start | bytes 1572872 | tf_op jit(solution)/shard_map/ppermute | solution.py:89
  466.1 373.9 %reduce-scatter.10.cloned.1.call-start = ((), (), s32[]{:S(2)}) async-start(), calls=%async_computation.10 | async-start | bytes 4718592 | tf_op jit(solution)/shard_map/reduce_scatter | solution.py:548
  484.5 26.8 %collective-permute-start.53 = (f32[4,128]{1,0:T(4,128)S(1)}, f32[4,128]{1,0:T(4,128)S(1)}, u32[]{:S(2)}, u32[]{:S(2)}) collective-permute-start(f32[4,128]{1,0:T(4,128)S(1)} %bitcast_add_fusion), channel_id=1, source_target_pairs={{0,2},{1,3},{2,0},{3,1},{4,6},{5,7},{6,4},{7,5},{8,10},{9,11},{10,... | collective-permute-start | bytes 6152 | tf_op jit(solution)/shard_map/ppermute | solution.py:106
  500.2 24.0 %collective-permute-start.37 = (bf16[512,512]{1,0:T(8,128)(2,1)S(1)}, bf16[512,512]{1,0:T(8,128)(2,1)}, u32[]{:S(2)}, u32[]{:S(2)}) collective-permute-start(bf16[512,512]{1,0:T(8,128)(2,1)S(1)} %get-tuple-element.89), channel_id=1, source_target_pairs={{0,1},{1,2},{2,3},{4,5},{5,6},{6,7},{8,9},{9,10},{10,11},{12,13},{... | collective-permute-start | bytes 1572872 | tf_op jit(solution)/shard_map/ppermute | solution.py:50
  514.7 36.9 %collective-permute-start.54 = (bf16[512,512]{1,0:T(8,128)(2,1)S(1)}, bf16[512,512]{1,0:T(8,128)(2,1)}, u32[]{:S(2)}, u32[]{:S(2)}) collective-permute-start(bf16[512,512]{1,0:T(8,128)(2,1)S(1)} %get-tuple-element.77), channel_id=1, source_target_pairs={{0,1},{1,2},{2,3},{4,5},{5,6},{6,7},{8,9},{9,10},{10,11},{12,13},{... | collective-permute-start | bytes 1572872 | tf_op jit(solution)/shard_map/ppermute | solution.py:50
  522.9 29.4 %collective-permute-start.56 = (bf16[512,512]{1,0:T(8,128)(2,1)S(1)}, bf16[512,512]{1,0:T(8,128)(2,1)}, u32[]{:S(2)}, u32[]{:S(2)}) collective-permute-start(bf16[512,512]{1,0:T(8,128)(2,1)S(1)} %get-tuple-element.77), channel_id=1, source_target_pairs={{3,2},{2,1},{1,0},{7,6},{6,5},{5,4},{11,10},{10,9},{9,8},{15,14},{... | collective-permute-start | bytes 1572872 | tf_op jit(solution)/shard_map/ppermute | solution.py:51
  524.2 29.5 %collective-permute-start.38 = (bf16[512,512]{1,0:T(8,128)(2,1)}, bf16[512,512]{1,0:T(8,128)(2,1)S(1)}, u32[]{:S(2)}, u32[]{:S(2)}) collective-permute-start(bf16[512,512]{1,0:T(8,128)(2,1)} %collective-permute-done.37), channel_id=1, source_target_pairs={{1,2},{2,3},{5,6},{6,7},{9,10},{10,11},{13,14},{14,15},{17,18},{18... | collective-permute-start | bytes 1572872 | tf_op jit(solution)/shard_map/ppermute | solution.py:50
  524.9 28.8 %collective-permute-start.40 = (bf16[512,512]{1,0:T(8,128)(2,1)}, bf16[512,512]{1,0:T(8,128)(2,1)}, u32[]{:S(2)}, u32[]{:S(2)}) collective-permute-start(bf16[512,512]{1,0:T(8,128)(2,1)} %collective-permute-done.39), channel_id=1, source_target_pairs={{2,1},{1,0},{6,5},{5,4},{10,9},{9,8},{14,13},{13,12},{18,17},{17,1... | collective-permute-start | bytes 1572872 | tf_op jit(solution)/shard_map/ppermute | solution.py:51
  552.4 22.8 %collective-permute-start.57 = (bf16[512,512]{1,0:T(8,128)(2,1)}, bf16[512,512]{1,0:T(8,128)(2,1)S(1)}, u32[]{:S(2)}, u32[]{:S(2)}) collective-permute-start(bf16[512,512]{1,0:T(8,128)(2,1)} %collective-permute-done.56), channel_id=1, source_target_pairs={{2,1},{1,0},{6,5},{5,4},{10,9},{9,8},{14,13},{13,12},{18,17},{17,1... | collective-permute-start | bytes 1572872 | tf_op jit(solution)/shard_map/ppermute | solution.py:51
  554.8 27.8 %collective-permute-start.41 = (bf16[512,512]{1,0:T(8,128)(2,1)S(1)}, bf16[512,512]{1,0:T(8,128)(2,1)S(1)}, u32[]{:S(2)}, u32[]{:S(2)}) collective-permute-start(bf16[512,512]{1,0:T(8,128)(2,1)S(1)} %broadcast_select_fusion.10), channel_id=1, source_target_pairs={{2,3},{1,0},{6,7},{5,4},{10,11},{9,8},{14,15},{13,12},{18,19},{17,... | collective-permute-start | bytes 1572872 | tf_op jit(solution)/shard_map/ppermute | solution.py:46
  585.3 35.7 %collective-permute-start.42 = (bf16[1024,512]{1,0:T(8,128)(2,1)}, bf16[1024,512]{1,0:T(8,128)(2,1)}, u32[]{:S(2)}, u32[]{:S(2)}) collective-permute-start(bf16[1024,512]{1,0:T(8,128)(2,1)} %constant_dynamic-slice_fusion.3), channel_id=1, source_target_pairs={{0,1},{3,2},{4,5},{7,6},{8,9},{11,10},{12,13},{15,14},{16,17},{19,... | collective-permute-start | bytes 3145736 | tf_op jit(solution)/shard_map/ppermute | solution.py:81
  630.8 211.3 %reduce-scatter.8.cloned.1.call-start = ((), (), s32[]{:S(2)}) async-start(), calls=%async_computation.9 | async-start | bytes 4718592 | tf_op jit(solution)/shard_map/reduce_scatter | solution.py:548
  642.9 201.4 %reduce-scatter.12.cloned.1.call-start = ((), (), s32[]{:S(2)}) async-start(), calls=%async_computation.11 | async-start | bytes 9437184 | tf_op jit(solution)/shard_map/reduce_scatter | solution.py:548
  643.6 249.3 %reduce-scatter.6.cloned.1.call-start = ((), (), s32[]{:S(2)}) async-start(), calls=%async_computation.8 | async-start | bytes 9437184 | tf_op jit(solution)/shard_map/reduce_scatter | solution.py:548
  643.7 33.5 %collective-permute-start.43 = (bf16[1024,512]{1,0:T(8,128)(2,1)}, bf16[1024,512]{1,0:T(8,128)(2,1)}, u32[]{:S(2)}, u32[]{:S(2)}) collective-permute-start(bf16[1024,512]{1,0:T(8,128)(2,1)} %get-tuple-element.84), channel_id=1, source_target_pairs={{0,1},{1,2},{4,5},{5,6},{8,9},{9,10},{12,13},{13,14},{16,17},{17,1... | collective-permute-start | bytes 3145736 | tf_op jit(solution)/shard_map/ppermute | solution.py:89
  646.6 30.6 %collective-permute-start.45 = (bf16[1024,512]{1,0:T(8,128)(2,1)}, bf16[1024,512]{1,0:T(8,128)(2,1)}, u32[]{:S(2)}, u32[]{:S(2)}) collective-permute-start(bf16[1024,512]{1,0:T(8,128)(2,1)} %get-tuple-element.112), channel_id=1, source_target_pairs={{3,2},{2,1},{7,6},{6,5},{11,10},{10,9},{15,14},{14,13},{19,18},{18... | collective-permute-start | bytes 3145736 | tf_op jit(solution)/shard_map/ppermute | solution.py:90
  650.4 24.6 %collective-permute-start.60 = (bf16[2,256,512]{2,1,0:T(8,128)(2,1)}, bf16[2,256,512]{2,1,0:T(8,128)(2,1)S(1)}, u32[]{:S(2)}, u32[]{:S(2)}) collective-permute-start(bf16[2,256,512]{2,1,0:T(8,128)(2,1)} %select_convert_fusion), channel_id=1, source_target_pairs={{0,8},{4,12},{8,0},{12,4},{1,9},{5,13},{9,1},{13,5},{2,10},{6,14},... | collective-permute-start | bytes 1572872 | tf_op jit(solution)/shard_map/ppermute | solution.py:130
  681.2 56.6 %collective-permute-start.44 = (bf16[1024,512]{1,0:T(8,128)(2,1)}, bf16[1024,512]{1,0:T(8,128)(2,1)}, u32[]{:S(2)}, u32[]{:S(2)}) collective-permute-start(bf16[1024,512]{1,0:T(8,128)(2,1)} %get-tuple-element.114), channel_id=1, source_target_pairs={{0,1},{1,2},{2,3},{4,5},{5,6},{6,7},{8,9},{9,10},{10,11},{12,13},{... | collective-permute-start | bytes 3145736 | tf_op jit(solution)/shard_map/ppermute | solution.py:89
  683.5 54.3 %collective-permute-start.46 = (bf16[1024,512]{1,0:T(8,128)(2,1)}, bf16[1024,512]{1,0:T(8,128)(2,1)}, u32[]{:S(2)}, u32[]{:S(2)}) collective-permute-start(bf16[1024,512]{1,0:T(8,128)(2,1)} %get-tuple-element.115), channel_id=1, source_target_pairs={{3,2},{2,1},{1,0},{7,6},{6,5},{5,4},{11,10},{10,9},{9,8},{15,14},{... | collective-permute-start | bytes 3145736 | tf_op jit(solution)/shard_map/ppermute | solution.py:90
  762.4 22.4 %collective-permute-start.68 = (bf16[512,512]{1,0:T(8,128)(2,1)S(1)}, bf16[512,512]{1,0:T(8,128)(2,1)S(1)}, u32[]{:S(2)}, u32[]{:S(2)}) collective-permute-start(bf16[512,512]{1,0:T(8,128)(2,1)S(1)} %constant_dynamic-slice_fusion), channel_id=1, source_target_pairs={{0,1},{3,2},{4,5},{7,6},{8,9},{11,10},{12,13},{15,14},{16,17},{19,... | collective-permute-start | bytes 1572872 | tf_op jit(solution)/shard_map/ppermute | solution.py:81
  798.0 30.5 %collective-permute-start.63 = (bf16[512,512]{1,0:T(8,128)(2,1)S(1)}, bf16[512,512]{1,0:T(8,128)(2,1)S(1)}, u32[]{:S(2)}, u32[]{:S(2)}) collective-permute-start(bf16[512,512]{1,0:T(8,128)(2,1)S(1)} %get-tuple-element.130), channel_id=1, source_target_pairs={{0,1},{1,2},{2,3},{4,5},{5,6},{6,7},{8,9},{9,10},{10,11},{12,13},{... | collective-permute-start | bytes 1572872 | tf_op jit(solution)/shard_map/ppermute | solution.py:89
  802.6 25.9 %collective-permute-start.65 = (bf16[512,512]{1,0:T(8,128)(2,1)S(1)}, bf16[512,512]{1,0:T(8,128)(2,1)S(1)}, u32[]{:S(2)}, u32[]{:S(2)}) collective-permute-start(bf16[512,512]{1,0:T(8,128)(2,1)S(1)} %get-tuple-element.131), channel_id=1, source_target_pairs={{3,2},{2,1},{1,0},{7,6},{6,5},{5,4},{11,10},{10,9},{9,8},{15,14},{... | collective-permute-start | bytes 1572872 | tf_op jit(solution)/shard_map/ppermute | solution.py:90
  (119 other events, 1756.8 us)
Sparse Core Ops, SparseCore 0:
  12.1 92.4 all-gather.3
  107.8 86.3 all-gather.5
  224.3 112.9 all-gather.7
  466.2 48.8 reduce-scatter.13
  631.0 57.4 reduce-scatter.9
  691.7 51.1 reduce-scatter.7
  746.3 71.5 reduce-scatter.11
  821.4 71.5 reduce-scatter.5
where the time goes:
time: 914 us; the launch traced here: 903 us
  waiting for transfers between devices  336 us (37%)
  matrix products  177 us (19%)
  starting transfers between devices  175 us (19%)
  other arithmetic  100 us (11%)
  Pallas kernels  54 us (6%)
  local copies, waits for them, and re-layouts  45.1 us (5%)
  between operations  16.4 us (2%)
    ppermute x10, waiting for transfers between devices, line_gather(): lefts.append(lax.ppermute(lefts[-1], axis, l_pairs))  85.2 us
    dot_general x7, matrix products, tn(): lax.dot_general(a, b, (((0,), (0,)), ((), ())), preferred_element_type=F32)  64 us
    dot_general x8, matrix products, nn(): lax.dot_general(a, b, (((1,), (0,)), ((), ())), preferred_element_type=F32)  60.6 us
    ppermute x14, starting transfers between devices, line_scatter(): from_left = lax.ppermute(r_data, axis, r_pairs)  59.1 us
    dot_general x7, matrix products, nt(): lax.dot_general(a, b, (((1,), (1,)), ((), ())), preferred_element_type=F32)  51.9 us
    ppermute x5, waiting for transfers between devices, line_gather(): lax.ppermute(jnp.where(i >= k - 1, rights[-1], lefts[-1]), axis, r_pairs...  49.8 us
    reduce_scatter x5, waiting for transfers between devices, shard(): lax.psum_scatter(grad, data, scatter_dimension=0, tiled=True).astype(F32)  45.9 us
    ppermute x14, waiting for transfers between devices, line_scatter(): from_right = lax.ppermute(l_data, axis, l_pairs)  42.4 us
  transfers between devices with their start and end apart: 84, of which 34 were waited for; matrix products, arithmetic and copies ran while one was open for 33% of the time, Pallas kernels for 6%

commit v1 on v0

v1 whole, which is shorter than its diff:
```python
import math

import jax
import jax.numpy as jnp
from jax import lax
from jax.experimental import pallas as pl
from jax.experimental.pallas import tpu as pltpu
from jax.sharding import PartitionSpec as P


HK = 256
HV = 512
EPSILON = 1e-06
BLOCK = 256
F32 = jnp.float32
BF16 = jnp.bfloat16


def nn(a, b):
    return lax.dot_general(a, b, (((1,), (0,)), ((), ())), preferred_element_type=F32)


def tn(a, b):
    return lax.dot_general(a, b, (((0,), (0,)), ((), ())), preferred_element_type=F32)


def nt(a, b):
    return lax.dot_general(a, b, (((1,), (1,)), ((), ())), preferred_element_type=F32)


def after(x, *before):
    return lax.optimization_barrier((x, *before))[0]


def right(lo, hi):
    return [(i, i + 1) for i in range(lo, hi)]


def left(lo, hi):
    return [(i, i - 1) for i in range(hi, lo, -1)]


def line_gather(x, axis, before=()):
    n, i = lax.axis_size(axis), lax.axis_index(axis)
    rights, lefts = [x], [x]
    for k in range(1, n):
        r_pairs = right(k - 1, n - 1)
        l_pairs = left(0, n - k)
        if k == 2 and before:
            rights[-1] = after(rights[-1], *before)
        if 2 * k > n + 1:
            both = lax.ppermute(jnp.where(i >= k - 1, rights[-1], lefts[-1]), axis, r_pairs + l_pairs)
            rights.append(both)
            lefts.append(both)
        else:
            rights.append(lax.ppermute(rights[-1], axis, r_pairs))
            lefts.append(lax.ppermute(lefts[-1], axis, l_pairs))
    return [(rights[k], lefts[n - k]) for k in range(1, n)]


def place(blocks, axis, dtype):
    n, i = lax.axis_size(axis), lax.axis_index(axis)
    rows, width = blocks[0].shape
    full = jnp.zeros((rows, n * width), dtype)
    for k, block in enumerate(blocks):
        at = ((i - k) % n) * width
        full = lax.dynamic_update_slice(full, block.astype(dtype), (0, at))
    return full


def line_scatter(parts, axis):
    n, i = lax.axis_size(axis), lax.axis_index(axis)
    width = parts.shape[1] // n

    def block(j):
        return lax.dynamic_slice(parts, (0, jnp.clip(j, 0, n - 1) * width), (parts.shape[0], width))

    from_left = from_right = None
    early = []
    for k in range(1, n):
        r_pairs = right(0, k)
        l_pairs = left(n - 1 - k, n - 1)
        if 2 * k < n - 1:
            data = block(jnp.where(i < k, i + n - k, i - n + k))
            if from_left is not None:
                data = (data.astype(F32) + jnp.where(i < k, from_left, from_right).astype(F32)).astype(BF16)
            from_left = from_right = lax.ppermute(data, axis, r_pairs + l_pairs)
            from_left = jnp.where(i <= k, from_left, jnp.zeros_like(from_left))
            from_right = jnp.where(i >= n - 1 - k, from_right, jnp.zeros_like(from_right))
        else:
            r_data, l_data = block(i + n - k), block(i - n + k)
            if from_left is not None:
                r_data = (r_data.astype(F32) + from_left.astype(F32)).astype(BF16)
                l_data = (l_data.astype(F32) + from_right.astype(F32)).astype(BF16)
            from_left = lax.ppermute(r_data, axis, r_pairs)
            from_right = lax.ppermute(l_data, axis, l_pairs)
        if k < n - 1:
            early.append((from_left, from_right))
    return block(i).astype(F32) + from_left.astype(F32) + from_right.astype(F32), early


def small_gather(x, axis):
    n = lax.axis_size(axis)
    blocks = [x] + [lax.ppermute(x, axis, [(j, (j + s) % n) for j in range(n)]) for s in range(1, n)]
    return place(blocks, axis, x.dtype)


def swap_sum(x, axis):
    n = lax.axis_size(axis)
    g = 1
    while g < n:
        x = x + lax.ppermute(x, axis, [(j, j ^ g) for j in range(n)])
        g *= 2
    return x


def states_before(local, log_block, axis):
    n, b = lax.axis_size(axis), lax.axis_index(axis)
    total, prefix, g = local, jnp.zeros_like(local), 1
    while g < n:
        got = lax.ppermute(total.astype(BF16), axis, [(j, j ^ g) for j in range(n)]).astype(F32)
        upper = (b // g) % 2 == 1
        mine = jnp.exp((b % g).astype(F32) * log_block)[:, None, None]
        whole = jnp.exp(g * log_block)[:, None, None]
        prefix = jnp.where(upper, prefix + mine * got, prefix)
        total = jnp.where(upper, whole * got + total, whole * total + got)
        g *= 2
    return prefix


def states_after(local, log_block, axis):
    first = None
    n, b = lax.axis_size(axis), lax.axis_index(axis)
    total, suffix, g = local, jnp.zeros_like(local), 1
    while g < n:
        got = lax.ppermute(total.astype(BF16), axis, [(j, j ^ g) for j in range(n)]).astype(F32)
        first = got if first is None else first
        upper = (b // g) % 2 == 1
        mine = jnp.exp((g - 1 - b % g).astype(F32) * log_block)[:, None, None]
        whole = jnp.exp(g * log_block)[:, None, None]
        suffix = jnp.where(upper, suffix, suffix + mine * got)
        total = jnp.where(upper, got + whole * total, total + whole * got)
        g *= 2
    return suffix, first


def pair_swap(x):
    lane = lax.broadcasted_iota(jnp.int32, x.shape, 1)
    width = x.shape[1]
    return jnp.where(lane % 2 == 0, pltpu.roll(x, width - 1, 1), pltpu.roll(x, 1, 1))


def side_by_side(*arrays):
    rows = arrays[0].shape[0]
    widths = [a.shape[1] for a in arrays]

    def kernel(*refs):
        parts, out, sems = refs[:-2], refs[-2], refs[-1]
        copies, column = [], 0
        for i, width in enumerate(widths):
            copies.append(pltpu.make_async_copy(parts[i], out.at[:, column : column + width], sems.at[i]))
            column += width
        for copy in copies:
            copy.start()
        for copy in copies:
            copy.wait()

    return pl.pallas_call(
        kernel,
        in_specs=[pl.BlockSpec(memory_space=pl.ANY)] * len(arrays),
        out_specs=pl.BlockSpec(memory_space=pl.ANY),
        out_shape=jax.ShapeDtypeStruct((rows, sum(widths)), arrays[0].dtype),
        scratch_shapes=[pltpu.SemaphoreType.DMA((len(arrays),))],
        cost_estimate=pl.CostEstimate(flops=0, bytes_accessed=4 * rows * sum(widths), transcendentals=0),
        name="side_by_side",
    )(*arrays)


def fill_normed(at, refs, gain_ref, full_ref):
    n = len(refs) // 2 + 1
    width = refs[0].shape[1]
    blocks = [refs[0][...].astype(F32)]
    for k in range(1, n):
        blocks.append(jnp.where(at >= k, refs[2 * k - 1][...], refs[2 * k][...]).astype(F32))
    squares = sum(jnp.sum(b * b, axis=1, keepdims=True) for b in blocks)
    scale = lax.rsqrt(squares / (n * width) + EPSILON)
    for k, b in enumerate(blocks):
        where = pl.ds(pl.multiple_of(((at + n - k) % n) * width, width), width)
        full_ref[:, where] = (b * scale * gain_ref[:, where]).astype(BF16)
    return scale


def flat(x, pairs):
    return [x] + [p for pair in pairs for p in pair]


def project_kernel(heads, count, at_ref, lg_ref, gain_ref, w_ref, cos_ref, sin_ref, *refs):
    blocks, (full_ref, scale_ref, q_ref, k_ref, v_ref, state_ref) = refs[:count], refs[count:]
    step = pl.program_id(0)
    rows = pl.num_programs(0) * BLOCK
    scale_ref[...] = fill_normed(at_ref[0], blocks, gain_ref, full_ref)
    x = full_ref[...]
    qk = heads * HK
    c, s = cos_ref[...], sin_ref[...]
    k_out = nn(x, w_ref[:, qk : 2 * qk])
    v_out = nn(x, w_ref[:, 2 * qk :]).astype(BF16)
    q_out = nn(x, w_ref[:, :qk])
    v_ref[...] = v_out
    m = lax.broadcasted_iota(jnp.int32, (BLOCK, 1), 0) + step * BLOCK
    for h in range(heads):
        at = slice(h * HK, (h + 1) * HK)
        one = k_out[:, at]
        key = ((one * c + pair_swap(one) * s) * (1.0 / math.sqrt(HK))).astype(BF16)
        k_ref[:, at] = key
        tail = jnp.exp((rows - m).astype(F32) * lg_ref[h])
        add = tn((key.astype(F32) * tail).astype(BF16), v_out[:, h * HV : (h + 1) * HV])

        @pl.when(step == 0)
        def _(h=h, add=add):
            state_ref[h] = add

        @pl.when(step > 0)
        def _(h=h, add=add):
            state_ref[h] += add

        one = q_out[:, at]
        q_ref[:, at] = (one * c + pair_swap(one) * s).astype(BF16)


def project(at, log_gamma, gain, w, x, pairs, heads, cosine, sine):
    rows, width = x.shape
    features = w.shape[0]
    outs = 2 * heads * HK + heads * HV
    blocks = flat(x, pairs)

    def by_rows(columns):
        return pl.BlockSpec((BLOCK, columns), lambda r: (r, 0))

    return pl.pallas_call(
        lambda *refs: project_kernel(heads, len(blocks), *refs),
        grid=(rows // BLOCK,),
        in_specs=[
            pl.BlockSpec(memory_space=pltpu.SMEM),
            pl.BlockSpec(memory_space=pltpu.SMEM),
            pl.BlockSpec((1, features), lambda r: (0, 0)),
            pl.BlockSpec((features, outs), lambda r: (0, 0)),
            by_rows(HK),
            by_rows(HK),
            *[by_rows(width)] * len(blocks),
        ],
        out_specs=[
            by_rows(features),
            by_rows(1),
            by_rows(heads * HK),
            by_rows(heads * HK),
            by_rows(heads * HV),
            pl.BlockSpec((heads, HK, HV), lambda r: (0, 0, 0)),
        ],
        out_shape=[
            jax.ShapeDtypeStruct((rows, features), BF16),
            jax.ShapeDtypeStruct((rows, 1), F32),
            jax.ShapeDtypeStruct((rows, heads * HK), BF16),
            jax.ShapeDtypeStruct((rows, heads * HK), BF16),
            jax.ShapeDtypeStruct((rows, heads * HV), BF16),
            jax.ShapeDtypeStruct((heads, HK, HV), F32),
        ],
        cost_estimate=pl.CostEstimate(
            flops=2 * rows * features * outs, bytes_accessed=2 * features * outs + 12 * rows * features, transcendentals=0
        ),
        name="project",
    )(at, log_gamma, gain, w, cosine, sine, *blocks)


def product_kernel(x_ref, w_ref, out_ref):
    out_ref[...] = nn(x_ref[...], w_ref[...])


def product(x, w, at, columns):
    rows, inner = x.shape
    return pl.pallas_call(
        product_kernel,
        grid=(rows // BLOCK,),
        in_specs=[
            pl.BlockSpec((BLOCK, inner), lambda r: (r, 0)),
            pl.BlockSpec((inner, columns), lambda r: (0, at)),
        ],
        out_specs=pl.BlockSpec((BLOCK, columns), lambda r: (r, 0)),
        out_shape=jax.ShapeDtypeStruct((rows, columns), F32),
        cost_estimate=pl.CostEstimate(
            flops=2 * rows * inner * columns, bytes_accessed=2 * inner * columns + 8 * rows * columns, transcendentals=0
        ),
        name="product",
    )(x, w)


def mlp_kernel(units, count, at_ref, gain_ref, w_ref, grad_ref, *refs):
    blocks, (full_ref, hidden_ref, acts_ref, scale_ref, inner_ref, back_ref) = refs[:count], refs[-6:]
    scale_ref[...] = fill_normed(at_ref[0], blocks, gain_ref, full_ref)
    x = full_ref[...]
    gate = nn(x, w_ref[:, :units])
    up = nn(x, w_ref[:, units : 2 * units])
    grad = nn(grad_ref[...], w_ref[:, 2 * units :])
    cdf = 0.5 * (1.0 + lax.erf(gate * math.sqrt(0.5)))
    gelu = gate * cdf
    density = jnp.exp(-0.5 * gate * gate) * (1.0 / math.sqrt(2.0 * math.pi))
    hidden_ref[...] = (gelu * up).astype(BF16)
    g_gate = (grad * up * (cdf + gate * density)).astype(BF16)
    g_up = (grad * gelu).astype(BF16)
    acts_ref[:, :units] = g_gate
    acts_ref[:, units:] = g_up
    inner_ref[...] = jnp.sum(g_gate.astype(F32) * gate + g_up.astype(F32) * up, axis=1, keepdims=True)
    back_ref[...] = (nt(g_gate, w_ref[:, :units]) + nt(g_up, w_ref[:, units : 2 * units])).astype(BF16)


def mlp(at, gain, w, part, grad, x, pairs, shared):
    rows, width = x.shape
    features = w.shape[0]
    units = w.shape[1] // 3
    blocks = flat(x, pairs)
    steps = rows // BLOCK
    total = grad.shape[0]

    def by_rows(columns):
        return pl.BlockSpec((BLOCK, columns), lambda r: (r, 0))

    def own_rows(columns):
        return pl.BlockSpec((BLOCK, columns), lambda r: (part * steps + r, 0))

    return pl.pallas_call(
        lambda *refs: mlp_kernel(units, len(blocks), *refs),
        grid=(steps,),
        in_specs=[
            pl.BlockSpec(memory_space=pltpu.SMEM),
            pl.BlockSpec((1, features), lambda r: (0, 0)),
            pl.BlockSpec((features, 3 * units), lambda r: (0, 0)),
            own_rows(features),
            *[by_rows(width)] * len(blocks),
            *[pl.BlockSpec(memory_space=pl.ANY)] * len(shared),
        ],
        out_specs=[own_rows(features), own_rows(units), own_rows(2 * units), by_rows(1), by_rows(1), by_rows(features)],
        out_shape=[
            jax.ShapeDtypeStruct((total, features), BF16),
            jax.ShapeDtypeStruct((total, units), BF16),
            jax.ShapeDtypeStruct((total, 2 * units), BF16),
            jax.ShapeDtypeStruct((rows, 1), F32),
            jax.ShapeDtypeStruct((rows, 1), F32),
            jax.ShapeDtypeStruct((rows, features), BF16),
        ],
        input_output_aliases={4 + len(blocks) + i: i for i in range(len(shared))},
        cost_estimate=pl.CostEstimate(
            flops=10 * rows * features * units,
            bytes_accessed=6 * features * units + 14 * rows * features,
            transcendentals=2 * rows * units,
        ),
        name="mlp",
    )(at, gain, w, grad, *blocks, *shared)


def decay_vectors(log_gamma):
    down = lax.broadcasted_iota(jnp.int32, (BLOCK, 1), 0).astype(F32)
    across = lax.broadcasted_iota(jnp.int32, (1, BLOCK), 1).astype(F32)
    return jnp.exp(down * log_gamma), jnp.exp(-across * log_gamma)


def block_decay(scores, r, j, log_gamma, down, across):
    out = scores * (down * jnp.exp(log_gamma * (BLOCK * (r - j)))) * across
    if r == j:
        n = lax.broadcasted_iota(jnp.int32, scores.shape, 0)
        m = lax.broadcasted_iota(jnp.int32, scores.shape, 1)
        out = jnp.where(n >= m, out, 0.0)
    return out.astype(BF16)


def cut(r):
    return slice(r * BLOCK, (r + 1) * BLOCK)


def forward_kernel(first, count, lg_ref, q_ref, k_ref, v_ref, gate_ref, state_ref, w_ref, *refs):
    gated_ref, ret_ref, out_ref, acc_ref = refs[-4:]
    head = pl.program_id(0)
    log_gamma = lg_ref[head]
    down, across = decay_vectors(log_gamma)
    state = state_ref[0]
    for at in range(count):
        r = first + at
        q = q_ref[cut(at), :]
        ret = nn(q, state) * (down * jnp.exp(log_gamma * (BLOCK * r)))
        for j in range(r + 1):
            weights = block_decay(nt(q, k_ref[cut(j), :]), r, j, log_gamma, down, across)
            ret = ret + nn(weights, v_ref[cut(j), :])
        ret_ref[cut(at), :] = ret
        scale = lax.rsqrt(jnp.mean(ret * ret, axis=1, keepdims=True) + EPSILON)
        gate = gate_ref[cut(at), :]
        gated = (gate / (1.0 + jnp.exp(-gate)) * (ret * scale)).astype(BF16)
        gated_ref[cut(at), :] = gated
        out = nt(gated, w_ref[...])

        @pl.when(head == 0)
        def _(at=at, out=out):
            acc_ref[cut(at), :] = out

        @pl.when(head > 0)
        def _(at=at, out=out):
            acc_ref[cut(at), :] += out

        @pl.when(head == pl.num_programs(0) - 1)
        def _(at=at):
            out_ref[cut(at), :] = acc_ref[cut(at), :].astype(BF16)


def retention_forward(part, parts, log_gamma, q, k, v, gate, state, w, first_column, shared):
    rows = q.shape[0]
    heads = q.shape[1] // HK
    features = w.shape[0]
    own = rows // parts
    seen = own * (part + 1)
    count = own // BLOCK
    pairs = sum(part * count + at + 1 for at in range(count))
    flops = heads * (pairs * 2 * BLOCK * BLOCK * (HK + HV) + 2 * own * HK * HV + 2 * own * HV * features)
    head_out = pl.BlockSpec((own, HV), lambda h: (part, h))
    return pl.pallas_call(
        lambda *refs: forward_kernel(part * count, count, *refs),
        grid=(heads,),
        in_specs=[
            pl.BlockSpec(memory_space=pltpu.SMEM),
            pl.BlockSpec((own, HK), lambda h: (part, h)),
            pl.BlockSpec((seen, HK), lambda h: (0, h)),
            pl.BlockSpec((seen, HV), lambda h: (0, h)),
            pl.BlockSpec((own, HV), lambda h: (part, h)),
            pl.BlockSpec((1, HK, HV), lambda h: (h, 0, 0)),
            pl.BlockSpec((features, HV), lambda h: (0, first_column // HV + h)),
            *[pl.BlockSpec(memory_space=pl.ANY)] * len(shared),
        ],
        out_specs=[head_out, head_out, pl.BlockSpec((own, features), lambda h: (0, 0))],
        input_output_aliases={7 + i: i for i in range(len(shared))},
        out_shape=[
            jax.ShapeDtypeStruct((rows, heads * HV), BF16),
            jax.ShapeDtypeStruct((rows, heads * HV), F32),
            jax.ShapeDtypeStruct((own, features), BF16),
        ],
        scratch_shapes=[pltpu.VMEM((own, features), F32)],
        cost_estimate=pl.CostEstimate(flops=flops, bytes_accessed=20 * own * heads * HV, transcendentals=own * heads * HV),
        name="retention_forward",
    )(log_gamma, q, k, v, gate, state, w, *shared)


def gate_backward_kernel(first, count, n_blocks, at_ref, lg_ref, q_ref, w_ref, gate_ref, ret_ref, *refs):
    blocks, (g_gate_ref, g_ret_ref, full_ref, state_ref, inner_ref) = refs[:n_blocks], refs[-5:]
    head = pl.program_id(0)
    log_gamma = lg_ref[head]
    down, _ = decay_vectors(log_gamma)
    n = n_blocks // 2 + 1
    width = blocks[0].shape[1]
    here = at_ref[0]
    state = None
    for at in range(count):
        r = first + at

        @pl.when(head == 0)
        def _(at=at):
            for k in range(n):
                block = blocks[0][cut(at), :]
                if k:
                    block = jnp.where(here >= k, blocks[2 * k - 1][cut(at), :], blocks[2 * k][cut(at), :])
                where = pl.ds(pl.multiple_of(((here + n - k) % n) * width, width), width)
                full_ref[cut(at), where] = block

        grad = nn(full_ref[cut(at), :], w_ref[...])
        ret = ret_ref[cut(at), :]
        gate = gate_ref[cut(at), :]
        scale = lax.rsqrt(jnp.mean(ret * ret, axis=1, keepdims=True) + EPSILON)
        grouped = ret * scale
        sig = 1.0 / (1.0 + jnp.exp(-gate))
        g_gate = (grad * grouped * (sig * (1.0 + gate * (1.0 - sig)))).astype(BF16)
        g = grad * (gate * sig)
        g_ret = (scale * (g - grouped * jnp.mean(g * grouped, axis=1, keepdims=True))).astype(BF16)
        g_gate_ref[cut(at), :] = g_gate
        g_ret_ref[cut(at), :] = g_ret
        inner_ref[0, cut(at), :] = jnp.sum(g_gate.astype(F32) * gate, axis=1, keepdims=True)
        q = (q_ref[cut(at), :].astype(F32) * (down * jnp.exp(log_gamma * (BLOCK * r)))).astype(BF16)
        add = tn(q, g_ret)
        state = add if state is None else state + add
    state_ref[0] = state


def gate_backward(part, parts, here, log_gamma, q, w, first_column, gate, ret, x, pairs, shared):
    rows = q.shape[0]
    heads = q.shape[1] // HK
    features = w.shape[0]
    own = rows // parts
    count = own // BLOCK
    blocks = flat(x, pairs)
    head_out = pl.BlockSpec((own, HV), lambda h: (part, h))
    return pl.pallas_call(
        lambda *refs: gate_backward_kernel(part * count, count, len(blocks), *refs),
        grid=(heads,),
        in_specs=[
            pl.BlockSpec(memory_space=pltpu.SMEM),
            pl.BlockSpec(memory_space=pltpu.SMEM),
            pl.BlockSpec((own, HK), lambda h: (part, h)),
            pl.BlockSpec((features, HV), lambda h: (0, first_column // HV + h)),
            head_out,
            head_out,
            *[pl.BlockSpec((own, x.shape[1]), lambda h: (0, 0))] * len(blocks),
            *[pl.BlockSpec(memory_space=pl.ANY)] * len(shared),
        ],
        out_specs=[
            head_out,
            head_out,
            pl.BlockSpec((own, features), lambda h: (part, 0)),
            pl.BlockSpec((1, HK, HV), lambda h: (h, 0, 0)),
            pl.BlockSpec((1, own, 1), lambda h: (h, 0, 0)),
        ],
        input_output_aliases={6 + len(blocks) + i: i for i in range(len(shared))},
        out_shape=[
            jax.ShapeDtypeStruct((rows, heads * HV), BF16),
            jax.ShapeDtypeStruct((rows, heads * HV), BF16),
            jax.ShapeDtypeStruct((rows, features), BF16),
            jax.ShapeDtypeStruct((heads, HK, HV), F32),
            jax.ShapeDtypeStruct((heads, own, 1), F32),
        ],
        cost_estimate=pl.CostEstimate(
            flops=heads * 2 * own * HV * (HK + features),
            bytes_accessed=16 * own * heads * HV,
            transcendentals=own * heads * HV,
        ),
        name="gate_backward",
    )(here, log_gamma, q, w, gate, ret, *blocks, *shared)


def backward_kernel(total, lg_ref, q_ref, k_ref, v_ref, state_in_ref, state_grad_ref, cos_ref, sin_ref, *refs):
    g_ref, gate_ref, all_ref, inner_ref, acc_k, acc_v, g_q_ref, g_k_ref, g_v_ref, sems = refs
    head, heads = pl.program_id(0), pl.num_programs(0)
    log_gamma = lg_ref[head]
    down, across = decay_vectors(log_gamma)
    state_in, state_grad = state_in_ref[0], state_grad_ref[0]
    key_scale = 1.0 / math.sqrt(HK)

    def send(ref, column, width, i):
        target = all_ref.at[:, pl.ds(pl.multiple_of(column, HK), width)]
        return pltpu.make_async_copy(ref, target, sems.at[i])

    gates = send(gate_ref, heads * (2 * HK + HV) + head * HV, HV, 0)
    gates.start()

    def put(ref, r, x, factor):
        turned = x * cos_ref[cut(r), :] - pair_swap(x) * sin_ref[cut(r), :]
        ref[cut(r), :] = (turned * factor).astype(BF16)

    for r in range(total):
        g = g_ref[cut(r), :]
        q, k, v = q_ref[cut(r), :], k_ref[cut(r), :], v_ref[cut(r), :]
        tail = down_tail(log_gamma, total * BLOCK - r * BLOCK)
        acc_v[cut(r), :] = nn((k.astype(F32) * tail).astype(BF16), state_grad)
        acc_k[cut(r), :] = nt(v, state_grad) * tail
        g_q = nt(g, state_in) * (down * jnp.exp(log_gamma * (BLOCK * r)))
        for j in range(r + 1):
            kj, vj = k_ref[cut(j), :], v_ref[cut(j), :]
            weights = block_decay(nt(q, kj), r, j, log_gamma, down, across)
            g_scores = block_decay(nt(g, vj), r, j, log_gamma, down, across)
            acc_v[cut(j), :] += tn(weights, g)
            acc_k[cut(j), :] += tn(g_scores, q)
            g_q = g_q + nn(g_scores, kj)
        inner_ref[0, cut(r), :] = jnp.sum(g_q * q.astype(F32), axis=1, keepdims=True)
        put(g_q_ref, r, g_q, 1.0)
    for r in range(total):
        g_k = acc_k[cut(r), :]
        g_v = acc_v[cut(r), :].astype(BF16)
        g_v_ref[cut(r), :] = g_v
        inner_ref[0, cut(r), :] += jnp.sum(g_k * k_ref[cut(r), :].astype(F32), axis=1, keepdims=True) + jnp.sum(
            g_v.astype(F32) * v_ref[cut(r), :].astype(F32), axis=1, keepdims=True
        )
        put(g_k_ref, r, g_k, key_scale)
    copies = [
        send(g_q_ref, head * HK, HK, 1),
        send(g_k_ref, (heads + head) * HK, HK, 2),
        send(g_v_ref, 2 * heads * HK + head * HV, HV, 3),
    ]
    for copy in copies:
        copy.start()
    for copy in [gates] + copies:
        copy.wait()


def down_tail(log_gamma, start):
    m = lax.broadcasted_iota(jnp.int32, (BLOCK, 1), 0).astype(F32)
    return jnp.exp((start - m) * log_gamma)


def retention_backward(log_gamma, q, k, v, state_in, state_grad, cosine, sine, g_ret, g_gate):
    rows = q.shape[0]
    heads = q.shape[1] // HK
    blocks = rows // BLOCK
    pairs = blocks * (blocks + 1) // 2
    flops = heads * 2 * (pairs * BLOCK * BLOCK * (3 * HK + 2 * HV) + 3 * rows * HK * HV)
    head_keys = pl.BlockSpec((rows, HK), lambda h: (0, h))
    head_values = pl.BlockSpec((rows, HV), lambda h: (0, h))
    head_state = pl.BlockSpec((1, HK, HV), lambda h: (h, 0, 0))
    table = pl.BlockSpec((rows, HK), lambda h: (0, 0))
    return pl.pallas_call(
        lambda *refs: backward_kernel(blocks, *refs),
        grid=(heads,),
        in_specs=[
            pl.BlockSpec(memory_space=pltpu.SMEM),
            head_keys,
            head_keys,
            head_values,
            head_state,
            head_state,
            table,
            table,
            head_values,
            head_values,
        ],
        out_specs=[pl.BlockSpec(memory_space=pl.ANY), pl.BlockSpec((1, rows, 1), lambda h: (h, 0, 0))],
        out_shape=[
            jax.ShapeDtypeStruct((rows, heads * 2 * (HK + HV)), BF16),
            jax.ShapeDtypeStruct((heads, rows, 1), F32),
        ],
        scratch_shapes=[
            pltpu.VMEM((rows, HK), F32),
            pltpu.VMEM((rows, HV), F32),
            pltpu.VMEM((rows, HK), BF16),
            pltpu.VMEM((rows, HK), BF16),
            pltpu.VMEM((rows, HV), BF16),
            pltpu.SemaphoreType.DMA((4,)),
        ],
        cost_estimate=pl.CostEstimate(flops=flops, bytes_accessed=24 * rows * heads * HK, transcendentals=0),
        name="retention_backward",
    )(log_gamma, q, k, v, state_in, state_grad, cosine, sine, g_ret, g_gate)


def on_device(
    layer_input,
    gain_attn,
    w_query,
    w_key,
    w_value,
    w_retgate,
    w_out,
    gain_mlp,
    w_gate,
    w_up,
    w_down,
    cotangent,
):
    data = ("dp", "ctx")
    rows, width = layer_input.shape
    n_tp, at_tp = lax.axis_size("tp"), lax.axis_index("tp")
    features = width * n_tp
    heads = w_query.shape[1] // HK
    units = w_gate.shape[1]

    parts = 2
    own = rows // parts
    cuts = [slice(c * own, (c + 1) * own) for c in range(parts)]

    qk = heads * HK
    vw = heads * HV
    attn_shard = side_by_side(w_query, w_key, w_value, w_retgate, w_out)
    attn_full = lax.all_gather(attn_shard, data, axis=0, tiled=True)

    gains = small_gather(jnp.stack([gain_attn, gain_mlp]), "tp")

    log_gamma = jnp.log1p(-jnp.exp2(-5.0 - (at_tp * heads + jnp.arange(heads)).astype(F32)))
    log_block = rows * log_gamma
    positions = lax.axis_index("ctx") * rows + jnp.arange(rows)
    frequencies = jnp.exp(-math.log(10000.0) * jnp.linspace(0.0, 1.0, HK // 2, dtype=F32))
    angles = positions.astype(F32)[:, None] * jnp.repeat(frequencies, 2)[None, :]
    cosine = jnp.cos(angles)
    sine = jnp.sin(angles) * jnp.where(jnp.arange(HK) % 2 == 0, -1.0, 1.0)[None, :]
    here = at_tp.reshape(1)
    mlp_shard = side_by_side(w_gate, w_up, w_down)

    pairs = line_gather(layer_input, "tp", (cosine, sine, mlp_shard, log_gamma))
    normed, scale_attn, q, k, v, local_state = project(
        here, log_gamma, gains[0:1], attn_full, layer_input, pairs, heads, cosine, sine
    )
    grad_full = lax.all_gather(after(cotangent, pairs[0][0]), "tp", axis=1, tiled=True)
    mlp_full = lax.all_gather(after(mlp_shard, pairs[0][1]), data, axis=0, tiled=True)
    gate_pre = product(after(normed, local_state), attn_full, (2 * qk + vw) // vw, vw)
    state_in = states_before(local_state, log_block, "ctx").astype(BF16)
    heads_out, branch = [], []
    for c in range(parts):
        *heads_out, out = retention_forward(
            c, parts, log_gamma, q, k, v, gate_pre, state_in, attn_full, 2 * qk + 2 * vw, heads_out
        )
        branch.append(out)
    gated, retained = heads_out

    x_own = layer_input.astype(F32)
    middle, mid_pairs, scale_mlp, inner_mlp, back, grad_middle, grad_own, grad_pairs = ([] for _ in range(8))
    gain_mlp_sum = 0.0

    def norm_back(own_rows, scale, gain, inner, grad_normed):
        hat = own_rows * scale
        grad = scale * (grad_normed * gain[None, :] - hat * (inner[:, None] / features))
        return grad, jnp.sum(grad_normed * hat, axis=0)

    def row_total(inner):
        lanes = 128
        return swap_sum(inner.reshape(-1, lanes), "tp").reshape(-1)

    early = ()
    for c in range(parts):
        total, steps = line_scatter(after(branch[c], *early), "tp")
        early = steps[-1]
        if c:
            total = after(total, mid_pairs[c - 1][0][0])
        middle.append(x_own[cuts[c]] + total)
        mid_pairs.append(line_gather(middle[c].astype(BF16), "tp"))
    shared = []
    for c in range(parts):
        *results, scale, inner, out = mlp(
            here, gains[1:2], mlp_full, c, grad_full, middle[c].astype(BF16), mid_pairs[c], shared
        )
        shared = results
        scale_mlp.append(scale)
        inner_mlp.append(inner[:, 0])
        back.append(out)
    normed_mlp, hidden, grad_acts = shared
    early = ()
    for c in range(parts):
        inner = row_total(inner_mlp[c])
        total, steps = line_scatter(after(back[c], *early), "tp")
        early = steps[-1]
        if c:
            total = after(total, grad_pairs[c - 1][0][0])
        grad_mid, gain_sum = norm_back(middle[c], scale_mlp[c], gain_mlp, inner, total)
        gain_mlp_sum = gain_mlp_sum + gain_sum
        grad_middle.append(cotangent[cuts[c]].astype(F32) + grad_mid)
        grad_own.append(grad_middle[c].astype(BF16))
        grad_pairs.append(line_gather(grad_own[c], "tp"))
    grad_down = tn(grad_full, hidden).astype(BF16)
    grad_gate_up = tn(after(normed_mlp, grad_down), grad_acts).astype(BF16)
    mlp_parts = nt(hidden, mlp_full[:, 2 * units :]).astype(BF16)

    grad_own[0] = after(grad_own[0], grad_gate_up, grad_down, mlp_parts)
    mlp_out, _ = line_scatter(after(mlp_parts, grad_pairs[-1][0][0]), "tp")
    layer_output = (jnp.concatenate(middle) + mlp_out).astype(BF16)
    shared = []
    partial_state = 0.0
    inner_attn = []
    for c in range(parts):
        *shared, ps, inner = gate_backward(
            c,
            parts,
            here,
            log_gamma,
            q,
            attn_full,
            2 * qk + 2 * vw,
            gate_pre,
            retained,
            grad_own[c],
            grad_pairs[c],
            shared,
        )
        partial_state = partial_state + ps
        inner_attn.append(jnp.sum(inner[:, :, 0], axis=0))
    g_gate, g_ret, grad_attn = shared
    state_grad, got = states_after(partial_state, log_block, "ctx")
    state_grad = state_grad.astype(BF16)
    grad_out = tn(after(grad_attn, got), gated).astype(BF16)
    grad_retgate = tn(normed, after(g_gate, got)).astype(BF16)
    grads_attn, inner = retention_backward(
        log_gamma, q, k, v, state_in, after(state_grad, grad_out, grad_retgate), cosine, sine, g_ret, g_gate
    )
    inner_attn = jnp.concatenate(inner_attn) + jnp.sum(inner[:, :, 0], axis=0)
    in_full = attn_full[:, : 2 * qk + 2 * vw]
    back = []
    for c in range(parts):
        back.append(nt(after(grads_attn, *back)[cuts[c]], in_full).astype(BF16))
    grad_qkv_w = tn(normed, after(grads_attn, *back)[:, : 2 * qk + vw]).astype(BF16)
    inner_attn = row_total(inner_attn)
    grad_input, gain_attn_sum = [], 0.0
    early = ()
    for c in range(parts):
        total, steps = line_scatter(after(back[c], *early), "tp")
        early = steps[0]
        grad_in, gain_sum = norm_back(x_own[cuts[c]], scale_attn[cuts[c]], gain_attn, inner_attn[cuts[c]], total)
        grad_input.append((grad_middle[c] + grad_in).astype(BF16))
        gain_attn_sum = gain_attn_sum + gain_sum
    grad_input = jnp.concatenate(grad_input)

    def shard(grad):
        return lax.psum_scatter(grad, data, scatter_dimension=0, tiled=True).astype(F32)

    s_down = shard(grad_down)
    s_gate_up = shard(grad_gate_up)
    s_out = shard(grad_out)
    s_retgate = shard(grad_retgate)
    s_qkv = shard(grad_qkv_w)
    s_query, s_key, s_value = s_qkv[:, :qk], s_qkv[:, qk : 2 * qk], s_qkv[:, 2 * qk :]
    gain_sums = swap_sum(swap_sum(jnp.stack([gain_attn_sum, gain_mlp_sum]), "ctx"), "dp")
    return (
        layer_output,
        grad_input,
        gain_sums[0],
        s_query,
        s_key,
        s_value,
        s_retgate,
        s_out,
        gain_sums[1],
        s_gate_up[:, :units],
        s_gate_up[:, units:],
        s_down,
    )


def solution(mesh):
    tokens = P(("dp", "ctx"), "tp")
    gain = P("tp")
    weight = P(("dp", "ctx"), "tp")

    return jax.shard_map(
        on_device,
        mesh=mesh,
        in_specs=(tokens, gain, weight, weight, weight, weight, weight, gain, weight, weight, weight, tokens),
        out_specs=(tokens, tokens, gain, weight, weight, weight, weight, weight, gain, weight, weight, weight),
        check_vma=False,
    )
```

time: 914 us -> 999 us (1.093)
  Pallas kernels: 54 us -> 253 us
  matrix products: 177 us -> 81.5 us
  other arithmetic: 100 us -> 70.4 us
  local copies, waits for them, and re-layouts: 45.1 us -> 24.2 us
  waiting for transfers between devices: 336 us -> 352 us
  starting transfers between devices: 175 us -> 190 us
    pallas_call x4 -> x9, Pallas kernels: 41.7 us -> 230 us  [the longest x2 113 us: side_by_side(): pl.pallas_call(kernel, in_specs=[pl.BlockSpec(memory_space=pl.ANY)] * len...]
    dot_general x8 -> x0, matrix products: 60.6 us -> none  [nn(): lax.dot_general(a, b, (((1,), (0,)), ((), ())), preferred_element_type=F32)]
    ppermute x7, waiting for transfers between devices: 18 us -> 62.4 us  [line_scatter(): from_left = from_right = lax.ppermute(data, axis, r_pairs + l_pairs)]
    reduce_scatter x5, waiting for transfers between devices: 45.9 us -> 4.68 us  [shard(): lax.psum_scatter(grad, data, scatter_dimension=0, tiled=True).astype(F32)]
    ppermute x14, waiting for transfers between devices: 42.4 us -> 1.32 us  [line_scatter(): from_right = lax.ppermute(l_data, axis, l_pairs)]
    ppermute x5, waiting for transfers between devices: 49.8 us -> 79.9 us  [line_gather(): lax.ppermute(jnp.where(i >= k - 1, rights[-1], lefts[-1]), axis, r_pairs...]
    ppermute x9, waiting for transfers between devices: 11.5 us -> 36.2 us  [swap_sum(): x = x + lax.ppermute(x, axis, [(j, j ^ g) for j in range(n)])]
    dot_general x7 -> x3, matrix products: 51.9 us -> 31 us  [nt(): lax.dot_general(a, b, (((1,), (1,)), ((), ())), preferred_element_type=F32)]
  transfers between devices with their start and end apart: 84 -> 84, of which waited for: 34 -> 35; matrix products, arithmetic and copies ran while one was open for 33% -> 17% of each run, Pallas kernels for 6% -> 19%
where the time goes in v1:
time: 999 us; the launch traced here: 988 us
  waiting for transfers between devices  352 us (35%)
  Pallas kernels  253 us (25%)
  starting transfers between devices  190 us (19%)
  matrix products  81.5 us (8%)
  other arithmetic  70.4 us (7%)
  local copies, waits for them, and re-layouts  24.2 us (2%)
  between operations  16.1 us (2%)
    pallas_call x2, Pallas kernels, side_by_side(): pl.pallas_call(kernel, in_specs=[pl.BlockSpec(memory_space=pl.ANY)] * len...  113 us
    ppermute x10, waiting for transfers between devices, line_gather(): lefts.append(lax.ppermute(lefts[-1], axis, l_pairs))  85.2 us
    ppermute x5, waiting for transfers between devices, line_gather(): lax.ppermute(jnp.where(i >= k - 1, rights[-1], lefts[-1]), axis, r_pairs...  79.9 us
    ppermute x14, starting transfers between devices, line_scatter(): from_left = lax.ppermute(r_data, axis, r_pairs)  69.7 us
    ppermute x7, waiting for transfers between devices, line_scatter(): from_left = from_right = lax.ppermute(data, axis, r_pairs + l_pairs)  62.4 us
    dot_general x5, matrix products, tn(): lax.dot_general(a, b, (((0,), (0,)), ((), ())), preferred_element_type=F32)  50.5 us
    ppermute x14, waiting for transfers between devices, line_scatter(): from_left = lax.ppermute(r_data, axis, r_pairs)  43.4 us
    pallas_call x2, Pallas kernels, mlp(): pl.pallas_call(lambda *refs: mlp_kernel(units, len(blocks), *refs), grid=...  38.9 us
  transfers between devices with their start and end apart: 84, of which 35 were waited for; matrix products, arithmetic and copies ran while one was open for 17% of the time, Pallas kernels for 19%

profile of v1, /device:TPU:0, one launch (start us, length us, event | category | flops | bytes accessed | tf_op | source)
XLA Modules:
  0.0 988.0 jit_solution(9363139727079534117)
XLA Ops:
  7.2 64.7 %side_by_side.2 = bf16[256,4096]{1,0:T(8,128)(2,1)} custom-call(bf16[256,512]{1,0:T(8,128)(2,1)} %refs_0_.2, bf16[256,512]{1,0:T(8,128)(2,1)} %refs_1_.2, bf16[256,1024]{1,0:T(8,128)(2,1)} %refs_2_.2, bf16[256,1024]{1,0:T(8,128)(2,1)} %refs_3_.1, bf16[256,1024]{1,0:T(8,128)(2,1)} %refs_4_.1), custom_call_target="tpu_custom_call" | custom-call | bytes 4194304 | tf_op jit(solution)/shard_map/side_by_side/pallas_call | solution.py:168
  78.5 48.8 %side_by_side.3 = bf16[256,3072]{1,0:T(8,128)(2,1)} custom-call(bf16[256,1024]{1,0:T(8,128)(2,1)} %refs_0_.3, bf16[256,1024]{1,0:T(8,128)(2,1)} %refs_1_.3, bf16[256,1024]{1,0:T(8,128)(2,1)} %refs_2_.3), custom_call_target="tpu_custom_call" | custom-call | bytes 3145728 | tf_op jit(solution)/shard_map/side_by_side/pallas_call | solution.py:168
  127.8 5.5 fusion.23
  134.7 25.3 %collective-permute-done.5.refs_12_ = bf16[1024,512]{1,0:T(8,128)(2,1)} collective-permute-done((bf16[1024,512]{1,0:T(8,128)(2,1)S(1)}, bf16[1024,512]{1,0:T(8,128)(2,1)}, u32[]{:S(2)}, u32[]{:S(2)}) %collective-permute-start.5) | collective-permute-done | bytes 1048608 | tf_op jit(solution)/shard_map/ppermute | solution.py:57
  162.1 40.7 %collective-permute-done.6.refs_10_ = bf16[1024,512]{1,0:T(8,128)(2,1)S(1)} collective-permute-done((bf16[1024,512]{1,0:T(8,128)(2,1)}, bf16[1024,512]{1,0:T(8,128)(2,1)S(1)}, u32[]{:S(2)}, u32[]{:S(2)}) %collective-permute-start.6) | collective-permute-done | bytes 1048608 | tf_op jit(solution)/shard_map/ppermute | solution.py:57
  204.3 71.6 %collective-permute-done.7.refs_8_.refs_11_ = bf16[1024,512]{1,0:T(8,128)(2,1)} collective-permute-done((bf16[1024,512]{1,0:T(8,128)(2,1)S(1)}, bf16[1024,512]{1,0:T(8,128)(2,1)}, u32[]{:S(2)}, u32[]{:S(2)}) %collective-permute-start.7) | collective-permute-done | bytes 1048608 | tf_op jit(solution)/shard_map/ppermute | solution.py:52
  285.1 22.2 %project.1 = (bf16[1024,2048]{1,0:T(8,128)(2,1)}, f32[1024,1]{1,0:T(8,128)}, bf16[1024,512]{1,0:T(8,128)(2,1)}, bf16[1024,512]{1,0:T(8,128)(2,1)}, bf16[1024,1024]{1,0:T(8,128)(2,1)}, /*index=5*/f32[2,256,512]{2,1,0:T(8,128)}) custom-call(s32[1]{0:T(128)} %bitcast.refs_0_, f32[2]{0:T(128)} %negate_log-plus-one_fusion.refs_1_.refs_0_, ...), custom_call_target="tpu_custom_call" | custom-call | flops 8589934592 | bytes 33554432 | tf_op jit(solution)/shard_map/project/pallas_call | solution.py:239
  312.8 9.4 product.1.refs_4_
  322.2 14.4 %collective-permute-done.9 = bf16[2,256,512]{2,1,0:T(8,128)(2,1)S(1)} collective-permute-done((bf16[2,256,512]{2,1,0:T(8,128)(2,1)S(1)}, bf16[2,256,512]{2,1,0:T(8,128)(2,1)S(1)}, u32[]{:S(2)}, u32[]{:S(2)}) %collective-permute-start.9) | collective-permute-done | bytes 524320 | tf_op jit(solution)/shard_map/ppermute | solution.py:121
  337.7 10.3 %retention_forward.2 = (bf16[1024,1024]{1,0:T(8,128)(2,1)}, f32[1024,1024]{1,0:T(8,128)}, bf16[512,2048]{1,0:T(8,128)(2,1)}) custom-call(f32[2]{0:T(128)} %negate_log-plus-one_fusion.refs_1_.refs_0_, bf16[1024,512]{1,0:T(8,128)(2,1)} %get-tuple-element.66.refs_1_.refs_2_, bf16[1024,512]{1,0:T(8,128)(2,1)} %get-tuple-element.67.refs_2_, ...), custom_call_target="tpu_custom_call" | custom-call | flops 3019898880 | bytes 10485760 | tf_op jit(solution)/shard_map/retention_forward/pallas_call | solution.py:421
  351.3 10.1 %collective-permute-done.10 = bf16[512,512]{1,0:T(8,128)(2,1)S(1)} collective-permute-done((bf16[512,512]{1,0:T(8,128)(2,1)S(1)}, bf16[512,512]{1,0:T(8,128)(2,1)S(1)}, u32[]{:S(2)}, u32[]{:S(2)}) %collective-permute-start.10) | collective-permute-done | bytes 524320 | tf_op jit(solution)/shard_map/ppermute | solution.py:87
  364.5 5.3 collective-permute-start.11
  369.8 12.3 %retention_forward.3 = (bf16[1024,1024]{1,0:T(8,128)(2,1)}, f32[1024,1024]{1,0:T(8,128)}, bf16[512,2048]{1,0:T(8,128)(2,1)}) custom-call(f32[2]{0:T(128)} %negate_log-plus-one_fusion.refs_1_.refs_0_, bf16[1024,512]{1,0:T(8,128)(2,1)} %get-tuple-element.66.refs_1_.refs_2_, ...), custom_call_target="tpu_custom_call", output_to_operand_aliasing={{0}: (7, {}), {1}: (8, {})} | custom-call | flops 3825205248 | bytes 10485760 | tf_op jit(solution)/shard_map/retention_forward/pallas_call | solution.py:421
  384.1 5.3 collective-permute-start.15
  395.5 5.4 collective-permute-done.15
  403.2 5.3 collective-permute-start.16
  435.3 7.0 collective-permute-done.17
  445.4 6.0 collective-permute-start.21
  455.1 10.0 %collective-permute-done.23.refs_10_ = bf16[512,512]{1,0:T(8,128)(2,1)} collective-permute-done((bf16[512,512]{1,0:T(8,128)(2,1)S(1)}, bf16[512,512]{1,0:T(8,128)(2,1)}, u32[]{:S(2)}, u32[]{:S(2)}) %collective-permute-start.23) | collective-permute-done | bytes 524320 | tf_op jit(solution)/shard_map/ppermute | solution.py:57
  467.9 8.3 collective-permute-done.29.refs_6_.refs_9_
  477.0 19.5 %mlp.2 = (bf16[1024,2048]{1,0:T(8,128)(2,1)}, bf16[1024,1024]{1,0:T(8,128)(2,1)}, bf16[1024,2048]{1,0:T(8,128)(2,1)}, f32[512,1]{1,0:T(8,128)}, f32[512,1]{1,0:T(8,128)}, /*index=5*/bf16[512,2048]{1,0:T(8,128)(2,1)}) custom-call(s32[1]{0:T(128)} %bitcast.refs_0_, f32[1,2048]{1,0:T(1,128)} %get-tuple-element.170.refs_1_, ...), custom_call_target="tpu_custom_call" | custom-call | flops 10737418240 | bytes 27262976 | tf_op jit(solution)/shard_map/mlp/pallas_call | solution.py:329
  501.6 6.9 collective-permute-done.30
  511.3 13.5 %collective-permute-start.31 = (bf16[512,512]{1,0:T(8,128)(2,1)}, bf16[512,512]{1,0:T(8,128)(2,1)}, u32[]{:S(2)}, u32[]{:S(2)}) collective-permute-start(bf16[512,512]{1,0:T(8,128)(2,1)} %get-tuple-element.147), channel_id=1, source_target_pairs={{0,1},{1,2},{4,5},{5,6},{8,9},{9,10},{12,13},{13,14},{16,17},{17,1... | collective-permute-start | bytes 1572872 | tf_op jit(solution)/shard_map/ppermute | solution.py:95
  525.6 19.4 %mlp.3 = (bf16[1024,2048]{1,0:T(8,128)(2,1)}, bf16[1024,1024]{1,0:T(8,128)(2,1)}, bf16[1024,2048]{1,0:T(8,128)(2,1)}, f32[512,1]{1,0:T(8,128)}, f32[512,1]{1,0:T(8,128)}, /*index=5*/bf16[512,2048]{1,0:T(8,128)(2,1)}) custom-call(s32[1]{0:T(128)} %bitcast.refs_0_, ...), custom_call_target="tpu_custom_call", output_to_operand_aliasing={{0}: (11, {}), {1}: (12, {}), {2}: (13, {})} | custom-call | flops 10737418240 | bytes 27262976 | tf_op jit(solution)/shard_map/mlp/pallas_call | solution.py:329
  546.9 8.2 collective-permute-start.33
  555.4 11.6 %collective-permute-done.33 = bf16[512,512]{1,0:T(8,128)(2,1)} collective-permute-done((bf16[512,512]{1,0:T(8,128)(2,1)}, bf16[512,512]{1,0:T(8,128)(2,1)}, u32[]{:S(2)}, u32[]{:S(2)}) %collective-permute-start.33) | collective-permute-done | bytes 524320 | tf_op jit(solution)/shard_map/ppermute | solution.py:87
  569.6 5.3 collective-permute-start.34
  586.3 9.9 collective-permute-done.41
  609.9 5.4 collective-permute-start.42
  627.6 6.3 collective-permute-start.45
  633.8 7.7 convolution_convert_fusion.4
  650.3 14.6 %convolution_convert_fusion.1 = bf16[2048,2048]{1,0:T(8,128)(2,1)} fusion(bf16[1024,2048]{1,0:T(8,128)(2,1)} %get-tuple-element.96, bf16[1024,2048]{1,0:T(8,128)(2,1)} %get-tuple-element.97), kind=kOutput, calls=%fused_computation.5 | convolution fusion | flops 8594128896 | bytes 16777216 | tf_op jit(solution)/shard_map/dot_general | solution.py:24
  671.4 8.4 fusion.7
  680.6 11.3 %gate_backward.2 = (bf16[1024,1024]{1,0:T(8,128)(2,1)}, bf16[1024,1024]{1,0:T(8,128)(2,1)}, bf16[1024,2048]{1,0:T(8,128)(2,1)}, f32[2,256,512]{2,1,0:T(8,128)}, f32[2,512,1]{2,1,0:T(8,128)}) custom-call(s32[1]{0:T(128)} %bitcast.refs_0_, f32[2]{0:T(128)} %negate_log-plus-one_fusion.refs_1_.refs_0_, bf16[1024,512]{1,0:T(8,128)(2,1)} %get-tuple-element.66.refs_1_.refs_2_, ...), custom_call_target="tpu_custom_call" | custom-call | flops 2415919104 | bytes 8388608 | tf_op jit(solution)/shard_map/gate_backward/pallas_call | solution.py:494
  692.7 11.2 %gate_backward.3 = (bf16[1024,1024]{1,0:T(8,128)(2,1)}, bf16[1024,1024]{1,0:T(8,128)(2,1)}, bf16[1024,2048]{1,0:T(8,128)(2,1)}, f32[2,256,512]{2,1,0:T(8,128)}, f32[2,512,1]{2,1,0:T(8,128)}) custom-call(s32[1]{0:T(128)} %bitcast.refs_0_, f32[2]{0:T(128)} %negate_log-plus-one_fusion.refs_1_.refs_0_, ...), custom_call_target="tpu_custom_call", output_to_operand_aliasing={{0}: (13, {}), {1}: (14, {}), {2}: (15, {})} | custom-call | flops 2415919104 | bytes 8388608 | tf_op jit(solution)/shard_map/gate_backward/pallas_call | solution.py:494
  707.7 8.4 convolution_convert_fusion.3
  717.7 8.3 convolution_convert_fusion.2
  732.5 14.3 %collective-permute-done.60 = bf16[2,256,512]{2,1,0:T(8,128)(2,1)S(1)} collective-permute-done((bf16[2,256,512]{2,1,0:T(8,128)(2,1)S(1)}, bf16[2,256,512]{2,1,0:T(8,128)(2,1)S(1)}, u32[]{:S(2)}, u32[]{:S(2)}) %collective-permute-start.60) | collective-permute-done | bytes 524320 | tf_op jit(solution)/shard_map/ppermute | solution.py:136
  748.9 24.0 %retention_backward.1 = (bf16[1024,3072]{1,0:T(8,128)(2,1)}, f32[2,1024,1]{2,1,0:T(8,128)}) custom-call(f32[2]{0:T(128)} %negate_log-plus-one_fusion.refs_1_.refs_0_, bf16[1024,512]{1,0:T(8,128)(2,1)} %get-tuple-element.66.refs_1_.refs_2_, bf16[1024,512]{1,0:T(8,128)(2,1)} %get-tuple-element.67.refs_2_, bf16[1024,1024]{1,0:T(8,128)(2,1)} %get-tuple-element.68.refs_3_, ...), custom_call_target="tpu_custom_call" | custom-call | flops 6308233216 | bytes 12582912 | tf_op jit(solution)/shard_map/retention_backward/pallas_call | solution.py:600
  773.0 11.8 %fusion.12 = bf16[512,2048]{1,0:T(8,128)(2,1)} fusion(bf16[2048,4096]{1,0:T(8,128)(2,1)} %all-gather.4.cloned.1.call-done.refs_3_.w_ref.refs_6_, bf16[1024,3072]{1,0:T(8,128)(2,1)} %get-tuple-element.117), kind=kOutput, calls=%fused_computation.15 | convolution fusion | flops 6443499520 | bytes 17825792 | tf_op jit(solution)/shard_map/dot_general | solution.py:28
  784.8 10.8 %fusion.17 = bf16[512,2048]{1,0:T(8,128)(2,1)S(1)} fusion(bf16[2048,4096]{1,0:T(8,128)(2,1)} %all-gather.4.cloned.1.call-done.refs_3_.w_ref.refs_6_, bf16[1024,3072]{1,0:T(8,128)(2,1)S(1)} %copy-done.59), kind=kOutput, calls=%fused_computation.16 | convolution fusion | flops 6443499520 | bytes 17825792 | tf_op jit(solution)/shard_map/dot_general | solution.py:28
  795.6 11.4 %convolution_convert_fusion = bf16[2048,2048]{1,0:T(8,128)(2,1)} fusion(bf16[1024,2048]{1,0:T(8,128)(2,1)S(1)} %copy-done.20, bf16[1024,3072]{1,0:T(8,128)(2,1)S(1)} %copy-done.59), kind=kOutput, calls=%fused_computation.4 | convolution fusion | flops 8594128896 | bytes 16777216 | tf_op jit(solution)/shard_map/dot_general | solution.py:24
  808.3 7.0 collective-permute-start.61
  818.3 9.3 collective-permute-done.61
  833.3 16.7 %collective-permute-done.46 = bf16[1024,512]{1,0:T(8,128)(2,1)S(1)} collective-permute-done((bf16[1024,512]{1,0:T(8,128)(2,1)S(1)}, bf16[1024,512]{1,0:T(8,128)(2,1)S(1)}, u32[]{:S(2)}, u32[]{:S(2)}) %collective-permute-start.46) | collective-permute-done | bytes 1048608 | tf_op jit(solution)/shard_map/ppermute | solution.py:87
  851.7 5.4 collective-permute-start.47
  874.4 18.1 %collective-permute-done.66 = f32[8,128]{1,0:T(8,128)S(1)} collective-permute-done((f32[8,128]{1,0:T(8,128)S(1)}, f32[8,128]{1,0:T(8,128)S(1)}, u32[]{:S(2)}, u32[]{:S(2)}) %collective-permute-start.66) | collective-permute-done | bytes 4128 | tf_op jit(solution)/shard_map/ppermute | solution.py:112
  924.3 28.0 %collective-permute-done.63 = bf16[512,512]{1,0:T(8,128)(2,1)S(1)} collective-permute-done((bf16[512,512]{1,0:T(8,128)(2,1)S(1)}, bf16[512,512]{1,0:T(8,128)(2,1)S(1)}, u32[]{:S(2)}, u32[]{:S(2)}) %collective-permute-start.63) | collective-permute-done | bytes 524320 | tf_op jit(solution)/shard_map/ppermute | solution.py:95
  (358 shorter events, 251.4 us)
Async XLA Ops:
  7.2 277.9 %all-gather.4.cloned.1.call-start = ((), (), s32[]{:S(2)}) async-start(), calls=%async_computation.5 | async-start | bytes 18874368 | tf_op jit(solution)/shard_map/all_gather | solution.py:661
  71.9 396.0 %all-gather.8.cloned.1.call-start = ((), (), s32[]{:S(2)}) async-start(), calls=%async_computation.7 | async-start | bytes 5242880 | tf_op jit(solution)/shard_map/all_gather | solution.py:679
  73.1 60.2 %collective-permute-start.3 = (bf16[1024,512]{1,0:T(8,128)(2,1)S(1)}, bf16[1024,512]{1,0:T(8,128)(2,1)S(1)}, u32[]{:S(2)}, u32[]{:S(2)}) collective-permute-start(bf16[1024,512]{1,0:T(8,128)(2,1)S(1)} %copy-done.30), channel_id=1, source_target_pairs={{0,1},{1,2},{2,3},{4,5},{5,6},{6,7},{8,9},{9,10},{10,11},{12,13},{... | collective-permute-start | bytes 3145736 | tf_op jit(solution)/shard_map/ppermute | solution.py:56
  133.4 334.5 %all-gather.6.cloned.1.call-start = ((), (), s32[]{:S(2)}) async-start(), calls=%async_computation.6 | async-start | bytes 14155776 | tf_op jit(solution)/shard_map/all_gather | solution.py:680
  133.4 26.6 %collective-permute-start.5 = (bf16[1024,512]{1,0:T(8,128)(2,1)S(1)}, bf16[1024,512]{1,0:T(8,128)(2,1)}, u32[]{:S(2)}, u32[]{:S(2)}) collective-permute-start(bf16[1024,512]{1,0:T(8,128)(2,1)S(1)} %copy-done.30), channel_id=1, source_target_pairs={{3,2},{2,1},{1,0},{7,6},{6,5},{5,4},{11,10},{10,9},{9,8},{15,14},{... | collective-permute-start | bytes 3145736 | tf_op jit(solution)/shard_map/ppermute | solution.py:57
  160.1 42.8 %collective-permute-start.6 = (bf16[1024,512]{1,0:T(8,128)(2,1)}, bf16[1024,512]{1,0:T(8,128)(2,1)S(1)}, u32[]{:S(2)}, u32[]{:S(2)}) collective-permute-start(bf16[1024,512]{1,0:T(8,128)(2,1)} %collective-permute-done.5.refs_12_), channel_id=1, source_target_pairs={{2,1},{1,0},{6,5},{5,4},{10,9},{9,8},{14,13},{13,12},{18,17},{17,1... | collective-permute-start | bytes 3145736 | tf_op jit(solution)/shard_map/ppermute | solution.py:57
  161.3 41.5 %collective-permute-start.4 = (bf16[1024,512]{1,0:T(8,128)(2,1)S(1)}, bf16[1024,512]{1,0:T(8,128)(2,1)S(1)}, u32[]{:S(2)}, u32[]{:S(2)}) collective-permute-start(bf16[1024,512]{1,0:T(8,128)(2,1)S(1)} %collective-permute-done.3.refs_7_), channel_id=1, source_target_pairs={{1,2},{2,3},{5,6},{6,7},{9,10},{10,11},{13,14},{14,15},{17,18},{18... | collective-permute-start | bytes 3145736 | tf_op jit(solution)/shard_map/ppermute | solution.py:56
  203.0 72.9 %collective-permute-start.7 = (bf16[1024,512]{1,0:T(8,128)(2,1)S(1)}, bf16[1024,512]{1,0:T(8,128)(2,1)}, u32[]{:S(2)}, u32[]{:S(2)}) collective-permute-start(bf16[1024,512]{1,0:T(8,128)(2,1)S(1)} %broadcast_select_fusion), channel_id=1, source_target_pairs={{2,3},{1,0},{6,7},{5,4},{10,11},{9,8},{14,15},{13,12},{18,19},{17,... | collective-permute-start | bytes 3145736 | tf_op jit(solution)/shard_map/ppermute | solution.py:52
  276.0 683.4 %reduce-scatter.14.cloned.1.call-start = ((), (), s32[]{:S(2)}) async-start(), calls=%async_computation.12 | async-start | bytes 4718592 | tf_op jit(solution)/shard_map/reduce_scatter | solution.py:787
  311.1 25.5 %collective-permute-start.9 = (bf16[2,256,512]{2,1,0:T(8,128)(2,1)S(1)}, bf16[2,256,512]{2,1,0:T(8,128)(2,1)S(1)}, u32[]{:S(2)}, u32[]{:S(2)}) collective-permute-start(bf16[2,256,512]{2,1,0:T(8,128)(2,1)S(1)} %fusion.27), channel_id=1, source_target_pairs={{0,8},{4,12},{8,0},{12,4},{1,9},{5,13},{9,1},{13,5},{2,10},{6,14},... | collective-permute-start | bytes 1572872 | tf_op jit(solution)/shard_map/ppermute | solution.py:121
  430.8 22.9 %collective-permute-start.28 = (bf16[512,512]{1,0:T(8,128)(2,1)S(1)}, bf16[512,512]{1,0:T(8,128)(2,1)S(1)}, u32[]{:S(2)}, u32[]{:S(2)}) collective-permute-start(bf16[512,512]{1,0:T(8,128)(2,1)S(1)} %collective-permute-done.27.refs_10_), channel_id=1, source_target_pairs={{2,1},{1,0},{6,5},{5,4},{10,9},{9,8},{14,13},{13,12},{18,17},{17,1... | collective-permute-start | bytes 1572872 | tf_op jit(solution)/shard_map/ppermute | solution.py:57
  444.1 20.9 %collective-permute-start.23 = (bf16[512,512]{1,0:T(8,128)(2,1)S(1)}, bf16[512,512]{1,0:T(8,128)(2,1)}, u32[]{:S(2)}, u32[]{:S(2)}) collective-permute-start(bf16[512,512]{1,0:T(8,128)(2,1)S(1)} %get-tuple-element.130.refs_4_), channel_id=1, source_target_pairs={{3,2},{2,1},{1,0},{7,6},{6,5},{5,4},{11,10},{10,9},{9,8},{15,14},{... | collective-permute-start | bytes 1572872 | tf_op jit(solution)/shard_map/ppermute | solution.py:57
  445.4 20.9 %collective-permute-start.21 = (bf16[512,512]{1,0:T(8,128)(2,1)S(1)}, bf16[512,512]{1,0:T(8,128)(2,1)}, u32[]{:S(2)}, u32[]{:S(2)}) collective-permute-start(bf16[512,512]{1,0:T(8,128)(2,1)S(1)} %get-tuple-element.130.refs_4_), channel_id=1, source_target_pairs={{0,1},{1,2},{2,3},{4,5},{5,6},{6,7},{8,9},{9,10},{10,11},{12,13},{... | collective-permute-start | bytes 1572872 | tf_op jit(solution)/shard_map/ppermute | solution.py:56
  453.8 22.4 %collective-permute-start.29 = (bf16[512,512]{1,0:T(8,128)(2,1)S(1)}, bf16[512,512]{1,0:T(8,128)(2,1)S(1)}, u32[]{:S(2)}, u32[]{:S(2)}) collective-permute-start(bf16[512,512]{1,0:T(8,128)(2,1)S(1)} %broadcast_select_fusion.4), channel_id=1, source_target_pairs={{2,3},{1,0},{6,7},{5,4},{10,11},{9,8},{14,15},{13,12},{18,19},{17,... | collective-permute-start | bytes 1572872 | tf_op jit(solution)/shard_map/ppermute | solution.py:52
  465.0 34.1 %collective-permute-start.24 = (bf16[512,512]{1,0:T(8,128)(2,1)}, bf16[512,512]{1,0:T(8,128)(2,1)}, u32[]{:S(2)}, u32[]{:S(2)}) collective-permute-start(bf16[512,512]{1,0:T(8,128)(2,1)} %collective-permute-done.23.refs_10_), channel_id=1, source_target_pairs={{2,1},{1,0},{6,5},{5,4},{10,9},{9,8},{14,13},{13,12},{18,17},{17,1... | collective-permute-start | bytes 1572872 | tf_op jit(solution)/shard_map/ppermute | solution.py:57
  466.4 32.8 %collective-permute-start.22 = (bf16[512,512]{1,0:T(8,128)(2,1)}, bf16[512,512]{1,0:T(8,128)(2,1)}, u32[]{:S(2)}, u32[]{:S(2)}) collective-permute-start(bf16[512,512]{1,0:T(8,128)(2,1)} %collective-permute-done.21.refs_5_), channel_id=1, source_target_pairs={{1,2},{2,3},{5,6},{6,7},{9,10},{10,11},{13,14},{14,15},{17,18},{18... | collective-permute-start | bytes 1572872 | tf_op jit(solution)/shard_map/ppermute | solution.py:56
  500.3 24.5 %collective-permute-start.25 = (bf16[512,512]{1,0:T(8,128)(2,1)S(1)}, bf16[512,512]{1,0:T(8,128)(2,1)S(1)}, u32[]{:S(2)}, u32[]{:S(2)}) collective-permute-start(bf16[512,512]{1,0:T(8,128)(2,1)S(1)} %broadcast_select_fusion.5), channel_id=1, source_target_pairs={{2,3},{1,0},{6,7},{5,4},{10,11},{9,8},{14,15},{13,12},{18,19},{17,... | collective-permute-start | bytes 1572872 | tf_op jit(solution)/shard_map/ppermute | solution.py:52
  509.8 35.2 %collective-permute-start.32 = (bf16[512,512]{1,0:T(8,128)(2,1)}, bf16[512,512]{1,0:T(8,128)(2,1)}, u32[]{:S(2)}, u32[]{:S(2)}) collective-permute-start(bf16[512,512]{1,0:T(8,128)(2,1)} %get-tuple-element.146), channel_id=1, source_target_pairs={{3,2},{2,1},{7,6},{6,5},{11,10},{10,9},{15,14},{14,13},{19,18},{18... | collective-permute-start | bytes 1572872 | tf_op jit(solution)/shard_map/ppermute | solution.py:96
  511.3 33.8 %collective-permute-start.31 = (bf16[512,512]{1,0:T(8,128)(2,1)}, bf16[512,512]{1,0:T(8,128)(2,1)}, u32[]{:S(2)}, u32[]{:S(2)}) collective-permute-start(bf16[512,512]{1,0:T(8,128)(2,1)} %get-tuple-element.147), channel_id=1, source_target_pairs={{0,1},{1,2},{4,5},{5,6},{8,9},{9,10},{12,13},{13,14},{16,17},{17,1... | collective-permute-start | bytes 1572872 | tf_op jit(solution)/shard_map/ppermute | solution.py:95
  555.3 27.2 %collective-permute-start.40 = (f32[4,128]{1,0:T(4,128)S(1)}, f32[4,128]{1,0:T(4,128)S(1)}, u32[]{:S(2)}, u32[]{:S(2)}) collective-permute-start(f32[4,128]{1,0:T(4,128)S(1)} %bitcast.46), channel_id=1, source_target_pairs={{0,1},{1,0},{2,3},{3,2},{4,5},{5,4},{6,7},{7,6},{8,9},{9,8},{10,11... | collective-permute-start | bytes 6152 | tf_op jit(solution)/shard_map/ppermute | solution.py:112
  569.6 27.8 %collective-permute-start.34 = (bf16[512,512]{1,0:T(8,128)(2,1)}, bf16[512,512]{1,0:T(8,128)(2,1)}, u32[]{:S(2)}, u32[]{:S(2)}) collective-permute-start(bf16[512,512]{1,0:T(8,128)(2,1)} %get-tuple-element.144), channel_id=1, source_target_pairs={{0,1},{1,2},{4,5},{5,6},{8,9},{9,10},{12,13},{13,14},{16,17},{17,1... | collective-permute-start | bytes 1572872 | tf_op jit(solution)/shard_map/ppermute | solution.py:95
  574.9 22.4 %collective-permute-start.36 = (bf16[512,512]{1,0:T(8,128)(2,1)}, bf16[512,512]{1,0:T(8,128)(2,1)}, u32[]{:S(2)}, u32[]{:S(2)}) collective-permute-start(bf16[512,512]{1,0:T(8,128)(2,1)} %get-tuple-element.145), channel_id=1, source_target_pairs={{3,2},{2,1},{7,6},{6,5},{11,10},{10,9},{15,14},{14,13},{19,18},{18... | collective-permute-start | bytes 1572872 | tf_op jit(solution)/shard_map/ppermute | solution.py:96
  578.9 27.2 %collective-permute-start.38 = (bf16[512,512]{1,0:T(8,128)(2,1)}, bf16[512,512]{1,0:T(8,128)(2,1)}, u32[]{:S(2)}, u32[]{:S(2)}) collective-permute-start(bf16[512,512]{1,0:T(8,128)(2,1)} %get-tuple-element.158), channel_id=1, source_target_pairs={{0,1},{1,2},{2,3},{4,5},{5,6},{6,7},{8,9},{9,10},{10,11},{12,13},{... | collective-permute-start | bytes 1572872 | tf_op jit(solution)/shard_map/ppermute | solution.py:95
  581.2 25.0 %collective-permute-start.39 = (bf16[512,512]{1,0:T(8,128)(2,1)}, bf16[512,512]{1,0:T(8,128)(2,1)}, u32[]{:S(2)}, u32[]{:S(2)}) collective-permute-start(bf16[512,512]{1,0:T(8,128)(2,1)} %get-tuple-element.159), channel_id=1, source_target_pairs={{3,2},{2,1},{1,0},{7,6},{6,5},{5,4},{11,10},{10,9},{9,8},{15,14},{... | collective-permute-start | bytes 1572872 | tf_op jit(solution)/shard_map/ppermute | solution.py:96
  600.1 23.4 %collective-permute-start.35 = (bf16[512,512]{1,0:T(8,128)(2,1)}, bf16[512,512]{1,0:T(8,128)(2,1)}, u32[]{:S(2)}, u32[]{:S(2)}) collective-permute-start(bf16[512,512]{1,0:T(8,128)(2,1)} %get-tuple-element.160), channel_id=1, source_target_pairs={{0,1},{1,2},{2,3},{4,5},{5,6},{6,7},{8,9},{9,10},{10,11},{12,13},{... | collective-permute-start | bytes 1572872 | tf_op jit(solution)/shard_map/ppermute | solution.py:95
  626.3 21.6 %collective-permute-start.56 = (bf16[512,512]{1,0:T(8,128)(2,1)S(1)}, bf16[512,512]{1,0:T(8,128)(2,1)S(1)}, u32[]{:S(2)}, u32[]{:S(2)}) collective-permute-start(bf16[512,512]{1,0:T(8,128)(2,1)S(1)} %fusion.32.refs_6_), channel_id=1, source_target_pairs={{3,2},{2,1},{1,0},{7,6},{6,5},{5,4},{11,10},{10,9},{9,8},{15,14},{... | collective-permute-start | bytes 1572872 | tf_op jit(solution)/shard_map/ppermute | solution.py:57
  627.6 22.0 %collective-permute-start.45 = (bf16[512,512]{1,0:T(8,128)(2,1)S(1)}, bf16[512,512]{1,0:T(8,128)(2,1)}, u32[]{:S(2)}, u32[]{:S(2)}) collective-permute-start(bf16[512,512]{1,0:T(8,128)(2,1)S(1)} %fusion.32.refs_6_), channel_id=1, source_target_pairs={{0,1},{1,2},{2,3},{4,5},{5,6},{6,7},{8,9},{9,10},{10,11},{12,13},{... | collective-permute-start | bytes 1572872 | tf_op jit(solution)/shard_map/ppermute | solution.py:56
  641.6 324.1 %reduce-scatter.10.cloned.1.call-start = ((), (), s32[]{:S(2)}) async-start(), calls=%async_computation.10 | async-start | bytes 4718592 | tf_op jit(solution)/shard_map/reduce_scatter | solution.py:787
  641.7 23.2 %collective-permute-start.51 = (bf16[512,512]{1,0:T(8,128)(2,1)}, bf16[512,512]{1,0:T(8,128)(2,1)S(1)}, u32[]{:S(2)}, u32[]{:S(2)}) collective-permute-start(bf16[512,512]{1,0:T(8,128)(2,1)} %collective-permute-done.42.refs_7_), channel_id=1, source_target_pairs={{1,2},{2,3},{5,6},{6,7},{9,10},{10,11},{13,14},{14,15},{17,18},{18... | collective-permute-start | bytes 1572872 | tf_op jit(solution)/shard_map/ppermute | solution.py:56
  642.4 22.5 %collective-permute-start.53 = (bf16[512,512]{1,0:T(8,128)(2,1)}, bf16[512,512]{1,0:T(8,128)(2,1)S(1)}, u32[]{:S(2)}, u32[]{:S(2)}) collective-permute-start(bf16[512,512]{1,0:T(8,128)(2,1)} %collective-permute-done.52.refs_12_), channel_id=1, source_target_pairs={{2,1},{1,0},{6,5},{5,4},{10,9},{9,8},{14,13},{13,12},{18,17},{17,1... | collective-permute-start | bytes 1572872 | tf_op jit(solution)/shard_map/ppermute | solution.py:57
  647.9 21.3 %collective-permute-start.57 = (bf16[512,512]{1,0:T(8,128)(2,1)S(1)}, bf16[512,512]{1,0:T(8,128)(2,1)S(1)}, u32[]{:S(2)}, u32[]{:S(2)}) collective-permute-start(bf16[512,512]{1,0:T(8,128)(2,1)S(1)} %collective-permute-done.56.refs_12_), channel_id=1, source_target_pairs={{2,1},{1,0},{6,5},{5,4},{10,9},{9,8},{14,13},{13,12},{18,17},{17,1... | collective-permute-start | bytes 1572872 | tf_op jit(solution)/shard_map/ppermute | solution.py:57
  670.1 21.8 %collective-permute-start.58 = (bf16[512,512]{1,0:T(8,128)(2,1)}, bf16[512,512]{1,0:T(8,128)(2,1)S(1)}, u32[]{:S(2)}, u32[]{:S(2)}) collective-permute-start(bf16[512,512]{1,0:T(8,128)(2,1)} %broadcast_select_fusion.2), channel_id=1, source_target_pairs={{2,3},{1,0},{6,7},{5,4},{10,11},{9,8},{14,15},{13,12},{18,19},{17,... | collective-permute-start | bytes 1572872 | tf_op jit(solution)/shard_map/ppermute | solution.py:52
  716.1 251.8 %reduce-scatter.8.cloned.1.call-start = ((), (), s32[]{:S(2)}) async-start(), calls=%async_computation.9 | async-start | bytes 4718592 | tf_op jit(solution)/shard_map/reduce_scatter | solution.py:787
  726.0 244.0 %reduce-scatter.12.cloned.1.call-start = ((), (), s32[]{:S(2)}) async-start(), calls=%async_computation.11 | async-start | bytes 9437184 | tf_op jit(solution)/shard_map/reduce_scatter | solution.py:787
  726.8 250.7 %reduce-scatter.6.cloned.1.call-start = ((), (), s32[]{:S(2)}) async-start(), calls=%async_computation.8 | async-start | bytes 9437184 | tf_op jit(solution)/shard_map/reduce_scatter | solution.py:787
  816.8 33.3 %collective-permute-start.46 = (bf16[1024,512]{1,0:T(8,128)(2,1)S(1)}, bf16[1024,512]{1,0:T(8,128)(2,1)S(1)}, u32[]{:S(2)}, u32[]{:S(2)}) collective-permute-start(bf16[1024,512]{1,0:T(8,128)(2,1)S(1)} %constant_dynamic-slice_fusion.2), channel_id=1, source_target_pairs={{0,1},{3,2},{4,5},{7,6},{8,9},{11,10},{12,13},{15,14},{16,17},{19,... | collective-permute-start | bytes 3145736 | tf_op jit(solution)/shard_map/ppermute | solution.py:87
  828.9 32.3 %collective-permute-start.68 = (bf16[512,512]{1,0:T(8,128)(2,1)S(1)}, bf16[512,512]{1,0:T(8,128)(2,1)S(1)}, u32[]{:S(2)}, u32[]{:S(2)}) collective-permute-start(bf16[512,512]{1,0:T(8,128)(2,1)S(1)} %constant_dynamic-slice_fusion), channel_id=1, source_target_pairs={{0,1},{3,2},{4,5},{7,6},{8,9},{11,10},{12,13},{15,14},{16,17},{19,... | collective-permute-start | bytes 1572872 | tf_op jit(solution)/shard_map/ppermute | solution.py:87
  851.7 48.2 %collective-permute-start.47 = (bf16[1024,512]{1,0:T(8,128)(2,1)}, bf16[1024,512]{1,0:T(8,128)(2,1)}, u32[]{:S(2)}, u32[]{:S(2)}) collective-permute-start(bf16[1024,512]{1,0:T(8,128)(2,1)} %get-tuple-element.135), channel_id=1, source_target_pairs={{0,1},{1,2},{4,5},{5,6},{8,9},{9,10},{12,13},{13,14},{16,17},{17,1... | collective-permute-start | bytes 3145736 | tf_op jit(solution)/shard_map/ppermute | solution.py:95
  857.2 47.3 %collective-permute-start.49 = (bf16[1024,512]{1,0:T(8,128)(2,1)S(1)}, bf16[1024,512]{1,0:T(8,128)(2,1)}, u32[]{:S(2)}, u32[]{:S(2)}) collective-permute-start(bf16[1024,512]{1,0:T(8,128)(2,1)S(1)} %get-tuple-element.136), channel_id=1, source_target_pairs={{3,2},{2,1},{7,6},{6,5},{11,10},{10,9},{15,14},{14,13},{19,18},{18... | collective-permute-start | bytes 3145736 | tf_op jit(solution)/shard_map/ppermute | solution.py:96
  862.6 30.6 %collective-permute-start.69 = (bf16[512,512]{1,0:T(8,128)(2,1)}, bf16[512,512]{1,0:T(8,128)(2,1)}, u32[]{:S(2)}, u32[]{:S(2)}) collective-permute-start(bf16[512,512]{1,0:T(8,128)(2,1)} %get-tuple-element.140), channel_id=1, source_target_pairs={{0,1},{1,2},{4,5},{5,6},{8,9},{9,10},{12,13},{13,14},{16,17},{17,1... | collective-permute-start | bytes 1572872 | tf_op jit(solution)/shard_map/ppermute | solution.py:95
  867.8 26.1 %collective-permute-start.71 = (bf16[512,512]{1,0:T(8,128)(2,1)}, bf16[512,512]{1,0:T(8,128)(2,1)}, u32[]{:S(2)}, u32[]{:S(2)}) collective-permute-start(bf16[512,512]{1,0:T(8,128)(2,1)} %get-tuple-element.141), channel_id=1, source_target_pairs={{3,2},{2,1},{7,6},{6,5},{11,10},{10,9},{15,14},{14,13},{19,18},{18... | collective-permute-start | bytes 1572872 | tf_op jit(solution)/shard_map/ppermute | solution.py:96
  893.2 21.0 %collective-permute-start.64 = (bf16[512,512]{1,0:T(8,128)(2,1)}, bf16[512,512]{1,0:T(8,128)(2,1)S(1)}, u32[]{:S(2)}, u32[]{:S(2)}) collective-permute-start(bf16[512,512]{1,0:T(8,128)(2,1)} %get-tuple-element.124), channel_id=1, source_target_pairs={{3,2},{2,1},{7,6},{6,5},{11,10},{10,9},{15,14},{14,13},{19,18},{18... | collective-permute-start | bytes 1572872 | tf_op jit(solution)/shard_map/ppermute | solution.py:96
  893.9 20.3 %collective-permute-start.62 = (bf16[512,512]{1,0:T(8,128)(2,1)}, bf16[512,512]{1,0:T(8,128)(2,1)S(1)}, u32[]{:S(2)}, u32[]{:S(2)}) collective-permute-start(bf16[512,512]{1,0:T(8,128)(2,1)} %get-tuple-element.142), channel_id=1, source_target_pairs={{0,1},{1,2},{4,5},{5,6},{8,9},{9,10},{12,13},{13,14},{16,17},{17,1... | collective-permute-start | bytes 1572872 | tf_op jit(solution)/shard_map/ppermute | solution.py:95
  899.9 22.1 %collective-permute-start.70 = (bf16[512,512]{1,0:T(8,128)(2,1)S(1)}, bf16[512,512]{1,0:T(8,128)(2,1)S(1)}, u32[]{:S(2)}, u32[]{:S(2)}) collective-permute-start(bf16[512,512]{1,0:T(8,128)(2,1)S(1)} %get-tuple-element.156), channel_id=1, source_target_pairs={{0,1},{1,2},{2,3},{4,5},{5,6},{6,7},{8,9},{9,10},{10,11},{12,13},{... | collective-permute-start | bytes 1572872 | tf_op jit(solution)/shard_map/ppermute | solution.py:95
  909.0 47.5 %collective-permute-start.48 = (bf16[1024,512]{1,0:T(8,128)(2,1)S(1)}, bf16[1024,512]{1,0:T(8,128)(2,1)S(1)}, u32[]{:S(2)}, u32[]{:S(2)}) collective-permute-start(bf16[1024,512]{1,0:T(8,128)(2,1)S(1)} %get-tuple-element.138), channel_id=1, source_target_pairs={{0,1},{1,2},{2,3},{4,5},{5,6},{6,7},{8,9},{9,10},{10,11},{12,13},{... | collective-permute-start | bytes 3145736 | tf_op jit(solution)/shard_map/ppermute | solution.py:95
  914.6 37.7 %collective-permute-start.63 = (bf16[512,512]{1,0:T(8,128)(2,1)S(1)}, bf16[512,512]{1,0:T(8,128)(2,1)S(1)}, u32[]{:S(2)}, u32[]{:S(2)}) collective-permute-start(bf16[512,512]{1,0:T(8,128)(2,1)S(1)} %get-tuple-element.154), channel_id=1, source_target_pairs={{0,1},{1,2},{2,3},{4,5},{5,6},{6,7},{8,9},{9,10},{10,11},{12,13},{... | collective-permute-start | bytes 1572872 | tf_op jit(solution)/shard_map/ppermute | solution.py:95
  916.5 35.8 %collective-permute-start.65 = (bf16[512,512]{1,0:T(8,128)(2,1)S(1)}, bf16[512,512]{1,0:T(8,128)(2,1)S(1)}, u32[]{:S(2)}, u32[]{:S(2)}) collective-permute-start(bf16[512,512]{1,0:T(8,128)(2,1)S(1)} %get-tuple-element.155), channel_id=1, source_target_pairs={{3,2},{2,1},{1,0},{7,6},{6,5},{5,4},{11,10},{10,9},{9,8},{15,14},{... | collective-permute-start | bytes 1572872 | tf_op jit(solution)/shard_map/ppermute | solution.py:96
  922.0 34.5 %collective-permute-start.50 = (bf16[1024,512]{1,0:T(8,128)(2,1)S(1)}, bf16[1024,512]{1,0:T(8,128)(2,1)S(1)}, u32[]{:S(2)}, u32[]{:S(2)}) collective-permute-start(bf16[1024,512]{1,0:T(8,128)(2,1)S(1)} %get-tuple-element.139), channel_id=1, source_target_pairs={{3,2},{2,1},{1,0},{7,6},{6,5},{5,4},{11,10},{10,9},{9,8},{15,14},{... | collective-permute-start | bytes 3145736 | tf_op jit(solution)/shard_map/ppermute | solution.py:96
  (97 other events, 1811.5 us)
Sparse Core Ops, SparseCore 0:
  72.1 92.4 all-gather.3
  166.1 98.6 all-gather.7
  276.1 84.9 all-gather.5
  641.7 55.1 reduce-scatter.13
  716.2 56.6 reduce-scatter.9
  776.1 51.1 reduce-scatter.7
  830.8 71.5 reduce-scatter.11
  905.8 71.5 reduce-scatter.5

commit v2 on v1

--- a/solution.py
+++ b/solution.py
@@ -11,7 +11,7 @@
 HK = 256
 HV = 512
 EPSILON = 1e-06
-BLOCK = 256
+BLOCK = 512
 F32 = jnp.float32
 BF16 = jnp.bfloat16
 
@@ -155,37 +155,41 @@
     widths = [a.shape[1] for a in arrays]
 
     def kernel(*refs):
-        parts, out, sems = refs[:-2], refs[-2], refs[-1]
-        copies, column = [], 0
-        for i, width in enumerate(widths):
-            copies.append(pltpu.make_async_copy(parts[i], out.at[:, column : column + width], sems.at[i]))
+        column = 0
+        for ref, width in zip(refs, widths):
+            refs[-1][:, column : column + width] = ref[...]
             column += width
-        for copy in copies:
-            copy.start()
-        for copy in copies:
-            copy.wait()
-
+
+    block = min(rows, 64)
     return pl.pallas_call(
         kernel,
-        in_specs=[pl.BlockSpec(memory_space=pl.ANY)] * len(arrays),
-        out_specs=pl.BlockSpec(memory_space=pl.ANY),
+        grid=(rows // block,),
+        in_specs=[pl.BlockSpec((block, width), lambda r: (r, 0)) for width in widths],
+        out_specs=pl.BlockSpec((block, sum(widths)), lambda r: (r, 0)),
         out_shape=jax.ShapeDtypeStruct((rows, sum(widths)), arrays[0].dtype),
-        scratch_shapes=[pltpu.SemaphoreType.DMA((len(arrays),))],
         cost_estimate=pl.CostEstimate(flops=0, bytes_accessed=4 * rows * sum(widths), transcendentals=0),
         name="side_by_side",
     )(*arrays)
 
 
+def gathered(at, refs, k, rows=slice(None)):
+    if k == 0:
+        return refs[0][rows, :]
+    return jnp.where(at >= k, refs[2 * k - 1][rows, :], refs[2 * k][rows, :])
+
+
+def columns_of(at, n, k, width):
+    return pl.ds(pl.multiple_of(((at + n - k) % n) * width, width), width)
+
+
 def fill_normed(at, refs, gain_ref, full_ref):
     n = len(refs) // 2 + 1
     width = refs[0].shape[1]
-    blocks = [refs[0][...].astype(F32)]
-    for k in range(1, n):
-        blocks.append(jnp.where(at >= k, refs[2 * k - 1][...], refs[2 * k][...]).astype(F32))
+    blocks = [gathered(at, refs, k).astype(F32) for k in range(n)]
     squares = sum(jnp.sum(b * b, axis=1, keepdims=True) for b in blocks)
     scale = lax.rsqrt(squares / (n * width) + EPSILON)
     for k, b in enumerate(blocks):
-        where = pl.ds(pl.multiple_of(((at + n - k) % n) * width, width), width)
+        where = columns_of(at, n, k, width)
         full_ref[:, where] = (b * scale * gain_ref[:, where]).astype(BF16)
     return scale
 
@@ -293,9 +297,13 @@
     )(x, w)
 
 
-def mlp_kernel(units, count, at_ref, gain_ref, w_ref, grad_ref, *refs):
-    blocks, (full_ref, hidden_ref, acts_ref, scale_ref, inner_ref, back_ref) = refs[:count], refs[-6:]
-    scale_ref[...] = fill_normed(at_ref[0], blocks, gain_ref, full_ref)
+def mlp_kernel(units, count, at_ref, gain_ref, w_ref, *refs):
+    blocks, grads = refs[:count], refs[count : 2 * count]
+    full_ref, hidden_ref, acts_ref, grad_ref, scale_ref, inner_ref, back_ref = refs[-7:]
+    at, n = at_ref[0], count // 2 + 1
+    scale_ref[...] = fill_normed(at, blocks, gain_ref, full_ref)
+    for k in range(n):
+        grad_ref[:, columns_of(at, n, k, grads[0].shape[1])] = gathered(at, grads, k)
     x = full_ref[...]
     gate = nn(x, w_ref[:, :units])
     up = nn(x, w_ref[:, units : 2 * units])
@@ -312,13 +320,13 @@
     back_ref[...] = (nt(g_gate, w_ref[:, :units]) + nt(g_up, w_ref[:, units : 2 * units])).astype(BF16)
 
 
-def mlp(at, gain, w, part, grad, x, pairs, shared):
+def mlp(at, gain, w, part, grads, x, pairs, shared):
     rows, width = x.shape
     features = w.shape[0]
     units = w.shape[1] // 3
     blocks = flat(x, pairs)
     steps = rows // BLOCK
-    total = grad.shape[0]
+    total = grads[0].shape[0]
 
     def by_rows(columns):
         return pl.BlockSpec((BLOCK, columns), lambda r: (r, 0))
@@ -333,27 +341,36 @@
             pl.BlockSpec(memory_space=pltpu.SMEM),
             pl.BlockSpec((1, features), lambda r: (0, 0)),
             pl.BlockSpec((features, 3 * units), lambda r: (0, 0)),
+            *[by_rows(width)] * len(blocks),
+            *[own_rows(width)] * len(grads),
+            *[pl.BlockSpec(memory_space=pl.ANY)] * len(shared),
+        ],
+        out_specs=[
             own_rows(features),
-            *[by_rows(width)] * len(blocks),
-            *[pl.BlockSpec(memory_space=pl.ANY)] * len(shared),
-        ],
-        out_specs=[own_rows(features), own_rows(units), own_rows(2 * units), by_rows(1), by_rows(1), by_rows(features)],
+            own_rows(units),
+            own_rows(2 * units),
+            own_rows(features),
+            by_rows(1),
+            by_rows(1),
+            by_rows(features),
+        ],
         out_shape=[
             jax.ShapeDtypeStruct((total, features), BF16),
             jax.ShapeDtypeStruct((total, units), BF16),
             jax.ShapeDtypeStruct((total, 2 * units), BF16),
+            jax.ShapeDtypeStruct((total, features), BF16),
             jax.ShapeDtypeStruct((rows, 1), F32),
             jax.ShapeDtypeStruct((rows, 1), F32),
             jax.ShapeDtypeStruct((rows, features), BF16),
         ],
-        input_output_aliases={4 + len(blocks) + i: i for i in range(len(shared))},
+        input_output_aliases={3 + 2 * len(blocks) + i: i for i in range(len(shared))},
         cost_estimate=pl.CostEstimate(
             flops=10 * rows * features * units,
             bytes_accessed=6 * features * units + 14 * rows * features,
             transcendentals=2 * rows * units,
         ),
         name="mlp",
-    )(at, gain, w, grad, *blocks, *shared)
+    )(at, gain, w, *blocks, *grads, *shared)
 
 
 def decay_vectors(log_gamma):
@@ -459,11 +476,7 @@
         @pl.when(head == 0)
         def _(at=at):
             for k in range(n):
-                block = blocks[0][cut(at), :]
-                if k:
-                    block = jnp.where(here >= k, blocks[2 * k - 1][cut(at), :], blocks[2 * k][cut(at), :])
-                where = pl.ds(pl.multiple_of(((here + n - k) % n) * width, width), width)
-                full_ref[cut(at), where] = block
+                full_ref[cut(at), columns_of(here, n, k, width)] = gathered(here, blocks, k, cut(at))
 
         grad = nn(full_ref[cut(at), :], w_ref[...])
         ret = ret_ref[cut(at), :]
@@ -676,7 +689,8 @@
     normed, scale_attn, q, k, v, local_state = project(
         here, log_gamma, gains[0:1], attn_full, layer_input, pairs, heads, cosine, sine
     )
-    grad_full = lax.all_gather(after(cotangent, pairs[0][0]), "tp", axis=1, tiled=True)
+    cot = after(cotangent, pairs[-1][0])
+    cot_blocks = flat(cot, line_gather(cot, "tp"))
     mlp_full = lax.all_gather(after(mlp_shard, pairs[0][1]), data, axis=0, tiled=True)
     gate_pre = product(after(normed, local_state), attn_full, (2 * qk + vw) // vw, vw)
     state_in = states_before(local_state, log_block, "ctx").astype(BF16)
@@ -688,6 +702,10 @@
         branch.append(out)
     gated, retained = heads_out
 
+    def stacked(*grads):
+        devices = math.prod(lax.axis_size(axis) for axis in data)
+        return jnp.concatenate([g.reshape(devices, -1, g.shape[1]) for g in grads], axis=1)
+
     x_own = layer_input.astype(F32)
     middle, mid_pairs, scale_mlp, inner_mlp, back, grad_middle, grad_own, grad_pairs = ([] for _ in range(8))
     gain_mlp_sum = 0.0
@@ -701,10 +719,8 @@
         lanes = 128
         return swap_sum(inner.reshape(-1, lanes), "tp").reshape(-1)
 
-    early = ()
     for c in range(parts):
-        total, steps = line_scatter(after(branch[c], *early), "tp")
-        early = steps[-1]
+        total = lax.psum_scatter(branch[c], "tp", scatter_dimension=1, tiled=True).astype(F32)
         if c:
             total = after(total, mid_pairs[c - 1][0][0])
         middle.append(x_own[cuts[c]] + total)
@@ -712,18 +728,16 @@
     shared = []
     for c in range(parts):
         *results, scale, inner, out = mlp(
-            here, gains[1:2], mlp_full, c, grad_full, middle[c].astype(BF16), mid_pairs[c], shared
+            here, gains[1:2], mlp_full, c, cot_blocks, middle[c].astype(BF16), mid_pairs[c], shared
         )
         shared = results
         scale_mlp.append(scale)
         inner_mlp.append(inner[:, 0])
         back.append(out)
-    normed_mlp, hidden, grad_acts = shared
-    early = ()
+    normed_mlp, hidden, grad_acts, grad_full = shared
     for c in range(parts):
         inner = row_total(inner_mlp[c])
-        total, steps = line_scatter(after(back[c], *early), "tp")
-        early = steps[-1]
+        total = lax.psum_scatter(back[c], "tp", scatter_dimension=1, tiled=True).astype(F32)
         if c:
             total = after(total, grad_pairs[c - 1][0][0])
         grad_mid, gain_sum = norm_back(middle[c], scale_mlp[c], gain_mlp, inner, total)
@@ -733,9 +747,10 @@
         grad_pairs.append(line_gather(grad_own[c], "tp"))
     grad_down = tn(grad_full, hidden).astype(BF16)
     grad_gate_up = tn(after(normed_mlp, grad_down), grad_acts).astype(BF16)
+    grad_mlp = stacked(grad_gate_up[:, :units], grad_gate_up[:, units:], grad_down)
     mlp_parts = nt(hidden, mlp_full[:, 2 * units :]).astype(BF16)
 
-    grad_own[0] = after(grad_own[0], grad_gate_up, grad_down, mlp_parts)
+    grad_own[0] = after(grad_own[0], grad_mlp, mlp_parts)
     mlp_out, _ = line_scatter(after(mlp_parts, grad_pairs[-1][0][0]), "tp")
     layer_output = (jnp.concatenate(middle) + mlp_out).astype(BF16)
     shared = []
@@ -763,8 +778,9 @@
     state_grad = state_grad.astype(BF16)
     grad_out = tn(after(grad_attn, got), gated).astype(BF16)
     grad_retgate = tn(normed, after(g_gate, got)).astype(BF16)
+    grad_heads = stacked(grad_retgate, grad_out)
     grads_attn, inner = retention_backward(
-        log_gamma, q, k, v, state_in, after(state_grad, grad_out, grad_retgate), cosine, sine, g_ret, g_gate
+        log_gamma, q, k, v, state_in, after(state_grad, grad_heads), cosine, sine, g_ret, g_gate
     )
     inner_attn = jnp.concatenate(inner_attn) + jnp.sum(inner[:, :, 0], axis=0)
     in_full = attn_full[:, : 2 * qk + 2 * vw]
@@ -786,10 +802,8 @@
     def shard(grad):
         return lax.psum_scatter(grad, data, scatter_dimension=0, tiled=True).astype(F32)
 
-    s_down = shard(grad_down)
-    s_gate_up = shard(grad_gate_up)
-    s_out = shard(grad_out)
-    s_retgate = shard(grad_retgate)
+    s_gate, s_up, s_down = jnp.split(shard(grad_mlp)[0], 3)
+    s_retgate, s_out = jnp.split(shard(grad_heads)[0], 2)
     s_qkv = shard(grad_qkv_w)
     s_query, s_key, s_value = s_qkv[:, :qk], s_qkv[:, qk : 2 * qk], s_qkv[:, 2 * qk :]
     gain_sums = swap_sum(swap_sum(jnp.stack([gain_attn_sum, gain_mlp_sum]), "ctx"), "dp")
@@ -803,8 +817,8 @@
         s_retgate,
         s_out,
         gain_sums[1],
-        s_gate_up[:, :units],
-        s_gate_up[:, units:],
+        s_gate,
+        s_up,
         s_down,
     )
 

time: 999 us -> 874 us (0.87)
  Pallas kernels: 253 us -> 142 us
  starting transfers between devices: 190 us -> 134 us
  waiting for transfers between devices: 352 us -> 397 us
  other arithmetic: 70.4 us -> 82 us
    pallas_call x2, Pallas kernels: 113 us -> 7.67 us  [side_by_side(): pl.pallas_call(kernel, grid=(rows // block,), in_specs=[pl.BlockSpec((blo...]
    ppermute x10 -> x12, waiting for transfers between devices: 85.2 us -> 181 us  [line_gather(): lefts.append(lax.ppermute(lefts[-1], axis, l_pairs))]
    ppermute x5 -> x6, waiting for transfers between devices: 79.9 us -> 34.8 us  [line_gather(): lax.ppermute(jnp.where(i >= k - 1, rights[-1], lefts[-1]), axis, r_pairs...]
    ppermute x14 -> x6, starting transfers between devices: 69.7 us -> 24.7 us  [line_scatter(): from_left = lax.ppermute(r_data, axis, r_pairs)]
    ppermute x7 -> x3, waiting for transfers between devices: 62.4 us -> 28.4 us  [line_scatter(): from_left = from_right = lax.ppermute(data, axis, r_pairs + l_pairs)]
    reduce_scatter x0 -> x4, waiting for transfers between devices: none -> 23.1 us  [the longest x2 23 us: on_device(): lax.psum_scatter(branch[c], 'tp', scatter_dimension=1, tiled=True)]
    concatenate x0 -> x2, other arithmetic: none -> 21.2 us  [stacked(): jnp.concatenate([g.reshape(devices, -1, g.shape[1]) for g in grads], axis=1)]
    ppermute x7 -> x3, starting transfers between devices: 30.1 us -> 12.1 us  [line_scatter(): from_left = from_right = lax.ppermute(data, axis, r_pairs + l_pairs)]
  transfers between devices with their start and end apart: 84 -> 70, of which waited for: 35 -> 35; matrix products, arithmetic and copies ran while one was open for 17% -> 19% of each run, Pallas kernels for 19% -> 12%
where the time goes in v2:
time: 874 us; the launch traced here: 869 us
  waiting for transfers between devices  397 us (45%)
  Pallas kernels  142 us (16%)
  starting transfers between devices  134 us (15%)
  other arithmetic  82 us (9%)
  matrix products  77.6 us (9%)
  local copies, waits for them, and re-layouts  21.6 us (2%)
  between operations  15.2 us (2%)
    ppermute x12, waiting for transfers between devices, line_gather(): lefts.append(lax.ppermute(lefts[-1], axis, l_pairs))  181 us
    dot_general x5, matrix products, tn(): lax.dot_general(a, b, (((0,), (0,)), ((), ())), preferred_element_type=F32)  45.1 us
    pallas_call x2, Pallas kernels, mlp(): pl.pallas_call(lambda *refs: mlp_kernel(units, len(blocks), *refs), grid=...  41.5 us
    ppermute x12, starting transfers between devices, line_gather(): rights.append(lax.ppermute(rights[-1], axis, r_pairs))  40.9 us
    ppermute x6, waiting for transfers between devices, line_gather(): lax.ppermute(jnp.where(i >= k - 1, rights[-1], lefts[-1]), axis, r_pairs...  34.8 us
    ppermute x6, waiting for transfers between devices, line_scatter(): from_left = lax.ppermute(r_data, axis, r_pairs)  33.5 us
    ppermute x9, waiting for transfers between devices, swap_sum(): x = x + lax.ppermute(x, axis, [(j, j ^ g) for j in range(n)])  32.7 us
    dot_general x3, matrix products, nt(): lax.dot_general(a, b, (((1,), (1,)), ((), ())), preferred_element_type=F32)  32.5 us
  transfers between devices with their start and end apart: 70, of which 35 were waited for; matrix products, arithmetic and copies ran while one was open for 19% of the time, Pallas kernels for 12%

profile of v2, /device:TPU:0, one launch (start us, length us, event | category | flops | bytes accessed | tf_op | source)
XLA Modules:
  0.0 869.0 jit_solution(18037204198153638762)
XLA Ops:
  22.2 5.5 fusion.27
  27.8 10.8 %collective-permute-done.3.refs_7_ = bf16[1024,512]{1,0:T(8,128)(2,1)S(1)} collective-permute-done((bf16[1024,512]{1,0:T(8,128)(2,1)S(1)}, bf16[1024,512]{1,0:T(8,128)(2,1)S(1)}, u32[]{:S(2)}, u32[]{:S(2)}) %collective-permute-start.3) | collective-permute-done | bytes 1048608 | tf_op jit(solution)/shard_map/ppermute | solution.py:56
  44.9 23.8 %collective-permute-done.6.refs_10_ = bf16[1024,512]{1,0:T(8,128)(2,1)S(1)} collective-permute-done((bf16[1024,512]{1,0:T(8,128)(2,1)}, bf16[1024,512]{1,0:T(8,128)(2,1)S(1)}, u32[]{:S(2)}, u32[]{:S(2)}) %collective-permute-start.6) | collective-permute-done | bytes 1048608 | tf_op jit(solution)/shard_map/ppermute | solution.py:57
  79.8 14.3 %collective-permute-done.2 = f32[2,512]{1,0:T(2,128)S(1)} collective-permute-done((f32[2,512]{1,0:T(2,128)S(1)}, f32[2,512]{1,0:T(2,128)S(1)}, u32[]{:S(2)}, u32[]{:S(2)}) %collective-permute-start.2) | collective-permute-done | bytes 4128 | tf_op jit(solution)/shard_map/ppermute | solution.py:104
  94.7 9.0 %all-gather.3.cloned.1.call-done.refs_3_.w_ref.refs_6_ = bf16[2048,4096]{1,0:T(8,128)(2,1)} async-done(((bf16[256,4096]{1,0:T(8,128)(2,1)}), bf16[2048,4096]{1,0:T(8,128)(2,1)}) %all-gather.3.cloned.1.call-update) | async-done | bytes 16777232 | tf_op jit(solution)/shard_map/all_gather | solution.py:674
  103.8 22.1 %project.1 = (bf16[1024,2048]{1,0:T(8,128)(2,1)}, f32[1024,1]{1,0:T(8,128)}, bf16[1024,512]{1,0:T(8,128)(2,1)}, bf16[1024,512]{1,0:T(8,128)(2,1)}, bf16[1024,1024]{1,0:T(8,128)(2,1)}, /*index=5*/f32[2,256,512]{2,1,0:T(8,128)}) custom-call(s32[1]{0:T(128)} %bitcast.refs_0_, f32[2]{0:T(128)} %negate_log-plus-one_fusion.refs_1_.refs_0_, ...), custom_call_target="tpu_custom_call" | custom-call | flops 8589934592 | bytes 33554432 | tf_op jit(solution)/shard_map/project/pallas_call | solution.py:243
  131.6 8.8 %product.1.refs_4_ = f32[1024,1024]{1,0:T(8,128)} custom-call(bf16[1024,2048]{1,0:T(8,128)(2,1)} %get-tuple-element.71.x_ref, bf16[2048,4096]{1,0:T(8,128)(2,1)} %all-gather.3.cloned.1.call-done.refs_3_.w_ref.refs_6_), custom_call_target="tpu_custom_call" | custom-call | flops 4294967296 | bytes 12582912 | tf_op jit(solution)/shard_map/product/pallas_call | solution.py:284
  146.0 9.2 %retention_forward.2 = (bf16[1024,1024]{1,0:T(8,128)(2,1)}, f32[1024,1024]{1,0:T(8,128)}, bf16[512,2048]{1,0:T(8,128)(2,1)}) custom-call(f32[2]{0:T(128)} %negate_log-plus-one_fusion.refs_1_.refs_0_, bf16[1024,512]{1,0:T(8,128)(2,1)} %get-tuple-element.66.refs_1_.refs_2_, bf16[1024,512]{1,0:T(8,128)(2,1)} %get-tuple-element.67.refs_2_, ...), custom_call_target="tpu_custom_call" | custom-call | flops 3221225472 | bytes 10485760 | tf_op jit(solution)/shard_map/retention_forward/pallas_call | solution.py:438
  157.4 6.1 collective-permute-start.16
  163.5 10.2 %retention_forward.3 = (bf16[1024,1024]{1,0:T(8,128)(2,1)}, f32[1024,1024]{1,0:T(8,128)}, bf16[512,2048]{1,0:T(8,128)(2,1)}) custom-call(f32[2]{0:T(128)} %negate_log-plus-one_fusion.refs_1_.refs_0_, bf16[1024,512]{1,0:T(8,128)(2,1)} %get-tuple-element.66.refs_1_.refs_2_, ...), custom_call_target="tpu_custom_call", output_to_operand_aliasing={{0}: (7, {}), {1}: (8, {})} | custom-call | flops 4026531840 | bytes 10485760 | tf_op jit(solution)/shard_map/retention_forward/pallas_call | solution.py:438
  173.8 41.0 %collective-permute-done.18.refs_16_ = bf16[1024,512]{1,0:T(8,128)(2,1)} collective-permute-done((bf16[1024,512]{1,0:T(8,128)(2,1)S(1)}, bf16[1024,512]{1,0:T(8,128)(2,1)}, u32[]{:S(2)}, u32[]{:S(2)}) %collective-permute-start.18) | collective-permute-done | bytes 1048608 | tf_op jit(solution)/shard_map/ppermute | solution.py:57
  222.5 10.3 %collective-permute-start.10 = (bf16[512,512]{1,0:T(8,128)(2,1)S(1)}, bf16[512,512]{1,0:T(8,128)(2,1)S(1)}, u32[]{:S(2)}, u32[]{:S(2)}) collective-permute-start(bf16[512,512]{1,0:T(8,128)(2,1)S(1)} %get-tuple-element.130.refs_3_), channel_id=1, source_target_pairs={{0,1},{1,2},{2,3},{4,5},{5,6},{6,7},{8,9},{9,10},{10,11},{12,13},{... | collective-permute-start | bytes 1572872 | tf_op jit(solution)/shard_map/ppermute | solution.py:56
  232.8 17.8 %collective-permute-done.22.refs_9_ = bf16[512,512]{1,0:T(8,128)(2,1)S(1)} collective-permute-done((bf16[512,512]{1,0:T(8,128)(2,1)S(1)}, bf16[512,512]{1,0:T(8,128)(2,1)S(1)}, u32[]{:S(2)}, u32[]{:S(2)}) %collective-permute-start.22) | collective-permute-done | bytes 524320 | tf_op jit(solution)/shard_map/ppermute | solution.py:57
  255.7 7.8 collective-permute-done.23.refs_7_
  266.7 20.0 %collective-permute-done.20.refs_12_.refs_15_ = bf16[1024,512]{1,0:T(8,128)(2,1)} collective-permute-done((bf16[1024,512]{1,0:T(8,128)(2,1)S(1)}, bf16[1024,512]{1,0:T(8,128)(2,1)}, u32[]{:S(2)}, u32[]{:S(2)}) %collective-permute-start.20) | collective-permute-done | bytes 1048608 | tf_op jit(solution)/shard_map/ppermute | solution.py:52
  286.7 6.9 all-gather.5.cloned.1.call-done.refs_2_
  295.6 20.9 %mlp.2 = (bf16[1024,2048]{1,0:T(8,128)(2,1)}, bf16[1024,1024]{1,0:T(8,128)(2,1)}, bf16[1024,2048]{1,0:T(8,128)(2,1)}, bf16[1024,2048]{1,0:T(8,128)(2,1)}, f32[51...) custom-call(s32[1]{0:T(128)} %bitcast.refs_0_, f32[1,2048]{1,0:T(1,128)} %get-tuple-element.157.refs_1_, ...), custom_call_target="tpu_custom_call" | custom-call | flops 10737418240 | bytes 27262976 | tf_op jit(solution)/shard_map/mlp/pallas_call | solution.py:337
  316.5 22.8 %reduce-scatter.10.cloned.1.call-done = bf16[512,512]{1,0:T(8,128)(2,1)} async-done(((bf16[512,2048]{1,0:T(8,128)(2,1)}), bf16[512,512]{1,0:T(8,128)(2,1)}) %reduce-scatter.10.cloned.1.call-update) | async-done | bytes 524304 | tf_op jit(solution)/shard_map/reduce_scatter | solution.py:723
  346.7 26.6 %collective-permute-done.13.refs_9_ = bf16[512,512]{1,0:T(8,128)(2,1)S(1)} collective-permute-done((bf16[512,512]{1,0:T(8,128)(2,1)S(1)}, bf16[512,512]{1,0:T(8,128)(2,1)S(1)}, u32[]{:S(2)}, u32[]{:S(2)}) %collective-permute-start.13) | collective-permute-done | bytes 524320 | tf_op jit(solution)/shard_map/ppermute | solution.py:57
  375.4 25.6 %collective-permute-done.14.refs_7_ = bf16[512,512]{1,0:T(8,128)(2,1)S(1)} collective-permute-done((bf16[512,512]{1,0:T(8,128)(2,1)S(1)}, bf16[512,512]{1,0:T(8,128)(2,1)S(1)}, u32[]{:S(2)}, u32[]{:S(2)}) %collective-permute-start.14) | collective-permute-done | bytes 524320 | tf_op jit(solution)/shard_map/ppermute | solution.py:57
  402.5 12.7 %collective-permute-done.15.refs_5_.refs_8_ = bf16[512,512]{1,0:T(8,128)(2,1)S(1)} collective-permute-done((bf16[512,512]{1,0:T(8,128)(2,1)S(1)}, bf16[512,512]{1,0:T(8,128)(2,1)S(1)}, u32[]{:S(2)}, u32[]{:S(2)}) %collective-permute-start.15) | collective-permute-done | bytes 524320 | tf_op jit(solution)/shard_map/ppermute | solution.py:52
  416.0 20.6 %mlp.3 = (bf16[1024,2048]{1,0:T(8,128)(2,1)}, bf16[1024,1024]{1,0:T(8,128)(2,1)}, bf16[1024,2048]{1,0:T(8,128)(2,1)}, bf16[1024,2048]{1,0:T(8,128)(2,1)}, f32[51...) custom-call(s32[1]{0:T(128)} %bitcast.refs_0_, ...), custom_call_target="tpu_custom_call", output_to_operand_aliasing={{0}: (17, {}), {1}: (18, {}), {2}: (19, {}), {3}: (20, {})} | custom-call | flops 10737418240 | bytes 27262976 | tf_op jit(solution)/shard_map/mlp/pallas_call | solution.py:337
  437.1 7.6 convolution_convert_fusion.4
  444.7 9.8 %convolution_convert_fusion.1 = bf16[2048,2048]{1,0:T(8,128)(2,1)S(1)} fusion(bf16[1024,2048]{1,0:T(8,128)(2,1)S(1)} %copy-done.43, bf16[1024,2048]{1,0:T(8,128)(2,1)S(1)} %copy-done.44), kind=kOutput, calls=%fused_computation.7 | convolution fusion | flops 8594128896 | bytes 16777216 | tf_op jit(solution)/shard_map/dot_general | solution.py:24
  455.7 13.5 %pad_maximum_fusion = bf16[8,768,1024]{2,1,0:T(8,128)(2,1)} fusion(bf16[8,256,1024]{2,1,0:T(8,128)(2,1)S(1)} %bitcast.54, bf16[8,256,1024]{2,1,0:T(8,128)(2,1)S(1)} %bitcast.53, bf16[8,256,1024]{2,1,0:T(8,128)(2,1)S(1)} %bitcast.52), kind=kLoop, calls=%fused_computation | loop fusion | flops 37748736 | bytes 25165824 | tf_op jit(solution)/shard_map/concatenate | solution.py:707
  488.6 5.2 collective-permute-done.28
  504.9 5.7 collective-permute-start.30
  510.7 6.2 collective-permute-done.37.refs_12_
  518.8 9.1 %collective-permute-done.41.refs_12_ = bf16[512,512]{1,0:T(8,128)(2,1)S(1)} collective-permute-done((bf16[512,512]{1,0:T(8,128)(2,1)S(1)}, bf16[512,512]{1,0:T(8,128)(2,1)S(1)}, u32[]{:S(2)}, u32[]{:S(2)}) %collective-permute-start.41) | collective-permute-done | bytes 524320 | tf_op jit(solution)/shard_map/ppermute | solution.py:57
  530.0 9.2 %collective-permute-done.38.refs_10_ = bf16[512,512]{1,0:T(8,128)(2,1)S(1)} collective-permute-done((bf16[512,512]{1,0:T(8,128)(2,1)}, bf16[512,512]{1,0:T(8,128)(2,1)S(1)}, u32[]{:S(2)}, u32[]{:S(2)}) %collective-permute-start.38) | collective-permute-done | bytes 524320 | tf_op jit(solution)/shard_map/ppermute | solution.py:57
  540.6 9.9 %collective-permute-done.42.refs_10_ = bf16[512,512]{1,0:T(8,128)(2,1)S(1)} collective-permute-done((bf16[512,512]{1,0:T(8,128)(2,1)S(1)}, bf16[512,512]{1,0:T(8,128)(2,1)S(1)}, u32[]{:S(2)}, u32[]{:S(2)}) %collective-permute-start.42) | collective-permute-done | bytes 524320 | tf_op jit(solution)/shard_map/ppermute | solution.py:57
  553.7 8.4 fusion.7
  562.1 10.9 %gate_backward.2 = (bf16[1024,1024]{1,0:T(8,128)(2,1)}, bf16[1024,1024]{1,0:T(8,128)(2,1)}, bf16[1024,2048]{1,0:T(8,128)(2,1)}, f32[2,256,512]{2,1,0:T(8,128)}, f32[2,512,1]{2,1,0:T(8,128)}) custom-call(s32[1]{0:T(128)} %bitcast.refs_0_, f32[2]{0:T(128)} %negate_log-plus-one_fusion.refs_1_.refs_0_, bf16[1024,512]{1,0:T(8,128)(2,1)} %get-tuple-element.66.refs_1_.refs_2_, ...), custom_call_target="tpu_custom_call" | custom-call | flops 2415919104 | bytes 8388608 | tf_op jit(solution)/shard_map/gate_backward/pallas_call | solution.py:507
  573.0 10.9 %gate_backward.3 = (bf16[1024,1024]{1,0:T(8,128)(2,1)}, bf16[1024,1024]{1,0:T(8,128)(2,1)}, bf16[1024,2048]{1,0:T(8,128)(2,1)}, f32[2,256,512]{2,1,0:T(8,128)}, f32[2,512,1]{2,1,0:T(8,128)}) custom-call(s32[1]{0:T(128)} %bitcast.refs_0_, f32[2]{0:T(128)} %negate_log-plus-one_fusion.refs_1_.refs_0_, ...), custom_call_target="tpu_custom_call", output_to_operand_aliasing={{0}: (13, {}), {1}: (14, {}), {2}: (15, {})} | custom-call | flops 2415919104 | bytes 8388608 | tf_op jit(solution)/shard_map/gate_backward/pallas_call | solution.py:507
  589.5 9.6 %convolution_convert_fusion.3 = bf16[2048,1024]{1,0:T(8,128)(2,1)} fusion(bf16[1024,2048]{1,0:T(8,128)(2,1)} %get-tuple-element.71.x_ref, bf16[1024,1024]{1,0:T(8,128)(2,1)} %get-tuple-element.105.refs_9_), kind=kOutput, calls=%fused_computation.13 | convolution fusion | flops 4297064448 | bytes 10485760 | tf_op jit(solution)/shard_map/dot_general | solution.py:24
  599.1 6.3 convolution_convert_fusion.2
  605.3 7.7 pad_maximum_fusion.1
  617.4 13.0 %collective-permute-done.45 = bf16[2,256,512]{2,1,0:T(8,128)(2,1)} collective-permute-done((bf16[2,256,512]{2,1,0:T(8,128)(2,1)}, bf16[2,256,512]{2,1,0:T(8,128)(2,1)}, u32[]{:S(2)}, u32[]{:S(2)}) %collective-permute-start.45) | collective-permute-done | bytes 524320 | tf_op jit(solution)/shard_map/ppermute | solution.py:136
  632.8 20.9 %retention_backward.1 = (bf16[1024,3072]{1,0:T(8,128)(2,1)}, f32[2,1024,1]{2,1,0:T(8,128)}) custom-call(f32[2]{0:T(128)} %negate_log-plus-one_fusion.refs_1_.refs_0_, bf16[1024,512]{1,0:T(8,128)(2,1)} %get-tuple-element.66.refs_1_.refs_2_, bf16[1024,512]{1,0:T(8,128)(2,1)} %get-tuple-element.67.refs_2_, bf16[1024,1024]{1,0:T(8,128)(2,1)} %get-tuple-element.68.refs_3_, ...), custom_call_target="tpu_custom_call" | custom-call | flops 7247757312 | bytes 12582912 | tf_op jit(solution)/shard_map/retention_backward/pallas_call | solution.py:613
  653.7 13.2 %fusion.12 = bf16[512,2048]{1,0:T(8,128)(2,1)} fusion(bf16[2048,4096]{1,0:T(8,128)(2,1)} %all-gather.3.cloned.1.call-done.refs_3_.w_ref.refs_6_, bf16[1024,3072]{1,0:T(8,128)(2,1)} %get-tuple-element.117), kind=kOutput, calls=%fused_computation.17 | convolution fusion | flops 6443499520 | bytes 17825792 | tf_op jit(solution)/shard_map/dot_general | solution.py:28
  666.9 10.9 %fusion.17 = bf16[512,2048]{1,0:T(8,128)(2,1)} fusion(bf16[2048,4096]{1,0:T(8,128)(2,1)} %all-gather.3.cloned.1.call-done.refs_3_.w_ref.refs_6_, bf16[1024,3072]{1,0:T(8,128)(2,1)S(1)} %copy-done.46), kind=kOutput, calls=%fused_computation.18 | convolution fusion | flops 6443499520 | bytes 17825792 | tf_op jit(solution)/shard_map/dot_general | solution.py:28
  677.8 11.8 %convolution_convert_fusion = bf16[2048,2048]{1,0:T(8,128)(2,1)} fusion(bf16[1024,2048]{1,0:T(8,128)(2,1)S(1)} %copy-done.9, bf16[1024,3072]{1,0:T(8,128)(2,1)S(1)} %copy-done.46), kind=kOutput, calls=%fused_computation.6 | convolution fusion | flops 8594128896 | bytes 16777216 | tf_op jit(solution)/shard_map/dot_general | solution.py:24
  701.0 28.4 %collective-permute-done.46 = bf16[512,512]{1,0:T(8,128)(2,1)} collective-permute-done((bf16[512,512]{1,0:T(8,128)(2,1)}, bf16[512,512]{1,0:T(8,128)(2,1)}, u32[]{:S(2)}, u32[]{:S(2)}) %collective-permute-start.46) | collective-permute-done | bytes 524320 | tf_op jit(solution)/shard_map/ppermute | solution.py:87
  752.2 18.8 %collective-permute-done.51 = f32[8,128]{1,0:T(8,128)S(1)} collective-permute-done((f32[8,128]{1,0:T(8,128)S(1)}, f32[8,128]{1,0:T(8,128)S(1)}, u32[]{:S(2)}, u32[]{:S(2)}) %collective-permute-start.51) | collective-permute-done | bytes 4128 | tf_op jit(solution)/shard_map/ppermute | solution.py:112
  771.0 5.2 collective-permute-start.47
  782.4 5.6 collective-permute-done.47
  799.8 5.2 collective-permute-start.33
  813.1 27.8 %collective-permute-done.55 = bf16[512,512]{1,0:T(8,128)(2,1)S(1)} collective-permute-done((bf16[512,512]{1,0:T(8,128)(2,1)S(1)}, bf16[512,512]{1,0:T(8,128)(2,1)S(1)}, u32[]{:S(2)}, u32[]{:S(2)}) %collective-permute-start.55) | collective-permute-done | bytes 524320 | tf_op jit(solution)/shard_map/ppermute | solution.py:95
  (296 shorter events, 209.8 us)
Async XLA Ops:
  7.2 96.6 %all-gather.3.cloned.1.call-start = ((), (), s32[]{:S(2)}) async-start(), calls=%async_computation.7 | async-start | bytes 18874368 | tf_op jit(solution)/shard_map/all_gather | solution.py:674
  11.2 207.4 %reduce-scatter.8.cloned.1.call-start = ((), (), s32[]{:S(2)}) async-start(), calls=%async_computation.8 | async-start | bytes 2621440 | tf_op jit(solution)/shard_map/reduce_scatter | solution.py:723
  11.2 27.4 %collective-permute-start.3 = (bf16[1024,512]{1,0:T(8,128)(2,1)S(1)}, bf16[1024,512]{1,0:T(8,128)(2,1)S(1)}, u32[]{:S(2)}, u32[]{:S(2)}) collective-permute-start(bf16[1024,512]{1,0:T(8,128)(2,1)S(1)} %copy-done.19), channel_id=1, source_target_pairs={{0,1},{1,2},{2,3},{4,5},{5,6},{6,7},{8,9},{9,10},{10,11},{12,13},{... | collective-permute-start | bytes 3145736 | tf_op jit(solution)/shard_map/ppermute | solution.py:56
  16.3 26.6 %collective-permute-start.5 = (bf16[1024,512]{1,0:T(8,128)(2,1)S(1)}, bf16[1024,512]{1,0:T(8,128)(2,1)}, u32[]{:S(2)}, u32[]{:S(2)}) collective-permute-start(bf16[1024,512]{1,0:T(8,128)(2,1)S(1)} %copy-done.19), channel_id=1, source_target_pairs={{3,2},{2,1},{1,0},{7,6},{6,5},{5,4},{11,10},{10,9},{9,8},{15,14},{... | collective-permute-start | bytes 3145736 | tf_op jit(solution)/shard_map/ppermute | solution.py:57
  42.9 25.9 %collective-permute-start.6 = (bf16[1024,512]{1,0:T(8,128)(2,1)}, bf16[1024,512]{1,0:T(8,128)(2,1)S(1)}, u32[]{:S(2)}, u32[]{:S(2)}) collective-permute-start(bf16[1024,512]{1,0:T(8,128)(2,1)} %collective-permute-done.5.refs_12_), channel_id=1, source_target_pairs={{2,1},{1,0},{6,5},{5,4},{10,9},{9,8},{14,13},{13,12},{18,17},{17,1... | collective-permute-start | bytes 3145736 | tf_op jit(solution)/shard_map/ppermute | solution.py:57
  44.2 24.6 %collective-permute-start.4 = (bf16[1024,512]{1,0:T(8,128)(2,1)S(1)}, bf16[1024,512]{1,0:T(8,128)(2,1)S(1)}, u32[]{:S(2)}, u32[]{:S(2)}) collective-permute-start(bf16[1024,512]{1,0:T(8,128)(2,1)S(1)} %collective-permute-done.3.refs_7_), channel_id=1, source_target_pairs={{1,2},{2,3},{5,6},{6,7},{9,10},{10,11},{13,14},{14,15},{17,18},{18... | collective-permute-start | bytes 3145736 | tf_op jit(solution)/shard_map/ppermute | solution.py:56
  68.9 25.9 %collective-permute-start.7 = (bf16[1024,512]{1,0:T(8,128)(2,1)S(1)}, bf16[1024,512]{1,0:T(8,128)(2,1)}, u32[]{:S(2)}, u32[]{:S(2)}) collective-permute-start(bf16[1024,512]{1,0:T(8,128)(2,1)S(1)} %broadcast_select_fusion.1), channel_id=1, source_target_pairs={{2,3},{1,0},{6,7},{5,4},{10,11},{9,8},{14,15},{13,12},{18,19},{17,... | collective-permute-start | bytes 3145736 | tf_op jit(solution)/shard_map/ppermute | solution.py:52
  155.3 138.3 %all-gather.5.cloned.1.call-start = ((), (), s32[]{:S(2)}) async-start(), calls=%async_computation.10 | async-start | bytes 14155776 | tf_op jit(solution)/shard_map/all_gather | solution.py:694
  156.0 183.4 %reduce-scatter.10.cloned.1.call-start = ((), (), s32[]{:S(2)}) async-start(), calls=%async_computation.9 | async-start | bytes 2621440 | tf_op jit(solution)/shard_map/reduce_scatter | solution.py:723
  156.1 58.8 %collective-permute-start.18 = (bf16[1024,512]{1,0:T(8,128)(2,1)S(1)}, bf16[1024,512]{1,0:T(8,128)(2,1)}, u32[]{:S(2)}, u32[]{:S(2)}) collective-permute-start(bf16[1024,512]{1,0:T(8,128)(2,1)S(1)} %copy-done.6), channel_id=1, source_target_pairs={{3,2},{2,1},{1,0},{7,6},{6,5},{5,4},{11,10},{10,9},{9,8},{15,14},{... | collective-permute-start | bytes 3145736 | tf_op jit(solution)/shard_map/ppermute | solution.py:57
  157.4 58.8 %collective-permute-start.16 = (bf16[1024,512]{1,0:T(8,128)(2,1)S(1)}, bf16[1024,512]{1,0:T(8,128)(2,1)}, u32[]{:S(2)}, u32[]{:S(2)}) collective-permute-start(bf16[1024,512]{1,0:T(8,128)(2,1)S(1)} %copy-done.6), channel_id=1, source_target_pairs={{0,1},{1,2},{2,3},{4,5},{5,6},{6,7},{8,9},{9,10},{10,11},{12,13},{... | collective-permute-start | bytes 3145736 | tf_op jit(solution)/shard_map/ppermute | solution.py:56
  173.8 306.1 %reduce-scatter.14.cloned.1.call-start = ((), (), s32[]{:S(2)}) async-start(), calls=%async_computation.12 | async-start | bytes 2621440 | tf_op jit(solution)/shard_map/reduce_scatter | solution.py:740
  214.8 37.8 %collective-permute-start.19 = (bf16[1024,512]{1,0:T(8,128)(2,1)}, bf16[1024,512]{1,0:T(8,128)(2,1)}, u32[]{:S(2)}, u32[]{:S(2)}) collective-permute-start(bf16[1024,512]{1,0:T(8,128)(2,1)} %collective-permute-done.18.refs_16_), channel_id=1, source_target_pairs={{2,1},{1,0},{6,5},{5,4},{10,9},{9,8},{14,13},{13,12},{18,17},{17,1... | collective-permute-start | bytes 3145736 | tf_op jit(solution)/shard_map/ppermute | solution.py:57
  216.1 36.5 %collective-permute-start.17 = (bf16[1024,512]{1,0:T(8,128)(2,1)}, bf16[1024,512]{1,0:T(8,128)(2,1)S(1)}, u32[]{:S(2)}, u32[]{:S(2)}) collective-permute-start(bf16[1024,512]{1,0:T(8,128)(2,1)} %collective-permute-done.16.refs_11_), channel_id=1, source_target_pairs={{1,2},{2,3},{5,6},{6,7},{9,10},{10,11},{13,14},{14,15},{17,18},{18... | collective-permute-start | bytes 3145736 | tf_op jit(solution)/shard_map/ppermute | solution.py:56
  221.2 29.4 %collective-permute-start.22 = (bf16[512,512]{1,0:T(8,128)(2,1)S(1)}, bf16[512,512]{1,0:T(8,128)(2,1)S(1)}, u32[]{:S(2)}, u32[]{:S(2)}) collective-permute-start(bf16[512,512]{1,0:T(8,128)(2,1)S(1)} %get-tuple-element.130.refs_3_), channel_id=1, source_target_pairs={{3,2},{2,1},{1,0},{7,6},{6,5},{5,4},{11,10},{10,9},{9,8},{15,14},{... | collective-permute-start | bytes 1572872 | tf_op jit(solution)/shard_map/ppermute | solution.py:57
  222.5 29.4 %collective-permute-start.10 = (bf16[512,512]{1,0:T(8,128)(2,1)S(1)}, bf16[512,512]{1,0:T(8,128)(2,1)S(1)}, u32[]{:S(2)}, u32[]{:S(2)}) collective-permute-start(bf16[512,512]{1,0:T(8,128)(2,1)S(1)} %get-tuple-element.130.refs_3_), channel_id=1, source_target_pairs={{0,1},{1,2},{2,3},{4,5},{5,6},{6,7},{8,9},{9,10},{10,11},{12,13},{... | collective-permute-start | bytes 1572872 | tf_op jit(solution)/shard_map/ppermute | solution.py:56
  254.4 32.3 %collective-permute-start.20 = (bf16[1024,512]{1,0:T(8,128)(2,1)S(1)}, bf16[1024,512]{1,0:T(8,128)(2,1)}, u32[]{:S(2)}, u32[]{:S(2)}) collective-permute-start(bf16[1024,512]{1,0:T(8,128)(2,1)S(1)} %broadcast_select_fusion), channel_id=1, source_target_pairs={{2,3},{1,0},{6,7},{5,4},{10,11},{9,8},{14,15},{13,12},{18,19},{17,... | collective-permute-start | bytes 3145736 | tf_op jit(solution)/shard_map/ppermute | solution.py:52
  265.4 30.2 %collective-permute-start.24 = (bf16[512,512]{1,0:T(8,128)(2,1)}, bf16[512,512]{1,0:T(8,128)(2,1)}, u32[]{:S(2)}, u32[]{:S(2)}) collective-permute-start(bf16[512,512]{1,0:T(8,128)(2,1)} %broadcast_select_fusion.6), channel_id=1, source_target_pairs={{2,3},{1,0},{6,7},{5,4},{10,11},{9,8},{14,15},{13,12},{18,19},{17,... | collective-permute-start | bytes 1572872 | tf_op jit(solution)/shard_map/ppermute | solution.py:52
  316.5 184.2 %reduce-scatter.12.cloned.1.call-start = ((), (), s32[]{:S(2)}) async-start(), calls=%async_computation.11 | async-start | bytes 2621440 | tf_op jit(solution)/shard_map/reduce_scatter | solution.py:740
  340.8 32.5 %collective-permute-start.13 = (bf16[512,512]{1,0:T(8,128)(2,1)S(1)}, bf16[512,512]{1,0:T(8,128)(2,1)S(1)}, u32[]{:S(2)}, u32[]{:S(2)}) collective-permute-start(bf16[512,512]{1,0:T(8,128)(2,1)S(1)} %get-tuple-element.128.refs_3_), channel_id=1, source_target_pairs={{3,2},{2,1},{1,0},{7,6},{6,5},{5,4},{11,10},{10,9},{9,8},{15,14},{... | collective-permute-start | bytes 1572872 | tf_op jit(solution)/shard_map/ppermute | solution.py:57
  342.1 32.5 %collective-permute-start.11 = (bf16[512,512]{1,0:T(8,128)(2,1)S(1)}, bf16[512,512]{1,0:T(8,128)(2,1)S(1)}, u32[]{:S(2)}, u32[]{:S(2)}) collective-permute-start(bf16[512,512]{1,0:T(8,128)(2,1)S(1)} %get-tuple-element.128.refs_3_), channel_id=1, source_target_pairs={{0,1},{1,2},{2,3},{4,5},{5,6},{6,7},{8,9},{9,10},{10,11},{12,13},{... | collective-permute-start | bytes 1572872 | tf_op jit(solution)/shard_map/ppermute | solution.py:56
  373.3 27.6 %collective-permute-start.14 = (bf16[512,512]{1,0:T(8,128)(2,1)S(1)}, bf16[512,512]{1,0:T(8,128)(2,1)S(1)}, u32[]{:S(2)}, u32[]{:S(2)}) collective-permute-start(bf16[512,512]{1,0:T(8,128)(2,1)S(1)} %collective-permute-done.13.refs_9_), channel_id=1, source_target_pairs={{2,1},{1,0},{6,5},{5,4},{10,9},{9,8},{14,13},{13,12},{18,17},{17,1... | collective-permute-start | bytes 1572872 | tf_op jit(solution)/shard_map/ppermute | solution.py:57
  374.7 26.3 %collective-permute-start.12 = (bf16[512,512]{1,0:T(8,128)(2,1)S(1)}, bf16[512,512]{1,0:T(8,128)(2,1)S(1)}, u32[]{:S(2)}, u32[]{:S(2)}) collective-permute-start(bf16[512,512]{1,0:T(8,128)(2,1)S(1)} %collective-permute-done.11.refs_4_), channel_id=1, source_target_pairs={{1,2},{2,3},{5,6},{6,7},{9,10},{10,11},{13,14},{14,15},{17,18},{18... | collective-permute-start | bytes 1572872 | tf_op jit(solution)/shard_map/ppermute | solution.py:56
  436.6 414.9 %reduce-scatter.20.cloned.1.call-start = ((), (), s32[]{:S(2)}) async-start(), calls=%async_computation.15 | async-start | bytes 14155776 | tf_op jit(solution)/shard_map/reduce_scatter | solution.py:803
  469.2 384.2 %reduce-scatter.18.cloned.1.call-start = ((), (), s32[]{:S(2)}) async-start(), calls=%async_computation.14 | async-start | bytes 9437184 | tf_op jit(solution)/shard_map/reduce_scatter | solution.py:803
  503.6 24.4 %collective-permute-start.41 = (bf16[512,512]{1,0:T(8,128)(2,1)S(1)}, bf16[512,512]{1,0:T(8,128)(2,1)S(1)}, u32[]{:S(2)}, u32[]{:S(2)}) collective-permute-start(bf16[512,512]{1,0:T(8,128)(2,1)S(1)} %fusion.37.refs_6_), channel_id=1, source_target_pairs={{3,2},{2,1},{1,0},{7,6},{6,5},{5,4},{11,10},{10,9},{9,8},{15,14},{... | collective-permute-start | bytes 1572872 | tf_op jit(solution)/shard_map/ppermute | solution.py:57
  504.9 24.3 %collective-permute-start.30 = (bf16[512,512]{1,0:T(8,128)(2,1)S(1)}, bf16[512,512]{1,0:T(8,128)(2,1)S(1)}, u32[]{:S(2)}, u32[]{:S(2)}) collective-permute-start(bf16[512,512]{1,0:T(8,128)(2,1)S(1)} %fusion.37.refs_6_), channel_id=1, source_target_pairs={{0,1},{1,2},{2,3},{4,5},{5,6},{6,7},{8,9},{9,10},{10,11},{12,13},{... | collective-permute-start | bytes 1572872 | tf_op jit(solution)/shard_map/ppermute | solution.py:56
  516.9 22.4 %collective-permute-start.38 = (bf16[512,512]{1,0:T(8,128)(2,1)}, bf16[512,512]{1,0:T(8,128)(2,1)S(1)}, u32[]{:S(2)}, u32[]{:S(2)}) collective-permute-start(bf16[512,512]{1,0:T(8,128)(2,1)} %collective-permute-done.37.refs_12_), channel_id=1, source_target_pairs={{2,1},{1,0},{6,5},{5,4},{10,9},{9,8},{14,13},{13,12},{18,17},{17,1... | collective-permute-start | bytes 1572872 | tf_op jit(solution)/shard_map/ppermute | solution.py:57
  518.1 21.1 %collective-permute-start.36 = (bf16[512,512]{1,0:T(8,128)(2,1)}, bf16[512,512]{1,0:T(8,128)(2,1)S(1)}, u32[]{:S(2)}, u32[]{:S(2)}) collective-permute-start(bf16[512,512]{1,0:T(8,128)(2,1)} %collective-permute-done.27.refs_7_), channel_id=1, source_target_pairs={{1,2},{2,3},{5,6},{6,7},{9,10},{10,11},{13,14},{14,15},{17,18},{18... | collective-permute-start | bytes 1572872 | tf_op jit(solution)/shard_map/ppermute | solution.py:56
  528.0 22.5 %collective-permute-start.42 = (bf16[512,512]{1,0:T(8,128)(2,1)S(1)}, bf16[512,512]{1,0:T(8,128)(2,1)S(1)}, u32[]{:S(2)}, u32[]{:S(2)}) collective-permute-start(bf16[512,512]{1,0:T(8,128)(2,1)S(1)} %collective-permute-done.41.refs_12_), channel_id=1, source_target_pairs={{2,1},{1,0},{6,5},{5,4},{10,9},{9,8},{14,13},{13,12},{18,17},{17,1... | collective-permute-start | bytes 1572872 | tf_op jit(solution)/shard_map/ppermute | solution.py:57
  529.3 21.2 %collective-permute-start.40 = (bf16[512,512]{1,0:T(8,128)(2,1)S(1)}, bf16[512,512]{1,0:T(8,128)(2,1)S(1)}, u32[]{:S(2)}, u32[]{:S(2)}) collective-permute-start(bf16[512,512]{1,0:T(8,128)(2,1)S(1)} %collective-permute-done.30.refs_7_), channel_id=1, source_target_pairs={{1,2},{2,3},{5,6},{6,7},{9,10},{10,11},{13,14},{14,15},{17,18},{18... | collective-permute-start | bytes 1572872 | tf_op jit(solution)/shard_map/ppermute | solution.py:56
  539.3 22.8 %collective-permute-start.39 = (bf16[512,512]{1,0:T(8,128)(2,1)S(1)}, bf16[512,512]{1,0:T(8,128)(2,1)}, u32[]{:S(2)}, u32[]{:S(2)}) collective-permute-start(bf16[512,512]{1,0:T(8,128)(2,1)S(1)} %broadcast_select_fusion.5), channel_id=1, source_target_pairs={{2,3},{1,0},{6,7},{5,4},{10,11},{9,8},{14,15},{13,12},{18,19},{17,... | collective-permute-start | bytes 1572872 | tf_op jit(solution)/shard_map/ppermute | solution.py:52
  552.2 20.8 %collective-permute-start.43 = (bf16[512,512]{1,0:T(8,128)(2,1)}, bf16[512,512]{1,0:T(8,128)(2,1)}, u32[]{:S(2)}, u32[]{:S(2)}) collective-permute-start(bf16[512,512]{1,0:T(8,128)(2,1)} %broadcast_select_fusion.4), channel_id=1, source_target_pairs={{2,3},{1,0},{6,7},{5,4},{10,11},{9,8},{14,15},{13,12},{18,19},{17,... | collective-permute-start | bytes 1572872 | tf_op jit(solution)/shard_map/ppermute | solution.py:52
  613.1 245.0 %reduce-scatter.16.cloned.1.call-start = ((), (), s32[]{:S(2)}) async-start(), calls=%async_computation.13 | async-start | bytes 9437184 | tf_op jit(solution)/shard_map/reduce_scatter | solution.py:803
  691.9 47.1 %collective-permute-start.31 = (bf16[1024,512]{1,0:T(8,128)(2,1)}, bf16[1024,512]{1,0:T(8,128)(2,1)}, u32[]{:S(2)}, u32[]{:S(2)}) collective-permute-start(bf16[1024,512]{1,0:T(8,128)(2,1)} %constant_dynamic-slice_fusion.2), channel_id=1, source_target_pairs={{0,1},{3,2},{4,5},{7,6},{8,9},{11,10},{12,13},{15,14},{16,17},{19,... | collective-permute-start | bytes 3145736 | tf_op jit(solution)/shard_map/ppermute | solution.py:87
  698.9 30.4 %collective-permute-start.46 = (bf16[512,512]{1,0:T(8,128)(2,1)}, bf16[512,512]{1,0:T(8,128)(2,1)}, u32[]{:S(2)}, u32[]{:S(2)}) collective-permute-start(bf16[512,512]{1,0:T(8,128)(2,1)} %constant_dynamic-slice_fusion.1), channel_id=1, source_target_pairs={{0,1},{3,2},{4,5},{7,6},{8,9},{11,10},{12,13},{15,14},{16,17},{19,... | collective-permute-start | bytes 1572872 | tf_op jit(solution)/shard_map/ppermute | solution.py:87
  734.0 43.5 %collective-permute-start.53 = (bf16[512,512]{1,0:T(8,128)(2,1)}, bf16[512,512]{1,0:T(8,128)(2,1)}, u32[]{:S(2)}, u32[]{:S(2)}) collective-permute-start(bf16[512,512]{1,0:T(8,128)(2,1)} %constant_dynamic-slice_fusion), channel_id=1, source_target_pairs={{0,1},{3,2},{4,5},{7,6},{8,9},{11,10},{12,13},{15,14},{16,17},{19,... | collective-permute-start | bytes 1572872 | tf_op jit(solution)/shard_map/ppermute | solution.py:87
  742.8 47.8 %collective-permute-start.32 = (bf16[1024,512]{1,0:T(8,128)(2,1)}, bf16[1024,512]{1,0:T(8,128)(2,1)}, u32[]{:S(2)}, u32[]{:S(2)}) collective-permute-start(bf16[1024,512]{1,0:T(8,128)(2,1)} %get-tuple-element.134), channel_id=1, source_target_pairs={{0,1},{1,2},{4,5},{5,6},{8,9},{9,10},{12,13},{13,14},{16,17},{17,1... | collective-permute-start | bytes 3145736 | tf_op jit(solution)/shard_map/ppermute | solution.py:95
  745.1 50.5 %collective-permute-start.34 = (bf16[1024,512]{1,0:T(8,128)(2,1)}, bf16[1024,512]{1,0:T(8,128)(2,1)}, u32[]{:S(2)}, u32[]{:S(2)}) collective-permute-start(bf16[1024,512]{1,0:T(8,128)(2,1)} %get-tuple-element.135), channel_id=1, source_target_pairs={{3,2},{2,1},{7,6},{6,5},{11,10},{10,9},{15,14},{14,13},{19,18},{18... | collective-permute-start | bytes 3145736 | tf_op jit(solution)/shard_map/ppermute | solution.py:96
  750.6 20.4 %collective-permute-start.51 = (f32[8,128]{1,0:T(8,128)S(1)}, f32[8,128]{1,0:T(8,128)S(1)}, u32[]{:S(2)}, u32[]{:S(2)}) collective-permute-start(f32[8,128]{1,0:T(8,128)S(1)} %maximum_add_fusion.1), channel_id=1, source_target_pairs={{0,1},{1,0},{2,3},{3,2},{4,5},{5,4},{6,7},{7,6},{8,9},{9,8},{10,11... | collective-permute-start | bytes 12296 | tf_op jit(solution)/shard_map/ppermute | solution.py:112
  750.7 28.6 %collective-permute-start.49 = (bf16[512,512]{1,0:T(8,128)(2,1)}, bf16[512,512]{1,0:T(8,128)(2,1)}, u32[]{:S(2)}, u32[]{:S(2)}) collective-permute-start(bf16[512,512]{1,0:T(8,128)(2,1)} %get-tuple-element.124), channel_id=1, source_target_pairs={{3,2},{2,1},{7,6},{6,5},{11,10},{10,9},{15,14},{14,13},{19,18},{18... | collective-permute-start | bytes 1572872 | tf_op jit(solution)/shard_map/ppermute | solution.py:96
  777.6 22.2 %collective-permute-start.52 = (f32[8,128]{1,0:T(8,128)S(1)}, f32[8,128]{1,0:T(8,128)S(1)}, u32[]{:S(2)}, u32[]{:S(2)}) collective-permute-start(f32[8,128]{1,0:T(8,128)S(1)} %add.370), channel_id=1, source_target_pairs={{0,2},{1,3},{2,0},{3,1},{4,6},{5,7},{6,4},{7,5},{8,10},{9,11},{10,... | collective-permute-start | bytes 12296 | tf_op jit(solution)/shard_map/ppermute | solution.py:112
  779.3 25.8 %collective-permute-start.54 = (bf16[512,512]{1,0:T(8,128)(2,1)S(1)}, bf16[512,512]{1,0:T(8,128)(2,1)S(1)}, u32[]{:S(2)}, u32[]{:S(2)}) collective-permute-start(bf16[512,512]{1,0:T(8,128)(2,1)S(1)} %get-tuple-element.141), channel_id=1, source_target_pairs={{0,1},{1,2},{4,5},{5,6},{8,9},{9,10},{12,13},{13,14},{16,17},{17,1... | collective-permute-start | bytes 1572872 | tf_op jit(solution)/shard_map/ppermute | solution.py:95
  790.6 20.1 %collective-permute-start.48 = (bf16[512,512]{1,0:T(8,128)(2,1)S(1)}, bf16[512,512]{1,0:T(8,128)(2,1)S(1)}, u32[]{:S(2)}, u32[]{:S(2)}) collective-permute-start(bf16[512,512]{1,0:T(8,128)(2,1)S(1)} %get-tuple-element.149), channel_id=1, source_target_pairs={{0,1},{1,2},{2,3},{4,5},{5,6},{6,7},{8,9},{9,10},{10,11},{12,13},{... | collective-permute-start | bytes 1572872 | tf_op jit(solution)/shard_map/ppermute | solution.py:95
  799.8 45.3 %collective-permute-start.33 = (bf16[1024,512]{1,0:T(8,128)(2,1)S(1)}, bf16[1024,512]{1,0:T(8,128)(2,1)S(1)}, u32[]{:S(2)}, u32[]{:S(2)}) collective-permute-start(bf16[1024,512]{1,0:T(8,128)(2,1)S(1)} %get-tuple-element.136), channel_id=1, source_target_pairs={{0,1},{1,2},{2,3},{4,5},{5,6},{6,7},{8,9},{9,10},{10,11},{12,13},{... | collective-permute-start | bytes 3145736 | tf_op jit(solution)/shard_map/ppermute | solution.py:95
  805.5 35.4 %collective-permute-start.55 = (bf16[512,512]{1,0:T(8,128)(2,1)S(1)}, bf16[512,512]{1,0:T(8,128)(2,1)S(1)}, u32[]{:S(2)}, u32[]{:S(2)}) collective-permute-start(bf16[512,512]{1,0:T(8,128)(2,1)S(1)} %get-tuple-element.151), channel_id=1, source_target_pairs={{0,1},{1,2},{2,3},{4,5},{5,6},{6,7},{8,9},{9,10},{10,11},{12,13},{... | collective-permute-start | bytes 1572872 | tf_op jit(solution)/shard_map/ppermute | solution.py:95
  809.4 31.6 %collective-permute-start.57 = (bf16[512,512]{1,0:T(8,128)(2,1)S(1)}, bf16[512,512]{1,0:T(8,128)(2,1)S(1)}, u32[]{:S(2)}, u32[]{:S(2)}) collective-permute-start(bf16[512,512]{1,0:T(8,128)(2,1)S(1)} %get-tuple-element.152), channel_id=1, source_target_pairs={{3,2},{2,1},{1,0},{7,6},{6,5},{5,4},{11,10},{10,9},{9,8},{15,14},{... | collective-permute-start | bytes 1572872 | tf_op jit(solution)/shard_map/ppermute | solution.py:96
  810.7 34.4 %collective-permute-start.35 = (bf16[1024,512]{1,0:T(8,128)(2,1)S(1)}, bf16[1024,512]{1,0:T(8,128)(2,1)S(1)}, u32[]{:S(2)}, u32[]{:S(2)}) collective-permute-start(bf16[1024,512]{1,0:T(8,128)(2,1)S(1)} %get-tuple-element.137), channel_id=1, source_target_pairs={{3,2},{2,1},{1,0},{7,6},{6,5},{5,4},{11,10},{10,9},{9,8},{15,14},{... | collective-permute-start | bytes 3145736 | tf_op jit(solution)/shard_map/ppermute | solution.py:96
  (69 other events, 1186.0 us)
Sparse Core Ops, SparseCore 0:
  11.3 92.4 all-gather.2
  155.4 63.1 reduce-scatter.7
  220.5 73.0 all-gather.4
  295.7 43.6 reduce-scatter.9
  341.5 57.9 reduce-scatter.13
  436.8 46.4 reduce-scatter.11
  486.8 91.4 reduce-scatter.19
  613.2 72.3 reduce-scatter.17
  689.8 70.9 reduce-scatter.15

commit v3 on v2

--- a/solution.py
+++ b/solution.py
@@ -12,6 +12,8 @@
 HV = 512
 EPSILON = 1e-06
 BLOCK = 512
+COLUMNS = 1024
+TP, CTX, DP = "tp", "ctx", "dp"
 F32 = jnp.float32
 BF16 = jnp.bfloat16
 
@@ -168,8 +170,36 @@
         out_specs=pl.BlockSpec((block, sum(widths)), lambda r: (r, 0)),
         out_shape=jax.ShapeDtypeStruct((rows, sum(widths)), arrays[0].dtype),
         cost_estimate=pl.CostEstimate(flops=0, bytes_accessed=4 * rows * sum(widths), transcendentals=0),
-        name="side_by_side",
+        name="join",
     )(*arrays)
+
+
+def stacked(devices, *grads):
+    rows = grads[0].shape[0] // devices
+    counts = [g.shape[1] // COLUMNS for g in grads]
+    firsts = [sum(counts[:i]) for i in range(len(counts))]
+
+    def kernel(*refs):
+        t = pl.program_id(1)
+        for ref, first, count in zip(refs, firsts, counts):
+
+            @pl.when((t >= first) & (t < first + count))
+            def _(ref=ref):
+                refs[-1][0] = ref[...]
+
+    def spec(first, count):
+        return pl.BlockSpec((rows, COLUMNS), lambda d, t: (d, jnp.clip(t - first, 0, count - 1)))
+
+    total = sum(counts)
+    return pl.pallas_call(
+        kernel,
+        grid=(devices, total),
+        in_specs=[spec(first, count) for first, count in zip(firsts, counts)],
+        out_specs=pl.BlockSpec((1, rows, COLUMNS), lambda d, t: (d, t, 0)),
+        out_shape=jax.ShapeDtypeStruct((devices, total * rows, COLUMNS), grads[0].dtype),
+        cost_estimate=pl.CostEstimate(flops=0, bytes_accessed=4 * devices * total * rows * COLUMNS, transcendentals=0),
+        name="stack",
+    )(*grads)
 
 
 def gathered(at, refs, k, rows=slice(None)):
@@ -271,7 +301,7 @@
         cost_estimate=pl.CostEstimate(
             flops=2 * rows * features * outs, bytes_accessed=2 * features * outs + 12 * rows * features, transcendentals=0
         ),
-        name="project",
+        name="proj",
     )(at, log_gamma, gain, w, cosine, sine, *blocks)
 
 
@@ -293,17 +323,13 @@
         cost_estimate=pl.CostEstimate(
             flops=2 * rows * inner * columns, bytes_accessed=2 * inner * columns + 8 * rows * columns, transcendentals=0
         ),
-        name="product",
+        name="prod",
     )(x, w)
 
 
-def mlp_kernel(units, count, at_ref, gain_ref, w_ref, *refs):
-    blocks, grads = refs[:count], refs[count : 2 * count]
-    full_ref, hidden_ref, acts_ref, grad_ref, scale_ref, inner_ref, back_ref = refs[-7:]
-    at, n = at_ref[0], count // 2 + 1
-    scale_ref[...] = fill_normed(at, blocks, gain_ref, full_ref)
-    for k in range(n):
-        grad_ref[:, columns_of(at, n, k, grads[0].shape[1])] = gathered(at, grads, k)
+def mlp_kernel(units, count, at_ref, gain_ref, w_ref, grad_ref, *refs):
+    blocks, (full_ref, hidden_ref, acts_ref, scale_ref, inner_ref, back_ref) = refs[:count], refs[-6:]
+    scale_ref[...] = fill_normed(at_ref[0], blocks, gain_ref, full_ref)
     x = full_ref[...]
     gate = nn(x, w_ref[:, :units])
     up = nn(x, w_ref[:, units : 2 * units])
@@ -320,13 +346,13 @@
     back_ref[...] = (nt(g_gate, w_ref[:, :units]) + nt(g_up, w_ref[:, units : 2 * units])).astype(BF16)
 
 
-def mlp(at, gain, w, part, grads, x, pairs, shared):
+def mlp(at, gain, w, part, grad, x, pairs, shared):
     rows, width = x.shape
     features = w.shape[0]
     units = w.shape[1] // 3
     blocks = flat(x, pairs)
     steps = rows // BLOCK
-    total = grads[0].shape[0]
+    total = grad.shape[0]
 
     def by_rows(columns):
         return pl.BlockSpec((BLOCK, columns), lambda r: (r, 0))
@@ -341,15 +367,14 @@
             pl.BlockSpec(memory_space=pltpu.SMEM),
             pl.BlockSpec((1, features), lambda r: (0, 0)),
             pl.BlockSpec((features, 3 * units), lambda r: (0, 0)),
+            own_rows(features),
             *[by_rows(width)] * len(blocks),
-            *[own_rows(width)] * len(grads),
             *[pl.BlockSpec(memory_space=pl.ANY)] * len(shared),
         ],
         out_specs=[
             own_rows(features),
             own_rows(units),
             own_rows(2 * units),
-            own_rows(features),
             by_rows(1),
             by_rows(1),
             by_rows(features),
@@ -358,19 +383,18 @@
             jax.ShapeDtypeStruct((total, features), BF16),
             jax.ShapeDtypeStruct((total, units), BF16),
             jax.ShapeDtypeStruct((total, 2 * units), BF16),
-            jax.ShapeDtypeStruct((total, features), BF16),
             jax.ShapeDtypeStruct((rows, 1), F32),
             jax.ShapeDtypeStruct((rows, 1), F32),
             jax.ShapeDtypeStruct((rows, features), BF16),
         ],
-        input_output_aliases={3 + 2 * len(blocks) + i: i for i in range(len(shared))},
+        input_output_aliases={4 + len(blocks) + i: i for i in range(len(shared))},
         cost_estimate=pl.CostEstimate(
             flops=10 * rows * features * units,
             bytes_accessed=6 * features * units + 14 * rows * features,
             transcendentals=2 * rows * units,
         ),
         name="mlp",
-    )(at, gain, w, *blocks, *grads, *shared)
+    )(at, gain, w, grad, *blocks, *shared)
 
 
 def decay_vectors(log_gamma):
@@ -457,7 +481,7 @@
         ],
         scratch_shapes=[pltpu.VMEM((own, features), F32)],
         cost_estimate=pl.CostEstimate(flops=flops, bytes_accessed=20 * own * heads * HV, transcendentals=own * heads * HV),
-        name="retention_forward",
+        name="fwd",
     )(log_gamma, q, k, v, gate, state, w, *shared)
 
 
@@ -537,7 +561,7 @@
             bytes_accessed=16 * own * heads * HV,
             transcendentals=own * heads * HV,
         ),
-        name="gate_backward",
+        name="gate",
     )(here, log_gamma, q, w, gate, ret, *blocks, *shared)
 
 
@@ -639,7 +663,7 @@
             pltpu.SemaphoreType.DMA((4,)),
         ],
         cost_estimate=pl.CostEstimate(flops=flops, bytes_accessed=24 * rows * heads * HK, transcendentals=0),
-        name="retention_backward",
+        name="bwd",
     )(log_gamma, q, k, v, state_in, state_grad, cosine, sine, g_ret, g_gate)
 
 
@@ -657,9 +681,9 @@
     w_down,
     cotangent,
 ):
-    data = ("dp", "ctx")
+    data = (DP, CTX)
     rows, width = layer_input.shape
-    n_tp, at_tp = lax.axis_size("tp"), lax.axis_index("tp")
+    n_tp, at_tp = lax.axis_size(TP), lax.axis_index(TP)
     features = width * n_tp
     heads = w_query.shape[1] // HK
     units = w_gate.shape[1]
@@ -673,11 +697,11 @@
     attn_shard = side_by_side(w_query, w_key, w_value, w_retgate, w_out)
     attn_full = lax.all_gather(attn_shard, data, axis=0, tiled=True)
 
-    gains = small_gather(jnp.stack([gain_attn, gain_mlp]), "tp")
+    gains = small_gather(jnp.stack([gain_attn, gain_mlp]), TP)
 
     log_gamma = jnp.log1p(-jnp.exp2(-5.0 - (at_tp * heads + jnp.arange(heads)).astype(F32)))
     log_block = rows * log_gamma
-    positions = lax.axis_index("ctx") * rows + jnp.arange(rows)
+    positions = lax.axis_index(CTX) * rows + jnp.arange(rows)
     frequencies = jnp.exp(-math.log(10000.0) * jnp.linspace(0.0, 1.0, HK // 2, dtype=F32))
     angles = positions.astype(F32)[:, None] * jnp.repeat(frequencies, 2)[None, :]
     cosine = jnp.cos(angles)
@@ -685,15 +709,14 @@
     here = at_tp.reshape(1)
     mlp_shard = side_by_side(w_gate, w_up, w_down)
 
-    pairs = line_gather(layer_input, "tp", (cosine, sine, mlp_shard, log_gamma))
+    pairs = line_gather(layer_input, TP, (cosine, sine, mlp_shard, log_gamma, gains))
     normed, scale_attn, q, k, v, local_state = project(
         here, log_gamma, gains[0:1], attn_full, layer_input, pairs, heads, cosine, sine
     )
-    cot = after(cotangent, pairs[-1][0])
-    cot_blocks = flat(cot, line_gather(cot, "tp"))
+    grad_full = lax.all_gather(after(cotangent, pairs[0][0]), TP, axis=1, tiled=True)
     mlp_full = lax.all_gather(after(mlp_shard, pairs[0][1]), data, axis=0, tiled=True)
     gate_pre = product(after(normed, local_state), attn_full, (2 * qk + vw) // vw, vw)
-    state_in = states_before(local_state, log_block, "ctx").astype(BF16)
+    state_in = states_before(local_state, log_block, CTX).astype(BF16)
     heads_out, branch = [], []
     for c in range(parts):
         *heads_out, out = retention_forward(
@@ -702,9 +725,7 @@
         branch.append(out)
     gated, retained = heads_out
 
-    def stacked(*grads):
-        devices = math.prod(lax.axis_size(axis) for axis in data)
-        return jnp.concatenate([g.reshape(devices, -1, g.shape[1]) for g in grads], axis=1)
+    devices = math.prod(lax.axis_size(axis) for axis in data)
 
     x_own = layer_input.astype(F32)
     middle, mid_pairs, scale_mlp, inner_mlp, back, grad_middle, grad_own, grad_pairs = ([] for _ in range(8))
@@ -717,42 +738,46 @@
 
     def row_total(inner):
         lanes = 128
-        return swap_sum(inner.reshape(-1, lanes), "tp").reshape(-1)
-
+        return swap_sum(inner.reshape(-1, lanes), TP).reshape(-1)
+
+    early = ()
     for c in range(parts):
-        total = lax.psum_scatter(branch[c], "tp", scatter_dimension=1, tiled=True).astype(F32)
+        total, steps = line_scatter(after(branch[c], *early), TP)
+        early = steps[-1]
         if c:
             total = after(total, mid_pairs[c - 1][0][0])
         middle.append(x_own[cuts[c]] + total)
-        mid_pairs.append(line_gather(middle[c].astype(BF16), "tp"))
+        mid_pairs.append(line_gather(middle[c].astype(BF16), TP))
     shared = []
     for c in range(parts):
         *results, scale, inner, out = mlp(
-            here, gains[1:2], mlp_full, c, cot_blocks, middle[c].astype(BF16), mid_pairs[c], shared
+            here, gains[1:2], mlp_full, c, grad_full, middle[c].astype(BF16), mid_pairs[c], shared
         )
         shared = results
         scale_mlp.append(scale)
         inner_mlp.append(inner[:, 0])
         back.append(out)
-    normed_mlp, hidden, grad_acts, grad_full = shared
+    normed_mlp, hidden, grad_acts = shared
+    early = ()
     for c in range(parts):
         inner = row_total(inner_mlp[c])
-        total = lax.psum_scatter(back[c], "tp", scatter_dimension=1, tiled=True).astype(F32)
+        total, steps = line_scatter(after(back[c], *early), TP)
+        early = steps[-1]
         if c:
             total = after(total, grad_pairs[c - 1][0][0])
         grad_mid, gain_sum = norm_back(middle[c], scale_mlp[c], gain_mlp, inner, total)
         gain_mlp_sum = gain_mlp_sum + gain_sum
         grad_middle.append(cotangent[cuts[c]].astype(F32) + grad_mid)
         grad_own.append(grad_middle[c].astype(BF16))
-        grad_pairs.append(line_gather(grad_own[c], "tp"))
+        grad_pairs.append(line_gather(grad_own[c], TP))
     grad_down = tn(grad_full, hidden).astype(BF16)
     grad_gate_up = tn(after(normed_mlp, grad_down), grad_acts).astype(BF16)
-    grad_mlp = stacked(grad_gate_up[:, :units], grad_gate_up[:, units:], grad_down)
+    grad_mlp = stacked(devices, grad_gate_up, grad_down)
     mlp_parts = nt(hidden, mlp_full[:, 2 * units :]).astype(BF16)
 
-    grad_own[0] = after(grad_own[0], grad_mlp, mlp_parts)
-    mlp_out, _ = line_scatter(after(mlp_parts, grad_pairs[-1][0][0]), "tp")
-    layer_output = (jnp.concatenate(middle) + mlp_out).astype(BF16)
+    grad_own[0] = after(grad_own[0], grad_mlp)
+    mlp_out = lax.psum_scatter(after(mlp_parts, grad_pairs[-1][0][0]), TP, scatter_dimension=1, tiled=True)
+    layer_output = (jnp.concatenate(middle) + mlp_out.astype(F32)).astype(BF16)
     shared = []
     partial_state = 0.0
     inner_attn = []
@@ -774,11 +799,11 @@
         partial_state = partial_state + ps
         inner_attn.append(jnp.sum(inner[:, :, 0], axis=0))
     g_gate, g_ret, grad_attn = shared
-    state_grad, got = states_after(partial_state, log_block, "ctx")
+    state_grad, got = states_after(partial_state, log_block, CTX)
     state_grad = state_grad.astype(BF16)
     grad_out = tn(after(grad_attn, got), gated).astype(BF16)
     grad_retgate = tn(normed, after(g_gate, got)).astype(BF16)
-    grad_heads = stacked(grad_retgate, grad_out)
+    grad_heads = stacked(devices, grad_retgate, grad_out)
     grads_attn, inner = retention_backward(
         log_gamma, q, k, v, state_in, after(state_grad, grad_heads), cosine, sine, g_ret, g_gate
     )
@@ -786,13 +811,15 @@
     in_full = attn_full[:, : 2 * qk + 2 * vw]
     back = []
     for c in range(parts):
-        back.append(nt(after(grads_attn, *back)[cuts[c]], in_full).astype(BF16))
-    grad_qkv_w = tn(normed, after(grads_attn, *back)[:, : 2 * qk + vw]).astype(BF16)
+        rows_grads = after(grads_attn, *back, *([grad_qkv_w] if c else []))
+        back.append(nt(rows_grads[cuts[c]], in_full).astype(BF16))
+        if c == 0:
+            grad_qkv_w = tn(normed, after(grads_attn, *back)[:, : 2 * qk + vw]).astype(BF16)
     inner_attn = row_total(inner_attn)
     grad_input, gain_attn_sum = [], 0.0
     early = ()
     for c in range(parts):
-        total, steps = line_scatter(after(back[c], *early), "tp")
+        total, steps = line_scatter(after(back[c], *early), TP)
         early = steps[0]
         grad_in, gain_sum = norm_back(x_own[cuts[c]], scale_attn[cuts[c]], gain_attn, inner_attn[cuts[c]], total)
         grad_input.append((grad_middle[c] + grad_in).astype(BF16))
@@ -806,7 +833,7 @@
     s_retgate, s_out = jnp.split(shard(grad_heads)[0], 2)
     s_qkv = shard(grad_qkv_w)
     s_query, s_key, s_value = s_qkv[:, :qk], s_qkv[:, qk : 2 * qk], s_qkv[:, 2 * qk :]
-    gain_sums = swap_sum(swap_sum(jnp.stack([gain_attn_sum, gain_mlp_sum]), "ctx"), "dp")
+    gain_sums = swap_sum(swap_sum(jnp.stack([gain_attn_sum, gain_mlp_sum]), CTX), DP)
     return (
         layer_output,
         grad_input,
@@ -824,9 +851,9 @@
 
 
 def solution(mesh):
-    tokens = P(("dp", "ctx"), "tp")
-    gain = P("tp")
-    weight = P(("dp", "ctx"), "tp")
+    tokens = P((DP, CTX), TP)
+    gain = P(TP)
+    weight = P((DP, CTX), TP)
 
     return jax.shard_map(
         on_device,

time: 874 us -> 919 us (1.051)
  Pallas kernels: 142 us -> 173 us
  starting transfers between devices: 134 us -> 156 us
  other arithmetic: 82 us -> 66.6 us
    reduce_scatter x3, waiting for transfers between devices: 0.02 us -> 71.3 us  [shard(): lax.psum_scatter(grad, data, scatter_dimension=0, tiled=True).astype(F32)]
    pallas_call x0 -> x2, Pallas kernels: none -> 32.2 us  [stacked(): pl.pallas_call(kernel, grid=(devices, total), in_specs=[spec(first, count...]
    ppermute x12 -> x10, waiting for transfers between devices: 181 us -> 154 us  [line_gather(): lefts.append(lax.ppermute(lefts[-1], axis, l_pairs))]
    ppermute x6 -> x12, starting transfers between devices: 24.7 us -> 49.7 us  [line_scatter(): from_left = lax.ppermute(r_data, axis, r_pairs)]
    reduce_scatter x4 -> x1, waiting for transfers between devices: 23.1 us -> 0.01 us  [on_device(): lax.psum_scatter(after(mlp_parts, grad_pairs[-1][0][0]), TP, scatter_dime...]
    ppermute x3 -> x6, waiting for transfers between devices: 28.4 us -> 50.9 us  [line_scatter(): from_left = from_right = lax.ppermute(data, axis, r_pairs + l_pairs)]
    concatenate x2 -> x0, other arithmetic: 21.2 us -> none  [stacked(): jnp.concatenate([g.reshape(devices, -1, g.shape[1]) for g in grads], axis=1)]
    ppermute x6 -> x12, waiting for transfers between devices: 33.5 us -> 16.9 us  [line_scatter(): from_left = lax.ppermute(r_data, axis, r_pairs)]
  transfers between devices with their start and end apart: 70 -> 78, of which waited for: 35 -> 38; matrix products, arithmetic and copies ran while one was open for 19% -> 17% of each run, Pallas kernels for 12% -> 19%
where the time goes in v3:
time: 919 us; the launch traced here: 913 us
  waiting for transfers between devices  404 us (44%)
  Pallas kernels  173 us (19%)
  starting transfers between devices  156 us (17%)
  matrix products  77.9 us (8%)
  other arithmetic  66.6 us (7%)
  local copies, waits for them, and re-layouts  19.5 us (2%)
  between operations  16 us (2%)
    ppermute x10, waiting for transfers between devices, line_gather(): lefts.append(lax.ppermute(lefts[-1], axis, l_pairs))  154 us
    reduce_scatter x3, waiting for transfers between devices, shard(): lax.psum_scatter(grad, data, scatter_dimension=0, tiled=True).astype(F32)  71.3 us
    ppermute x6, waiting for transfers between devices, line_scatter(): from_left = from_right = lax.ppermute(data, axis, r_pairs + l_pairs)  50.9 us
    ppermute x12, starting transfers between devices, line_scatter(): from_left = lax.ppermute(r_data, axis, r_pairs)  49.7 us
    dot_general x5, matrix products, tn(): lax.dot_general(a, b, (((0,), (0,)), ((), ())), preferred_element_type=F32)  47.6 us
    pallas_call x2, Pallas kernels, mlp(): pl.pallas_call(lambda *refs: mlp_kernel(units, len(blocks), *refs), grid=...  39.8 us
    ppermute x5, waiting for transfers between devices, line_gather(): lax.ppermute(jnp.where(i >= k - 1, rights[-1], lefts[-1]), axis, r_pairs...  34.4 us
    pallas_call x2, Pallas kernels, stacked(): pl.pallas_call(kernel, grid=(devices, total), in_specs=[spec(first, count...  32.2 us
  transfers between devices with their start and end apart: 78, of which 38 were waited for; matrix products, arithmetic and copies ran while one was open for 17% of the time, Pallas kernels for 19%

profile of v3, /device:TPU:0, one launch (start us, length us, event | category | flops | bytes accessed | tf_op | source)
XLA Modules:
  0.0 913.4 jit_solution(12180435857425246774)
XLA Ops:
  21.4 5.5 fusion.23
  31.3 11.3 %collective-permute-done.3.refs_7_ = bf16[1024,512]{1,0:T(8,128)(2,1)S(1)} collective-permute-done((bf16[1024,512]{1,0:T(8,128)(2,1)S(1)}, bf16[1024,512]{1,0:T(8,128)(2,1)S(1)}, u32[]{:S(2)}, u32[]{:S(2)}) %collective-permute-start.3) | collective-permute-done | bytes 1048608 | tf_op jit(solution)/shard_map/ppermute | solution.py:58
  44.0 24.8 %collective-permute-done.5.refs_12_ = bf16[1024,512]{1,0:T(8,128)(2,1)} collective-permute-done((bf16[1024,512]{1,0:T(8,128)(2,1)S(1)}, bf16[1024,512]{1,0:T(8,128)(2,1)}, u32[]{:S(2)}, u32[]{:S(2)}) %collective-permute-start.5) | collective-permute-done | bytes 1048608 | tf_op jit(solution)/shard_map/ppermute | solution.py:59
  70.8 22.8 %collective-permute-done.6.refs_10_ = bf16[1024,512]{1,0:T(8,128)(2,1)S(1)} collective-permute-done((bf16[1024,512]{1,0:T(8,128)(2,1)}, bf16[1024,512]{1,0:T(8,128)(2,1)S(1)}, u32[]{:S(2)}, u32[]{:S(2)}) %collective-permute-start.6) | collective-permute-done | bytes 1048608 | tf_op jit(solution)/shard_map/ppermute | solution.py:59
  95.1 25.6 %collective-permute-done.7.refs_8_.refs_11_ = bf16[1024,512]{1,0:T(8,128)(2,1)} collective-permute-done((bf16[1024,512]{1,0:T(8,128)(2,1)S(1)}, bf16[1024,512]{1,0:T(8,128)(2,1)}, u32[]{:S(2)}, u32[]{:S(2)}) %collective-permute-start.7) | collective-permute-done | bytes 1048608 | tf_op jit(solution)/shard_map/ppermute | solution.py:54
  121.5 22.2 %proj.1 = (bf16[1024,2048]{1,0:T(8,128)(2,1)}, f32[1024,1]{1,0:T(8,128)}, bf16[1024,512]{1,0:T(8,128)(2,1)}, bf16[1024,512]{1,0:T(8,128)(2,1)}, bf16[1024,1024]{1,0:T(8,128)(2,1)}, /*index=5*/f32[2,256,512]{2,1,0:T(8,128)}) custom-call(s32[1]{0:T(128)} %bitcast.refs_0_, f32[2]{0:T(128)} %negate_log-plus-one_fusion.refs_1_.refs_0_, ...), custom_call_target="tpu_custom_call" | custom-call | flops 8589934592 | bytes 33554432 | tf_op jit(solution)/shard_map/proj/pallas_call | solution.py:273
  150.3 8.9 prod.1.refs_4_
  163.7 9.2 %fwd.2 = (bf16[1024,1024]{1,0:T(8,128)(2,1)}, f32[1024,1024]{1,0:T(8,128)}, bf16[512,2048]{1,0:T(8,128)(2,1)}) custom-call(f32[2]{0:T(128)} %negate_log-plus-one_fusion.refs_1_.refs_0_, bf16[1024,512]{1,0:T(8,128)(2,1)} %get-tuple-element.66.refs_1_.refs_2_, bf16[1024,512]{1,0:T(8,128)(2,1)} %get-tuple-element.67.refs_2_, ...), custom_call_target="tpu_custom_call" | custom-call | flops 3221225472 | bytes 10485760 | tf_op jit(solution)/shard_map/fwd/pallas_call | solution.py:462
  175.4 18.0 %collective-permute-done.10 = bf16[512,512]{1,0:T(8,128)(2,1)S(1)} collective-permute-done((bf16[512,512]{1,0:T(8,128)(2,1)S(1)}, bf16[512,512]{1,0:T(8,128)(2,1)S(1)}, u32[]{:S(2)}, u32[]{:S(2)}) %collective-permute-start.10) | collective-permute-done | bytes 524320 | tf_op jit(solution)/shard_map/ppermute | solution.py:89
  196.5 5.2 collective-permute-start.11
  201.8 10.3 %fwd.3 = (bf16[1024,1024]{1,0:T(8,128)(2,1)}, f32[1024,1024]{1,0:T(8,128)}, bf16[512,2048]{1,0:T(8,128)(2,1)}) custom-call(f32[2]{0:T(128)} %negate_log-plus-one_fusion.refs_1_.refs_0_, bf16[1024,512]{1,0:T(8,128)(2,1)} %get-tuple-element.66.refs_1_.refs_2_, ...), custom_call_target="tpu_custom_call", output_to_operand_aliasing={{0}: (7, {}), {1}: (8, {})} | custom-call | flops 4026531840 | bytes 10485760 | tf_op jit(solution)/shard_map/fwd/pallas_call | solution.py:462
  214.7 6.7 collective-permute-start.15
  226.6 6.3 collective-permute-done.15
  235.3 5.3 collective-permute-start.16
  267.3 8.1 collective-permute-done.17
  279.7 5.4 collective-permute-start.21
  289.4 9.9 %collective-permute-done.23.refs_10_ = bf16[512,512]{1,0:T(8,128)(2,1)S(1)} collective-permute-done((bf16[512,512]{1,0:T(8,128)(2,1)S(1)}, bf16[512,512]{1,0:T(8,128)(2,1)S(1)}, u32[]{:S(2)}, u32[]{:S(2)}) %collective-permute-start.23) | collective-permute-done | bytes 524320 | tf_op jit(solution)/shard_map/ppermute | solution.py:59
  301.8 8.9 collective-permute-done.29.refs_6_.refs_9_
  310.6 19.9 %mlp.2 = (bf16[1024,2048]{1,0:T(8,128)(2,1)}, bf16[1024,1024]{1,0:T(8,128)(2,1)}, bf16[1024,2048]{1,0:T(8,128)(2,1)}, f32[512,1]{1,0:T(8,128)}, f32[512,1]{1,0:T(8,128)}, /*index=5*/bf16[512,2048]{1,0:T(8,128)(2,1)}) custom-call(s32[1]{0:T(128)} %bitcast.refs_0_, f32[1,2048]{1,0:T(1,128)} %get-tuple-element.169.refs_1_, ...), custom_call_target="tpu_custom_call" | custom-call | flops 10737418240 | bytes 27262976 | tf_op jit(solution)/shard_map/mlp/pallas_call | solution.py:363
  334.6 8.0 collective-permute-done.30
  344.6 5.2 collective-permute-start.31
  350.6 19.9 %mlp.3 = (bf16[1024,2048]{1,0:T(8,128)(2,1)}, bf16[1024,1024]{1,0:T(8,128)(2,1)}, bf16[1024,2048]{1,0:T(8,128)(2,1)}, f32[512,1]{1,0:T(8,128)}, f32[512,1]{1,0:T(8,128)}, /*index=5*/bf16[512,2048]{1,0:T(8,128)(2,1)}) custom-call(s32[1]{0:T(128)} %bitcast.refs_0_, ...), custom_call_target="tpu_custom_call", output_to_operand_aliasing={{0}: (11, {}), {1}: (12, {}), {2}: (13, {})} | custom-call | flops 10737418240 | bytes 27262976 | tf_op jit(solution)/shard_map/mlp/pallas_call | solution.py:363
  377.8 8.4 collective-permute-done.33
  388.7 5.2 collective-permute-start.34
  405.6 8.1 collective-permute-done.41
  427.7 5.4 collective-permute-start.42
  433.2 7.6 collective-permute-done.44
  448.3 8.4 fusion.7
  460.1 18.7 %collective-permute-done.47.refs_12_ = bf16[512,512]{1,0:T(8,128)(2,1)S(1)} collective-permute-done((bf16[512,512]{1,0:T(8,128)(2,1)}, bf16[512,512]{1,0:T(8,128)(2,1)S(1)}, u32[]{:S(2)}, u32[]{:S(2)}) %collective-permute-start.47) | collective-permute-done | bytes 524320 | tf_op jit(solution)/shard_map/ppermute | solution.py:59
  480.8 37.3 %collective-permute-done.51.refs_12_ = bf16[512,512]{1,0:T(8,128)(2,1)S(1)} collective-permute-done((bf16[512,512]{1,0:T(8,128)(2,1)}, bf16[512,512]{1,0:T(8,128)(2,1)S(1)}, u32[]{:S(2)}, u32[]{:S(2)}) %collective-permute-start.51) | collective-permute-done | bytes 524320 | tf_op jit(solution)/shard_map/ppermute | solution.py:59
  519.4 9.6 %convolution_convert_fusion.4.refs_1_ = bf16[2048,1024]{1,0:T(8,128)(2,1)} fusion(bf16[1024,2048]{1,0:T(8,128)(2,1)} %all-gather.8.cloned.1.call-done.refs_3_, bf16[1024,1024]{1,0:T(8,128)(2,1)} %get-tuple-element.83), kind=kOutput, calls=%fused_computation.12 | convolution fusion | flops 4297064448 | bytes 10485760 | tf_op jit(solution)/shard_map/dot_general | solution.py:26
  529.1 25.0 %collective-permute-done.48.refs_10_ = bf16[512,512]{1,0:T(8,128)(2,1)S(1)} collective-permute-done((bf16[512,512]{1,0:T(8,128)(2,1)S(1)}, bf16[512,512]{1,0:T(8,128)(2,1)S(1)}, u32[]{:S(2)}, u32[]{:S(2)}) %collective-permute-start.48) | collective-permute-done | bytes 524320 | tf_op jit(solution)/shard_map/ppermute | solution.py:59
  556.3 12.7 %collective-permute-done.52.refs_10_ = bf16[512,512]{1,0:T(8,128)(2,1)S(1)} collective-permute-done((bf16[512,512]{1,0:T(8,128)(2,1)S(1)}, bf16[512,512]{1,0:T(8,128)(2,1)S(1)}, u32[]{:S(2)}, u32[]{:S(2)}) %collective-permute-start.52) | collective-permute-done | bytes 524320 | tf_op jit(solution)/shard_map/ppermute | solution.py:59
  571.6 11.4 %convolution_convert_fusion.1.refs_0_ = bf16[2048,2048]{1,0:T(8,128)(2,1)} fusion(bf16[1024,2048]{1,0:T(8,128)(2,1)S(1)} %copy-done.63, bf16[1024,2048]{1,0:T(8,128)(2,1)S(1)} %copy-done.64), kind=kOutput, calls=%fused_computation.5 | convolution fusion | flops 8594128896 | bytes 16777216 | tf_op jit(solution)/shard_map/dot_general | solution.py:26
  583.1 18.6 %stack.20 = bf16[8,768,1024]{2,1,0:T(8,128)(2,1)} custom-call(bf16[2048,2048]{1,0:T(8,128)(2,1)} %convolution_convert_fusion.1.refs_0_, bf16[2048,1024]{1,0:T(8,128)(2,1)} %convolution_convert_fusion.4.refs_1_), custom_call_target="tpu_custom_call" | custom-call | bytes 25165824 | tf_op jit(solution)/shard_map/stack/pallas_call | solution.py:194
  602.5 10.9 %gate.2 = (bf16[1024,1024]{1,0:T(8,128)(2,1)}, bf16[1024,1024]{1,0:T(8,128)(2,1)}, bf16[1024,2048]{1,0:T(8,128)(2,1)}, f32[2,256,512]{2,1,0:T(8,128)}, f32[2,512,1]{2,1,0:T(8,128)}) custom-call(s32[1]{0:T(128)} %bitcast.refs_0_, f32[2]{0:T(128)} %negate_log-plus-one_fusion.refs_1_.refs_0_, bf16[1024,512]{1,0:T(8,128)(2,1)} %get-tuple-element.66.refs_1_.refs_2_, ...), custom_call_target="tpu_custom_call" | custom-call | flops 2415919104 | bytes 8388608 | tf_op jit(solution)/shard_map/gate/pallas_call | solution.py:531
  614.2 10.9 %gate.3 = (bf16[1024,1024]{1,0:T(8,128)(2,1)}, bf16[1024,1024]{1,0:T(8,128)(2,1)}, bf16[1024,2048]{1,0:T(8,128)(2,1)}, f32[2,256,512]{2,1,0:T(8,128)}, f32[2,512,1]{2,1,0:T(8,128)}) custom-call(s32[1]{0:T(128)} %bitcast.refs_0_, f32[2]{0:T(128)} %negate_log-plus-one_fusion.refs_1_.refs_0_, ...), custom_call_target="tpu_custom_call", output_to_operand_aliasing={{0}: (13, {}), {1}: (14, {}), {2}: (15, {})} | custom-call | flops 2415919104 | bytes 8388608 | tf_op jit(solution)/shard_map/gate/pallas_call | solution.py:531
  629.9 8.5 convolution_convert_fusion.3.refs_0_
  638.4 6.4 convolution_convert_fusion.2.refs_1_
  644.8 13.6 %stack.21 = bf16[8,512,1024]{2,1,0:T(8,128)(2,1)} custom-call(bf16[2048,1024]{1,0:T(8,128)(2,1)} %convolution_convert_fusion.3.refs_0_, bf16[2048,1024]{1,0:T(8,128)(2,1)} %convolution_convert_fusion.2.refs_1_), custom_call_target="tpu_custom_call" | custom-call | bytes 16777216 | tf_op jit(solution)/shard_map/stack/pallas_call | solution.py:194
  663.8 12.2 %collective-permute-done.55 = bf16[2,256,512]{2,1,0:T(8,128)(2,1)S(1)} collective-permute-done((bf16[2,256,512]{2,1,0:T(8,128)(2,1)S(1)}, bf16[2,256,512]{2,1,0:T(8,128)(2,1)S(1)}, u32[]{:S(2)}, u32[]{:S(2)}) %collective-permute-start.55) | collective-permute-done | bytes 524320 | tf_op jit(solution)/shard_map/ppermute | solution.py:138
  677.1 20.8 %bwd.1 = (bf16[1024,3072]{1,0:T(8,128)(2,1)}, f32[2,1024,1]{2,1,0:T(8,128)}) custom-call(f32[2]{0:T(128)} %negate_log-plus-one_fusion.refs_1_.refs_0_, bf16[1024,512]{1,0:T(8,128)(2,1)} %get-tuple-element.66.refs_1_.refs_2_, bf16[1024,512]{1,0:T(8,128)(2,1)} %get-tuple-element.67.refs_2_, bf16[1024,1024]{1,0:T(8,128)(2,1)} %get-tuple-element.68.refs_3_, ...), custom_call_target="tpu_custom_call" | custom-call | flops 7247757312 | bytes 12582912 | tf_op jit(solution)/shard_map/bwd/pallas_call | solution.py:637
  698.0 11.1 %fusion.12 = bf16[512,2048]{1,0:T(8,128)(2,1)S(1)} fusion(bf16[2048,4096]{1,0:T(8,128)(2,1)} %all-gather.4.cloned.1.call-done.refs_3_.w_ref.refs_6_, bf16[1024,3072]{1,0:T(8,128)(2,1)} %get-tuple-element.116), kind=kOutput, calls=%fused_computation.15 | convolution fusion | flops 6443499520 | bytes 17825792 | tf_op jit(solution)/shard_map/dot_general | solution.py:30
  709.1 11.6 %convolution_convert_fusion = bf16[2048,2048]{1,0:T(8,128)(2,1)} fusion(bf16[1024,2048]{1,0:T(8,128)(2,1)S(1)} %copy-done.18, bf16[1024,3072]{1,0:T(8,128)(2,1)S(1)} %copy-done.66), kind=kOutput, calls=%fused_computation.4 | convolution fusion | flops 8594128896 | bytes 16777216 | tf_op jit(solution)/shard_map/dot_general | solution.py:26
  726.2 10.7 %fusion.17 = bf16[512,2048]{1,0:T(8,128)(2,1)S(1)} fusion(bf16[2048,4096]{1,0:T(8,128)(2,1)} %all-gather.4.cloned.1.call-done.refs_3_.w_ref.refs_6_, bf16[1024,3072]{1,0:T(8,128)(2,1)} %get-tuple-element.116), kind=kOutput, calls=%fused_computation.16 | convolution fusion | flops 6443499520 | bytes 17825792 | tf_op jit(solution)/shard_map/dot_general | solution.py:30
  742.9 10.1 %collective-permute-done.63 = bf16[512,512]{1,0:T(8,128)(2,1)S(1)} collective-permute-done((bf16[512,512]{1,0:T(8,128)(2,1)S(1)}, bf16[512,512]{1,0:T(8,128)(2,1)S(1)}, u32[]{:S(2)}, u32[]{:S(2)}) %collective-permute-start.63) | collective-permute-done | bytes 524320 | tf_op jit(solution)/shard_map/ppermute | solution.py:89
  769.4 10.1 %collective-permute-done.61 = f32[8,128]{1,0:T(8,128)S(1)} collective-permute-done((f32[8,128]{1,0:T(8,128)S(1)}, f32[8,128]{1,0:T(8,128)S(1)}, u32[]{:S(2)}, u32[]{:S(2)}) %collective-permute-start.61) | collective-permute-done | bytes 4128 | tf_op jit(solution)/shard_map/ppermute | solution.py:114
  831.4 71.3 %reduce-scatter.11.cloned.1.call-done = bf16[1,768,1024]{2,1,0:T(8,128)(2,1)} async-done(((bf16[8,768,1024]{2,1,0:T(8,128)(2,1)}), bf16[1,768,1024]{2,1,0:T(8,128)(2,1)}) %reduce-scatter.11.cloned.1.call-update) | async-done | bytes 1572880 | tf_op jit(solution)/shard_map/reduce_scatter | solution.py:830
  (356 shorter events, 245.1 us)
Async XLA Ops:
  7.2 114.3 %all-gather.4.cloned.1.call-start = ((), (), s32[]{:S(2)}) async-start(), calls=%async_computation.4 | async-start | bytes 18874368 | tf_op jit(solution)/shard_map/all_gather | solution.py:698
  11.2 290.5 %all-gather.8.cloned.1.call-start = ((), (), s32[]{:S(2)}) async-start(), calls=%async_computation.6 | async-start | bytes 5242880 | tf_op jit(solution)/shard_map/all_gather | solution.py:716
  11.4 19.9 %collective-permute-start.1 = (f32[2,512]{1,0:T(2,128)S(1)}, f32[2,512]{1,0:T(2,128)S(1)}, u32[]{:S(2)}, u32[]{:S(2)}) collective-permute-start(f32[2,512]{1,0:T(2,128)S(1)} %get-tuple-element.177), channel_id=1, source_target_pairs={{0,2},{1,3},{2,0},{3,1},{4,6},{5,7},{6,4},{7,5},{8,10},{9,11},{10,... | collective-permute-start | bytes 12296 | tf_op jit(solution)/shard_map/ppermute | solution.py:106
  19.3 23.3 %collective-permute-start.3 = (bf16[1024,512]{1,0:T(8,128)(2,1)S(1)}, bf16[1024,512]{1,0:T(8,128)(2,1)S(1)}, u32[]{:S(2)}, u32[]{:S(2)}) collective-permute-start(bf16[1024,512]{1,0:T(8,128)(2,1)S(1)} %copy-done.30), channel_id=1, source_target_pairs={{0,1},{1,2},{2,3},{4,5},{5,6},{6,7},{8,9},{9,10},{10,11},{12,13},{... | collective-permute-start | bytes 3145736 | tf_op jit(solution)/shard_map/ppermute | solution.py:58
  42.6 259.1 %all-gather.6.cloned.1.call-start = ((), (), s32[]{:S(2)}) async-start(), calls=%async_computation.5 | async-start | bytes 14155776 | tf_op jit(solution)/shard_map/all_gather | solution.py:717
  42.7 26.1 %collective-permute-start.5 = (bf16[1024,512]{1,0:T(8,128)(2,1)S(1)}, bf16[1024,512]{1,0:T(8,128)(2,1)}, u32[]{:S(2)}, u32[]{:S(2)}) collective-permute-start(bf16[1024,512]{1,0:T(8,128)(2,1)S(1)} %copy-done.30), channel_id=1, source_target_pairs={{3,2},{2,1},{1,0},{7,6},{6,5},{5,4},{11,10},{10,9},{9,8},{15,14},{... | collective-permute-start | bytes 3145736 | tf_op jit(solution)/shard_map/ppermute | solution.py:59
  68.8 24.9 %collective-permute-start.6 = (bf16[1024,512]{1,0:T(8,128)(2,1)}, bf16[1024,512]{1,0:T(8,128)(2,1)S(1)}, u32[]{:S(2)}, u32[]{:S(2)}) collective-permute-start(bf16[1024,512]{1,0:T(8,128)(2,1)} %collective-permute-done.5.refs_12_), channel_id=1, source_target_pairs={{2,1},{1,0},{6,5},{5,4},{10,9},{9,8},{14,13},{13,12},{18,17},{17,1... | collective-permute-start | bytes 3145736 | tf_op jit(solution)/shard_map/ppermute | solution.py:59
  70.1 23.6 %collective-permute-start.4 = (bf16[1024,512]{1,0:T(8,128)(2,1)S(1)}, bf16[1024,512]{1,0:T(8,128)(2,1)S(1)}, u32[]{:S(2)}, u32[]{:S(2)}) collective-permute-start(bf16[1024,512]{1,0:T(8,128)(2,1)S(1)} %collective-permute-done.3.refs_7_), channel_id=1, source_target_pairs={{1,2},{2,3},{5,6},{6,7},{9,10},{10,11},{13,14},{14,15},{17,18},{18... | collective-permute-start | bytes 3145736 | tf_op jit(solution)/shard_map/ppermute | solution.py:58
  93.8 26.9 %collective-permute-start.7 = (bf16[1024,512]{1,0:T(8,128)(2,1)S(1)}, bf16[1024,512]{1,0:T(8,128)(2,1)}, u32[]{:S(2)}, u32[]{:S(2)}) collective-permute-start(bf16[1024,512]{1,0:T(8,128)(2,1)S(1)} %broadcast_select_fusion), channel_id=1, source_target_pairs={{2,3},{1,0},{6,7},{5,4},{10,11},{9,8},{14,15},{13,12},{18,19},{17,... | collective-permute-start | bytes 3145736 | tf_op jit(solution)/shard_map/ppermute | solution.py:54
  120.6 700.4 %reduce-scatter.5.cloned.1.call-start = ((), (), s32[]{:S(2)}) async-start(), calls=%async_computation.7 | async-start | bytes 5242880 | tf_op jit(solution)/shard_map/reduce_scatter | solution.py:779
  174.0 19.3 %collective-permute-start.10 = (bf16[512,512]{1,0:T(8,128)(2,1)S(1)}, bf16[512,512]{1,0:T(8,128)(2,1)S(1)}, u32[]{:S(2)}, u32[]{:S(2)}) collective-permute-start(bf16[512,512]{1,0:T(8,128)(2,1)S(1)} %constant_dynamic-slice_fusion.5), channel_id=1, source_target_pairs={{0,1},{3,2},{4,5},{7,6},{8,9},{11,10},{12,13},{15,14},{16,17},{19,... | collective-permute-start | bytes 1572872 | tf_op jit(solution)/shard_map/ppermute | solution.py:89
  214.7 18.2 %collective-permute-start.15 = (bf16[512,512]{1,0:T(8,128)(2,1)S(1)}, bf16[512,512]{1,0:T(8,128)(2,1)}, u32[]{:S(2)}, u32[]{:S(2)}) collective-permute-start(bf16[512,512]{1,0:T(8,128)(2,1)S(1)} %constant_dynamic-slice_fusion.4), channel_id=1, source_target_pairs={{0,1},{3,2},{4,5},{7,6},{8,9},{11,10},{12,13},{15,14},{16,17},{19,... | collective-permute-start | bytes 1572872 | tf_op jit(solution)/shard_map/ppermute | solution.py:89
  224.0 20.3 %collective-permute-start.12 = (bf16[512,512]{1,0:T(8,128)(2,1)}, bf16[512,512]{1,0:T(8,128)(2,1)S(1)}, u32[]{:S(2)}, u32[]{:S(2)}) collective-permute-start(bf16[512,512]{1,0:T(8,128)(2,1)} %get-tuple-element.163), channel_id=1, source_target_pairs={{0,1},{1,2},{2,3},{4,5},{5,6},{6,7},{8,9},{9,10},{10,11},{12,13},{... | collective-permute-start | bytes 1572872 | tf_op jit(solution)/shard_map/ppermute | solution.py:97
  225.3 18.9 %collective-permute-start.14 = (bf16[512,512]{1,0:T(8,128)(2,1)}, bf16[512,512]{1,0:T(8,128)(2,1)S(1)}, u32[]{:S(2)}, u32[]{:S(2)}) collective-permute-start(bf16[512,512]{1,0:T(8,128)(2,1)} %get-tuple-element.164), channel_id=1, source_target_pairs={{3,2},{2,1},{1,0},{7,6},{6,5},{5,4},{11,10},{10,9},{9,8},{15,14},{... | collective-permute-start | bytes 1572872 | tf_op jit(solution)/shard_map/ppermute | solution.py:98
  235.3 20.2 %collective-permute-start.16 = (bf16[512,512]{1,0:T(8,128)(2,1)}, bf16[512,512]{1,0:T(8,128)(2,1)}, u32[]{:S(2)}, u32[]{:S(2)}) collective-permute-start(bf16[512,512]{1,0:T(8,128)(2,1)} %get-tuple-element.147), channel_id=1, source_target_pairs={{0,1},{1,2},{4,5},{5,6},{8,9},{9,10},{12,13},{13,14},{16,17},{17,1... | collective-permute-start | bytes 1572872 | tf_op jit(solution)/shard_map/ppermute | solution.py:97
  257.1 18.3 %collective-permute-start.17 = (bf16[512,512]{1,0:T(8,128)(2,1)S(1)}, bf16[512,512]{1,0:T(8,128)(2,1)S(1)}, u32[]{:S(2)}, u32[]{:S(2)}) collective-permute-start(bf16[512,512]{1,0:T(8,128)(2,1)S(1)} %get-tuple-element.165), channel_id=1, source_target_pairs={{0,1},{1,2},{2,3},{4,5},{5,6},{6,7},{8,9},{9,10},{10,11},{12,13},{... | collective-permute-start | bytes 1572872 | tf_op jit(solution)/shard_map/ppermute | solution.py:97
  262.8 25.2 %collective-permute-start.28 = (bf16[512,512]{1,0:T(8,128)(2,1)S(1)}, bf16[512,512]{1,0:T(8,128)(2,1)S(1)}, u32[]{:S(2)}, u32[]{:S(2)}) collective-permute-start(bf16[512,512]{1,0:T(8,128)(2,1)S(1)} %collective-permute-done.27.refs_10_), channel_id=1, source_target_pairs={{2,1},{1,0},{6,5},{5,4},{10,9},{9,8},{14,13},{13,12},{18,17},{17,1... | collective-permute-start | bytes 1572872 | tf_op jit(solution)/shard_map/ppermute | solution.py:59
  266.6 21.4 %collective-permute-start.26 = (bf16[512,512]{1,0:T(8,128)(2,1)S(1)}, bf16[512,512]{1,0:T(8,128)(2,1)S(1)}, u32[]{:S(2)}, u32[]{:S(2)}) collective-permute-start(bf16[512,512]{1,0:T(8,128)(2,1)S(1)} %collective-permute-done.20.refs_5_), channel_id=1, source_target_pairs={{1,2},{2,3},{5,6},{6,7},{9,10},{10,11},{13,14},{14,15},{17,18},{18... | collective-permute-start | bytes 1572872 | tf_op jit(solution)/shard_map/ppermute | solution.py:58
  278.3 20.9 %collective-permute-start.23 = (bf16[512,512]{1,0:T(8,128)(2,1)S(1)}, bf16[512,512]{1,0:T(8,128)(2,1)S(1)}, u32[]{:S(2)}, u32[]{:S(2)}) collective-permute-start(bf16[512,512]{1,0:T(8,128)(2,1)S(1)} %get-tuple-element.130.refs_4_), channel_id=1, source_target_pairs={{3,2},{2,1},{1,0},{7,6},{6,5},{5,4},{11,10},{10,9},{9,8},{15,14},{... | collective-permute-start | bytes 1572872 | tf_op jit(solution)/shard_map/ppermute | solution.py:59
  279.7 20.9 %collective-permute-start.21 = (bf16[512,512]{1,0:T(8,128)(2,1)S(1)}, bf16[512,512]{1,0:T(8,128)(2,1)}, u32[]{:S(2)}, u32[]{:S(2)}) collective-permute-start(bf16[512,512]{1,0:T(8,128)(2,1)S(1)} %get-tuple-element.130.refs_4_), channel_id=1, source_target_pairs={{0,1},{1,2},{2,3},{4,5},{5,6},{6,7},{8,9},{9,10},{10,11},{12,13},{... | collective-permute-start | bytes 1572872 | tf_op jit(solution)/shard_map/ppermute | solution.py:58
  288.1 22.5 %collective-permute-start.29 = (bf16[512,512]{1,0:T(8,128)(2,1)S(1)}, bf16[512,512]{1,0:T(8,128)(2,1)}, u32[]{:S(2)}, u32[]{:S(2)}) collective-permute-start(bf16[512,512]{1,0:T(8,128)(2,1)S(1)} %broadcast_select_fusion.4), channel_id=1, source_target_pairs={{2,3},{1,0},{6,7},{5,4},{10,11},{9,8},{14,15},{13,12},{18,19},{17,... | collective-permute-start | bytes 1572872 | tf_op jit(solution)/shard_map/ppermute | solution.py:54
  299.3 33.9 %collective-permute-start.24 = (bf16[512,512]{1,0:T(8,128)(2,1)S(1)}, bf16[512,512]{1,0:T(8,128)(2,1)S(1)}, u32[]{:S(2)}, u32[]{:S(2)}) collective-permute-start(bf16[512,512]{1,0:T(8,128)(2,1)S(1)} %collective-permute-done.23.refs_10_), channel_id=1, source_target_pairs={{2,1},{1,0},{6,5},{5,4},{10,9},{9,8},{14,13},{13,12},{18,17},{17,1... | collective-permute-start | bytes 1572872 | tf_op jit(solution)/shard_map/ppermute | solution.py:59
  300.6 32.6 %collective-permute-start.22 = (bf16[512,512]{1,0:T(8,128)(2,1)}, bf16[512,512]{1,0:T(8,128)(2,1)S(1)}, u32[]{:S(2)}, u32[]{:S(2)}) collective-permute-start(bf16[512,512]{1,0:T(8,128)(2,1)} %collective-permute-done.21.refs_5_), channel_id=1, source_target_pairs={{1,2},{2,3},{5,6},{6,7},{9,10},{10,11},{13,14},{14,15},{17,18},{18... | collective-permute-start | bytes 1572872 | tf_op jit(solution)/shard_map/ppermute | solution.py:58
  343.9 26.6 %collective-permute-start.32 = (bf16[512,512]{1,0:T(8,128)(2,1)}, bf16[512,512]{1,0:T(8,128)(2,1)S(1)}, u32[]{:S(2)}, u32[]{:S(2)}) collective-permute-start(bf16[512,512]{1,0:T(8,128)(2,1)} %get-tuple-element.145), channel_id=1, source_target_pairs={{3,2},{2,1},{7,6},{6,5},{11,10},{10,9},{15,14},{14,13},{19,18},{18... | collective-permute-start | bytes 1572872 | tf_op jit(solution)/shard_map/ppermute | solution.py:98
  344.6 25.9 %collective-permute-start.31 = (bf16[512,512]{1,0:T(8,128)(2,1)}, bf16[512,512]{1,0:T(8,128)(2,1)S(1)}, u32[]{:S(2)}, u32[]{:S(2)}) collective-permute-start(bf16[512,512]{1,0:T(8,128)(2,1)} %get-tuple-element.146), channel_id=1, source_target_pairs={{0,1},{1,2},{4,5},{5,6},{8,9},{9,10},{12,13},{13,14},{16,17},{17,1... | collective-permute-start | bytes 1572872 | tf_op jit(solution)/shard_map/ppermute | solution.py:97
  377.8 23.9 %collective-permute-start.40 = (f32[4,128]{1,0:T(4,128)S(1)}, f32[4,128]{1,0:T(4,128)S(1)}, u32[]{:S(2)}, u32[]{:S(2)}) collective-permute-start(f32[4,128]{1,0:T(4,128)S(1)} %bitcast.56), channel_id=1, source_target_pairs={{0,1},{1,0},{2,3},{3,2},{4,5},{5,4},{6,7},{7,6},{8,9},{9,8},{10,11... | collective-permute-start | bytes 6152 | tf_op jit(solution)/shard_map/ppermute | solution.py:114
  388.7 26.2 %collective-permute-start.34 = (bf16[512,512]{1,0:T(8,128)(2,1)}, bf16[512,512]{1,0:T(8,128)(2,1)}, u32[]{:S(2)}, u32[]{:S(2)}) collective-permute-start(bf16[512,512]{1,0:T(8,128)(2,1)} %get-tuple-element.143), channel_id=1, source_target_pairs={{0,1},{1,2},{4,5},{5,6},{8,9},{9,10},{12,13},{13,14},{16,17},{17,1... | collective-permute-start | bytes 1572872 | tf_op jit(solution)/shard_map/ppermute | solution.py:97
  393.9 21.0 %collective-permute-start.36 = (bf16[512,512]{1,0:T(8,128)(2,1)}, bf16[512,512]{1,0:T(8,128)(2,1)}, u32[]{:S(2)}, u32[]{:S(2)}) collective-permute-start(bf16[512,512]{1,0:T(8,128)(2,1)} %get-tuple-element.144), channel_id=1, source_target_pairs={{3,2},{2,1},{7,6},{6,5},{11,10},{10,9},{15,14},{14,13},{19,18},{18... | collective-permute-start | bytes 1572872 | tf_op jit(solution)/shard_map/ppermute | solution.py:98
  398.3 25.7 %collective-permute-start.38 = (bf16[512,512]{1,0:T(8,128)(2,1)}, bf16[512,512]{1,0:T(8,128)(2,1)}, u32[]{:S(2)}, u32[]{:S(2)}) collective-permute-start(bf16[512,512]{1,0:T(8,128)(2,1)} %get-tuple-element.159), channel_id=1, source_target_pairs={{0,1},{1,2},{2,3},{4,5},{5,6},{6,7},{8,9},{9,10},{10,11},{12,13},{... | collective-permute-start | bytes 1572872 | tf_op jit(solution)/shard_map/ppermute | solution.py:97
  400.4 23.6 %collective-permute-start.39 = (bf16[512,512]{1,0:T(8,128)(2,1)}, bf16[512,512]{1,0:T(8,128)(2,1)}, u32[]{:S(2)}, u32[]{:S(2)}) collective-permute-start(bf16[512,512]{1,0:T(8,128)(2,1)} %get-tuple-element.160), channel_id=1, source_target_pairs={{3,2},{2,1},{1,0},{7,6},{6,5},{5,4},{11,10},{10,9},{9,8},{15,14},{... | collective-permute-start | bytes 1572872 | tf_op jit(solution)/shard_map/ppermute | solution.py:98
  414.8 18.3 %collective-permute-start.43 = (f32[4,128]{1,0:T(4,128)S(1)}, f32[4,128]{1,0:T(4,128)S(1)}, u32[]{:S(2)}, u32[]{:S(2)}) collective-permute-start(f32[4,128]{1,0:T(4,128)S(1)} %bitcast.55), channel_id=1, source_target_pairs={{0,1},{1,0},{2,3},{3,2},{4,5},{5,4},{6,7},{7,6},{8,9},{9,8},{10,11... | collective-permute-start | bytes 6152 | tf_op jit(solution)/shard_map/ppermute | solution.py:114
  417.7 23.1 %collective-permute-start.35 = (bf16[512,512]{1,0:T(8,128)(2,1)}, bf16[512,512]{1,0:T(8,128)(2,1)}, u32[]{:S(2)}, u32[]{:S(2)}) collective-permute-start(bf16[512,512]{1,0:T(8,128)(2,1)} %get-tuple-element.161), channel_id=1, source_target_pairs={{0,1},{1,2},{2,3},{4,5},{5,6},{6,7},{8,9},{9,10},{10,11},{12,13},{... | collective-permute-start | bytes 1572872 | tf_op jit(solution)/shard_map/ppermute | solution.py:97
  422.7 18.1 %collective-permute-start.37 = (bf16[512,512]{1,0:T(8,128)(2,1)}, bf16[512,512]{1,0:T(8,128)(2,1)}, u32[]{:S(2)}, u32[]{:S(2)}) collective-permute-start(bf16[512,512]{1,0:T(8,128)(2,1)} %get-tuple-element.162), channel_id=1, source_target_pairs={{3,2},{2,1},{1,0},{7,6},{6,5},{5,4},{11,10},{10,9},{9,8},{15,14},{... | collective-permute-start | bytes 1572872 | tf_op jit(solution)/shard_map/ppermute | solution.py:98
  456.8 367.0 %reduce-scatter.9.cloned.1.call-start = ((), (), s32[]{:S(2)}) async-start(), calls=%async_computation.9 | async-start | bytes 9437184 | tf_op jit(solution)/shard_map/reduce_scatter | solution.py:830
  456.8 22.0 %collective-permute-start.47 = (bf16[512,512]{1,0:T(8,128)(2,1)}, bf16[512,512]{1,0:T(8,128)(2,1)S(1)}, u32[]{:S(2)}, u32[]{:S(2)}) collective-permute-start(bf16[512,512]{1,0:T(8,128)(2,1)} %get-tuple-element.98.refs_6_), channel_id=1, source_target_pairs={{3,2},{2,1},{1,0},{7,6},{6,5},{5,4},{11,10},{10,9},{9,8},{15,14},{... | collective-permute-start | bytes 1572872 | tf_op jit(solution)/shard_map/ppermute | solution.py:59
  458.1 60.0 %collective-permute-start.51 = (bf16[512,512]{1,0:T(8,128)(2,1)}, bf16[512,512]{1,0:T(8,128)(2,1)S(1)}, u32[]{:S(2)}, u32[]{:S(2)}) collective-permute-start(bf16[512,512]{1,0:T(8,128)(2,1)} %fusion.32.refs_6_), channel_id=1, source_target_pairs={{3,2},{2,1},{1,0},{7,6},{6,5},{5,4},{11,10},{10,9},{9,8},{15,14},{... | collective-permute-start | bytes 1572872 | tf_op jit(solution)/shard_map/ppermute | solution.py:59
  459.4 94.7 %collective-permute-start.46 = (bf16[512,512]{1,0:T(8,128)(2,1)}, bf16[512,512]{1,0:T(8,128)(2,1)S(1)}, u32[]{:S(2)}, u32[]{:S(2)}) collective-permute-start(bf16[512,512]{1,0:T(8,128)(2,1)} %collective-permute-done.42.refs_7_), channel_id=1, source_target_pairs={{1,2},{2,3},{5,6},{6,7},{9,10},{10,11},{13,14},{14,15},{17,18},{18... | collective-permute-start | bytes 1572872 | tf_op jit(solution)/shard_map/ppermute | solution.py:58
  478.8 75.3 %collective-permute-start.48 = (bf16[512,512]{1,0:T(8,128)(2,1)S(1)}, bf16[512,512]{1,0:T(8,128)(2,1)S(1)}, u32[]{:S(2)}, u32[]{:S(2)}) collective-permute-start(bf16[512,512]{1,0:T(8,128)(2,1)S(1)} %collective-permute-done.47.refs_12_), channel_id=1, source_target_pairs={{2,1},{1,0},{6,5},{5,4},{10,9},{9,8},{14,13},{13,12},{18,17},{17,1... | collective-permute-start | bytes 1572872 | tf_op jit(solution)/shard_map/ppermute | solution.py:59
  480.1 88.9 %collective-permute-start.50 = (bf16[512,512]{1,0:T(8,128)(2,1)S(1)}, bf16[512,512]{1,0:T(8,128)(2,1)S(1)}, u32[]{:S(2)}, u32[]{:S(2)}) collective-permute-start(bf16[512,512]{1,0:T(8,128)(2,1)S(1)} %collective-permute-done.45.refs_7_), channel_id=1, source_target_pairs={{1,2},{2,3},{5,6},{6,7},{9,10},{10,11},{13,14},{14,15},{17,18},{18... | collective-permute-start | bytes 1572872 | tf_op jit(solution)/shard_map/ppermute | solution.py:58
  518.1 50.9 %collective-permute-start.52 = (bf16[512,512]{1,0:T(8,128)(2,1)S(1)}, bf16[512,512]{1,0:T(8,128)(2,1)S(1)}, u32[]{:S(2)}, u32[]{:S(2)}) collective-permute-start(bf16[512,512]{1,0:T(8,128)(2,1)S(1)} %collective-permute-done.51.refs_12_), channel_id=1, source_target_pairs={{2,1},{1,0},{6,5},{5,4},{10,9},{9,8},{14,13},{13,12},{18,17},{17,1... | collective-permute-start | bytes 1572872 | tf_op jit(solution)/shard_map/ppermute | solution.py:59
  555.0 46.7 %collective-permute-start.49 = (bf16[512,512]{1,0:T(8,128)(2,1)}, bf16[512,512]{1,0:T(8,128)(2,1)S(1)}, u32[]{:S(2)}, u32[]{:S(2)}) collective-permute-start(bf16[512,512]{1,0:T(8,128)(2,1)} %broadcast_select_fusion.3), channel_id=1, source_target_pairs={{2,3},{1,0},{6,7},{5,4},{10,11},{9,8},{14,15},{13,12},{18,19},{17,... | collective-permute-start | bytes 1572872 | tf_op jit(solution)/shard_map/ppermute | solution.py:54
  569.9 43.5 %collective-permute-start.53 = (bf16[512,512]{1,0:T(8,128)(2,1)}, bf16[512,512]{1,0:T(8,128)(2,1)S(1)}, u32[]{:S(2)}, u32[]{:S(2)}) collective-permute-start(bf16[512,512]{1,0:T(8,128)(2,1)} %broadcast_select_fusion.2), channel_id=1, source_target_pairs={{2,3},{1,0},{6,7},{5,4},{10,11},{9,8},{14,15},{13,12},{18,19},{17,... | collective-permute-start | bytes 1572872 | tf_op jit(solution)/shard_map/ppermute | solution.py:54
  658.5 168.5 %reduce-scatter.7.cloned.1.call-start = ((), (), s32[]{:S(2)}) async-start(), calls=%async_computation.8 | async-start | bytes 9437184 | tf_op jit(solution)/shard_map/reduce_scatter | solution.py:830
  720.8 181.9 %reduce-scatter.11.cloned.1.call-start = ((), (), s32[]{:S(2)}) async-start(), calls=%async_computation.10 | async-start | bytes 14155776 | tf_op jit(solution)/shard_map/reduce_scatter | solution.py:830
  754.3 25.4 %collective-permute-start.64 = (bf16[512,512]{1,0:T(8,128)(2,1)}, bf16[512,512]{1,0:T(8,128)(2,1)}, u32[]{:S(2)}, u32[]{:S(2)}) collective-permute-start(bf16[512,512]{1,0:T(8,128)(2,1)} %get-tuple-element.139), channel_id=1, source_target_pairs={{0,1},{1,2},{4,5},{5,6},{8,9},{9,10},{12,13},{13,14},{16,17},{17,1... | collective-permute-start | bytes 1572872 | tf_op jit(solution)/shard_map/ppermute | solution.py:97
  759.5 20.3 %collective-permute-start.66 = (bf16[512,512]{1,0:T(8,128)(2,1)}, bf16[512,512]{1,0:T(8,128)(2,1)}, u32[]{:S(2)}, u32[]{:S(2)}) collective-permute-start(bf16[512,512]{1,0:T(8,128)(2,1)} %get-tuple-element.140), channel_id=1, source_target_pairs={{3,2},{2,1},{7,6},{6,5},{11,10},{10,9},{15,14},{14,13},{19,18},{18... | collective-permute-start | bytes 1572872 | tf_op jit(solution)/shard_map/ppermute | solution.py:98
  763.6 24.0 %collective-permute-start.59 = (bf16[512,512]{1,0:T(8,128)(2,1)}, bf16[512,512]{1,0:T(8,128)(2,1)S(1)}, u32[]{:S(2)}, u32[]{:S(2)}) collective-permute-start(bf16[512,512]{1,0:T(8,128)(2,1)} %get-tuple-element.124), channel_id=1, source_target_pairs={{3,2},{2,1},{7,6},{6,5},{11,10},{10,9},{15,14},{14,13},{19,18},{18... | collective-permute-start | bytes 1572872 | tf_op jit(solution)/shard_map/ppermute | solution.py:98
  764.4 23.1 %collective-permute-start.57 = (bf16[512,512]{1,0:T(8,128)(2,1)}, bf16[512,512]{1,0:T(8,128)(2,1)S(1)}, u32[]{:S(2)}, u32[]{:S(2)}) collective-permute-start(bf16[512,512]{1,0:T(8,128)(2,1)} %get-tuple-element.141), channel_id=1, source_target_pairs={{0,1},{1,2},{4,5},{5,6},{8,9},{9,10},{12,13},{13,14},{16,17},{17,1... | collective-permute-start | bytes 1572872 | tf_op jit(solution)/shard_map/ppermute | solution.py:97
  (97 other events, 1893.9 us)
Sparse Core Ops, SparseCore 0:
  11.4 92.4 all-gather.3
  105.4 83.4 all-gather.7
  190.8 72.6 all-gather.5
  456.9 112.5 reduce-scatter.4
  658.6 73.4 reduce-scatter.8
  735.4 71.4 reduce-scatter.6
  810.4 92.2 reduce-scatter.10

commit v4 on v3

--- a/solution.py
+++ b/solution.py
@@ -12,7 +12,6 @@
 HV = 512
 EPSILON = 1e-06
 BLOCK = 512
-COLUMNS = 1024
 TP, CTX, DP = "tp", "ctx", "dp"
 F32 = jnp.float32
 BF16 = jnp.bfloat16
@@ -101,6 +100,19 @@
     return block(i).astype(F32) + from_left.astype(F32) + from_right.astype(F32), early
 
 
+def routed_scatter(parts, axis):
+    n, i = lax.axis_size(axis), lax.axis_index(axis)
+    width = parts.shape[1] // n
+
+    def block(j):
+        return lax.dynamic_slice(parts, (0, (j % n) * width), (parts.shape[0], width))
+
+    total = block(i).astype(F32)
+    for k in range(1, n):
+        total = total + lax.ppermute(block(i + k), axis, [(j, (j + k) % n) for j in range(n)]).astype(F32)
+    return total
+
+
 def small_gather(x, axis):
     n = lax.axis_size(axis)
     blocks = [x] + [lax.ppermute(x, axis, [(j, (j + s) % n) for j in range(n)]) for s in range(1, n)]
@@ -172,34 +184,6 @@
         cost_estimate=pl.CostEstimate(flops=0, bytes_accessed=4 * rows * sum(widths), transcendentals=0),
         name="join",
     )(*arrays)
-
-
-def stacked(devices, *grads):
-    rows = grads[0].shape[0] // devices
-    counts = [g.shape[1] // COLUMNS for g in grads]
-    firsts = [sum(counts[:i]) for i in range(len(counts))]
-
-    def kernel(*refs):
-        t = pl.program_id(1)
-        for ref, first, count in zip(refs, firsts, counts):
-
-            @pl.when((t >= first) & (t < first + count))
-            def _(ref=ref):
-                refs[-1][0] = ref[...]
-
-    def spec(first, count):
-        return pl.BlockSpec((rows, COLUMNS), lambda d, t: (d, jnp.clip(t - first, 0, count - 1)))
-
-    total = sum(counts)
-    return pl.pallas_call(
-        kernel,
-        grid=(devices, total),
-        in_specs=[spec(first, count) for first, count in zip(firsts, counts)],
-        out_specs=pl.BlockSpec((1, rows, COLUMNS), lambda d, t: (d, t, 0)),
-        out_shape=jax.ShapeDtypeStruct((devices, total * rows, COLUMNS), grads[0].dtype),
-        cost_estimate=pl.CostEstimate(flops=0, bytes_accessed=4 * devices * total * rows * COLUMNS, transcendentals=0),
-        name="stack",
-    )(*grads)
 
 
 def gathered(at, refs, k, rows=slice(None)):
@@ -327,9 +311,13 @@
     )(x, w)
 
 
-def mlp_kernel(units, count, at_ref, gain_ref, w_ref, grad_ref, *refs):
-    blocks, (full_ref, hidden_ref, acts_ref, scale_ref, inner_ref, back_ref) = refs[:count], refs[-6:]
-    scale_ref[...] = fill_normed(at_ref[0], blocks, gain_ref, full_ref)
+def mlp_kernel(units, count, at_ref, gain_ref, w_ref, *refs):
+    blocks, grads = refs[:count], refs[count : 2 * count]
+    full_ref, hidden_ref, acts_ref, grad_ref, scale_ref, inner_ref, back_ref = refs[-7:]
+    at, n = at_ref[0], count // 2 + 1
+    scale_ref[...] = fill_normed(at, blocks, gain_ref, full_ref)
+    for k in range(n):
+        grad_ref[:, columns_of(at, n, k, grads[0].shape[1])] = gathered(at, grads, k)
     x = full_ref[...]
     gate = nn(x, w_ref[:, :units])
     up = nn(x, w_ref[:, units : 2 * units])
@@ -346,13 +334,13 @@
     back_ref[...] = (nt(g_gate, w_ref[:, :units]) + nt(g_up, w_ref[:, units : 2 * units])).astype(BF16)
 
 
-def mlp(at, gain, w, part, grad, x, pairs, shared):
+def mlp(at, gain, w, part, grads, x, pairs, shared):
     rows, width = x.shape
     features = w.shape[0]
     units = w.shape[1] // 3
     blocks = flat(x, pairs)
     steps = rows // BLOCK
-    total = grad.shape[0]
+    total = grads[0].shape[0]
 
     def by_rows(columns):
         return pl.BlockSpec((BLOCK, columns), lambda r: (r, 0))
@@ -367,14 +355,15 @@
             pl.BlockSpec(memory_space=pltpu.SMEM),
             pl.BlockSpec((1, features), lambda r: (0, 0)),
             pl.BlockSpec((features, 3 * units), lambda r: (0, 0)),
-            own_rows(features),
             *[by_rows(width)] * len(blocks),
+            *[own_rows(width)] * len(grads),
             *[pl.BlockSpec(memory_space=pl.ANY)] * len(shared),
         ],
         out_specs=[
             own_rows(features),
             own_rows(units),
             own_rows(2 * units),
+            own_rows(features),
             by_rows(1),
             by_rows(1),
             by_rows(features),
@@ -383,18 +372,19 @@
             jax.ShapeDtypeStruct((total, features), BF16),
             jax.ShapeDtypeStruct((total, units), BF16),
             jax.ShapeDtypeStruct((total, 2 * units), BF16),
+            jax.ShapeDtypeStruct((total, features), BF16),
             jax.ShapeDtypeStruct((rows, 1), F32),
             jax.ShapeDtypeStruct((rows, 1), F32),
             jax.ShapeDtypeStruct((rows, features), BF16),
         ],
-        input_output_aliases={4 + len(blocks) + i: i for i in range(len(shared))},
+        input_output_aliases={3 + 2 * len(blocks) + i: i for i in range(len(shared))},
         cost_estimate=pl.CostEstimate(
             flops=10 * rows * features * units,
             bytes_accessed=6 * features * units + 14 * rows * features,
             transcendentals=2 * rows * units,
         ),
         name="mlp",
-    )(at, gain, w, grad, *blocks, *shared)
+    )(at, gain, w, *blocks, *grads, *shared)
 
 
 def decay_vectors(log_gamma):
@@ -713,10 +703,11 @@
     normed, scale_attn, q, k, v, local_state = project(
         here, log_gamma, gains[0:1], attn_full, layer_input, pairs, heads, cosine, sine
     )
-    grad_full = lax.all_gather(after(cotangent, pairs[0][0]), TP, axis=1, tiled=True)
-    mlp_full = lax.all_gather(after(mlp_shard, pairs[0][1]), data, axis=0, tiled=True)
+    cot = after(cotangent, pairs[-1][0])
+    cot_blocks = flat(cot, line_gather(cot, TP))
     gate_pre = product(after(normed, local_state), attn_full, (2 * qk + vw) // vw, vw)
     state_in = states_before(local_state, log_block, CTX).astype(BF16)
+    mlp_full = lax.all_gather(after(mlp_shard, state_in), data, axis=0, tiled=True)
     heads_out, branch = [], []
     for c in range(parts):
         *heads_out, out = retention_forward(
@@ -751,13 +742,13 @@
     shared = []
     for c in range(parts):
         *results, scale, inner, out = mlp(
-            here, gains[1:2], mlp_full, c, grad_full, middle[c].astype(BF16), mid_pairs[c], shared
+            here, gains[1:2], mlp_full, c, cot_blocks, middle[c].astype(BF16), mid_pairs[c], shared
         )
         shared = results
         scale_mlp.append(scale)
         inner_mlp.append(inner[:, 0])
         back.append(out)
-    normed_mlp, hidden, grad_acts = shared
+    normed_mlp, hidden, grad_acts, grad_full = shared
     early = ()
     for c in range(parts):
         inner = row_total(inner_mlp[c])
@@ -772,12 +763,11 @@
         grad_pairs.append(line_gather(grad_own[c], TP))
     grad_down = tn(grad_full, hidden).astype(BF16)
     grad_gate_up = tn(after(normed_mlp, grad_down), grad_acts).astype(BF16)
-    grad_mlp = stacked(devices, grad_gate_up, grad_down)
     mlp_parts = nt(hidden, mlp_full[:, 2 * units :]).astype(BF16)
 
-    grad_own[0] = after(grad_own[0], grad_mlp)
-    mlp_out = lax.psum_scatter(after(mlp_parts, grad_pairs[-1][0][0]), TP, scatter_dimension=1, tiled=True)
-    layer_output = (jnp.concatenate(middle) + mlp_out.astype(F32)).astype(BF16)
+    grad_own[0] = after(grad_own[0], grad_gate_up, grad_down)
+    mlp_out = routed_scatter(after(mlp_parts, grad_pairs[-1][-1][0]), TP)
+    layer_output = (jnp.concatenate(middle) + mlp_out).astype(BF16)
     shared = []
     partial_state = 0.0
     inner_attn = []
@@ -803,7 +793,7 @@
     state_grad = state_grad.astype(BF16)
     grad_out = tn(after(grad_attn, got), gated).astype(BF16)
     grad_retgate = tn(normed, after(g_gate, got)).astype(BF16)
-    grad_heads = stacked(devices, grad_retgate, grad_out)
+    grad_heads = jnp.concatenate([g.reshape(devices, -1, vw) for g in (grad_retgate, grad_out)], axis=1)
     grads_attn, inner = retention_backward(
         log_gamma, q, k, v, state_in, after(state_grad, grad_heads), cosine, sine, g_ret, g_gate
     )
@@ -829,7 +819,8 @@
     def shard(grad):
         return lax.psum_scatter(grad, data, scatter_dimension=0, tiled=True).astype(F32)
 
-    s_gate, s_up, s_down = jnp.split(shard(grad_mlp)[0], 3)
+    s_down = shard(grad_down)
+    s_gate_up = shard(grad_gate_up)
     s_retgate, s_out = jnp.split(shard(grad_heads)[0], 2)
     s_qkv = shard(grad_qkv_w)
     s_query, s_key, s_value = s_qkv[:, :qk], s_qkv[:, qk : 2 * qk], s_qkv[:, 2 * qk :]
@@ -844,8 +835,8 @@
         s_retgate,
         s_out,
         gain_sums[1],
-        s_gate,
-        s_up,
+        s_gate_up[:, :units],
+        s_gate_up[:, units:],
         s_down,
     )
 

time: 919 us -> 916 us (level)
  Pallas kernels: 173 us -> 143 us
  starting transfers between devices: 156 us -> 173 us
    reduce_scatter x3 -> x4, waiting for transfers between devices: 71.3 us -> 0.01 us  [shard(): lax.psum_scatter(grad, data, scatter_dimension=0, tiled=True).astype(F32)]
    ppermute x0 -> x3, waiting for transfers between devices: none -> 61.4 us  [routed_scatter(): lax.ppermute(block(i + k), axis, [(j, (j + k) % n) for j in range(n)])]
    ppermute x12, waiting for transfers between devices: 16.9 us -> 51.8 us  [line_scatter(): from_left = lax.ppermute(r_data, axis, r_pairs)]
    ppermute x10 -> x12, waiting for transfers between devices: 154 us -> 120 us  [line_gather(): lefts.append(lax.ppermute(lefts[-1], axis, l_pairs))]
    pallas_call x2 -> x0, Pallas kernels: 32.2 us -> none  [stacked(): pl.pallas_call(kernel, grid=(devices, total), in_specs=[spec(first, count...]
    ppermute x6, waiting for transfers between devices: 50.9 us -> 31.5 us  [line_scatter(): from_left = from_right = lax.ppermute(data, axis, r_pairs + l_pairs)]
    ppermute x12, waiting for transfers between devices: 10.8 us -> 27.2 us  [line_scatter(): from_right = lax.ppermute(l_data, axis, l_pairs)]
    ppermute x9, waiting for transfers between devices: 31.4 us -> 18.3 us  [swap_sum(): x = x + lax.ppermute(x, axis, [(j, j ^ g) for j in range(n)])]
  transfers between devices with their start and end apart: 78 -> 85, of which waited for: 38 -> 38; matrix products, arithmetic and copies ran while one was open for 17% -> 17% of each run, Pallas kernels for 19% -> 11%
where the time goes in v4:
time: 916 us; the launch traced here: 906 us
  waiting for transfers between devices  396 us (43%)
  starting transfers between devices  173 us (19%)
  Pallas kernels  143 us (16%)
  matrix products  81.5 us (9%)
  other arithmetic  74.9 us (8%)
  local copies, waits for them, and re-layouts  23.1 us (3%)
  between operations  16 us (2%)
    ppermute x12, waiting for transfers between devices, line_gather(): lefts.append(lax.ppermute(lefts[-1], axis, l_pairs))  120 us
    ppermute x3, waiting for transfers between devices, routed_scatter(): lax.ppermute(block(i + k), axis, [(j, (j + k) % n) for j in range(n)])  61.4 us
    ppermute x12, waiting for transfers between devices, line_scatter(): from_left = lax.ppermute(r_data, axis, r_pairs)  51.8 us
    dot_general x5, matrix products, tn(): lax.dot_general(a, b, (((0,), (0,)), ((), ())), preferred_element_type=F32)  51.2 us
    ppermute x12, starting transfers between devices, line_scatter(): from_left = lax.ppermute(r_data, axis, r_pairs)  46 us
    pallas_call x2, Pallas kernels, mlp(): pl.pallas_call(lambda *refs: mlp_kernel(units, len(blocks), *refs), grid=...  41.5 us
    ppermute x6, waiting for transfers between devices, line_gather(): lax.ppermute(jnp.where(i >= k - 1, rights[-1], lefts[-1]), axis, r_pairs...  32.9 us
    ppermute x12, starting transfers between devices, line_gather(): rights.append(lax.ppermute(rights[-1], axis, r_pairs))  32.7 us
  transfers between devices with their start and end apart: 85, of which 38 were waited for; matrix products, arithmetic and copies ran while one was open for 17% of the time, Pallas kernels for 11%

profile of v4, /device:TPU:0, one launch (start us, length us, event | category | flops | bytes accessed | tf_op | source)
XLA Modules:
  0.0 906.4 jit_solution(643345312474387075)
XLA Ops:
  22.7 5.5 fusion.23
  32.5 10.1 %collective-permute-done.3.refs_7_ = bf16[1024,512]{1,0:T(8,128)(2,1)S(1)} collective-permute-done((bf16[1024,512]{1,0:T(8,128)(2,1)S(1)}, bf16[1024,512]{1,0:T(8,128)(2,1)S(1)}, u32[]{:S(2)}, u32[]{:S(2)}) %collective-permute-start.3) | collective-permute-done | bytes 1048608 | tf_op jit(solution)/shard_map/ppermute | solution.py:57
  48.8 23.0 %collective-permute-done.6.refs_10_ = bf16[1024,512]{1,0:T(8,128)(2,1)S(1)} collective-permute-done((bf16[1024,512]{1,0:T(8,128)(2,1)}, bf16[1024,512]{1,0:T(8,128)(2,1)S(1)}, u32[]{:S(2)}, u32[]{:S(2)}) %collective-permute-start.6) | collective-permute-done | bytes 1048608 | tf_op jit(solution)/shard_map/ppermute | solution.py:58
  73.9 22.3 %collective-permute-done.7.refs_8_.refs_11_ = bf16[1024,512]{1,0:T(8,128)(2,1)} collective-permute-done((bf16[1024,512]{1,0:T(8,128)(2,1)S(1)}, bf16[1024,512]{1,0:T(8,128)(2,1)}, u32[]{:S(2)}, u32[]{:S(2)}) %collective-permute-start.7) | collective-permute-done | bytes 1048608 | tf_op jit(solution)/shard_map/ppermute | solution.py:53
  96.1 7.7 all-gather.3.cloned.1.call-done.refs_3_.w_ref.refs_6_
  103.8 22.1 %proj.1 = (bf16[1024,2048]{1,0:T(8,128)(2,1)}, f32[1024,1]{1,0:T(8,128)}, bf16[1024,512]{1,0:T(8,128)(2,1)}, bf16[1024,512]{1,0:T(8,128)(2,1)}, bf16[1024,1024]{1,0:T(8,128)(2,1)}, /*index=5*/f32[2,256,512]{2,1,0:T(8,128)}) custom-call(s32[1]{0:T(128)} %bitcast.refs_0_, f32[2]{0:T(128)} %negate_log-plus-one_fusion.refs_1_.refs_0_, ...), custom_call_target="tpu_custom_call" | custom-call | flops 8589934592 | bytes 33554432 | tf_op jit(solution)/shard_map/proj/pallas_call | solution.py:257
  131.6 13.3 %collective-permute-done.9 = bf16[2,256,512]{2,1,0:T(8,128)(2,1)S(1)} collective-permute-done((bf16[2,256,512]{2,1,0:T(8,128)(2,1)S(1)}, bf16[2,256,512]{2,1,0:T(8,128)(2,1)S(1)}, u32[]{:S(2)}, u32[]{:S(2)}) %collective-permute-start.9) | collective-permute-done | bytes 524320 | tf_op jit(solution)/shard_map/ppermute | solution.py:135
  146.4 8.9 prod.1.refs_4_
  155.2 9.7 %fwd.2 = (bf16[1024,1024]{1,0:T(8,128)(2,1)}, f32[1024,1024]{1,0:T(8,128)}, bf16[512,2048]{1,0:T(8,128)(2,1)}) custom-call(f32[2]{0:T(128)} %negate_log-plus-one_fusion.refs_1_.refs_0_, bf16[1024,512]{1,0:T(8,128)(2,1)} %get-tuple-element.68.refs_1_.refs_2_, bf16[1024,512]{1,0:T(8,128)(2,1)} %get-tuple-element.69.refs_2_, ...), custom_call_target="tpu_custom_call" | custom-call | flops 3221225472 | bytes 10485760 | tf_op jit(solution)/shard_map/fwd/pallas_call | solution.py:452
  169.5 10.6 %collective-permute-done.10 = bf16[512,512]{1,0:T(8,128)(2,1)S(1)} collective-permute-done((bf16[512,512]{1,0:T(8,128)(2,1)S(1)}, bf16[512,512]{1,0:T(8,128)(2,1)S(1)}, u32[]{:S(2)}, u32[]{:S(2)}) %collective-permute-start.10) | collective-permute-done | bytes 524320 | tf_op jit(solution)/shard_map/ppermute | solution.py:88
  189.4 10.4 %fwd.3 = (bf16[1024,1024]{1,0:T(8,128)(2,1)}, f32[1024,1024]{1,0:T(8,128)}, bf16[512,2048]{1,0:T(8,128)(2,1)}) custom-call(f32[2]{0:T(128)} %negate_log-plus-one_fusion.refs_1_.refs_0_, bf16[1024,512]{1,0:T(8,128)(2,1)} %get-tuple-element.68.refs_1_.refs_2_, ...), custom_call_target="tpu_custom_call", output_to_operand_aliasing={{0}: (7, {}), {1}: (8, {})} | custom-call | flops 4026531840 | bytes 10485760 | tf_op jit(solution)/shard_map/fwd/pallas_call | solution.py:452
  212.1 6.2 collective-permute-start.26
  236.2 22.6 %collective-permute-done.16 = bf16[512,512]{1,0:T(8,128)(2,1)} collective-permute-done((bf16[512,512]{1,0:T(8,128)(2,1)}, bf16[512,512]{1,0:T(8,128)(2,1)}, u32[]{:S(2)}, u32[]{:S(2)}) %collective-permute-start.16) | collective-permute-done | bytes 524320 | tf_op jit(solution)/shard_map/ppermute | solution.py:96
  270.1 5.3 collective-permute-done.20.refs_4_
  276.8 5.6 collective-permute-done.17
  285.4 20.6 %collective-permute-done.29.refs_14_ = bf16[1024,512]{1,0:T(8,128)(2,1)S(1)} collective-permute-done((bf16[1024,512]{1,0:T(8,128)(2,1)}, bf16[1024,512]{1,0:T(8,128)(2,1)S(1)}, u32[]{:S(2)}, u32[]{:S(2)}) %collective-permute-start.29) | collective-permute-done | bytes 1048608 | tf_op jit(solution)/shard_map/ppermute | solution.py:58
  312.3 16.2 %collective-permute-done.23.refs_9_ = bf16[512,512]{1,0:T(8,128)(2,1)S(1)} collective-permute-done((bf16[512,512]{1,0:T(8,128)(2,1)S(1)}, bf16[512,512]{1,0:T(8,128)(2,1)S(1)}, u32[]{:S(2)}, u32[]{:S(2)}) %collective-permute-start.23) | collective-permute-done | bytes 524320 | tf_op jit(solution)/shard_map/ppermute | solution.py:58
  332.0 30.3 %collective-permute-done.24.refs_7_ = bf16[512,512]{1,0:T(8,128)(2,1)S(1)} collective-permute-done((bf16[512,512]{1,0:T(8,128)(2,1)S(1)}, bf16[512,512]{1,0:T(8,128)(2,1)S(1)}, u32[]{:S(2)}, u32[]{:S(2)}) %collective-permute-start.24) | collective-permute-done | bytes 524320 | tf_op jit(solution)/shard_map/ppermute | solution.py:58
  365.1 8.5 collective-permute-done.34.refs_5_.refs_8_
  373.6 20.6 %mlp.2 = (bf16[1024,2048]{1,0:T(8,128)(2,1)}, bf16[1024,1024]{1,0:T(8,128)(2,1)}, bf16[1024,2048]{1,0:T(8,128)(2,1)}, bf16[1024,2048]{1,0:T(8,128)(2,1)}, f32[51...) custom-call(s32[1]{0:T(128)} %bitcast.refs_0_, f32[1,2048]{1,0:T(1,128)} %get-tuple-element.175.refs_1_, ...), custom_call_target="tpu_custom_call" | custom-call | flops 10737418240 | bytes 27262976 | tf_op jit(solution)/shard_map/mlp/pallas_call | solution.py:351
  394.2 20.9 %mlp.3 = (bf16[1024,2048]{1,0:T(8,128)(2,1)}, bf16[1024,1024]{1,0:T(8,128)(2,1)}, bf16[1024,2048]{1,0:T(8,128)(2,1)}, bf16[1024,2048]{1,0:T(8,128)(2,1)}, f32[51...) custom-call(s32[1]{0:T(128)} %bitcast.refs_0_, ...), custom_call_target="tpu_custom_call", output_to_operand_aliasing={{0}: (17, {}), {1}: (18, {}), {2}: (19, {}), {3}: (20, {})} | custom-call | flops 10737418240 | bytes 27262976 | tf_op jit(solution)/shard_map/mlp/pallas_call | solution.py:351
  415.1 9.6 %convolution_convert_fusion.4 = bf16[2048,1024]{1,0:T(8,128)(2,1)} fusion(bf16[1024,2048]{1,0:T(8,128)(2,1)} %get-tuple-element.99, bf16[1024,1024]{1,0:T(8,128)(2,1)} %get-tuple-element.86), kind=kOutput, calls=%fused_computation.13 | convolution fusion | flops 4297064448 | bytes 10485760 | tf_op jit(solution)/shard_map/dot_general | solution.py:25
  424.8 14.0 %convolution_convert_fusion.1 = bf16[2048,2048]{1,0:T(8,128)(2,1)} fusion(bf16[1024,2048]{1,0:T(8,128)(2,1)} %get-tuple-element.100, bf16[1024,2048]{1,0:T(8,128)(2,1)} %get-tuple-element.101), kind=kOutput, calls=%fused_computation.6 | convolution fusion | flops 8594128896 | bytes 16777216 | tf_op jit(solution)/shard_map/dot_general | solution.py:25
  441.8 10.6 %collective-permute-done.35 = bf16[512,512]{1,0:T(8,128)(2,1)S(1)} collective-permute-done((bf16[512,512]{1,0:T(8,128)(2,1)S(1)}, bf16[512,512]{1,0:T(8,128)(2,1)S(1)}, u32[]{:S(2)}, u32[]{:S(2)}) %collective-permute-start.35) | collective-permute-done | bytes 524320 | tf_op jit(solution)/shard_map/ppermute | solution.py:88
  459.3 10.2 %collective-permute-done.36 = bf16[512,512]{1,0:T(8,128)(2,1)} collective-permute-done((bf16[512,512]{1,0:T(8,128)(2,1)S(1)}, bf16[512,512]{1,0:T(8,128)(2,1)}, u32[]{:S(2)}, u32[]{:S(2)}) %collective-permute-start.36) | collective-permute-done | bytes 524320 | tf_op jit(solution)/shard_map/ppermute | solution.py:96
  471.3 5.3 collective-permute-start.38
  476.9 10.3 %collective-permute-done.38 = bf16[512,512]{1,0:T(8,128)(2,1)} collective-permute-done((bf16[512,512]{1,0:T(8,128)(2,1)}, bf16[512,512]{1,0:T(8,128)(2,1)}, u32[]{:S(2)}, u32[]{:S(2)}) %collective-permute-start.38) | collective-permute-done | bytes 524320 | tf_op jit(solution)/shard_map/ppermute | solution.py:88
  508.8 8.9 collective-permute-done.46
  529.6 5.4 collective-permute-start.47
  535.2 7.5 collective-permute-done.49
  548.3 6.8 collective-permute-start.50
  555.1 6.1 collective-permute-done.59.refs_12_
  563.2 9.2 %collective-permute-done.52.refs_12_ = bf16[512,512]{1,0:T(8,128)(2,1)S(1)} collective-permute-done((bf16[512,512]{1,0:T(8,128)(2,1)S(1)}, bf16[512,512]{1,0:T(8,128)(2,1)S(1)}, u32[]{:S(2)}, u32[]{:S(2)}) %collective-permute-start.52) | collective-permute-done | bytes 524320 | tf_op jit(solution)/shard_map/ppermute | solution.py:58
  574.4 5.7 collective-permute-done.60.refs_10_
  591.5 11.0 %gate.2 = (bf16[1024,1024]{1,0:T(8,128)(2,1)}, bf16[1024,1024]{1,0:T(8,128)(2,1)}, bf16[1024,2048]{1,0:T(8,128)(2,1)}, f32[2,256,512]{2,1,0:T(8,128)}, f32[2,512,1]{2,1,0:T(8,128)}) custom-call(s32[1]{0:T(128)} %bitcast.refs_0_, f32[2]{0:T(128)} %negate_log-plus-one_fusion.refs_1_.refs_0_, bf16[1024,512]{1,0:T(8,128)(2,1)} %get-tuple-element.68.refs_1_.refs_2_, ...), custom_call_target="tpu_custom_call" | custom-call | flops 2415919104 | bytes 8388608 | tf_op jit(solution)/shard_map/gate/pallas_call | solution.py:521
  602.4 10.8 %gate.3 = (bf16[1024,1024]{1,0:T(8,128)(2,1)}, bf16[1024,1024]{1,0:T(8,128)(2,1)}, bf16[1024,2048]{1,0:T(8,128)(2,1)}, f32[2,256,512]{2,1,0:T(8,128)}, f32[2,512,1]{2,1,0:T(8,128)}) custom-call(s32[1]{0:T(128)} %bitcast.refs_0_, f32[2]{0:T(128)} %negate_log-plus-one_fusion.refs_1_.refs_0_, ...), custom_call_target="tpu_custom_call", output_to_operand_aliasing={{0}: (13, {}), {1}: (14, {}), {2}: (15, {})} | custom-call | flops 2415919104 | bytes 8388608 | tf_op jit(solution)/shard_map/gate/pallas_call | solution.py:521
  618.7 9.5 %convolution_convert_fusion.3 = bf16[2048,1024]{1,0:T(8,128)(2,1)} fusion(bf16[1024,2048]{1,0:T(8,128)(2,1)} %get-tuple-element.73.x_ref, bf16[1024,1024]{1,0:T(8,128)(2,1)} %get-tuple-element.109.refs_9_), kind=kOutput, calls=%fused_computation.12 | convolution fusion | flops 4297064448 | bytes 10485760 | tf_op jit(solution)/shard_map/dot_general | solution.py:25
  628.3 6.4 convolution_convert_fusion.2
  634.7 7.8 pad_maximum_fusion
  646.8 12.5 %collective-permute-done.63 = bf16[2,256,512]{2,1,0:T(8,128)(2,1)} collective-permute-done((bf16[2,256,512]{2,1,0:T(8,128)(2,1)}, bf16[2,256,512]{2,1,0:T(8,128)(2,1)}, u32[]{:S(2)}, u32[]{:S(2)}) %collective-permute-start.63) | collective-permute-done | bytes 524320 | tf_op jit(solution)/shard_map/ppermute | solution.py:150
  661.7 20.8 %bwd.1 = (bf16[1024,3072]{1,0:T(8,128)(2,1)}, f32[2,1024,1]{2,1,0:T(8,128)}) custom-call(f32[2]{0:T(128)} %negate_log-plus-one_fusion.refs_1_.refs_0_, bf16[1024,512]{1,0:T(8,128)(2,1)} %get-tuple-element.68.refs_1_.refs_2_, bf16[1024,512]{1,0:T(8,128)(2,1)} %get-tuple-element.69.refs_2_, bf16[1024,1024]{1,0:T(8,128)(2,1)} %get-tuple-element.70.refs_3_, ...), custom_call_target="tpu_custom_call" | custom-call | flops 7247757312 | bytes 12582912 | tf_op jit(solution)/shard_map/bwd/pallas_call | solution.py:627
  682.5 11.9 %fusion.12 = bf16[512,2048]{1,0:T(8,128)(2,1)} fusion(bf16[2048,4096]{1,0:T(8,128)(2,1)} %all-gather.3.cloned.1.call-done.refs_3_.w_ref.refs_6_, bf16[1024,3072]{1,0:T(8,128)(2,1)} %get-tuple-element.120), kind=kOutput, calls=%fused_computation.16 | convolution fusion | flops 6443499520 | bytes 17825792 | tf_op jit(solution)/shard_map/dot_general | solution.py:29
  694.5 11.6 %convolution_convert_fusion = bf16[2048,2048]{1,0:T(8,128)(2,1)} fusion(bf16[1024,2048]{1,0:T(8,128)(2,1)S(1)} %copy-done.12, bf16[1024,3072]{1,0:T(8,128)(2,1)S(1)} %copy-done.50), kind=kOutput, calls=%fused_computation.5 | convolution fusion | flops 8594128896 | bytes 16777216 | tf_op jit(solution)/shard_map/dot_general | solution.py:25
  710.6 10.8 %fusion.17 = bf16[512,2048]{1,0:T(8,128)(2,1)S(1)} fusion(bf16[2048,4096]{1,0:T(8,128)(2,1)} %all-gather.3.cloned.1.call-done.refs_3_.w_ref.refs_6_, bf16[1024,3072]{1,0:T(8,128)(2,1)} %get-tuple-element.120), kind=kOutput, calls=%fused_computation.17 | convolution fusion | flops 6443499520 | bytes 17825792 | tf_op jit(solution)/shard_map/dot_general | solution.py:29
  746.6 7.6 fusion.7
  781.2 22.0 %collective-permute-done.75 = bf16[512,512]{1,0:T(8,128)(2,1)S(1)} collective-permute-done((bf16[512,512]{1,0:T(8,128)(2,1)S(1)}, bf16[512,512]{1,0:T(8,128)(2,1)S(1)}, u32[]{:S(2)}, u32[]{:S(2)}) %collective-permute-start.75) | collective-permute-done | bytes 524320 | tf_op jit(solution)/shard_map/ppermute | solution.py:97
  819.4 16.3 %collective-permute-done.57 = bf16[1024,512]{1,0:T(8,128)(2,1)S(1)} collective-permute-done((bf16[1024,512]{1,0:T(8,128)(2,1)S(1)}, bf16[1024,512]{1,0:T(8,128)(2,1)S(1)}, u32[]{:S(2)}, u32[]{:S(2)}) %collective-permute-start.57) | collective-permute-done | bytes 1048608 | tf_op jit(solution)/shard_map/ppermute | solution.py:112
  835.8 45.1 %collective-permute-done.56 = bf16[1024,512]{1,0:T(8,128)(2,1)S(1)} collective-permute-done((bf16[1024,512]{1,0:T(8,128)(2,1)S(1)}, bf16[1024,512]{1,0:T(8,128)(2,1)S(1)}, u32[]{:S(2)}, u32[]{:S(2)}) %collective-permute-start.56) | collective-permute-done | bytes 1048608 | tf_op jit(solution)/shard_map/ppermute | solution.py:112
  (338 shorter events, 276.2 us)
Async XLA Ops:
  7.2 96.6 %all-gather.3.cloned.1.call-start = ((), (), s32[]{:S(2)}) async-start(), calls=%async_computation.4 | async-start | bytes 18874368 | tf_op jit(solution)/shard_map/all_gather | solution.py:688
  11.2 362.4 %all-gather.5.cloned.1.call-start = ((), (), s32[]{:S(2)}) async-start(), calls=%async_computation.5 | async-start | bytes 14155776 | tf_op jit(solution)/shard_map/all_gather | solution.py:710
  11.3 21.1 %collective-permute-start.1 = (f32[2,512]{1,0:T(2,128)S(1)}, f32[2,512]{1,0:T(2,128)S(1)}, u32[]{:S(2)}, u32[]{:S(2)}) collective-permute-start(f32[2,512]{1,0:T(2,128)S(1)} %get-tuple-element.183), channel_id=1, source_target_pairs={{0,2},{1,3},{2,0},{3,1},{4,6},{5,7},{6,4},{7,5},{8,10},{9,11},{10,... | collective-permute-start | bytes 12296 | tf_op jit(solution)/shard_map/ppermute | solution.py:118
  19.3 23.3 %collective-permute-start.3 = (bf16[1024,512]{1,0:T(8,128)(2,1)S(1)}, bf16[1024,512]{1,0:T(8,128)(2,1)S(1)}, u32[]{:S(2)}, u32[]{:S(2)}) collective-permute-start(bf16[1024,512]{1,0:T(8,128)(2,1)S(1)} %copy-done.25), channel_id=1, source_target_pairs={{0,1},{1,2},{2,3},{4,5},{5,6},{6,7},{8,9},{9,10},{10,11},{12,13},{... | collective-permute-start | bytes 3145736 | tf_op jit(solution)/shard_map/ppermute | solution.py:57
  21.0 25.8 %collective-permute-start.5 = (bf16[1024,512]{1,0:T(8,128)(2,1)S(1)}, bf16[1024,512]{1,0:T(8,128)(2,1)}, u32[]{:S(2)}, u32[]{:S(2)}) collective-permute-start(bf16[1024,512]{1,0:T(8,128)(2,1)S(1)} %copy-done.25), channel_id=1, source_target_pairs={{3,2},{2,1},{1,0},{7,6},{6,5},{5,4},{11,10},{10,9},{9,8},{15,14},{... | collective-permute-start | bytes 3145736 | tf_op jit(solution)/shard_map/ppermute | solution.py:58
  46.8 25.0 %collective-permute-start.6 = (bf16[1024,512]{1,0:T(8,128)(2,1)}, bf16[1024,512]{1,0:T(8,128)(2,1)S(1)}, u32[]{:S(2)}, u32[]{:S(2)}) collective-permute-start(bf16[1024,512]{1,0:T(8,128)(2,1)} %collective-permute-done.5.refs_12_), channel_id=1, source_target_pairs={{2,1},{1,0},{6,5},{5,4},{10,9},{9,8},{14,13},{13,12},{18,17},{17,1... | collective-permute-start | bytes 3145736 | tf_op jit(solution)/shard_map/ppermute | solution.py:58
  48.1 23.7 %collective-permute-start.4 = (bf16[1024,512]{1,0:T(8,128)(2,1)S(1)}, bf16[1024,512]{1,0:T(8,128)(2,1)S(1)}, u32[]{:S(2)}, u32[]{:S(2)}) collective-permute-start(bf16[1024,512]{1,0:T(8,128)(2,1)S(1)} %collective-permute-done.3.refs_7_), channel_id=1, source_target_pairs={{1,2},{2,3},{5,6},{6,7},{9,10},{10,11},{13,14},{14,15},{17,18},{18... | collective-permute-start | bytes 3145736 | tf_op jit(solution)/shard_map/ppermute | solution.py:57
  71.9 24.2 %collective-permute-start.7 = (bf16[1024,512]{1,0:T(8,128)(2,1)S(1)}, bf16[1024,512]{1,0:T(8,128)(2,1)}, u32[]{:S(2)}, u32[]{:S(2)}) collective-permute-start(bf16[1024,512]{1,0:T(8,128)(2,1)S(1)} %broadcast_select_fusion.1), channel_id=1, source_target_pairs={{2,3},{1,0},{6,7},{5,4},{10,11},{9,8},{14,15},{13,12},{18,19},{17,... | collective-permute-start | bytes 3145736 | tf_op jit(solution)/shard_map/ppermute | solution.py:53
  146.1 736.7 %reduce-scatter.11.cloned.1.call-start = ((), (), s32[]{:S(2)}) async-start(), calls=%async_computation.9 | async-start | bytes 4718592 | tf_op jit(solution)/shard_map/reduce_scatter | solution.py:820
  207.4 21.1 %collective-permute-start.12 = (bf16[512,512]{1,0:T(8,128)(2,1)S(1)}, bf16[512,512]{1,0:T(8,128)(2,1)}, u32[]{:S(2)}, u32[]{:S(2)}) collective-permute-start(bf16[512,512]{1,0:T(8,128)(2,1)S(1)} %get-tuple-element.167), channel_id=1, source_target_pairs={{0,1},{1,2},{2,3},{4,5},{5,6},{6,7},{8,9},{9,10},{10,11},{12,13},{... | collective-permute-start | bytes 1572872 | tf_op jit(solution)/shard_map/ppermute | solution.py:96
  209.5 22.0 %collective-permute-start.14 = (bf16[512,512]{1,0:T(8,128)(2,1)}, bf16[512,512]{1,0:T(8,128)(2,1)}, u32[]{:S(2)}, u32[]{:S(2)}) collective-permute-start(bf16[512,512]{1,0:T(8,128)(2,1)} %get-tuple-element.168), channel_id=1, source_target_pairs={{3,2},{2,1},{1,0},{7,6},{6,5},{5,4},{11,10},{10,9},{9,8},{15,14},{... | collective-permute-start | bytes 1572872 | tf_op jit(solution)/shard_map/ppermute | solution.py:97
  210.8 56.0 %collective-permute-start.28 = (bf16[1024,512]{1,0:T(8,128)(2,1)S(1)}, bf16[1024,512]{1,0:T(8,128)(2,1)}, u32[]{:S(2)}, u32[]{:S(2)}) collective-permute-start(bf16[1024,512]{1,0:T(8,128)(2,1)S(1)} %copy-done.14), channel_id=1, source_target_pairs={{3,2},{2,1},{1,0},{7,6},{6,5},{5,4},{11,10},{10,9},{9,8},{15,14},{... | collective-permute-start | bytes 3145736 | tf_op jit(solution)/shard_map/ppermute | solution.py:58
  212.1 56.0 %collective-permute-start.26 = (bf16[1024,512]{1,0:T(8,128)(2,1)S(1)}, bf16[1024,512]{1,0:T(8,128)(2,1)}, u32[]{:S(2)}, u32[]{:S(2)}) collective-permute-start(bf16[1024,512]{1,0:T(8,128)(2,1)S(1)} %copy-done.14), channel_id=1, source_target_pairs={{0,1},{1,2},{2,3},{4,5},{5,6},{6,7},{8,9},{9,10},{10,11},{12,13},{... | collective-permute-start | bytes 3145736 | tf_op jit(solution)/shard_map/ppermute | solution.py:57
  219.6 39.2 %collective-permute-start.16 = (bf16[512,512]{1,0:T(8,128)(2,1)}, bf16[512,512]{1,0:T(8,128)(2,1)}, u32[]{:S(2)}, u32[]{:S(2)}) collective-permute-start(bf16[512,512]{1,0:T(8,128)(2,1)} %get-tuple-element.151), channel_id=1, source_target_pairs={{0,1},{1,2},{4,5},{5,6},{8,9},{9,10},{12,13},{13,14},{16,17},{17,1... | collective-permute-start | bytes 1572872 | tf_op jit(solution)/shard_map/ppermute | solution.py:96
  228.5 34.7 %collective-permute-start.18 = (bf16[512,512]{1,0:T(8,128)(2,1)}, bf16[512,512]{1,0:T(8,128)(2,1)}, u32[]{:S(2)}, u32[]{:S(2)}) collective-permute-start(bf16[512,512]{1,0:T(8,128)(2,1)} %get-tuple-element.152), channel_id=1, source_target_pairs={{3,2},{2,1},{7,6},{6,5},{11,10},{10,9},{15,14},{14,13},{19,18},{18... | collective-permute-start | bytes 1572872 | tf_op jit(solution)/shard_map/ppermute | solution.py:97
  234.9 34.5 %collective-permute-start.32 = (bf16[512,512]{1,0:T(8,128)(2,1)S(1)}, bf16[512,512]{1,0:T(8,128)(2,1)S(1)}, u32[]{:S(2)}, u32[]{:S(2)}) collective-permute-start(bf16[512,512]{1,0:T(8,128)(2,1)S(1)} %get-tuple-element.136.refs_3_), channel_id=1, source_target_pairs={{3,2},{2,1},{1,0},{7,6},{6,5},{5,4},{11,10},{10,9},{9,8},{15,14},{... | collective-permute-start | bytes 1572872 | tf_op jit(solution)/shard_map/ppermute | solution.py:58
  268.1 38.0 %collective-permute-start.29 = (bf16[1024,512]{1,0:T(8,128)(2,1)}, bf16[1024,512]{1,0:T(8,128)(2,1)S(1)}, u32[]{:S(2)}, u32[]{:S(2)}) collective-permute-start(bf16[1024,512]{1,0:T(8,128)(2,1)} %collective-permute-done.28.refs_16_), channel_id=1, source_target_pairs={{2,1},{1,0},{6,5},{5,4},{10,9},{9,8},{14,13},{13,12},{18,17},{17,1... | collective-permute-start | bytes 3145736 | tf_op jit(solution)/shard_map/ppermute | solution.py:58
  269.4 40.6 %collective-permute-start.27 = (bf16[1024,512]{1,0:T(8,128)(2,1)}, bf16[1024,512]{1,0:T(8,128)(2,1)S(1)}, u32[]{:S(2)}, u32[]{:S(2)}) collective-permute-start(bf16[1024,512]{1,0:T(8,128)(2,1)} %collective-permute-done.26.refs_11_), channel_id=1, source_target_pairs={{1,2},{2,3},{5,6},{6,7},{9,10},{10,11},{13,14},{14,15},{17,18},{18... | collective-permute-start | bytes 3145736 | tf_op jit(solution)/shard_map/ppermute | solution.py:57
  275.5 55.1 %collective-permute-start.33 = (bf16[512,512]{1,0:T(8,128)(2,1)S(1)}, bf16[512,512]{1,0:T(8,128)(2,1)S(1)}, u32[]{:S(2)}, u32[]{:S(2)}) collective-permute-start(bf16[512,512]{1,0:T(8,128)(2,1)S(1)} %collective-permute-done.32.refs_9_), channel_id=1, source_target_pairs={{2,1},{1,0},{6,5},{5,4},{10,9},{9,8},{14,13},{13,12},{18,17},{17,1... | collective-permute-start | bytes 1572872 | tf_op jit(solution)/shard_map/ppermute | solution.py:58
  282.4 48.2 %collective-permute-start.31 = (bf16[512,512]{1,0:T(8,128)(2,1)S(1)}, bf16[512,512]{1,0:T(8,128)(2,1)S(1)}, u32[]{:S(2)}, u32[]{:S(2)}) collective-permute-start(bf16[512,512]{1,0:T(8,128)(2,1)S(1)} %collective-permute-done.20.refs_4_), channel_id=1, source_target_pairs={{1,2},{2,3},{5,6},{6,7},{9,10},{10,11},{13,14},{14,15},{17,18},{18... | collective-permute-start | bytes 1572872 | tf_op jit(solution)/shard_map/ppermute | solution.py:57
  284.1 44.4 %collective-permute-start.23 = (bf16[512,512]{1,0:T(8,128)(2,1)S(1)}, bf16[512,512]{1,0:T(8,128)(2,1)S(1)}, u32[]{:S(2)}, u32[]{:S(2)}) collective-permute-start(bf16[512,512]{1,0:T(8,128)(2,1)S(1)} %get-tuple-element.134.refs_3_), channel_id=1, source_target_pairs={{3,2},{2,1},{1,0},{7,6},{6,5},{5,4},{11,10},{10,9},{9,8},{15,14},{... | collective-permute-start | bytes 1572872 | tf_op jit(solution)/shard_map/ppermute | solution.py:58
  306.1 23.8 %collective-permute-start.21 = (bf16[512,512]{1,0:T(8,128)(2,1)S(1)}, bf16[512,512]{1,0:T(8,128)(2,1)S(1)}, u32[]{:S(2)}, u32[]{:S(2)}) collective-permute-start(bf16[512,512]{1,0:T(8,128)(2,1)S(1)} %get-tuple-element.134.refs_3_), channel_id=1, source_target_pairs={{0,1},{1,2},{2,3},{4,5},{5,6},{6,7},{8,9},{9,10},{10,11},{12,13},{... | collective-permute-start | bytes 1572872 | tf_op jit(solution)/shard_map/ppermute | solution.py:57
  311.0 53.1 %collective-permute-start.30 = (bf16[1024,512]{1,0:T(8,128)(2,1)S(1)}, bf16[1024,512]{1,0:T(8,128)(2,1)S(1)}, u32[]{:S(2)}, u32[]{:S(2)}) collective-permute-start(bf16[1024,512]{1,0:T(8,128)(2,1)S(1)} %broadcast_select_fusion), channel_id=1, source_target_pairs={{2,3},{1,0},{6,7},{5,4},{10,11},{9,8},{14,15},{13,12},{18,19},{17,... | collective-permute-start | bytes 3145736 | tf_op jit(solution)/shard_map/ppermute | solution.py:53
  328.5 33.7 %collective-permute-start.24 = (bf16[512,512]{1,0:T(8,128)(2,1)S(1)}, bf16[512,512]{1,0:T(8,128)(2,1)S(1)}, u32[]{:S(2)}, u32[]{:S(2)}) collective-permute-start(bf16[512,512]{1,0:T(8,128)(2,1)S(1)} %collective-permute-done.23.refs_9_), channel_id=1, source_target_pairs={{2,1},{1,0},{6,5},{5,4},{10,9},{9,8},{14,13},{13,12},{18,17},{17,1... | collective-permute-start | bytes 1572872 | tf_op jit(solution)/shard_map/ppermute | solution.py:58
  329.8 32.4 %collective-permute-start.22 = (bf16[512,512]{1,0:T(8,128)(2,1)S(1)}, bf16[512,512]{1,0:T(8,128)(2,1)S(1)}, u32[]{:S(2)}, u32[]{:S(2)}) collective-permute-start(bf16[512,512]{1,0:T(8,128)(2,1)S(1)} %collective-permute-done.21.refs_4_), channel_id=1, source_target_pairs={{1,2},{2,3},{5,6},{6,7},{9,10},{10,11},{13,14},{14,15},{17,18},{18... | collective-permute-start | bytes 1572872 | tf_op jit(solution)/shard_map/ppermute | solution.py:57
  330.7 42.9 %collective-permute-start.34 = (bf16[512,512]{1,0:T(8,128)(2,1)S(1)}, bf16[512,512]{1,0:T(8,128)(2,1)}, u32[]{:S(2)}, u32[]{:S(2)}) collective-permute-start(bf16[512,512]{1,0:T(8,128)(2,1)S(1)} %broadcast_select_fusion.5), channel_id=1, source_target_pairs={{2,3},{1,0},{6,7},{5,4},{10,11},{9,8},{14,15},{13,12},{18,19},{17,... | collective-permute-start | bytes 1572872 | tf_op jit(solution)/shard_map/ppermute | solution.py:53
  362.3 31.9 %collective-permute-start.25 = (bf16[512,512]{1,0:T(8,128)(2,1)S(1)}, bf16[512,512]{1,0:T(8,128)(2,1)}, u32[]{:S(2)}, u32[]{:S(2)}) collective-permute-start(bf16[512,512]{1,0:T(8,128)(2,1)S(1)} %broadcast_select_fusion.6), channel_id=1, source_target_pairs={{2,3},{1,0},{6,7},{5,4},{10,11},{9,8},{14,15},{13,12},{18,19},{17,... | collective-permute-start | bytes 1572872 | tf_op jit(solution)/shard_map/ppermute | solution.py:53
  424.7 464.4 %reduce-scatter.9.cloned.1.call-start = ((), (), s32[]{:S(2)}) async-start(), calls=%async_computation.8 | async-start | bytes 9437184 | tf_op jit(solution)/shard_map/reduce_scatter | solution.py:820
  438.9 453.1 %reduce-scatter.7.cloned.1.call-start = ((), (), s32[]{:S(2)}) async-start(), calls=%async_computation.7 | async-start | bytes 9437184 | tf_op jit(solution)/shard_map/reduce_scatter | solution.py:820
  476.8 26.1 %collective-permute-start.45 = (f32[4,128]{1,0:T(4,128)S(1)}, f32[4,128]{1,0:T(4,128)S(1)}, u32[]{:S(2)}, u32[]{:S(2)}) collective-permute-start(f32[4,128]{1,0:T(4,128)S(1)} %bitcast.54), channel_id=1, source_target_pairs={{0,1},{1,0},{2,3},{3,2},{4,5},{5,4},{6,7},{7,6},{8,9},{9,8},{10,11... | collective-permute-start | bytes 6152 | tf_op jit(solution)/shard_map/ppermute | solution.py:126
  490.1 29.3 %collective-permute-start.39 = (bf16[512,512]{1,0:T(8,128)(2,1)}, bf16[512,512]{1,0:T(8,128)(2,1)}, u32[]{:S(2)}, u32[]{:S(2)}) collective-permute-start(bf16[512,512]{1,0:T(8,128)(2,1)} %get-tuple-element.147), channel_id=1, source_target_pairs={{0,1},{1,2},{4,5},{5,6},{8,9},{9,10},{12,13},{13,14},{16,17},{17,1... | collective-permute-start | bytes 1572872 | tf_op jit(solution)/shard_map/ppermute | solution.py:96
  495.3 24.1 %collective-permute-start.41 = (bf16[512,512]{1,0:T(8,128)(2,1)}, bf16[512,512]{1,0:T(8,128)(2,1)}, u32[]{:S(2)}, u32[]{:S(2)}) collective-permute-start(bf16[512,512]{1,0:T(8,128)(2,1)} %get-tuple-element.148), channel_id=1, source_target_pairs={{3,2},{2,1},{7,6},{6,5},{11,10},{10,9},{15,14},{14,13},{19,18},{18... | collective-permute-start | bytes 1572872 | tf_op jit(solution)/shard_map/ppermute | solution.py:97
  499.5 27.0 %collective-permute-start.43 = (bf16[512,512]{1,0:T(8,128)(2,1)}, bf16[512,512]{1,0:T(8,128)(2,1)}, u32[]{:S(2)}, u32[]{:S(2)}) collective-permute-start(bf16[512,512]{1,0:T(8,128)(2,1)} %get-tuple-element.163), channel_id=1, source_target_pairs={{0,1},{1,2},{2,3},{4,5},{5,6},{6,7},{8,9},{9,10},{10,11},{12,13},{... | collective-permute-start | bytes 1572872 | tf_op jit(solution)/shard_map/ppermute | solution.py:96
  501.6 25.0 %collective-permute-start.44 = (bf16[512,512]{1,0:T(8,128)(2,1)}, bf16[512,512]{1,0:T(8,128)(2,1)}, u32[]{:S(2)}, u32[]{:S(2)}) collective-permute-start(bf16[512,512]{1,0:T(8,128)(2,1)} %get-tuple-element.164), channel_id=1, source_target_pairs={{3,2},{2,1},{1,0},{7,6},{6,5},{5,4},{11,10},{10,9},{9,8},{15,14},{... | collective-permute-start | bytes 1572872 | tf_op jit(solution)/shard_map/ppermute | solution.py:97
  522.2 21.8 %collective-permute-start.40 = (bf16[512,512]{1,0:T(8,128)(2,1)}, bf16[512,512]{1,0:T(8,128)(2,1)}, u32[]{:S(2)}, u32[]{:S(2)}) collective-permute-start(bf16[512,512]{1,0:T(8,128)(2,1)} %get-tuple-element.165), channel_id=1, source_target_pairs={{0,1},{1,2},{2,3},{4,5},{5,6},{6,7},{8,9},{9,10},{10,11},{12,13},{... | collective-permute-start | bytes 1572872 | tf_op jit(solution)/shard_map/ppermute | solution.py:96
  547.0 25.4 %collective-permute-start.52 = (bf16[512,512]{1,0:T(8,128)(2,1)S(1)}, bf16[512,512]{1,0:T(8,128)(2,1)S(1)}, u32[]{:S(2)}, u32[]{:S(2)}) collective-permute-start(bf16[512,512]{1,0:T(8,128)(2,1)S(1)} %fusion.32.refs_6_), channel_id=1, source_target_pairs={{3,2},{2,1},{1,0},{7,6},{6,5},{5,4},{11,10},{10,9},{9,8},{15,14},{... | collective-permute-start | bytes 1572872 | tf_op jit(solution)/shard_map/ppermute | solution.py:58
  548.3 25.4 %collective-permute-start.50 = (bf16[512,512]{1,0:T(8,128)(2,1)S(1)}, bf16[512,512]{1,0:T(8,128)(2,1)S(1)}, u32[]{:S(2)}, u32[]{:S(2)}) collective-permute-start(bf16[512,512]{1,0:T(8,128)(2,1)S(1)} %fusion.32.refs_6_), channel_id=1, source_target_pairs={{0,1},{1,2},{2,3},{4,5},{5,6},{6,7},{8,9},{9,10},{10,11},{12,13},{... | collective-permute-start | bytes 1572872 | tf_op jit(solution)/shard_map/ppermute | solution.py:57
  642.5 252.4 %reduce-scatter.5.cloned.1.call-start = ((), (), s32[]{:S(2)}) async-start(), calls=%async_computation.6 | async-start | bytes 9437184 | tf_op jit(solution)/shard_map/reduce_scatter | solution.py:820
  734.0 20.3 %collective-permute-start.69 = (f32[8,128]{1,0:T(8,128)S(1)}, f32[8,128]{1,0:T(8,128)S(1)}, u32[]{:S(2)}, u32[]{:S(2)}) collective-permute-start(f32[8,128]{1,0:T(8,128)S(1)} %maximum_add_fusion.1), channel_id=1, source_target_pairs={{0,1},{1,0},{2,3},{3,2},{4,5},{5,4},{6,7},{7,6},{8,9},{9,8},{10,11... | collective-permute-start | bytes 12296 | tf_op jit(solution)/shard_map/ppermute | solution.py:126
  734.1 36.1 %collective-permute-start.67 = (bf16[512,512]{1,0:T(8,128)(2,1)}, bf16[512,512]{1,0:T(8,128)(2,1)S(1)}, u32[]{:S(2)}, u32[]{:S(2)}) collective-permute-start(bf16[512,512]{1,0:T(8,128)(2,1)} %get-tuple-element.128), channel_id=1, source_target_pairs={{3,2},{2,1},{7,6},{6,5},{11,10},{10,9},{15,14},{14,13},{19,18},{18... | collective-permute-start | bytes 1572872 | tf_op jit(solution)/shard_map/ppermute | solution.py:97
  734.8 35.5 %collective-permute-start.65 = (bf16[512,512]{1,0:T(8,128)(2,1)}, bf16[512,512]{1,0:T(8,128)(2,1)S(1)}, u32[]{:S(2)}, u32[]{:S(2)}) collective-permute-start(bf16[512,512]{1,0:T(8,128)(2,1)} %get-tuple-element.145), channel_id=1, source_target_pairs={{0,1},{1,2},{4,5},{5,6},{8,9},{9,10},{12,13},{13,14},{16,17},{17,1... | collective-permute-start | bytes 1572872 | tf_op jit(solution)/shard_map/ppermute | solution.py:96
  765.3 37.9 %collective-permute-start.75 = (bf16[512,512]{1,0:T(8,128)(2,1)S(1)}, bf16[512,512]{1,0:T(8,128)(2,1)S(1)}, u32[]{:S(2)}, u32[]{:S(2)}) collective-permute-start(bf16[512,512]{1,0:T(8,128)(2,1)S(1)} %get-tuple-element.162), channel_id=1, source_target_pairs={{3,2},{2,1},{1,0},{7,6},{6,5},{5,4},{11,10},{10,9},{9,8},{15,14},{... | collective-permute-start | bytes 1572872 | tf_op jit(solution)/shard_map/ppermute | solution.py:97
  767.2 52.2 %collective-permute-start.55 = (bf16[1024,512]{1,0:T(8,128)(2,1)S(1)}, bf16[1024,512]{1,0:T(8,128)(2,1)S(1)}, u32[]{:S(2)}, u32[]{:S(2)}) collective-permute-start(bf16[1024,512]{1,0:T(8,128)(2,1)S(1)} %get-tuple-element.140), channel_id=1, source_target_pairs={{0,1},{1,2},{2,3},{3,0},{4,5},{5,6},{6,7},{7,4},{8,9},{9,10},{10,1... | collective-permute-start | bytes 3145736 | tf_op jit(solution)/shard_map/ppermute | solution.py:112
  770.7 40.5 %collective-permute-start.66 = (bf16[512,512]{1,0:T(8,128)(2,1)S(1)}, bf16[512,512]{1,0:T(8,128)(2,1)S(1)}, u32[]{:S(2)}, u32[]{:S(2)}) collective-permute-start(bf16[512,512]{1,0:T(8,128)(2,1)S(1)} %get-tuple-element.159), channel_id=1, source_target_pairs={{0,1},{1,2},{2,3},{4,5},{5,6},{6,7},{8,9},{9,10},{10,11},{12,13},{... | collective-permute-start | bytes 1572872 | tf_op jit(solution)/shard_map/ppermute | solution.py:96
  774.6 41.2 %collective-permute-start.68 = (bf16[512,512]{1,0:T(8,128)(2,1)S(1)}, bf16[512,512]{1,0:T(8,128)(2,1)S(1)}, u32[]{:S(2)}, u32[]{:S(2)}) collective-permute-start(bf16[512,512]{1,0:T(8,128)(2,1)S(1)} %get-tuple-element.160), channel_id=1, source_target_pairs={{3,2},{2,1},{1,0},{7,6},{6,5},{5,4},{11,10},{10,9},{9,8},{15,14},{... | collective-permute-start | bytes 1572872 | tf_op jit(solution)/shard_map/ppermute | solution.py:97
  777.5 58.3 %collective-permute-start.57 = (bf16[1024,512]{1,0:T(8,128)(2,1)S(1)}, bf16[1024,512]{1,0:T(8,128)(2,1)S(1)}, u32[]{:S(2)}, u32[]{:S(2)}) collective-permute-start(bf16[1024,512]{1,0:T(8,128)(2,1)S(1)} %get-tuple-element.141), channel_id=1, source_target_pairs={{0,3},{1,0},{2,1},{3,2},{4,7},{5,4},{6,5},{7,6},{8,11},{9,8},{10,9... | collective-permute-start | bytes 3145736 | tf_op jit(solution)/shard_map/ppermute | solution.py:112
  803.2 77.6 %collective-permute-start.56 = (bf16[1024,512]{1,0:T(8,128)(2,1)S(1)}, bf16[1024,512]{1,0:T(8,128)(2,1)S(1)}, u32[]{:S(2)}, u32[]{:S(2)}) collective-permute-start(bf16[1024,512]{1,0:T(8,128)(2,1)S(1)} %get-tuple-element.142), channel_id=1, source_target_pairs={{0,2},{1,3},{2,0},{3,1},{4,6},{5,7},{6,4},{7,5},{8,10},{9,11},{10,... | collective-permute-start | bytes 3145736 | tf_op jit(solution)/shard_map/ppermute | solution.py:112
  817.9 67.0 %collective-permute-start.77 = (f32[2,512]{1,0:T(2,128)S(1)}, f32[2,512]{1,0:T(2,128)S(1)}, u32[]{:S(2)}, u32[]{:S(2)}) collective-permute-start(f32[2,512]{1,0:T(2,128)S(1)} %fusion.31), channel_id=1, source_target_pairs={{0,8},{4,12},{8,0},{12,4},{1,9},{5,13},{9,1},{13,5},{2,10},{6,14},... | collective-permute-start | bytes 12296 | tf_op jit(solution)/shard_map/ppermute | solution.py:126
  (88 other events, 1852.4 us)
Sparse Core Ops, SparseCore 0:
  11.3 92.4 all-gather.2
  146.2 71.9 all-gather.4
  424.8 48.9 reduce-scatter.10
  477.1 71.5 reduce-scatter.8
  642.6 70.7 reduce-scatter.6
  716.7 71.4 reduce-scatter.4

commit v5 on v4

--- a/solution.py
+++ b/solution.py
@@ -684,8 +684,9 @@
 
     qk = heads * HK
     vw = heads * HV
-    attn_shard = side_by_side(w_query, w_key, w_value, w_retgate, w_out)
+    attn_shard = side_by_side(w_query, w_key, w_value, w_retgate)
     attn_full = lax.all_gather(attn_shard, data, axis=0, tiled=True)
+    out_full = lax.all_gather(w_out, data, axis=0, tiled=True)
 
     gains = small_gather(jnp.stack([gain_attn, gain_mlp]), TP)
 
@@ -710,13 +711,9 @@
     mlp_full = lax.all_gather(after(mlp_shard, state_in), data, axis=0, tiled=True)
     heads_out, branch = [], []
     for c in range(parts):
-        *heads_out, out = retention_forward(
-            c, parts, log_gamma, q, k, v, gate_pre, state_in, attn_full, 2 * qk + 2 * vw, heads_out
-        )
+        *heads_out, out = retention_forward(c, parts, log_gamma, q, k, v, gate_pre, state_in, out_full, 0, heads_out)
         branch.append(out)
     gated, retained = heads_out
-
-    devices = math.prod(lax.axis_size(axis) for axis in data)
 
     x_own = layer_input.astype(F32)
     middle, mid_pairs, scale_mlp, inner_mlp, back, grad_middle, grad_own, grad_pairs = ([] for _ in range(8))
@@ -778,8 +775,8 @@
             here,
             log_gamma,
             q,
-            attn_full,
-            2 * qk + 2 * vw,
+            out_full,
+            0,
             gate_pre,
             retained,
             grad_own[c],
@@ -792,19 +789,28 @@
     state_grad, got = states_after(partial_state, log_block, CTX)
     state_grad = state_grad.astype(BF16)
     grad_out = tn(after(grad_attn, got), gated).astype(BF16)
-    grad_retgate = tn(normed, after(g_gate, got)).astype(BF16)
-    grad_heads = jnp.concatenate([g.reshape(devices, -1, vw) for g in (grad_retgate, grad_out)], axis=1)
     grads_attn, inner = retention_backward(
-        log_gamma, q, k, v, state_in, after(state_grad, grad_heads), cosine, sine, g_ret, g_gate
+        log_gamma, q, k, v, state_in, after(state_grad, grad_out), cosine, sine, g_ret, g_gate
     )
     inner_attn = jnp.concatenate(inner_attn) + jnp.sum(inner[:, :, 0], axis=0)
-    in_full = attn_full[:, : 2 * qk + 2 * vw]
     back = []
     for c in range(parts):
-        rows_grads = after(grads_attn, *back, *([grad_qkv_w] if c else []))
-        back.append(nt(rows_grads[cuts[c]], in_full).astype(BF16))
+        rows_grads = after(grads_attn, *back, *([grad_in_w] if c else []))
+        back.append(nt(rows_grads[cuts[c]], attn_full).astype(BF16))
         if c == 0:
-            grad_qkv_w = tn(normed, after(grads_attn, *back)[:, : 2 * qk + vw]).astype(BF16)
+            grad_in_w = tn(normed, after(grads_attn, *back)).astype(BF16)
+
+    def shard(grad):
+        return lax.psum_scatter(grad, data, scatter_dimension=0, tiled=True).astype(F32)
+
+    s_down = shard(grad_down)
+    s_gate_up = shard(grad_gate_up)
+    s_gate, s_up = s_gate_up[:, :units], s_gate_up[:, units:]
+    s_out = shard(grad_out)
+    s_in = shard(grad_in_w)
+    inner_attn, s_down, s_gate, s_up, s_out, layer_output = lax.optimization_barrier(
+        (inner_attn, s_down, s_gate, s_up, s_out, layer_output)
+    )
     inner_attn = row_total(inner_attn)
     grad_input, gain_attn_sum = [], 0.0
     early = ()
@@ -816,27 +822,19 @@
         gain_attn_sum = gain_attn_sum + gain_sum
     grad_input = jnp.concatenate(grad_input)
 
-    def shard(grad):
-        return lax.psum_scatter(grad, data, scatter_dimension=0, tiled=True).astype(F32)
-
-    s_down = shard(grad_down)
-    s_gate_up = shard(grad_gate_up)
-    s_retgate, s_out = jnp.split(shard(grad_heads)[0], 2)
-    s_qkv = shard(grad_qkv_w)
-    s_query, s_key, s_value = s_qkv[:, :qk], s_qkv[:, qk : 2 * qk], s_qkv[:, 2 * qk :]
     gain_sums = swap_sum(swap_sum(jnp.stack([gain_attn_sum, gain_mlp_sum]), CTX), DP)
     return (
         layer_output,
         grad_input,
         gain_sums[0],
-        s_query,
-        s_key,
-        s_value,
-        s_retgate,
+        s_in[:, :qk],
+        s_in[:, qk : 2 * qk],
+        s_in[:, 2 * qk : 2 * qk + vw],
+        s_in[:, 2 * qk + vw :],
         s_out,
         gain_sums[1],
-        s_gate_up[:, :units],
-        s_gate_up[:, units:],
+        s_gate,
+        s_up,
         s_down,
     )
 

time: 916 us -> 829 us (0.905)
  waiting for transfers between devices: 396 us -> 310 us
    ppermute x3, waiting for transfers between devices: 61.4 us -> 0.01 us  [routed_scatter(): lax.ppermute(block(i + k), axis, [(j, (j + k) % n) for j in range(n)])]
    ppermute x6, waiting for transfers between devices: 31.5 us -> 91.7 us  [line_scatter(): from_left = from_right = lax.ppermute(data, axis, r_pairs + l_pairs)]
    ppermute x12, waiting for transfers between devices: 51.8 us -> 7.66 us  [line_scatter(): from_left = lax.ppermute(r_data, axis, r_pairs)]
    ppermute x12, waiting for transfers between devices: 120 us -> 92.5 us  [line_gather(): lefts.append(lax.ppermute(lefts[-1], axis, l_pairs))]
    ppermute x12, waiting for transfers between devices: 27.2 us -> 8.94 us  [line_scatter(): from_right = lax.ppermute(l_data, axis, l_pairs)]
    ppermute x12, starting transfers between devices: 46 us -> 62.6 us  [line_scatter(): from_left = lax.ppermute(r_data, axis, r_pairs)]
    ppermute x9, waiting for transfers between devices: 18.3 us -> 29.6 us  [swap_sum(): x = x + lax.ppermute(x, axis, [(j, j ^ g) for j in range(n)])]
    convert_element_type x9 -> x11, other arithmetic: 16.4 us -> 24 us  [line_scatter(): r_data = (r_data.astype(F32) + from_left.astype(F32)).astype(BF16)]
  transfers between devices with their start and end apart: 85 -> 86, of which waited for: 38 -> 33; matrix products, arithmetic and copies ran while one was open for 17% -> 20% of each run, Pallas kernels for 11% -> 17%
where the time goes in v5:
time: 829 us; the launch traced here: 820 us
  waiting for transfers between devices  310 us (37%)
  starting transfers between devices  180 us (22%)
  Pallas kernels  142 us (17%)
  matrix products  77.6 us (9%)
  other arithmetic  71.8 us (9%)
  local copies, waits for them, and re-layouts  22.4 us (3%)
  between operations  15.9 us (2%)
    ppermute x12, waiting for transfers between devices, line_gather(): lefts.append(lax.ppermute(lefts[-1], axis, l_pairs))  92.5 us
    ppermute x6, waiting for transfers between devices, line_scatter(): from_left = from_right = lax.ppermute(data, axis, r_pairs + l_pairs)  91.7 us
    ppermute x12, starting transfers between devices, line_scatter(): from_left = lax.ppermute(r_data, axis, r_pairs)  62.6 us
    dot_general x4, matrix products, tn(): lax.dot_general(a, b, (((0,), (0,)), ((), ())), preferred_element_type=F32)  45.5 us
    pallas_call x2, Pallas kernels, mlp(): pl.pallas_call(lambda *refs: mlp_kernel(units, len(blocks), *refs), grid=...  41.2 us
    ppermute x12, starting transfers between devices, line_gather(): rights.append(lax.ppermute(rights[-1], axis, r_pairs))  33.3 us
    dot_general x3, matrix products, nt(): lax.dot_general(a, b, (((1,), (1,)), ((), ())), preferred_element_type=F32)  32.1 us
    ppermute x6, waiting for transfers between devices, line_gather(): lax.ppermute(jnp.where(i >= k - 1, rights[-1], lefts[-1]), axis, r_pairs...  31.1 us
  transfers between devices with their start and end apart: 86, of which 33 were waited for; matrix products, arithmetic and copies ran while one was open for 20% of the time, Pallas kernels for 17%

profile of v5, /device:TPU:0, one launch (start us, length us, event | category | flops | bytes accessed | tf_op | source)
XLA Modules:
  0.0 820.3 jit_solution(6651185343369183695)
XLA Ops:
  23.3 5.5 fusion.16
  33.0 10.1 %collective-permute-done.3.refs_7_ = bf16[1024,512]{1,0:T(8,128)(2,1)S(1)} collective-permute-done((bf16[1024,512]{1,0:T(8,128)(2,1)S(1)}, bf16[1024,512]{1,0:T(8,128)(2,1)S(1)}, u32[]{:S(2)}, u32[]{:S(2)}) %collective-permute-start.3) | collective-permute-done | bytes 1048608 | tf_op jit(solution)/shard_map/ppermute | solution.py:57
  48.7 23.7 %collective-permute-done.6.refs_10_ = bf16[1024,512]{1,0:T(8,128)(2,1)S(1)} collective-permute-done((bf16[1024,512]{1,0:T(8,128)(2,1)}, bf16[1024,512]{1,0:T(8,128)(2,1)S(1)}, u32[]{:S(2)}, u32[]{:S(2)}) %collective-permute-start.6) | collective-permute-done | bytes 1048608 | tf_op jit(solution)/shard_map/ppermute | solution.py:58
  74.4 22.3 %collective-permute-done.7.refs_8_.refs_11_ = bf16[1024,512]{1,0:T(8,128)(2,1)} collective-permute-done((bf16[1024,512]{1,0:T(8,128)(2,1)S(1)}, bf16[1024,512]{1,0:T(8,128)(2,1)}, u32[]{:S(2)}, u32[]{:S(2)}) %collective-permute-start.7) | collective-permute-done | bytes 1048608 | tf_op jit(solution)/shard_map/ppermute | solution.py:53
  96.7 22.2 %proj.1 = (bf16[1024,2048]{1,0:T(8,128)(2,1)}, f32[1024,1]{1,0:T(8,128)}, bf16[1024,512]{1,0:T(8,128)(2,1)}, bf16[1024,512]{1,0:T(8,128)(2,1)}, bf16[1024,1024]{1,0:T(8,128)(2,1)}, /*index=5*/f32[2,256,512]{2,1,0:T(8,128)}) custom-call(s32[1]{0:T(128)} %bitcast.refs_0_, f32[2]{0:T(128)} %negate_log-plus-one_fusion.refs_1_.refs_0_, ...), custom_call_target="tpu_custom_call" | custom-call | flops 8589934592 | bytes 33554432 | tf_op jit(solution)/shard_map/proj/pallas_call | solution.py:257
  124.2 12.6 %collective-permute-done.9 = bf16[2,256,512]{2,1,0:T(8,128)(2,1)S(1)} collective-permute-done((bf16[2,256,512]{2,1,0:T(8,128)(2,1)S(1)}, bf16[2,256,512]{2,1,0:T(8,128)(2,1)S(1)}, u32[]{:S(2)}, u32[]{:S(2)}) %collective-permute-start.9) | collective-permute-done | bytes 524320 | tf_op jit(solution)/shard_map/ppermute | solution.py:135
  138.1 8.8 %prod.1.refs_4_ = f32[1024,1024]{1,0:T(8,128)} custom-call(bf16[1024,2048]{1,0:T(8,128)(2,1)} %get-tuple-element.76.x_ref, bf16[2048,3072]{1,0:T(8,128)(2,1)} %all-gather.4.cloned.1.call-done.refs_3_.w_ref), custom_call_target="tpu_custom_call" | custom-call | flops 4294967296 | bytes 12582912 | tf_op jit(solution)/shard_map/prod/pallas_call | solution.py:298
  147.0 9.2 %fwd.2 = (bf16[1024,1024]{1,0:T(8,128)(2,1)}, f32[1024,1024]{1,0:T(8,128)}, bf16[512,2048]{1,0:T(8,128)(2,1)}) custom-call(f32[2]{0:T(128)} %negate_log-plus-one_fusion.refs_1_.refs_0_, bf16[1024,512]{1,0:T(8,128)(2,1)} %get-tuple-element.73.refs_1_.refs_2_, bf16[1024,512]{1,0:T(8,128)(2,1)} %get-tuple-element.77.refs_2_, ...), custom_call_target="tpu_custom_call" | custom-call | flops 3221225472 | bytes 10485760 | tf_op jit(solution)/shard_map/fwd/pallas_call | solution.py:452
  159.5 10.5 %collective-permute-done.10 = bf16[512,512]{1,0:T(8,128)(2,1)S(1)} collective-permute-done((bf16[512,512]{1,0:T(8,128)(2,1)S(1)}, bf16[512,512]{1,0:T(8,128)(2,1)S(1)}, u32[]{:S(2)}, u32[]{:S(2)}) %collective-permute-start.10) | collective-permute-done | bytes 524320 | tf_op jit(solution)/shard_map/ppermute | solution.py:88
  172.7 5.2 collective-permute-start.11
  183.8 10.4 %fwd.3 = (bf16[1024,1024]{1,0:T(8,128)(2,1)}, f32[1024,1024]{1,0:T(8,128)}, bf16[512,2048]{1,0:T(8,128)(2,1)}) custom-call(f32[2]{0:T(128)} %negate_log-plus-one_fusion.refs_1_.refs_0_, bf16[1024,512]{1,0:T(8,128)(2,1)} %get-tuple-element.73.refs_1_.refs_2_, ...), custom_call_target="tpu_custom_call", output_to_operand_aliasing={{0}: (7, {}), {1}: (8, {})} | custom-call | flops 4026531840 | bytes 10485760 | tf_op jit(solution)/shard_map/fwd/pallas_call | solution.py:452
  195.5 4.6 collective-permute-start.32
  205.4 6.7 collective-permute-done.20.refs_11_
  215.0 8.3 %collective-permute-done.32 = bf16[512,512]{1,0:T(8,128)(2,1)S(1)} collective-permute-done((bf16[512,512]{1,0:T(8,128)(2,1)S(1)}, bf16[512,512]{1,0:T(8,128)(2,1)S(1)}, u32[]{:S(2)}, u32[]{:S(2)}) %collective-permute-start.32) | collective-permute-done | bytes 524320 | tf_op jit(solution)/shard_map/ppermute | solution.py:88
  224.6 5.2 collective-permute-start.33
  229.8 4.7 collective-permute-done.12
  248.8 15.8 %collective-permute-start.34 = (bf16[512,512]{1,0:T(8,128)(2,1)S(1)}, bf16[512,512]{1,0:T(8,128)(2,1)S(1)}, u32[]{:S(2)}, u32[]{:S(2)}) collective-permute-start(bf16[512,512]{1,0:T(8,128)(2,1)S(1)} %get-tuple-element.173), channel_id=1, source_target_pairs={{0,1},{1,2},{2,3},{4,5},{5,6},{6,7},{8,9},{9,10},{10,11},{12,13},{... | collective-permute-start | bytes 1572872 | tf_op jit(solution)/shard_map/ppermute | solution.py:96
  272.9 8.9 %collective-permute-done.36 = bf16[512,512]{1,0:T(8,128)(2,1)S(1)} collective-permute-done((bf16[512,512]{1,0:T(8,128)(2,1)S(1)}, bf16[512,512]{1,0:T(8,128)(2,1)S(1)}, u32[]{:S(2)}, u32[]{:S(2)}) %collective-permute-start.36) | collective-permute-done | bytes 524320 | tf_op jit(solution)/shard_map/ppermute | solution.py:97
  282.4 7.5 collective-permute-start.37
  291.2 24.3 %collective-permute-done.18.refs_7_ = bf16[512,512]{1,0:T(8,128)(2,1)S(1)} collective-permute-done((bf16[512,512]{1,0:T(8,128)(2,1)S(1)}, bf16[512,512]{1,0:T(8,128)(2,1)S(1)}, u32[]{:S(2)}, u32[]{:S(2)}) %collective-permute-start.18) | collective-permute-done | bytes 524320 | tf_op jit(solution)/shard_map/ppermute | solution.py:58
  318.6 8.3 %collective-permute-done.39.refs_9_ = bf16[512,512]{1,0:T(8,128)(2,1)} collective-permute-done((bf16[512,512]{1,0:T(8,128)(2,1)S(1)}, bf16[512,512]{1,0:T(8,128)(2,1)}, u32[]{:S(2)}, u32[]{:S(2)}) %collective-permute-start.39) | collective-permute-done | bytes 524320 | tf_op jit(solution)/shard_map/ppermute | solution.py:58
  329.2 8.8 %collective-permute-done.19.refs_5_.refs_8_ = bf16[512,512]{1,0:T(8,128)(2,1)S(1)} collective-permute-done((bf16[512,512]{1,0:T(8,128)(2,1)S(1)}, bf16[512,512]{1,0:T(8,128)(2,1)S(1)}, u32[]{:S(2)}, u32[]{:S(2)}) %collective-permute-start.19) | collective-permute-done | bytes 524320 | tf_op jit(solution)/shard_map/ppermute | solution.py:53
  338.8 20.7 %mlp.2 = (bf16[1024,2048]{1,0:T(8,128)(2,1)}, bf16[1024,1024]{1,0:T(8,128)(2,1)}, bf16[1024,2048]{1,0:T(8,128)(2,1)}, bf16[1024,2048]{1,0:T(8,128)(2,1)}, f32[51...) custom-call(s32[1]{0:T(128)} %bitcast.refs_0_, f32[1,2048]{1,0:T(1,128)} %get-tuple-element.185.refs_1_, ...), custom_call_target="tpu_custom_call" | custom-call | flops 10737418240 | bytes 27262976 | tf_op jit(solution)/shard_map/mlp/pallas_call | solution.py:351
  370.3 5.2 collective-permute-start.26
  378.2 20.6 %mlp.3 = (bf16[1024,2048]{1,0:T(8,128)(2,1)}, bf16[1024,1024]{1,0:T(8,128)(2,1)}, bf16[1024,2048]{1,0:T(8,128)(2,1)}, bf16[1024,2048]{1,0:T(8,128)(2,1)}, f32[51...) custom-call(s32[1]{0:T(128)} %bitcast.refs_0_, ...), custom_call_target="tpu_custom_call", output_to_operand_aliasing={{0}: (17, {}), {1}: (18, {}), {2}: (19, {}), {3}: (20, {})} | custom-call | flops 10737418240 | bytes 27262976 | tf_op jit(solution)/shard_map/mlp/pallas_call | solution.py:351
  403.6 6.0 collective-permute-done.30
  422.8 5.3 collective-permute-start.48
  429.8 8.5 %convolution_convert_fusion.3 = bf16[2048,1024]{1,0:T(8,128)(2,1)} fusion(bf16[1024,2048]{1,0:T(8,128)(2,1)} %get-tuple-element.96, bf16[1024,1024]{1,0:T(8,128)(2,1)S(1)} %copy-done.53), kind=kOutput, calls=%fused_computation.6 | convolution fusion | flops 4297064448 | bytes 10485760 | tf_op jit(solution)/shard_map/dot_general | solution.py:25
  450.9 5.3 collective-permute-start.42
  457.0 6.7 collective-permute-done.53
  480.4 9.2 %collective-permute-done.56.refs_12_ = bf16[512,512]{1,0:T(8,128)(2,1)S(1)} collective-permute-done((bf16[512,512]{1,0:T(8,128)(2,1)S(1)}, bf16[512,512]{1,0:T(8,128)(2,1)S(1)}, u32[]{:S(2)}, u32[]{:S(2)}) %collective-permute-start.56) | collective-permute-done | bytes 524320 | tf_op jit(solution)/shard_map/ppermute | solution.py:58
  490.9 9.9 %collective-permute-done.45.refs_10_ = bf16[512,512]{1,0:T(8,128)(2,1)S(1)} collective-permute-done((bf16[512,512]{1,0:T(8,128)(2,1)S(1)}, bf16[512,512]{1,0:T(8,128)(2,1)S(1)}, u32[]{:S(2)}, u32[]{:S(2)}) %collective-permute-start.45) | collective-permute-done | bytes 524320 | tf_op jit(solution)/shard_map/ppermute | solution.py:58
  503.0 9.0 %collective-permute-done.57.refs_10_ = bf16[512,512]{1,0:T(8,128)(2,1)S(1)} collective-permute-done((bf16[512,512]{1,0:T(8,128)(2,1)S(1)}, bf16[512,512]{1,0:T(8,128)(2,1)S(1)}, u32[]{:S(2)}, u32[]{:S(2)}) %collective-permute-start.57) | collective-permute-done | bytes 524320 | tf_op jit(solution)/shard_map/ppermute | solution.py:58
  514.4 11.5 %convolution_convert_fusion.1 = bf16[2048,2048]{1,0:T(8,128)(2,1)} fusion(bf16[1024,2048]{1,0:T(8,128)(2,1)S(1)} %copy-done.51, bf16[1024,2048]{1,0:T(8,128)(2,1)S(1)} %copy-done.52), kind=kOutput, calls=%fused_computation.1 | convolution fusion | flops 8594128896 | bytes 16777216 | tf_op jit(solution)/shard_map/dot_general | solution.py:25
  525.9 11.1 %gate.2 = (bf16[1024,1024]{1,0:T(8,128)(2,1)}, bf16[1024,1024]{1,0:T(8,128)(2,1)}, bf16[1024,2048]{1,0:T(8,128)(2,1)}, f32[2,256,512]{2,1,0:T(8,128)}, f32[2,512,1]{2,1,0:T(8,128)}) custom-call(s32[1]{0:T(128)} %bitcast.refs_0_, f32[2]{0:T(128)} %negate_log-plus-one_fusion.refs_1_.refs_0_, bf16[1024,512]{1,0:T(8,128)(2,1)} %get-tuple-element.73.refs_1_.refs_2_, ...), custom_call_target="tpu_custom_call" | custom-call | flops 2415919104 | bytes 8388608 | tf_op jit(solution)/shard_map/gate/pallas_call | solution.py:521
  537.0 10.8 %gate.3 = (bf16[1024,1024]{1,0:T(8,128)(2,1)}, bf16[1024,1024]{1,0:T(8,128)(2,1)}, bf16[1024,2048]{1,0:T(8,128)(2,1)}, f32[2,256,512]{2,1,0:T(8,128)}, f32[2,512,1]{2,1,0:T(8,128)}) custom-call(s32[1]{0:T(128)} %bitcast.refs_0_, f32[2]{0:T(128)} %negate_log-plus-one_fusion.refs_1_.refs_0_, ...), custom_call_target="tpu_custom_call", output_to_operand_aliasing={{0}: (13, {}), {1}: (14, {}), {2}: (15, {})} | custom-call | flops 2415919104 | bytes 8388608 | tf_op jit(solution)/shard_map/gate/pallas_call | solution.py:521
  547.7 9.4 %convolution_convert_fusion.2 = bf16[2048,1024]{1,0:T(8,128)(2,1)} fusion(bf16[1024,2048]{1,0:T(8,128)(2,1)} %get-tuple-element.114, bf16[1024,1024]{1,0:T(8,128)(2,1)} %get-tuple-element.115), kind=kOutput, calls=%fused_computation.5 | convolution fusion | flops 4297064448 | bytes 10485760 | tf_op jit(solution)/shard_map/dot_general | solution.py:25
  563.1 13.8 %collective-permute-done.60 = bf16[2,256,512]{2,1,0:T(8,128)(2,1)} collective-permute-done((bf16[2,256,512]{2,1,0:T(8,128)(2,1)}, bf16[2,256,512]{2,1,0:T(8,128)(2,1)}, u32[]{:S(2)}, u32[]{:S(2)}) %collective-permute-start.60) | collective-permute-done | bytes 524320 | tf_op jit(solution)/shard_map/ppermute | solution.py:150
  579.3 21.2 %bwd.1 = (bf16[1024,3072]{1,0:T(8,128)(2,1)}, f32[2,1024,1]{2,1,0:T(8,128)}) custom-call(f32[2]{0:T(128)} %negate_log-plus-one_fusion.refs_1_.refs_0_, bf16[1024,512]{1,0:T(8,128)(2,1)} %get-tuple-element.73.refs_1_.refs_2_, bf16[1024,512]{1,0:T(8,128)(2,1)} %get-tuple-element.77.refs_2_, bf16[1024,1024]{1,0:T(8,128)(2,1)} %get-tuple-element.78.refs_3_, ...), custom_call_target="tpu_custom_call" | custom-call | flops 7247757312 | bytes 12582912 | tf_op jit(solution)/shard_map/bwd/pallas_call | solution.py:627
  600.5 11.8 %fusion.12 = bf16[512,2048]{1,0:T(8,128)(2,1)} fusion(bf16[2048,3072]{1,0:T(8,128)(2,1)} %all-gather.4.cloned.1.call-done.refs_3_.w_ref, bf16[1024,3072]{1,0:T(8,128)(2,1)} %get-tuple-element.126), kind=kOutput, calls=%fused_computation.12 | convolution fusion | flops 6443499520 | bytes 17825792 | tf_op jit(solution)/shard_map/dot_general | solution.py:29
  612.3 16.1 %convolution_convert_fusion = bf16[2048,3072]{1,0:T(8,128)(2,1)} fusion(bf16[1024,2048]{1,0:T(8,128)(2,1)S(1)} %copy-done.13, bf16[1024,3072]{1,0:T(8,128)(2,1)S(1)} %copy-done.54), kind=kOutput, calls=%fused_computation | convolution fusion | flops 12891193344 | bytes 23068672 | tf_op jit(solution)/shard_map/dot_general | solution.py:25
  628.5 9.6 %fusion.2 = bf16[1024,2048]{1,0:T(8,128)(2,1)} fusion(bf16[1024,1024]{1,0:T(8,128)(2,1)} %get-tuple-element.97, bf16[2048,3072]{1,0:T(8,128)(2,1)} %all-gather.8.cloned.1.call-done.refs_2_), kind=kOutput, calls=%fused_computation.4 | convolution fusion | flops 4297064448 | bytes 10485760 | tf_op jit(solution)/shard_map/dot_general | solution.py:29
  653.1 10.7 %fusion.9 = bf16[512,2048]{1,0:T(8,128)(2,1)S(1)} fusion(bf16[2048,3072]{1,0:T(8,128)(2,1)} %all-gather.4.cloned.1.call-done.refs_3_.w_ref, bf16[1024,3072]{1,0:T(8,128)(2,1)} %get-tuple-element.126), kind=kOutput, calls=%fused_computation.11 | convolution fusion | flops 6443499520 | bytes 17825792 | tf_op jit(solution)/shard_map/dot_general | solution.py:29
  663.9 60.7 %collective-permute-done.64 = bf16[512,512]{1,0:T(8,128)(2,1)S(1)} collective-permute-done((bf16[512,512]{1,0:T(8,128)(2,1)S(1)}, bf16[512,512]{1,0:T(8,128)(2,1)S(1)}, u32[]{:S(2)}, u32[]{:S(2)}) %collective-permute-start.64) | collective-permute-done | bytes 524320 | tf_op jit(solution)/shard_map/ppermute | solution.py:88
  726.0 5.2 collective-permute-start.65
  743.6 7.9 collective-permute-done.71
  754.0 5.3 collective-permute-start.72
  786.4 10.8 %collective-permute-done.70 = f32[8,128]{1,0:T(8,128)S(1)} collective-permute-done((f32[8,128]{1,0:T(8,128)S(1)}, f32[8,128]{1,0:T(8,128)S(1)}, u32[]{:S(2)}, u32[]{:S(2)}) %collective-permute-start.70) | collective-permute-done | bytes 4128 | tf_op jit(solution)/shard_map/ppermute | solution.py:126
  (346 shorter events, 238.5 us)
Async XLA Ops:
  7.2 89.5 %all-gather.4.cloned.1.call-start = ((), (), s32[]{:S(2)}) async-start(), calls=%async_computation.4 | async-start | bytes 14155776 | tf_op jit(solution)/shard_map/all_gather | solution.py:688
  11.0 135.9 %all-gather.6.cloned.1.call-start = ((), (), s32[]{:S(2)}) async-start(), calls=%async_computation.5 | async-start | bytes 4718592 | tf_op jit(solution)/shard_map/all_gather | solution.py:689
  11.8 326.2 %all-gather.8.cloned.1.call-start = ((), (), s32[]{:S(2)}) async-start(), calls=%async_computation.6 | async-start | bytes 14155776 | tf_op jit(solution)/shard_map/all_gather | solution.py:711
  19.0 24.1 %collective-permute-start.3 = (bf16[1024,512]{1,0:T(8,128)(2,1)S(1)}, bf16[1024,512]{1,0:T(8,128)(2,1)S(1)}, u32[]{:S(2)}, u32[]{:S(2)}) collective-permute-start(bf16[1024,512]{1,0:T(8,128)(2,1)S(1)} %copy-done.25), channel_id=1, source_target_pairs={{0,1},{1,2},{2,3},{4,5},{5,6},{6,7},{8,9},{9,10},{10,11},{12,13},{... | collective-permute-start | bytes 3145736 | tf_op jit(solution)/shard_map/ppermute | solution.py:57
  21.6 25.8 %collective-permute-start.5 = (bf16[1024,512]{1,0:T(8,128)(2,1)S(1)}, bf16[1024,512]{1,0:T(8,128)(2,1)}, u32[]{:S(2)}, u32[]{:S(2)}) collective-permute-start(bf16[1024,512]{1,0:T(8,128)(2,1)S(1)} %copy-done.25), channel_id=1, source_target_pairs={{3,2},{2,1},{1,0},{7,6},{6,5},{5,4},{11,10},{10,9},{9,8},{15,14},{... | collective-permute-start | bytes 3145736 | tf_op jit(solution)/shard_map/ppermute | solution.py:58
  47.4 25.0 %collective-permute-start.6 = (bf16[1024,512]{1,0:T(8,128)(2,1)}, bf16[1024,512]{1,0:T(8,128)(2,1)S(1)}, u32[]{:S(2)}, u32[]{:S(2)}) collective-permute-start(bf16[1024,512]{1,0:T(8,128)(2,1)} %collective-permute-done.5.refs_12_), channel_id=1, source_target_pairs={{2,1},{1,0},{6,5},{5,4},{10,9},{9,8},{14,13},{13,12},{18,17},{17,1... | collective-permute-start | bytes 3145736 | tf_op jit(solution)/shard_map/ppermute | solution.py:58
  72.5 24.2 %collective-permute-start.7 = (bf16[1024,512]{1,0:T(8,128)(2,1)S(1)}, bf16[1024,512]{1,0:T(8,128)(2,1)}, u32[]{:S(2)}, u32[]{:S(2)}) collective-permute-start(bf16[1024,512]{1,0:T(8,128)(2,1)S(1)} %broadcast_select_fusion.1), channel_id=1, source_target_pairs={{2,3},{1,0},{6,7},{5,4},{10,11},{9,8},{14,15},{13,12},{18,19},{17,... | collective-permute-start | bytes 3145736 | tf_op jit(solution)/shard_map/ppermute | solution.py:53
  137.9 603.4 %reduce-scatter.5.cloned.1.call-start = ((), (), s32[]{:S(2)}) async-start(), calls=%async_computation.7 | async-start | bytes 4718592 | tf_op jit(solution)/shard_map/reduce_scatter | solution.py:804
  179.4 32.7 %collective-permute-start.20 = (bf16[1024,512]{1,0:T(8,128)(2,1)S(1)}, bf16[1024,512]{1,0:T(8,128)(2,1)}, u32[]{:S(2)}, u32[]{:S(2)}) collective-permute-start(bf16[1024,512]{1,0:T(8,128)(2,1)S(1)} %copy-done.16), channel_id=1, source_target_pairs={{0,1},{1,2},{2,3},{4,5},{5,6},{6,7},{8,9},{9,10},{10,11},{12,13},{... | collective-permute-start | bytes 3145736 | tf_op jit(solution)/shard_map/ppermute | solution.py:57
  182.5 31.3 %collective-permute-start.22 = (bf16[1024,512]{1,0:T(8,128)(2,1)S(1)}, bf16[1024,512]{1,0:T(8,128)(2,1)}, u32[]{:S(2)}, u32[]{:S(2)}) collective-permute-start(bf16[1024,512]{1,0:T(8,128)(2,1)S(1)} %copy-done.16), channel_id=1, source_target_pairs={{3,2},{2,1},{1,0},{7,6},{6,5},{5,4},{11,10},{10,9},{9,8},{15,14},{... | collective-permute-start | bytes 3145736 | tf_op jit(solution)/shard_map/ppermute | solution.py:58
  195.5 27.8 %collective-permute-start.32 = (bf16[512,512]{1,0:T(8,128)(2,1)S(1)}, bf16[512,512]{1,0:T(8,128)(2,1)S(1)}, u32[]{:S(2)}, u32[]{:S(2)}) collective-permute-start(bf16[512,512]{1,0:T(8,128)(2,1)S(1)} %constant_dynamic-slice_fusion.6), channel_id=1, source_target_pairs={{0,1},{3,2},{4,5},{7,6},{8,9},{11,10},{12,13},{15,14},{16,17},{19,... | collective-permute-start | bytes 1572872 | tf_op jit(solution)/shard_map/ppermute | solution.py:88
  202.5 32.0 %collective-permute-start.12 = (bf16[512,512]{1,0:T(8,128)(2,1)S(1)}, bf16[512,512]{1,0:T(8,128)(2,1)S(1)}, u32[]{:S(2)}, u32[]{:S(2)}) collective-permute-start(bf16[512,512]{1,0:T(8,128)(2,1)S(1)} %get-tuple-element.177), channel_id=1, source_target_pairs={{0,1},{1,2},{2,3},{4,5},{5,6},{6,7},{8,9},{9,10},{10,11},{12,13},{... | collective-permute-start | bytes 1572872 | tf_op jit(solution)/shard_map/ppermute | solution.py:96
  204.1 32.2 %collective-permute-start.14 = (bf16[512,512]{1,0:T(8,128)(2,1)}, bf16[512,512]{1,0:T(8,128)(2,1)}, u32[]{:S(2)}, u32[]{:S(2)}) collective-permute-start(bf16[512,512]{1,0:T(8,128)(2,1)} %get-tuple-element.178), channel_id=1, source_target_pairs={{3,2},{2,1},{1,0},{7,6},{6,5},{5,4},{11,10},{10,9},{9,8},{15,14},{... | collective-permute-start | bytes 1572872 | tf_op jit(solution)/shard_map/ppermute | solution.py:97
  212.1 52.6 %collective-permute-start.21 = (bf16[1024,512]{1,0:T(8,128)(2,1)}, bf16[1024,512]{1,0:T(8,128)(2,1)}, u32[]{:S(2)}, u32[]{:S(2)}) collective-permute-start(bf16[1024,512]{1,0:T(8,128)(2,1)} %collective-permute-done.20.refs_11_), channel_id=1, source_target_pairs={{1,2},{2,3},{5,6},{6,7},{9,10},{10,11},{13,14},{14,15},{17,18},{18... | collective-permute-start | bytes 3145736 | tf_op jit(solution)/shard_map/ppermute | solution.py:57
  213.7 52.2 %collective-permute-start.23 = (bf16[1024,512]{1,0:T(8,128)(2,1)}, bf16[1024,512]{1,0:T(8,128)(2,1)}, u32[]{:S(2)}, u32[]{:S(2)}) collective-permute-start(bf16[1024,512]{1,0:T(8,128)(2,1)} %collective-permute-done.22.refs_16_), channel_id=1, source_target_pairs={{2,1},{1,0},{6,5},{5,4},{10,9},{9,8},{14,13},{13,12},{18,17},{17,1... | collective-permute-start | bytes 3145736 | tf_op jit(solution)/shard_map/ppermute | solution.py:58
  239.7 28.9 %collective-permute-start.15 = (bf16[512,512]{1,0:T(8,128)(2,1)S(1)}, bf16[512,512]{1,0:T(8,128)(2,1)S(1)}, u32[]{:S(2)}, u32[]{:S(2)}) collective-permute-start(bf16[512,512]{1,0:T(8,128)(2,1)S(1)} %get-tuple-element.146.refs_3_), channel_id=1, source_target_pairs={{0,1},{1,2},{2,3},{4,5},{5,6},{6,7},{8,9},{9,10},{10,11},{12,13},{... | collective-permute-start | bytes 1572872 | tf_op jit(solution)/shard_map/ppermute | solution.py:57
  245.9 24.7 %collective-permute-start.17 = (bf16[512,512]{1,0:T(8,128)(2,1)S(1)}, bf16[512,512]{1,0:T(8,128)(2,1)S(1)}, u32[]{:S(2)}, u32[]{:S(2)}) collective-permute-start(bf16[512,512]{1,0:T(8,128)(2,1)S(1)} %get-tuple-element.146.refs_3_), channel_id=1, source_target_pairs={{3,2},{2,1},{1,0},{7,6},{6,5},{5,4},{11,10},{10,9},{9,8},{15,14},{... | collective-permute-start | bytes 1572872 | tf_op jit(solution)/shard_map/ppermute | solution.py:58
  248.8 24.2 %collective-permute-start.34 = (bf16[512,512]{1,0:T(8,128)(2,1)S(1)}, bf16[512,512]{1,0:T(8,128)(2,1)S(1)}, u32[]{:S(2)}, u32[]{:S(2)}) collective-permute-start(bf16[512,512]{1,0:T(8,128)(2,1)S(1)} %get-tuple-element.173), channel_id=1, source_target_pairs={{0,1},{1,2},{2,3},{4,5},{5,6},{6,7},{8,9},{9,10},{10,11},{12,13},{... | collective-permute-start | bytes 1572872 | tf_op jit(solution)/shard_map/ppermute | solution.py:96
  267.3 60.9 %collective-permute-start.24 = (bf16[1024,512]{1,0:T(8,128)(2,1)S(1)}, bf16[1024,512]{1,0:T(8,128)(2,1)S(1)}, u32[]{:S(2)}, u32[]{:S(2)}) collective-permute-start(bf16[1024,512]{1,0:T(8,128)(2,1)S(1)} %broadcast_select_fusion), channel_id=1, source_target_pairs={{2,3},{1,0},{6,7},{5,4},{10,11},{9,8},{14,15},{13,12},{18,19},{17,... | collective-permute-start | bytes 3145736 | tf_op jit(solution)/shard_map/ppermute | solution.py:53
  268.6 22.6 %collective-permute-start.16 = (bf16[512,512]{1,0:T(8,128)(2,1)S(1)}, bf16[512,512]{1,0:T(8,128)(2,1)S(1)}, u32[]{:S(2)}, u32[]{:S(2)}) collective-permute-start(bf16[512,512]{1,0:T(8,128)(2,1)S(1)} %collective-permute-done.15.refs_4_), channel_id=1, source_target_pairs={{1,2},{2,3},{5,6},{6,7},{9,10},{10,11},{13,14},{14,15},{17,18},{18... | collective-permute-start | bytes 1572872 | tf_op jit(solution)/shard_map/ppermute | solution.py:57
  270.6 44.9 %collective-permute-start.18 = (bf16[512,512]{1,0:T(8,128)(2,1)S(1)}, bf16[512,512]{1,0:T(8,128)(2,1)S(1)}, u32[]{:S(2)}, u32[]{:S(2)}) collective-permute-start(bf16[512,512]{1,0:T(8,128)(2,1)S(1)} %collective-permute-done.17.refs_9_), channel_id=1, source_target_pairs={{2,1},{1,0},{6,5},{5,4},{10,9},{9,8},{14,13},{13,12},{18,17},{17,1... | collective-permute-start | bytes 1572872 | tf_op jit(solution)/shard_map/ppermute | solution.py:58
  282.4 34.7 %collective-permute-start.37 = (bf16[512,512]{1,0:T(8,128)(2,1)S(1)}, bf16[512,512]{1,0:T(8,128)(2,1)}, u32[]{:S(2)}, u32[]{:S(2)}) collective-permute-start(bf16[512,512]{1,0:T(8,128)(2,1)S(1)} %get-tuple-element.142.refs_3_), channel_id=1, source_target_pairs={{0,1},{1,2},{2,3},{4,5},{5,6},{6,7},{8,9},{9,10},{10,11},{12,13},{... | collective-permute-start | bytes 1572872 | tf_op jit(solution)/shard_map/ppermute | solution.py:57
  289.9 37.0 %collective-permute-start.39 = (bf16[512,512]{1,0:T(8,128)(2,1)S(1)}, bf16[512,512]{1,0:T(8,128)(2,1)}, u32[]{:S(2)}, u32[]{:S(2)}) collective-permute-start(bf16[512,512]{1,0:T(8,128)(2,1)S(1)} %get-tuple-element.142.refs_3_), channel_id=1, source_target_pairs={{3,2},{2,1},{1,0},{7,6},{6,5},{5,4},{11,10},{10,9},{9,8},{15,14},{... | collective-permute-start | bytes 1572872 | tf_op jit(solution)/shard_map/ppermute | solution.py:58
  317.1 45.0 %collective-permute-start.38 = (bf16[512,512]{1,0:T(8,128)(2,1)}, bf16[512,512]{1,0:T(8,128)(2,1)}, u32[]{:S(2)}, u32[]{:S(2)}) collective-permute-start(bf16[512,512]{1,0:T(8,128)(2,1)} %collective-permute-done.37.refs_4_), channel_id=1, source_target_pairs={{1,2},{2,3},{5,6},{6,7},{9,10},{10,11},{13,14},{14,15},{17,18},{18... | collective-permute-start | bytes 1572872 | tf_op jit(solution)/shard_map/ppermute | solution.py:57
  326.9 35.3 %collective-permute-start.40 = (bf16[512,512]{1,0:T(8,128)(2,1)}, bf16[512,512]{1,0:T(8,128)(2,1)}, u32[]{:S(2)}, u32[]{:S(2)}) collective-permute-start(bf16[512,512]{1,0:T(8,128)(2,1)} %collective-permute-done.39.refs_9_), channel_id=1, source_target_pairs={{2,1},{1,0},{6,5},{5,4},{10,9},{9,8},{14,13},{13,12},{18,17},{17,1... | collective-permute-start | bytes 1572872 | tf_op jit(solution)/shard_map/ppermute | solution.py:58
  370.3 28.4 %collective-permute-start.26 = (bf16[512,512]{1,0:T(8,128)(2,1)}, bf16[512,512]{1,0:T(8,128)(2,1)}, u32[]{:S(2)}, u32[]{:S(2)}) collective-permute-start(bf16[512,512]{1,0:T(8,128)(2,1)} %get-tuple-element.161), channel_id=1, source_target_pairs={{0,1},{1,2},{4,5},{5,6},{8,9},{9,10},{12,13},{13,14},{16,17},{17,1... | collective-permute-start | bytes 1572872 | tf_op jit(solution)/shard_map/ppermute | solution.py:96
  375.5 23.3 %collective-permute-start.28 = (bf16[512,512]{1,0:T(8,128)(2,1)}, bf16[512,512]{1,0:T(8,128)(2,1)}, u32[]{:S(2)}, u32[]{:S(2)}) collective-permute-start(bf16[512,512]{1,0:T(8,128)(2,1)} %get-tuple-element.162), channel_id=1, source_target_pairs={{3,2},{2,1},{7,6},{6,5},{11,10},{10,9},{15,14},{14,13},{19,18},{18... | collective-permute-start | bytes 1572872 | tf_op jit(solution)/shard_map/ppermute | solution.py:97
  409.6 29.1 %collective-permute-start.31 = (f32[4,128]{1,0:T(4,128)S(1)}, f32[4,128]{1,0:T(4,128)S(1)}, u32[]{:S(2)}, u32[]{:S(2)}) collective-permute-start(f32[4,128]{1,0:T(4,128)S(1)} %bitcast_add_fusion.1), channel_id=1, source_target_pairs={{0,2},{1,3},{2,0},{3,1},{4,6},{5,7},{6,4},{7,5},{8,10},{9,11},{10,... | collective-permute-start | bytes 6152 | tf_op jit(solution)/shard_map/ppermute | solution.py:126
  416.7 30.8 %collective-permute-start.27 = (bf16[512,512]{1,0:T(8,128)(2,1)}, bf16[512,512]{1,0:T(8,128)(2,1)}, u32[]{:S(2)}, u32[]{:S(2)}) collective-permute-start(bf16[512,512]{1,0:T(8,128)(2,1)} %get-tuple-element.175), channel_id=1, source_target_pairs={{0,1},{1,2},{2,3},{4,5},{5,6},{6,7},{8,9},{9,10},{10,11},{12,13},{... | collective-permute-start | bytes 1572872 | tf_op jit(solution)/shard_map/ppermute | solution.py:96
  419.1 28.5 %collective-permute-start.29 = (bf16[512,512]{1,0:T(8,128)(2,1)}, bf16[512,512]{1,0:T(8,128)(2,1)}, u32[]{:S(2)}, u32[]{:S(2)}) collective-permute-start(bf16[512,512]{1,0:T(8,128)(2,1)} %get-tuple-element.176), channel_id=1, source_target_pairs={{3,2},{2,1},{1,0},{7,6},{6,5},{5,4},{11,10},{10,9},{9,8},{15,14},{... | collective-permute-start | bytes 1572872 | tf_op jit(solution)/shard_map/ppermute | solution.py:97
  438.6 329.5 %reduce-scatter.9.cloned.1.call-start = ((), (), s32[]{:S(2)}) async-start(), calls=%async_computation.9 | async-start | bytes 4718592 | tf_op jit(solution)/shard_map/reduce_scatter | solution.py:804
  441.7 23.3 %collective-permute-start.49 = (bf16[512,512]{1,0:T(8,128)(2,1)}, bf16[512,512]{1,0:T(8,128)(2,1)}, u32[]{:S(2)}, u32[]{:S(2)}) collective-permute-start(bf16[512,512]{1,0:T(8,128)(2,1)} %get-tuple-element.171), channel_id=1, source_target_pairs={{0,1},{1,2},{2,3},{4,5},{5,6},{6,7},{8,9},{9,10},{10,11},{12,13},{... | collective-permute-start | bytes 1572872 | tf_op jit(solution)/shard_map/ppermute | solution.py:96
  478.1 22.7 %collective-permute-start.45 = (bf16[512,512]{1,0:T(8,128)(2,1)S(1)}, bf16[512,512]{1,0:T(8,128)(2,1)S(1)}, u32[]{:S(2)}, u32[]{:S(2)}) collective-permute-start(bf16[512,512]{1,0:T(8,128)(2,1)S(1)} %collective-permute-done.44.refs_12_), channel_id=1, source_target_pairs={{2,1},{1,0},{6,5},{5,4},{10,9},{9,8},{14,13},{13,12},{18,17},{17,1... | collective-permute-start | bytes 1572872 | tf_op jit(solution)/shard_map/ppermute | solution.py:58
  479.7 23.3 %collective-permute-start.55 = (bf16[512,512]{1,0:T(8,128)(2,1)S(1)}, bf16[512,512]{1,0:T(8,128)(2,1)S(1)}, u32[]{:S(2)}, u32[]{:S(2)}) collective-permute-start(bf16[512,512]{1,0:T(8,128)(2,1)S(1)} %collective-permute-done.54.refs_7_), channel_id=1, source_target_pairs={{1,2},{2,3},{5,6},{6,7},{9,10},{10,11},{13,14},{14,15},{17,18},{18... | collective-permute-start | bytes 1572872 | tf_op jit(solution)/shard_map/ppermute | solution.py:57
  489.6 22.5 %collective-permute-start.57 = (bf16[512,512]{1,0:T(8,128)(2,1)S(1)}, bf16[512,512]{1,0:T(8,128)(2,1)S(1)}, u32[]{:S(2)}, u32[]{:S(2)}) collective-permute-start(bf16[512,512]{1,0:T(8,128)(2,1)S(1)} %collective-permute-done.56.refs_12_), channel_id=1, source_target_pairs={{2,1},{1,0},{6,5},{5,4},{10,9},{9,8},{14,13},{13,12},{18,17},{17,1... | collective-permute-start | bytes 1572872 | tf_op jit(solution)/shard_map/ppermute | solution.py:58
  501.7 24.2 %collective-permute-start.46 = (bf16[512,512]{1,0:T(8,128)(2,1)}, bf16[512,512]{1,0:T(8,128)(2,1)}, u32[]{:S(2)}, u32[]{:S(2)}) collective-permute-start(bf16[512,512]{1,0:T(8,128)(2,1)} %broadcast_select_fusion.4), channel_id=1, source_target_pairs={{2,3},{1,0},{6,7},{5,4},{10,11},{9,8},{14,15},{13,12},{18,19},{17,... | collective-permute-start | bytes 1572872 | tf_op jit(solution)/shard_map/ppermute | solution.py:53
  513.0 23.9 %collective-permute-start.58 = (bf16[512,512]{1,0:T(8,128)(2,1)}, bf16[512,512]{1,0:T(8,128)(2,1)}, u32[]{:S(2)}, u32[]{:S(2)}) collective-permute-start(bf16[512,512]{1,0:T(8,128)(2,1)} %broadcast_select_fusion.3), channel_id=1, source_target_pairs={{2,3},{1,0},{6,7},{5,4},{10,11},{9,8},{14,15},{13,12},{18,19},{17,... | collective-permute-start | bytes 1572872 | tf_op jit(solution)/shard_map/ppermute | solution.py:53
  557.2 213.1 %reduce-scatter.7.cloned.1.call-start = ((), (), s32[]{:S(2)}) async-start(), calls=%async_computation.8 | async-start | bytes 9437184 | tf_op jit(solution)/shard_map/reduce_scatter | solution.py:804
  557.7 251.5 %reduce-scatter.11.cloned.1.call-start = ((), (), s32[]{:S(2)}) async-start(), calls=%async_computation.10 | async-start | bytes 14155776 | tf_op jit(solution)/shard_map/reduce_scatter | solution.py:804
  642.9 90.5 %collective-permute-start.61 = (bf16[1024,512]{1,0:T(8,128)(2,1)}, bf16[1024,512]{1,0:T(8,128)(2,1)}, u32[]{:S(2)}, u32[]{:S(2)}) collective-permute-start(bf16[1024,512]{1,0:T(8,128)(2,1)} %get-tuple-element.150), channel_id=1, source_target_pairs={{0,1},{1,2},{2,3},{3,0},{4,5},{5,6},{6,7},{7,4},{8,9},{9,10},{10,1... | collective-permute-start | bytes 3145736 | tf_op jit(solution)/shard_map/ppermute | solution.py:112
  646.6 88.9 %collective-permute-start.62 = (bf16[1024,512]{1,0:T(8,128)(2,1)}, bf16[1024,512]{1,0:T(8,128)(2,1)}, u32[]{:S(2)}, u32[]{:S(2)}) collective-permute-start(bf16[1024,512]{1,0:T(8,128)(2,1)} %get-tuple-element.152), channel_id=1, source_target_pairs={{0,2},{1,3},{2,0},{3,1},{4,6},{5,7},{6,4},{7,5},{8,10},{9,11},{10,... | collective-permute-start | bytes 3145736 | tf_op jit(solution)/shard_map/ppermute | solution.py:112
  646.6 88.9 %collective-permute-start.63 = (bf16[1024,512]{1,0:T(8,128)(2,1)}, bf16[1024,512]{1,0:T(8,128)(2,1)}, u32[]{:S(2)}, u32[]{:S(2)}) collective-permute-start(bf16[1024,512]{1,0:T(8,128)(2,1)} %get-tuple-element.151), channel_id=1, source_target_pairs={{0,3},{1,0},{2,1},{3,2},{4,7},{5,4},{6,5},{7,6},{8,11},{9,8},{10,9... | collective-permute-start | bytes 3145736 | tf_op jit(solution)/shard_map/ppermute | solution.py:112
  651.5 73.1 %collective-permute-start.64 = (bf16[512,512]{1,0:T(8,128)(2,1)S(1)}, bf16[512,512]{1,0:T(8,128)(2,1)S(1)}, u32[]{:S(2)}, u32[]{:S(2)}) collective-permute-start(bf16[512,512]{1,0:T(8,128)(2,1)S(1)} %constant_dynamic-slice_fusion.1), channel_id=1, source_target_pairs={{0,1},{3,2},{4,5},{7,6},{8,9},{11,10},{12,13},{15,14},{16,17},{19,... | collective-permute-start | bytes 1572872 | tf_op jit(solution)/shard_map/ppermute | solution.py:88
  726.0 34.8 %collective-permute-start.65 = (bf16[512,512]{1,0:T(8,128)(2,1)}, bf16[512,512]{1,0:T(8,128)(2,1)}, u32[]{:S(2)}, u32[]{:S(2)}) collective-permute-start(bf16[512,512]{1,0:T(8,128)(2,1)} %get-tuple-element.155), channel_id=1, source_target_pairs={{0,1},{1,2},{4,5},{5,6},{8,9},{9,10},{12,13},{13,14},{16,17},{17,1... | collective-permute-start | bytes 1572872 | tf_op jit(solution)/shard_map/ppermute | solution.py:96
  731.1 29.7 %collective-permute-start.67 = (bf16[512,512]{1,0:T(8,128)(2,1)}, bf16[512,512]{1,0:T(8,128)(2,1)}, u32[]{:S(2)}, u32[]{:S(2)}) collective-permute-start(bf16[512,512]{1,0:T(8,128)(2,1)} %get-tuple-element.138), channel_id=1, source_target_pairs={{3,2},{2,1},{7,6},{6,5},{11,10},{10,9},{15,14},{14,13},{19,18},{18... | collective-permute-start | bytes 1572872 | tf_op jit(solution)/shard_map/ppermute | solution.py:97
  754.0 22.4 %collective-permute-start.72 = (bf16[512,512]{1,0:T(8,128)(2,1)}, bf16[512,512]{1,0:T(8,128)(2,1)}, u32[]{:S(2)}, u32[]{:S(2)}) collective-permute-start(bf16[512,512]{1,0:T(8,128)(2,1)} %get-tuple-element.153), channel_id=1, source_target_pairs={{0,1},{1,2},{4,5},{5,6},{8,9},{9,10},{12,13},{13,14},{16,17},{17,1... | collective-permute-start | bytes 1572872 | tf_op jit(solution)/shard_map/ppermute | solution.py:96
  763.4 33.8 %collective-permute-start.66 = (bf16[512,512]{1,0:T(8,128)(2,1)}, bf16[512,512]{1,0:T(8,128)(2,1)S(1)}, u32[]{:S(2)}, u32[]{:S(2)}) collective-permute-start(bf16[512,512]{1,0:T(8,128)(2,1)} %get-tuple-element.167), channel_id=1, source_target_pairs={{0,1},{1,2},{2,3},{4,5},{5,6},{6,7},{8,9},{9,10},{10,11},{12,13},{... | collective-permute-start | bytes 1572872 | tf_op jit(solution)/shard_map/ppermute | solution.py:96
  766.8 30.4 %collective-permute-start.68 = (bf16[512,512]{1,0:T(8,128)(2,1)}, bf16[512,512]{1,0:T(8,128)(2,1)S(1)}, u32[]{:S(2)}, u32[]{:S(2)}) collective-permute-start(bf16[512,512]{1,0:T(8,128)(2,1)} %get-tuple-element.168), channel_id=1, source_target_pairs={{3,2},{2,1},{1,0},{7,6},{6,5},{5,4},{11,10},{10,9},{9,8},{15,14},{... | collective-permute-start | bytes 1572872 | tf_op jit(solution)/shard_map/ppermute | solution.py:97
  (93 other events, 1660.9 us)
Sparse Core Ops, SparseCore 0:
  11.2 74.7 all-gather.3
  87.8 36.5 all-gather.5
  138.0 70.0 all-gather.7
  438.7 49.1 reduce-scatter.4
  557.3 51.3 reduce-scatter.8
  612.0 71.4 reduce-scatter.6
  687.0 92.2 reduce-scatter.10

commit v6 on v5

--- a/solution.py
+++ b/solution.py
@@ -88,6 +88,12 @@
             from_left = from_right = lax.ppermute(data, axis, r_pairs + l_pairs)
             from_left = jnp.where(i <= k, from_left, jnp.zeros_like(from_left))
             from_right = jnp.where(i >= n - 1 - k, from_right, jnp.zeros_like(from_right))
+        elif 2 * k <= n:
+            data = block(jnp.where(i < k, i + n - k, i - n + k))
+            if from_left is not None:
+                data = (data.astype(F32) + jnp.where(i < k, from_left, from_right).astype(F32)).astype(BF16)
+            from_left = lax.ppermute(data, axis, r_pairs)
+            from_right = lax.ppermute(data, axis, l_pairs)
         else:
             r_data, l_data = block(i + n - k), block(i - n + k)
             if from_left is not None:
@@ -128,34 +134,50 @@
     return x
 
 
-def states_before(local, log_block, axis):
+def state_factors(log_block, axis):
     n, b = lax.axis_size(axis), lax.axis_index(axis)
-    total, prefix, g = local, jnp.zeros_like(local), 1
+    before, behind, g = [], [], 1
     while g < n:
-        got = lax.ppermute(total.astype(BF16), axis, [(j, j ^ g) for j in range(n)]).astype(F32)
         upper = (b // g) % 2 == 1
-        mine = jnp.exp((b % g).astype(F32) * log_block)[:, None, None]
-        whole = jnp.exp(g * log_block)[:, None, None]
-        prefix = jnp.where(upper, prefix + mine * got, prefix)
-        total = jnp.where(upper, whole * got + total, whole * total + got)
+        before.append(jnp.where(upper, jnp.exp((b % g).astype(F32) * log_block), 0.0))
+        behind.append(jnp.where(upper, 0.0, jnp.exp((g - 1 - b % g).astype(F32) * log_block)))
         g *= 2
-    return prefix
-
-
-def states_after(local, log_block, axis):
-    first = None
+    return jnp.stack(before), jnp.stack(behind)
+
+
+def states_before(local, rounded, log_block, axis):
     n, b = lax.axis_size(axis), lax.axis_index(axis)
-    total, suffix, g = local, jnp.zeros_like(local), 1
+    total, pieces, g = local, [], 1
     while g < n:
-        got = lax.ppermute(total.astype(BF16), axis, [(j, j ^ g) for j in range(n)]).astype(F32)
-        first = got if first is None else first
+        got = lax.ppermute(rounded if g == 1 else total.astype(BF16), axis, [(j, j ^ g) for j in range(n)])
         upper = (b // g) % 2 == 1
-        mine = jnp.exp((g - 1 - b % g).astype(F32) * log_block)[:, None, None]
-        whole = jnp.exp(g * log_block)[:, None, None]
-        suffix = jnp.where(upper, suffix, suffix + mine * got)
-        total = jnp.where(upper, got + whole * total, total + whole * got)
+        pieces.append(got)
+        if 2 * g < n:
+            whole = jnp.exp(g * log_block)[:, None, None]
+            total = jnp.where(upper, whole, 1.0) * got.astype(F32) + jnp.where(upper, 1.0, whole) * total
         g *= 2
-    return suffix, first
+    return pieces
+
+
+def states_after(local, rounded, log_block, axis):
+    n, b = lax.axis_size(axis), lax.axis_index(axis)
+    total, pieces, g = local, [], 1
+    while g < n:
+        got = lax.ppermute(rounded if g == 1 else total.astype(BF16), axis, [(j, j ^ g) for j in range(n)])
+        upper = (b // g) % 2 == 1
+        pieces.append(got)
+        if 2 * g < n:
+            whole = jnp.exp(g * log_block)[:, None, None]
+            total = jnp.where(upper, 1.0, whole) * got.astype(F32) + jnp.where(upper, whole, 1.0) * total
+        g *= 2
+    return pieces
+
+
+def whole_state(refs, factor_ref, head):
+    state = refs[0][0].astype(F32) * factor_ref[0, head]
+    for i in range(1, len(refs)):
+        state = state + refs[i][0].astype(F32) * factor_ref[i, head]
+    return state.astype(BF16)
 
 
 def pair_swap(x):
@@ -212,81 +234,96 @@
     return [x] + [p for pair in pairs for p in pair]
 
 
-def project_kernel(heads, count, at_ref, lg_ref, gain_ref, w_ref, cos_ref, sin_ref, *refs):
-    blocks, (full_ref, scale_ref, q_ref, k_ref, v_ref, state_ref) = refs[:count], refs[count:]
-    step = pl.program_id(0)
-    rows = pl.num_programs(0) * BLOCK
+def project_kernel(part, parts, heads, count, at_ref, lg_ref, gain_ref, w_ref, cos_ref, sin_ref, *refs):
+    blocks = refs[:count]
+    full_ref, q_ref, k_ref, v_ref, scale_ref, state_ref, rounded_ref, kept_ref, sems = refs[-9:]
+    qk, vw = heads * HK, heads * HV
+    own = full_ref.shape[0]
+    copies = []
+    for i, (first, width) in enumerate(((qk, qk), (2 * qk, vw), (0, qk))):
+        columns = slice(first, first + width)
+        copies.append(pltpu.make_async_copy(w_ref.at[:, columns], kept_ref.at[:, columns], sems.at[i]))
+        copies[-1].start()
     scale_ref[...] = fill_normed(at_ref[0], blocks, gain_ref, full_ref)
     x = full_ref[...]
-    qk = heads * HK
     c, s = cos_ref[...], sin_ref[...]
-    k_out = nn(x, w_ref[:, qk : 2 * qk])
-    v_out = nn(x, w_ref[:, 2 * qk :]).astype(BF16)
-    q_out = nn(x, w_ref[:, :qk])
+    copies[0].wait()
+    k_out = nn(x, kept_ref[:, qk : 2 * qk])
+    copies[1].wait()
+    v_out = nn(x, kept_ref[:, 2 * qk : 2 * qk + vw]).astype(BF16)
+    copies[2].wait()
+    q_out = nn(x, kept_ref[:, :qk])
     v_ref[...] = v_out
-    m = lax.broadcasted_iota(jnp.int32, (BLOCK, 1), 0) + step * BLOCK
+    m = lax.broadcasted_iota(jnp.int32, (own, 1), 0) + part * own
     for h in range(heads):
         at = slice(h * HK, (h + 1) * HK)
         one = k_out[:, at]
         key = ((one * c + pair_swap(one) * s) * (1.0 / math.sqrt(HK))).astype(BF16)
         k_ref[:, at] = key
-        tail = jnp.exp((rows - m).astype(F32) * lg_ref[h])
-        add = tn((key.astype(F32) * tail).astype(BF16), v_out[:, h * HV : (h + 1) * HV])
-
-        @pl.when(step == 0)
-        def _(h=h, add=add):
-            state_ref[h] = add
-
-        @pl.when(step > 0)
-        def _(h=h, add=add):
-            state_ref[h] += add
-
+        tail = jnp.exp((parts * own - m).astype(F32) * lg_ref[h])
+        state = tn((key.astype(F32) * tail).astype(BF16), v_out[:, h * HV : (h + 1) * HV])
+        if part:
+            state = state + refs[count][h]
+        state_ref[h] = state
+        rounded_ref[h] = state.astype(BF16)
         one = q_out[:, at]
         q_ref[:, at] = (one * c + pair_swap(one) * s).astype(BF16)
 
 
-def project(at, log_gamma, gain, w, x, pairs, heads, cosine, sine):
-    rows, width = x.shape
+def project(part, parts, at, log_gamma, gain, w, x, pairs, heads, cosine, sine, shared, state):
+    own, width = x.shape
     features = w.shape[0]
     outs = 2 * heads * HK + heads * HV
     blocks = flat(x, pairs)
-
-    def by_rows(columns):
-        return pl.BlockSpec((BLOCK, columns), lambda r: (r, 0))
-
+    rows = parts * own
+
+    def here(columns):
+        return pl.BlockSpec((own, columns), lambda i: (0, 0))
+
+    def in_all(columns):
+        return pl.BlockSpec((own, columns), lambda i: (part, 0))
+
+    states = pl.BlockSpec((heads, HK, HV), lambda i: (0, 0, 0))
+    before = [state] if part else []
     return pl.pallas_call(
-        lambda *refs: project_kernel(heads, len(blocks), *refs),
-        grid=(rows // BLOCK,),
+        lambda *refs: project_kernel(part, parts, heads, len(blocks), *refs),
+        grid=(1,),
         in_specs=[
             pl.BlockSpec(memory_space=pltpu.SMEM),
             pl.BlockSpec(memory_space=pltpu.SMEM),
-            pl.BlockSpec((1, features), lambda r: (0, 0)),
-            pl.BlockSpec((features, outs), lambda r: (0, 0)),
-            by_rows(HK),
-            by_rows(HK),
-            *[by_rows(width)] * len(blocks),
+            pl.BlockSpec((1, features), lambda i: (0, 0)),
+            pl.BlockSpec(memory_space=pl.ANY),
+            in_all(HK),
+            in_all(HK),
+            *[here(width)] * len(blocks),
+            *[states] * len(before),
+            *[pl.BlockSpec(memory_space=pl.ANY)] * len(shared),
         ],
         out_specs=[
-            by_rows(features),
-            by_rows(1),
-            by_rows(heads * HK),
-            by_rows(heads * HK),
-            by_rows(heads * HV),
-            pl.BlockSpec((heads, HK, HV), lambda r: (0, 0, 0)),
+            in_all(features),
+            in_all(heads * HK),
+            in_all(heads * HK),
+            in_all(heads * HV),
+            here(1),
+            states,
+            states,
         ],
         out_shape=[
             jax.ShapeDtypeStruct((rows, features), BF16),
-            jax.ShapeDtypeStruct((rows, 1), F32),
             jax.ShapeDtypeStruct((rows, heads * HK), BF16),
             jax.ShapeDtypeStruct((rows, heads * HK), BF16),
             jax.ShapeDtypeStruct((rows, heads * HV), BF16),
+            jax.ShapeDtypeStruct((own, 1), F32),
             jax.ShapeDtypeStruct((heads, HK, HV), F32),
-        ],
+            jax.ShapeDtypeStruct((heads, HK, HV), BF16),
+        ],
+        input_output_aliases={6 + len(blocks) + len(before) + i: i for i in range(len(shared))},
+        scratch_shapes=[pltpu.VMEM((features, outs), BF16), pltpu.SemaphoreType.DMA((3,))],
         cost_estimate=pl.CostEstimate(
-            flops=2 * rows * features * outs, bytes_accessed=2 * features * outs + 12 * rows * features, transcendentals=0
+            flops=2 * own * features * outs, bytes_accessed=2 * features * outs + 12 * own * features, transcendentals=0
         ),
         name="proj",
-    )(at, log_gamma, gain, w, cosine, sine, *blocks)
+    )(at, log_gamma, gain, w, cosine, sine, *blocks, *before, *shared)
 
 
 def product_kernel(x_ref, w_ref, out_ref):
@@ -313,15 +350,32 @@
 
 def mlp_kernel(units, count, at_ref, gain_ref, w_ref, *refs):
     blocks, grads = refs[:count], refs[count : 2 * count]
-    full_ref, hidden_ref, acts_ref, grad_ref, scale_ref, inner_ref, back_ref = refs[-7:]
+    full_ref, hidden_ref, acts_ref, grad_ref, scale_ref, inner_ref, back_ref, kept_ref, sems = refs[-9:]
     at, n = at_ref[0], count // 2 + 1
+    first = pl.program_id(0) == 0
+
+    def piece(i):
+        columns = slice(i * units, (i + 1) * units)
+        return pltpu.make_async_copy(w_ref.at[:, columns], kept_ref.at[:, columns], sems.at[i])
+
+    @pl.when(first)
+    def _():
+        for i in range(3):
+            piece(i).start()
+
     scale_ref[...] = fill_normed(at, blocks, gain_ref, full_ref)
     for k in range(n):
         grad_ref[:, columns_of(at, n, k, grads[0].shape[1])] = gathered(at, grads, k)
     x = full_ref[...]
-    gate = nn(x, w_ref[:, :units])
-    up = nn(x, w_ref[:, units : 2 * units])
-    grad = nn(grad_ref[...], w_ref[:, 2 * units :])
+
+    @pl.when(first)
+    def _():
+        for i in range(3):
+            piece(i).wait()
+
+    gate = nn(x, kept_ref[:, :units])
+    up = nn(x, kept_ref[:, units : 2 * units])
+    grad = nn(grad_ref[...], kept_ref[:, 2 * units :])
     cdf = 0.5 * (1.0 + lax.erf(gate * math.sqrt(0.5)))
     gelu = gate * cdf
     density = jnp.exp(-0.5 * gate * gate) * (1.0 / math.sqrt(2.0 * math.pi))
@@ -331,7 +385,7 @@
     acts_ref[:, :units] = g_gate
     acts_ref[:, units:] = g_up
     inner_ref[...] = jnp.sum(g_gate.astype(F32) * gate + g_up.astype(F32) * up, axis=1, keepdims=True)
-    back_ref[...] = (nt(g_gate, w_ref[:, :units]) + nt(g_up, w_ref[:, units : 2 * units])).astype(BF16)
+    back_ref[...] = (nt(g_gate, kept_ref[:, :units]) + nt(g_up, kept_ref[:, units : 2 * units])).astype(BF16)
 
 
 def mlp(at, gain, w, part, grads, x, pairs, shared):
@@ -339,14 +393,15 @@
     features = w.shape[0]
     units = w.shape[1] // 3
     blocks = flat(x, pairs)
-    steps = rows // BLOCK
+    block = BLOCK // 2
+    steps = rows // block
     total = grads[0].shape[0]
 
     def by_rows(columns):
-        return pl.BlockSpec((BLOCK, columns), lambda r: (r, 0))
+        return pl.BlockSpec((block, columns), lambda r: (r, 0))
 
     def own_rows(columns):
-        return pl.BlockSpec((BLOCK, columns), lambda r: (part * steps + r, 0))
+        return pl.BlockSpec((block, columns), lambda r: (part * steps + r, 0))
 
     return pl.pallas_call(
         lambda *refs: mlp_kernel(units, len(blocks), *refs),
@@ -354,7 +409,7 @@
         in_specs=[
             pl.BlockSpec(memory_space=pltpu.SMEM),
             pl.BlockSpec((1, features), lambda r: (0, 0)),
-            pl.BlockSpec((features, 3 * units), lambda r: (0, 0)),
+            pl.BlockSpec(memory_space=pl.ANY),
             *[by_rows(width)] * len(blocks),
             *[own_rows(width)] * len(grads),
             *[pl.BlockSpec(memory_space=pl.ANY)] * len(shared),
@@ -378,6 +433,7 @@
             jax.ShapeDtypeStruct((rows, features), BF16),
         ],
         input_output_aliases={3 + 2 * len(blocks) + i: i for i in range(len(shared))},
+        scratch_shapes=[pltpu.VMEM((features, 3 * units), BF16), pltpu.SemaphoreType.DMA((3,))],
         cost_estimate=pl.CostEstimate(
             flops=10 * rows * features * units,
             bytes_accessed=6 * features * units + 14 * rows * features,
@@ -406,12 +462,12 @@
     return slice(r * BLOCK, (r + 1) * BLOCK)
 
 
-def forward_kernel(first, count, lg_ref, q_ref, k_ref, v_ref, gate_ref, state_ref, w_ref, *refs):
+def forward_kernel(first, count, n_pieces, lg_ref, factor_ref, q_ref, k_ref, v_ref, gate_ref, w_ref, *refs):
     gated_ref, ret_ref, out_ref, acc_ref = refs[-4:]
     head = pl.program_id(0)
     log_gamma = lg_ref[head]
     down, across = decay_vectors(log_gamma)
-    state = state_ref[0]
+    state = whole_state(refs[:n_pieces], factor_ref, head)
     for at in range(count):
         r = first + at
         q = q_ref[cut(at), :]
@@ -439,7 +495,7 @@
             out_ref[cut(at), :] = acc_ref[cut(at), :].astype(BF16)
 
 
-def retention_forward(part, parts, log_gamma, q, k, v, gate, state, w, first_column, shared):
+def retention_forward(part, parts, log_gamma, q, k, v, gate, pieces, factors, w, shared):
     rows = q.shape[0]
     heads = q.shape[1] // HK
     features = w.shape[0]
@@ -450,20 +506,21 @@
     flops = heads * (pairs * 2 * BLOCK * BLOCK * (HK + HV) + 2 * own * HK * HV + 2 * own * HV * features)
     head_out = pl.BlockSpec((own, HV), lambda h: (part, h))
     return pl.pallas_call(
-        lambda *refs: forward_kernel(part * count, count, *refs),
+        lambda *refs: forward_kernel(part * count, count, len(pieces), *refs),
         grid=(heads,),
         in_specs=[
+            pl.BlockSpec(memory_space=pltpu.SMEM),
             pl.BlockSpec(memory_space=pltpu.SMEM),
             pl.BlockSpec((own, HK), lambda h: (part, h)),
             pl.BlockSpec((seen, HK), lambda h: (0, h)),
             pl.BlockSpec((seen, HV), lambda h: (0, h)),
             pl.BlockSpec((own, HV), lambda h: (part, h)),
-            pl.BlockSpec((1, HK, HV), lambda h: (h, 0, 0)),
-            pl.BlockSpec((features, HV), lambda h: (0, first_column // HV + h)),
+            pl.BlockSpec((features, HV), lambda h: (0, h)),
+            *[pl.BlockSpec((1, HK, HV), lambda h: (h, 0, 0))] * len(pieces),
             *[pl.BlockSpec(memory_space=pl.ANY)] * len(shared),
         ],
         out_specs=[head_out, head_out, pl.BlockSpec((own, features), lambda h: (0, 0))],
-        input_output_aliases={7 + i: i for i in range(len(shared))},
+        input_output_aliases={7 + len(pieces) + i: i for i in range(len(shared))},
         out_shape=[
             jax.ShapeDtypeStruct((rows, heads * HV), BF16),
             jax.ShapeDtypeStruct((rows, heads * HV), F32),
@@ -472,18 +529,18 @@
         scratch_shapes=[pltpu.VMEM((own, features), F32)],
         cost_estimate=pl.CostEstimate(flops=flops, bytes_accessed=20 * own * heads * HV, transcendentals=own * heads * HV),
         name="fwd",
-    )(log_gamma, q, k, v, gate, state, w, *shared)
+    )(log_gamma, factors, q, k, v, gate, w, *pieces, *shared)
 
 
 def gate_backward_kernel(first, count, n_blocks, at_ref, lg_ref, q_ref, w_ref, gate_ref, ret_ref, *refs):
-    blocks, (g_gate_ref, g_ret_ref, full_ref, state_ref, inner_ref) = refs[:n_blocks], refs[-5:]
+    blocks, (g_gate_ref, g_ret_ref, full_ref, state_ref, rounded_ref, inner_ref) = refs[:n_blocks], refs[-6:]
     head = pl.program_id(0)
     log_gamma = lg_ref[head]
     down, _ = decay_vectors(log_gamma)
     n = n_blocks // 2 + 1
     width = blocks[0].shape[1]
     here = at_ref[0]
-    state = None
+    state = refs[n_blocks][0] if first else None
     for at in range(count):
         r = first + at
 
@@ -508,9 +565,10 @@
         add = tn(q, g_ret)
         state = add if state is None else state + add
     state_ref[0] = state
-
-
-def gate_backward(part, parts, here, log_gamma, q, w, first_column, gate, ret, x, pairs, shared):
+    rounded_ref[0] = state.astype(BF16)
+
+
+def gate_backward(part, parts, here, log_gamma, q, w, gate, ret, x, pairs, shared, state):
     rows = q.shape[0]
     heads = q.shape[1] // HK
     features = w.shape[0]
@@ -518,6 +576,8 @@
     count = own // BLOCK
     blocks = flat(x, pairs)
     head_out = pl.BlockSpec((own, HV), lambda h: (part, h))
+    head_state = pl.BlockSpec((1, HK, HV), lambda h: (h, 0, 0))
+    before = [state] if part else []
     return pl.pallas_call(
         lambda *refs: gate_backward_kernel(part * count, count, len(blocks), *refs),
         grid=(heads,),
@@ -525,25 +585,28 @@
             pl.BlockSpec(memory_space=pltpu.SMEM),
             pl.BlockSpec(memory_space=pltpu.SMEM),
             pl.BlockSpec((own, HK), lambda h: (part, h)),
-            pl.BlockSpec((features, HV), lambda h: (0, first_column // HV + h)),
+            pl.BlockSpec((features, HV), lambda h: (0, h)),
             head_out,
             head_out,
             *[pl.BlockSpec((own, x.shape[1]), lambda h: (0, 0))] * len(blocks),
+            *[head_state] * len(before),
             *[pl.BlockSpec(memory_space=pl.ANY)] * len(shared),
         ],
         out_specs=[
             head_out,
             head_out,
             pl.BlockSpec((own, features), lambda h: (part, 0)),
-            pl.BlockSpec((1, HK, HV), lambda h: (h, 0, 0)),
+            head_state,
+            head_state,
             pl.BlockSpec((1, own, 1), lambda h: (h, 0, 0)),
         ],
-        input_output_aliases={6 + len(blocks) + i: i for i in range(len(shared))},
+        input_output_aliases={6 + len(blocks) + len(before) + i: i for i in range(len(shared))},
         out_shape=[
             jax.ShapeDtypeStruct((rows, heads * HV), BF16),
             jax.ShapeDtypeStruct((rows, heads * HV), BF16),
             jax.ShapeDtypeStruct((rows, features), BF16),
             jax.ShapeDtypeStruct((heads, HK, HV), F32),
+            jax.ShapeDtypeStruct((heads, HK, HV), BF16),
             jax.ShapeDtypeStruct((heads, own, 1), F32),
         ],
         cost_estimate=pl.CostEstimate(
@@ -552,15 +615,16 @@
             transcendentals=own * heads * HV,
         ),
         name="gate",
-    )(here, log_gamma, q, w, gate, ret, *blocks, *shared)
-
-
-def backward_kernel(total, lg_ref, q_ref, k_ref, v_ref, state_in_ref, state_grad_ref, cos_ref, sin_ref, *refs):
-    g_ref, gate_ref, all_ref, inner_ref, acc_k, acc_v, g_q_ref, g_k_ref, g_v_ref, sems = refs
+    )(here, log_gamma, q, w, gate, ret, *blocks, *before, *shared)
+
+
+def backward_kernel(total, n_pieces, lg_ref, in_ref, out_ref, q_ref, k_ref, v_ref, cos_ref, sin_ref, *refs):
+    earlier, later = refs[:n_pieces], refs[n_pieces : 2 * n_pieces]
+    g_ref, gate_ref, all_ref, inner_ref, acc_k, acc_v, g_q_ref, g_k_ref, g_v_ref, sems = refs[2 * n_pieces :]
     head, heads = pl.program_id(0), pl.num_programs(0)
     log_gamma = lg_ref[head]
     down, across = decay_vectors(log_gamma)
-    state_in, state_grad = state_in_ref[0], state_grad_ref[0]
+    state_in, state_grad = whole_state(earlier, in_ref, head), whole_state(later, out_ref, head)
     key_scale = 1.0 / math.sqrt(HK)
 
     def send(ref, column, width, i):
@@ -614,7 +678,7 @@
     return jnp.exp((start - m) * log_gamma)
 
 
-def retention_backward(log_gamma, q, k, v, state_in, state_grad, cosine, sine, g_ret, g_gate):
+def retention_backward(log_gamma, q, k, v, before, behind, factors, cosine, sine, g_ret, g_gate):
     rows = q.shape[0]
     heads = q.shape[1] // HK
     blocks = rows // BLOCK
@@ -625,17 +689,16 @@
     head_state = pl.BlockSpec((1, HK, HV), lambda h: (h, 0, 0))
     table = pl.BlockSpec((rows, HK), lambda h: (0, 0))
     return pl.pallas_call(
-        lambda *refs: backward_kernel(blocks, *refs),
+        lambda *refs: backward_kernel(blocks, len(before), *refs),
         grid=(heads,),
         in_specs=[
-            pl.BlockSpec(memory_space=pltpu.SMEM),
+            *[pl.BlockSpec(memory_space=pltpu.SMEM)] * 3,
             head_keys,
             head_keys,
             head_values,
-            head_state,
-            head_state,
             table,
             table,
+            *[head_state] * (2 * len(before)),
             head_values,
             head_values,
         ],
@@ -654,7 +717,7 @@
         ],
         cost_estimate=pl.CostEstimate(flops=flops, bytes_accessed=24 * rows * heads * HK, transcendentals=0),
         name="bwd",
-    )(log_gamma, q, k, v, state_in, state_grad, cosine, sine, g_ret, g_gate)
+    )(log_gamma, *factors, q, k, v, cosine, sine, *before, *behind, g_ret, g_gate)
 
 
 def on_device(
@@ -698,20 +761,42 @@
     cosine = jnp.cos(angles)
     sine = jnp.sin(angles) * jnp.where(jnp.arange(HK) % 2 == 0, -1.0, 1.0)[None, :]
     here = at_tp.reshape(1)
+    factors = state_factors(log_block, CTX)
     mlp_shard = side_by_side(w_gate, w_up, w_down)
 
-    pairs = line_gather(layer_input, TP, (cosine, sine, mlp_shard, log_gamma, gains))
-    normed, scale_attn, q, k, v, local_state = project(
-        here, log_gamma, gains[0:1], attn_full, layer_input, pairs, heads, cosine, sine
-    )
-    cot = after(cotangent, pairs[-1][0])
+    x_pairs = [
+        line_gather(layer_input[cuts[c]], TP, () if c else (cosine, sine, mlp_shard, log_gamma, gains, *factors))
+        for c in range(parts)
+    ]
+    tokens, scale_attn, local_state = [], [], None
+    for c in range(parts):
+        *tokens, scale, local_state, rounded = project(
+            c,
+            parts,
+            here,
+            log_gamma,
+            gains[0:1],
+            attn_full,
+            layer_input[cuts[c]],
+            x_pairs[c],
+            heads,
+            cosine,
+            sine,
+            tokens,
+            local_state,
+        )
+        scale_attn.append(scale)
+    normed, q, k, v = tokens
+    cot = after(cotangent, x_pairs[-1][-1][0])
     cot_blocks = flat(cot, line_gather(cot, TP))
     gate_pre = product(after(normed, local_state), attn_full, (2 * qk + vw) // vw, vw)
-    state_in = states_before(local_state, log_block, CTX).astype(BF16)
-    mlp_full = lax.all_gather(after(mlp_shard, state_in), data, axis=0, tiled=True)
+    earlier = states_before(local_state, rounded, log_block, CTX)
+    mlp_full = lax.all_gather(after(mlp_shard, earlier[-1]), data, axis=0, tiled=True)
     heads_out, branch = [], []
     for c in range(parts):
-        *heads_out, out = retention_forward(c, parts, log_gamma, q, k, v, gate_pre, state_in, out_full, 0, heads_out)
+        *heads_out, out = retention_forward(
+            c, parts, log_gamma, q, k, v, gate_pre, earlier, factors[0], out_full, heads_out
+        )
         branch.append(out)
     gated, retained = heads_out
 
@@ -766,31 +851,29 @@
     mlp_out = routed_scatter(after(mlp_parts, grad_pairs[-1][-1][0]), TP)
     layer_output = (jnp.concatenate(middle) + mlp_out).astype(BF16)
     shared = []
-    partial_state = 0.0
+    partial_state = None
     inner_attn = []
     for c in range(parts):
-        *shared, ps, inner = gate_backward(
+        *shared, partial_state, rounded, inner = gate_backward(
             c,
             parts,
             here,
             log_gamma,
             q,
             out_full,
-            0,
             gate_pre,
             retained,
             grad_own[c],
             grad_pairs[c],
             shared,
+            partial_state,
         )
-        partial_state = partial_state + ps
         inner_attn.append(jnp.sum(inner[:, :, 0], axis=0))
     g_gate, g_ret, grad_attn = shared
-    state_grad, got = states_after(partial_state, log_block, CTX)
-    state_grad = state_grad.astype(BF16)
-    grad_out = tn(after(grad_attn, got), gated).astype(BF16)
+    later = states_after(partial_state, rounded, log_block, CTX)
+    grad_out = tn(after(grad_attn, later[0]), gated).astype(BF16)
     grads_attn, inner = retention_backward(
-        log_gamma, q, k, v, state_in, after(state_grad, grad_out), cosine, sine, g_ret, g_gate
+        log_gamma, q, k, v, earlier, [after(later[0], grad_out), *later[1:]], factors, cosine, sine, g_ret, g_gate
     )
     inner_attn = jnp.concatenate(inner_attn) + jnp.sum(inner[:, :, 0], axis=0)
     back = []
@@ -817,7 +900,7 @@
     for c in range(parts):
         total, steps = line_scatter(after(back[c], *early), TP)
         early = steps[0]
-        grad_in, gain_sum = norm_back(x_own[cuts[c]], scale_attn[cuts[c]], gain_attn, inner_attn[cuts[c]], total)
+        grad_in, gain_sum = norm_back(x_own[cuts[c]], scale_attn[c], gain_attn, inner_attn[cuts[c]], total)
         grad_input.append((grad_middle[c] + grad_in).astype(BF16))
         gain_attn_sum = gain_attn_sum + gain_sum
     grad_input = jnp.concatenate(grad_input)

time: 829 us -> 830 us (level)
  starting transfers between devices: 180 us -> 198 us
  waiting for transfers between devices: 310 us -> 297 us
    ppermute x4 -> x16, starting transfers between devices: 2.05 us -> 34.5 us  [the longest x6 24.7 us: line_scatter(): from_left = lax.ppermute(data, axis, r_pairs)]
    ppermute x12 -> x6, starting transfers between devices: 62.6 us -> 40.2 us  [line_scatter(): from_left = lax.ppermute(r_data, axis, r_pairs)]
    ppermute x6 -> x7, waiting for transfers between devices: 31.1 us -> 17 us  [line_gather(): lax.ppermute(jnp.where(i >= k - 1, rights[-1], lefts[-1]), axis, r_pairs...]
    ppermute x12 -> x14, waiting for transfers between devices: 17 us -> 3.12 us  [line_gather(): rights.append(lax.ppermute(rights[-1], axis, r_pairs))]
    ppermute x4 -> x16, waiting for transfers between devices: 30.3 us -> 43.1 us  [the longest x2 16.2 us: states_after(): lax.ppermute(rounded if g == 1 else total.astype(BF16), axis, [(j, j ^ g)...]
    convert_element_type x11 -> x6, other arithmetic: 24 us -> 11.6 us  [line_scatter(): r_data = (r_data.astype(F32) + from_left.astype(F32)).astype(BF16)]
    ppermute x12 -> x6, starting transfers between devices: 17.3 us -> 7.85 us  [line_scatter(): from_right = lax.ppermute(l_data, axis, l_pairs)]
    ppermute x12 -> x14, waiting for transfers between devices: 92.5 us -> 85.4 us  [line_gather(): lefts.append(lax.ppermute(lefts[-1], axis, l_pairs))]
  transfers between devices with their start and end apart: 86 -> 91, of which waited for: 33 -> 34; matrix products, arithmetic and copies ran while one was open for 20% -> 18% of each run, Pallas kernels for 17% -> 18%
where the time goes in v6:
time: 830 us; the launch traced here: 824 us
  waiting for transfers between devices  297 us (36%)
  starting transfers between devices  198 us (24%)
  Pallas kernels  149 us (18%)
  matrix products  76.2 us (9%)
  other arithmetic  65.2 us (8%)
  local copies, waits for them, and re-layouts  23.6 us (3%)
  between operations  16.1 us (2%)
    ppermute x6, waiting for transfers between devices, line_scatter(): from_left = from_right = lax.ppermute(data, axis, r_pairs + l_pairs)  93.3 us
    ppermute x14, waiting for transfers between devices, line_gather(): lefts.append(lax.ppermute(lefts[-1], axis, l_pairs))  85.4 us
    dot_general x4, matrix products, tn(): lax.dot_general(a, b, (((0,), (0,)), ((), ())), preferred_element_type=F32)  44.9 us
    pallas_call x2, Pallas kernels, mlp(): pl.pallas_call(lambda *refs: mlp_kernel(units, len(blocks), *refs), grid=...  42.4 us
    ppermute x6, starting transfers between devices, line_scatter(): from_left = lax.ppermute(r_data, axis, r_pairs)  40.2 us
    ppermute x14, starting transfers between devices, line_gather(): rights.append(lax.ppermute(rights[-1], axis, r_pairs))  40.2 us
    dot_general x3, matrix products, nt(): lax.dot_general(a, b, (((1,), (1,)), ((), ())), preferred_element_type=F32)  31.3 us
    ppermute x9, waiting for transfers between devices, swap_sum(): x = x + lax.ppermute(x, axis, [(j, j ^ g) for j in range(n)])  28.1 us
  transfers between devices with their start and end apart: 91, of which 34 were waited for; matrix products, arithmetic and copies ran while one was open for 18% of the time, Pallas kernels for 18%

profile of v6, /device:TPU:0, one launch (start us, length us, event | category | flops | bytes accessed | tf_op | source)
XLA Modules:
  0.0 824.4 jit_solution(10223210260267207020)
XLA Ops:
  26.6 5.5 fusion.16
  38.3 5.4 collective-permute-start.2
  43.7 7.9 collective-permute-done.2
  55.6 15.6 %collective-permute-done.11.refs_10_ = bf16[512,512]{1,0:T(8,128)(2,1)S(1)} collective-permute-done((bf16[512,512]{1,0:T(8,128)(2,1)}, bf16[512,512]{1,0:T(8,128)(2,1)S(1)}, u32[]{:S(2)}, u32[]{:S(2)}) %collective-permute-start.11) | collective-permute-done | bytes 524320 | tf_op jit(solution)/shard_map/ppermute | solution.py:58
  72.6 9.8 %collective-permute-done.6.refs_10_ = bf16[512,512]{1,0:T(8,128)(2,1)S(1)} collective-permute-done((bf16[512,512]{1,0:T(8,128)(2,1)}, bf16[512,512]{1,0:T(8,128)(2,1)S(1)}, u32[]{:S(2)}, u32[]{:S(2)}) %collective-permute-start.6) | collective-permute-done | bytes 524320 | tf_op jit(solution)/shard_map/ppermute | solution.py:58
  85.5 8.2 collective-permute-done.12.refs_8_.refs_11_
  94.5 12.6 %proj.2 = (bf16[1024,2048]{1,0:T(8,128)(2,1)}, bf16[1024,512]{1,0:T(8,128)(2,1)}, bf16[1024,512]{1,0:T(8,128)(2,1)}, bf16[1024,1024]{1,0:T(8,128)(2,1)}, f32[512...) custom-call(s32[1]{0:T(128)} %bitcast.refs_0_, f32[2]{0:T(128)} %negate_log-plus-one_fusion.1.refs_1_.refs_0_, ...), custom_call_target="tpu_custom_call" | custom-call | flops 4294967296 | bytes 20971520 | tf_op jit(solution)/shard_map/proj/pallas_call | solution.py:288
  107.9 13.8 %proj.3 = (bf16[1024,2048]{1,0:T(8,128)(2,1)}, bf16[1024,512]{1,0:T(8,128)(2,1)}, bf16[1024,512]{1,0:T(8,128)(2,1)}, bf16[1024,1024]{1,0:T(8,128)(2,1)}, f32[512...) custom-call(s32[1]{0:T(128)} %bitcast.refs_0_, ...), custom_call_target="tpu_custom_call", output_to_operand_aliasing={{0}: (14, {}), {1}: (15, {}), {2}: (16, {}), {3}: (17, {})} | custom-call | flops 4294967296 | bytes 20971520 | tf_op jit(solution)/shard_map/proj/pallas_call | solution.py:288
  127.3 12.6 %collective-permute-done.14.refs_8_.refs_9_ = bf16[2,256,512]{2,1,0:T(8,128)(2,1)S(1)} collective-permute-done((bf16[2,256,512]{2,1,0:T(8,128)(2,1)S(1)}, bf16[2,256,512]{2,1,0:T(8,128)(2,1)S(1)}, u32[]{:S(2)}, u32[]{:S(2)}) %collective-permute-start.14) | collective-permute-done | bytes 524320 | tf_op jit(solution)/shard_map/ppermute | solution.py:152
  140.1 8.8 %prod.1.refs_5_.refs_4_ = f32[1024,1024]{1,0:T(8,128)} custom-call(bf16[1024,2048]{1,0:T(8,128)(2,1)} %get-tuple-element.89.x_ref, bf16[2048,3072]{1,0:T(8,128)(2,1)} %all-gather.4.cloned.1.call-done.refs_3_.w_ref), custom_call_target="tpu_custom_call" | custom-call | flops 4294967296 | bytes 12582912 | tf_op jit(solution)/shard_map/prod/pallas_call | solution.py:335
  149.0 9.4 %fwd.2 = (bf16[1024,1024]{1,0:T(8,128)(2,1)}, f32[1024,1024]{1,0:T(8,128)}, bf16[512,2048]{1,0:T(8,128)(2,1)}) custom-call(f32[2]{0:T(128)} %negate_log-plus-one_fusion.1.refs_1_.refs_0_, f32[2,2]{1,0:T(2,128)} %pad_maximum_fusion.3.refs_1_, bf16[1024,512]{1,0:T(8,128)(2,1)} %get-tuple-element.86.refs_2_.refs_3_, ...), custom_call_target="tpu_custom_call" | custom-call | flops 3221225472 | bytes 10485760 | tf_op jit(solution)/shard_map/fwd/pallas_call | solution.py:508
  160.9 11.0 %collective-permute-done.15 = bf16[512,512]{1,0:T(8,128)(2,1)S(1)} collective-permute-done((bf16[512,512]{1,0:T(8,128)(2,1)S(1)}, bf16[512,512]{1,0:T(8,128)(2,1)S(1)}, u32[]{:S(2)}, u32[]{:S(2)}) %collective-permute-start.15) | collective-permute-done | bytes 524320 | tf_op jit(solution)/shard_map/ppermute | solution.py:88
  183.3 10.7 %fwd.3 = (bf16[1024,1024]{1,0:T(8,128)(2,1)}, f32[1024,1024]{1,0:T(8,128)}, bf16[512,2048]{1,0:T(8,128)(2,1)}) custom-call(f32[2]{0:T(128)} %negate_log-plus-one_fusion.1.refs_1_.refs_0_, f32[2,2]{1,0:T(2,128)} %pad_maximum_fusion.3.refs_1_, bf16[1024,512]{1,0:T(8,128)(2,1)} %get-tuple-element.86.refs_2_.refs_3_, ...), custom_call_target="tpu_custom_call", output_to_operand_aliasing={{0}: (9, {}), {1}: (10, {})} | custom-call | flops 4026531840 | bytes 10485760 | tf_op jit(solution)/shard_map/fwd/pallas_call | solution.py:508
  204.2 5.4 collective-permute-start.17
  215.6 8.2 collective-permute-done.37
  225.8 5.2 collective-permute-start.38
  250.5 15.3 %collective-permute-start.39 = (bf16[512,512]{1,0:T(8,128)(2,1)S(1)}, bf16[512,512]{1,0:T(8,128)(2,1)S(1)}, u32[]{:S(2)}, u32[]{:S(2)}) collective-permute-start(bf16[512,512]{1,0:T(8,128)(2,1)S(1)} %get-tuple-element.176), channel_id=1, source_target_pairs={{0,1},{1,2},{2,3},{4,5},{5,6},{6,7},{8,9},{9,10},{10,11},{12,13},{... | collective-permute-start | bytes 1572872 | tf_op jit(solution)/shard_map/ppermute | solution.py:102
  273.5 9.9 %collective-permute-done.41 = bf16[512,512]{1,0:T(8,128)(2,1)S(1)} collective-permute-done((bf16[512,512]{1,0:T(8,128)(2,1)S(1)}, bf16[512,512]{1,0:T(8,128)(2,1)S(1)}, u32[]{:S(2)}, u32[]{:S(2)}) %collective-permute-start.41) | collective-permute-done | bytes 524320 | tf_op jit(solution)/shard_map/ppermute | solution.py:103
  284.0 5.2 collective-permute-start.42
  290.9 26.2 %collective-permute-done.23.refs_7_ = bf16[512,512]{1,0:T(8,128)(2,1)S(1)} collective-permute-done((bf16[512,512]{1,0:T(8,128)(2,1)S(1)}, bf16[512,512]{1,0:T(8,128)(2,1)S(1)}, u32[]{:S(2)}, u32[]{:S(2)}) %collective-permute-start.23) | collective-permute-done | bytes 524320 | tf_op jit(solution)/shard_map/ppermute | solution.py:58
  320.0 8.5 %collective-permute-done.44.refs_9_ = bf16[512,512]{1,0:T(8,128)(2,1)} collective-permute-done((bf16[512,512]{1,0:T(8,128)(2,1)S(1)}, bf16[512,512]{1,0:T(8,128)(2,1)}, u32[]{:S(2)}, u32[]{:S(2)}) %collective-permute-start.44) | collective-permute-done | bytes 524320 | tf_op jit(solution)/shard_map/ppermute | solution.py:58
  330.8 8.8 %collective-permute-done.24.refs_5_.refs_8_ = bf16[512,512]{1,0:T(8,128)(2,1)S(1)} collective-permute-done((bf16[512,512]{1,0:T(8,128)(2,1)S(1)}, bf16[512,512]{1,0:T(8,128)(2,1)S(1)}, u32[]{:S(2)}, u32[]{:S(2)}) %collective-permute-start.24) | collective-permute-done | bytes 524320 | tf_op jit(solution)/shard_map/ppermute | solution.py:53
  340.4 21.1 %mlp.2 = (bf16[1024,2048]{1,0:T(8,128)(2,1)}, bf16[1024,1024]{1,0:T(8,128)(2,1)}, bf16[1024,2048]{1,0:T(8,128)(2,1)}, bf16[1024,2048]{1,0:T(8,128)(2,1)}, f32[51...) custom-call(s32[1]{0:T(128)} %bitcast.refs_0_, f32[1,2048]{1,0:T(1,128)} %get-tuple-element.186.refs_1_, ...), custom_call_target="tpu_custom_call" | custom-call | flops 10737418240 | bytes 27262976 | tf_op jit(solution)/shard_map/mlp/pallas_call | solution.py:406
  366.7 8.6 %collective-permute-done.30 = bf16[512,512]{1,0:T(8,128)(2,1)S(1)} collective-permute-done((bf16[512,512]{1,0:T(8,128)(2,1)S(1)}, bf16[512,512]{1,0:T(8,128)(2,1)S(1)}, u32[]{:S(2)}, u32[]{:S(2)}) %collective-permute-start.30) | collective-permute-done | bytes 524320 | tf_op jit(solution)/shard_map/ppermute | solution.py:88
  376.4 5.2 collective-permute-start.31
  384.0 21.2 %mlp.3 = (bf16[1024,2048]{1,0:T(8,128)(2,1)}, bf16[1024,1024]{1,0:T(8,128)(2,1)}, bf16[1024,2048]{1,0:T(8,128)(2,1)}, bf16[1024,2048]{1,0:T(8,128)(2,1)}, f32[51...) custom-call(s32[1]{0:T(128)} %bitcast.refs_0_, ...), custom_call_target="tpu_custom_call", output_to_operand_aliasing={{0}: (17, {}), {1}: (18, {}), {2}: (19, {}), {3}: (20, {})} | custom-call | flops 10737418240 | bytes 27262976 | tf_op jit(solution)/shard_map/mlp/pallas_call | solution.py:406
  409.4 9.4 %collective-permute-done.35 = f32[4,128]{1,0:T(4,128)S(1)} collective-permute-done((f32[4,128]{1,0:T(4,128)S(1)}, f32[4,128]{1,0:T(4,128)S(1)}, u32[]{:S(2)}, u32[]{:S(2)}) %collective-permute-start.35) | collective-permute-done | bytes 2080 | tf_op jit(solution)/shard_map/ppermute | solution.py:132
  418.8 6.1 collective-permute-start.36
  439.8 7.9 convolution_convert_fusion.3
  448.1 7.8 collective-permute-done.53
  460.1 5.8 collective-permute-start.54
  473.0 10.3 %collective-permute-done.58 = f32[4,128]{1,0:T(4,128)S(1)} collective-permute-done((f32[4,128]{1,0:T(4,128)S(1)}, f32[4,128]{1,0:T(4,128)S(1)}, u32[]{:S(2)}, u32[]{:S(2)}) %collective-permute-start.58) | collective-permute-done | bytes 2080 | tf_op jit(solution)/shard_map/ppermute | solution.py:132
  487.9 10.3 %collective-permute-start.59 = (bf16[512,512]{1,0:T(8,128)(2,1)S(1)}, bf16[512,512]{1,0:T(8,128)(2,1)S(1)}, u32[]{:S(2)}, u32[]{:S(2)}) collective-permute-start(bf16[512,512]{1,0:T(8,128)(2,1)S(1)} %fusion.19.refs_6_), channel_id=1, source_target_pairs={{0,1},{1,2},{2,3},{4,5},{5,6},{6,7},{8,9},{9,10},{10,11},{12,13},{... | collective-permute-start | bytes 1572872 | tf_op jit(solution)/shard_map/ppermute | solution.py:57
  500.6 5.3 collective-permute-done.49.refs_12_
  507.9 9.2 %collective-permute-done.61.refs_12_ = bf16[512,512]{1,0:T(8,128)(2,1)S(1)} collective-permute-done((bf16[512,512]{1,0:T(8,128)(2,1)S(1)}, bf16[512,512]{1,0:T(8,128)(2,1)S(1)}, u32[]{:S(2)}, u32[]{:S(2)}) %collective-permute-start.61) | collective-permute-done | bytes 524320 | tf_op jit(solution)/shard_map/ppermute | solution.py:58
  530.8 11.4 %convolution_convert_fusion.1 = bf16[2048,2048]{1,0:T(8,128)(2,1)} fusion(bf16[1024,2048]{1,0:T(8,128)(2,1)S(1)} %copy-done.55, bf16[1024,2048]{1,0:T(8,128)(2,1)S(1)} %copy-done.56), kind=kOutput, calls=%fused_computation.1 | convolution fusion | flops 8594128896 | bytes 16777216 | tf_op jit(solution)/shard_map/dot_general | solution.py:25
  542.2 10.9 %gate.2 = (bf16[1024,1024]{1,0:T(8,128)(2,1)}, bf16[1024,1024]{1,0:T(8,128)(2,1)}, bf16[1024,2048]{1,0:T(8,128)(2,1)}, f32[2,256,512]{2,1,0:T(8,128)}, bf16[2,25...) custom-call(s32[1]{0:T(128)} %bitcast.refs_0_, f32[2]{0:T(128)} %negate_log-plus-one_fusion.1.refs_1_.refs_0_, ...), custom_call_target="tpu_custom_call" | custom-call | flops 2415919104 | bytes 8388608 | tf_op jit(solution)/shard_map/gate/pallas_call | solution.py:581
  553.1 11.4 %gate.3 = (bf16[1024,1024]{1,0:T(8,128)(2,1)}, bf16[1024,1024]{1,0:T(8,128)(2,1)}, bf16[1024,2048]{1,0:T(8,128)(2,1)}, f32[2,256,512]{2,1,0:T(8,128)}, bf16[2,25...) custom-call(s32[1]{0:T(128)} %bitcast.refs_0_, ...), custom_call_target="tpu_custom_call", output_to_operand_aliasing={{0}: (14, {}), {1}: (15, {}), {2}: (16, {})} | custom-call | flops 2415919104 | bytes 8388608 | tf_op jit(solution)/shard_map/gate/pallas_call | solution.py:581
  566.9 9.4 %convolution_convert_fusion.2 = bf16[2048,1024]{1,0:T(8,128)(2,1)} fusion(bf16[1024,2048]{1,0:T(8,128)(2,1)} %get-tuple-element.128, bf16[1024,1024]{1,0:T(8,128)(2,1)} %get-tuple-element.129), kind=kOutput, calls=%fused_computation.5 | convolution fusion | flops 4297064448 | bytes 10485760 | tf_op jit(solution)/shard_map/dot_general | solution.py:25
  578.6 14.0 %collective-permute-done.65.refs_11_ = bf16[2,256,512]{2,1,0:T(8,128)(2,1)S(1)} collective-permute-done((bf16[2,256,512]{2,1,0:T(8,128)(2,1)S(1)}, bf16[2,256,512]{2,1,0:T(8,128)(2,1)S(1)}, u32[]{:S(2)}, u32[]{:S(2)}) %collective-permute-start.65) | collective-permute-done | bytes 524320 | tf_op jit(solution)/shard_map/ppermute | solution.py:166
  593.3 21.4 %bwd.1 = (bf16[1024,3072]{1,0:T(8,128)(2,1)}, f32[2,1024,1]{2,1,0:T(8,128)}) custom-call(f32[2]{0:T(128)} %negate_log-plus-one_fusion.1.refs_1_.refs_0_, f32[2,2]{1,0:T(2,128)} %pad_maximum_fusion.3.refs_1_, f32[2,2]{1,0:T(2,128)} %pad_maximum_fusion.4.refs_2_, bf16[1024,512]{1,0:T(8,128)(2,1)} %get-tuple-element.86.refs_2_.refs_3_, ...), custom_call_target="tpu_custom_call" | custom-call | flops 7247757312 | bytes 12582912 | tf_op jit(solution)/shard_map/bwd/pallas_call | solution.py:691
  614.7 12.2 %fusion.12 = bf16[512,2048]{1,0:T(8,128)(2,1)} fusion(bf16[2048,3072]{1,0:T(8,128)(2,1)} %all-gather.4.cloned.1.call-done.refs_3_.w_ref, bf16[1024,3072]{1,0:T(8,128)(2,1)} %get-tuple-element.142), kind=kOutput, calls=%fused_computation.12 | convolution fusion | flops 6443499520 | bytes 17825792 | tf_op jit(solution)/shard_map/dot_general | solution.py:29
  626.9 16.2 %convolution_convert_fusion = bf16[2048,3072]{1,0:T(8,128)(2,1)} fusion(bf16[1024,2048]{1,0:T(8,128)(2,1)S(1)} %copy-done.2, bf16[1024,3072]{1,0:T(8,128)(2,1)S(1)} %copy-done.58), kind=kOutput, calls=%fused_computation | convolution fusion | flops 12891193344 | bytes 23068672 | tf_op jit(solution)/shard_map/dot_general | solution.py:25
  643.1 8.2 fusion.2
  654.5 5.3 collective-permute-start.67
  662.4 10.9 %fusion.9 = bf16[512,2048]{1,0:T(8,128)(2,1)S(1)} fusion(bf16[2048,3072]{1,0:T(8,128)(2,1)} %all-gather.4.cloned.1.call-done.refs_3_.w_ref, bf16[1024,3072]{1,0:T(8,128)(2,1)} %get-tuple-element.142), kind=kOutput, calls=%fused_computation.11 | convolution fusion | flops 6443499520 | bytes 17825792 | tf_op jit(solution)/shard_map/dot_general | solution.py:29
  673.3 59.8 %collective-permute-done.69 = bf16[512,512]{1,0:T(8,128)(2,1)S(1)} collective-permute-done((bf16[512,512]{1,0:T(8,128)(2,1)S(1)}, bf16[512,512]{1,0:T(8,128)(2,1)S(1)}, u32[]{:S(2)}, u32[]{:S(2)}) %collective-permute-start.69) | collective-permute-done | bytes 524320 | tf_op jit(solution)/shard_map/ppermute | solution.py:88
  743.9 5.8 collective-permute-done.76
  (366 shorter events, 259.3 us)
Async XLA Ops:
  7.2 86.5 %all-gather.4.cloned.1.call-start = ((), (), s32[]{:S(2)}) async-start(), calls=%async_computation.4 | async-start | bytes 14155776 | tf_op jit(solution)/shard_map/all_gather | solution.py:751
  11.0 137.9 %all-gather.6.cloned.1.call-start = ((), (), s32[]{:S(2)}) async-start(), calls=%async_computation.5 | async-start | bytes 4718592 | tf_op jit(solution)/shard_map/all_gather | solution.py:752
  11.8 327.9 %all-gather.8.cloned.1.call-start = ((), (), s32[]{:S(2)}) async-start(), calls=%async_computation.6 | async-start | bytes 14155776 | tf_op jit(solution)/shard_map/all_gather | solution.py:794
  11.9 25.1 %collective-permute-start = (f32[2,512]{1,0:T(2,128)S(1)}, f32[2,512]{1,0:T(2,128)S(1)}, u32[]{:S(2)}, u32[]{:S(2)}) collective-permute-start(f32[2,512]{1,0:T(2,128)S(1)} %get-tuple-element.194), channel_id=1, source_target_pairs={{0,1},{1,2},{2,3},{3,0},{4,5},{5,6},{6,7},{7,4},{8,9},{9,10},{10,1... | collective-permute-start | bytes 12296 | tf_op jit(solution)/shard_map/ppermute | solution.py:124
  15.0 23.3 %collective-permute-start.1 = (f32[2,512]{1,0:T(2,128)S(1)}, f32[2,512]{1,0:T(2,128)S(1)}, u32[]{:S(2)}, u32[]{:S(2)}) collective-permute-start(f32[2,512]{1,0:T(2,128)S(1)} %get-tuple-element.194), channel_id=1, source_target_pairs={{0,2},{1,3},{2,0},{3,1},{4,6},{5,7},{6,4},{7,5},{8,10},{9,11},{10,... | collective-permute-start | bytes 12296 | tf_op jit(solution)/shard_map/ppermute | solution.py:124
  17.7 33.9 %collective-permute-start.8 = (bf16[512,512]{1,0:T(8,128)(2,1)S(1)}, bf16[512,512]{1,0:T(8,128)(2,1)S(1)}, u32[]{:S(2)}, u32[]{:S(2)}) collective-permute-start(bf16[512,512]{1,0:T(8,128)(2,1)S(1)} %get-tuple-element.184.refs_6_), channel_id=1, source_target_pairs={{0,1},{1,2},{2,3},{4,5},{5,6},{6,7},{8,9},{9,10},{10,11},{12,13},{... | collective-permute-start | bytes 1572872 | tf_op jit(solution)/shard_map/ppermute | solution.py:57
  19.7 32.6 %collective-permute-start.10 = (bf16[512,512]{1,0:T(8,128)(2,1)S(1)}, bf16[512,512]{1,0:T(8,128)(2,1)}, u32[]{:S(2)}, u32[]{:S(2)}) collective-permute-start(bf16[512,512]{1,0:T(8,128)(2,1)S(1)} %get-tuple-element.184.refs_6_), channel_id=1, source_target_pairs={{3,2},{2,1},{1,0},{7,6},{6,5},{5,4},{11,10},{10,9},{9,8},{15,14},{... | collective-permute-start | bytes 1572872 | tf_op jit(solution)/shard_map/ppermute | solution.py:58
  21.0 32.6 %collective-permute-start.3 = (bf16[512,512]{1,0:T(8,128)(2,1)S(1)}, bf16[512,512]{1,0:T(8,128)(2,1)S(1)}, u32[]{:S(2)}, u32[]{:S(2)}) collective-permute-start(bf16[512,512]{1,0:T(8,128)(2,1)S(1)} %get-tuple-element.185.refs_6_), channel_id=1, source_target_pairs={{0,1},{1,2},{2,3},{4,5},{5,6},{6,7},{8,9},{9,10},{10,11},{12,13},{... | collective-permute-start | bytes 1572872 | tf_op jit(solution)/shard_map/ppermute | solution.py:57
  54.3 28.2 %collective-permute-start.6 = (bf16[512,512]{1,0:T(8,128)(2,1)}, bf16[512,512]{1,0:T(8,128)(2,1)S(1)}, u32[]{:S(2)}, u32[]{:S(2)}) collective-permute-start(bf16[512,512]{1,0:T(8,128)(2,1)} %collective-permute-done.5.refs_12_), channel_id=1, source_target_pairs={{2,1},{1,0},{6,5},{5,4},{10,9},{9,8},{14,13},{13,12},{18,17},{17,1... | collective-permute-start | bytes 1572872 | tf_op jit(solution)/shard_map/ppermute | solution.py:58
  83.4 23.7 %collective-permute-start.7 = (bf16[512,512]{1,0:T(8,128)(2,1)}, bf16[512,512]{1,0:T(8,128)(2,1)S(1)}, u32[]{:S(2)}, u32[]{:S(2)}) collective-permute-start(bf16[512,512]{1,0:T(8,128)(2,1)} %broadcast_select_fusion.8), channel_id=1, source_target_pairs={{2,3},{1,0},{6,7},{5,4},{10,11},{9,8},{14,15},{13,12},{18,19},{17,... | collective-permute-start | bytes 1572872 | tf_op jit(solution)/shard_map/ppermute | solution.py:53
  139.9 627.0 %reduce-scatter.5.cloned.1.call-start = ((), (), s32[]{:S(2)}) async-start(), calls=%async_computation.7 | async-start | bytes 4718592 | tf_op jit(solution)/shard_map/reduce_scatter | solution.py:887
  179.2 33.4 %collective-permute-start.25 = (bf16[1024,512]{1,0:T(8,128)(2,1)}, bf16[1024,512]{1,0:T(8,128)(2,1)}, u32[]{:S(2)}, u32[]{:S(2)}) collective-permute-start(bf16[1024,512]{1,0:T(8,128)(2,1)} %refs_10_.1), channel_id=1, source_target_pairs={{0,1},{1,2},{2,3},{4,5},{5,6},{6,7},{8,9},{9,10},{10,11},{12,13},{... | collective-permute-start | bytes 3145736 | tf_op jit(solution)/shard_map/ppermute | solution.py:57
  182.0 32.3 %collective-permute-start.27 = (bf16[1024,512]{1,0:T(8,128)(2,1)}, bf16[1024,512]{1,0:T(8,128)(2,1)}, u32[]{:S(2)}, u32[]{:S(2)}) collective-permute-start(bf16[1024,512]{1,0:T(8,128)(2,1)} %refs_10_.1), channel_id=1, source_target_pairs={{3,2},{2,1},{1,0},{7,6},{6,5},{5,4},{11,10},{10,9},{9,8},{15,14},{... | collective-permute-start | bytes 3145736 | tf_op jit(solution)/shard_map/ppermute | solution.py:58
  195.9 27.9 %collective-permute-start.37 = (bf16[512,512]{1,0:T(8,128)(2,1)S(1)}, bf16[512,512]{1,0:T(8,128)(2,1)S(1)}, u32[]{:S(2)}, u32[]{:S(2)}) collective-permute-start(bf16[512,512]{1,0:T(8,128)(2,1)S(1)} %constant_dynamic-slice_fusion.6), channel_id=1, source_target_pairs={{0,1},{3,2},{4,5},{7,6},{8,9},{11,10},{12,13},{15,14},{16,17},{19,... | collective-permute-start | bytes 1572872 | tf_op jit(solution)/shard_map/ppermute | solution.py:88
  202.9 28.1 %collective-permute-start.19 = (bf16[512,512]{1,0:T(8,128)(2,1)S(1)}, bf16[512,512]{1,0:T(8,128)(2,1)}, u32[]{:S(2)}, u32[]{:S(2)}) collective-permute-start(bf16[512,512]{1,0:T(8,128)(2,1)S(1)} %get-tuple-element.175), channel_id=1, source_target_pairs={{3,2},{2,1},{1,0},{7,6},{6,5},{5,4},{11,10},{10,9},{9,8},{15,14},{... | collective-permute-start | bytes 1572872 | tf_op jit(solution)/shard_map/ppermute | solution.py:103
  204.2 30.9 %collective-permute-start.17 = (bf16[512,512]{1,0:T(8,128)(2,1)}, bf16[512,512]{1,0:T(8,128)(2,1)}, u32[]{:S(2)}, u32[]{:S(2)}) collective-permute-start(bf16[512,512]{1,0:T(8,128)(2,1)} %get-tuple-element.174), channel_id=1, source_target_pairs={{0,1},{1,2},{2,3},{4,5},{5,6},{6,7},{8,9},{9,10},{10,11},{12,13},{... | collective-permute-start | bytes 1572872 | tf_op jit(solution)/shard_map/ppermute | solution.py:102
  212.6 37.9 %collective-permute-start.26 = (bf16[1024,512]{1,0:T(8,128)(2,1)}, bf16[1024,512]{1,0:T(8,128)(2,1)}, u32[]{:S(2)}, u32[]{:S(2)}) collective-permute-start(bf16[1024,512]{1,0:T(8,128)(2,1)} %collective-permute-done.25.refs_11_), channel_id=1, source_target_pairs={{1,2},{2,3},{5,6},{6,7},{9,10},{10,11},{13,14},{14,15},{17,18},{18... | collective-permute-start | bytes 3145736 | tf_op jit(solution)/shard_map/ppermute | solution.py:57
  214.3 51.6 %collective-permute-start.28 = (bf16[1024,512]{1,0:T(8,128)(2,1)}, bf16[1024,512]{1,0:T(8,128)(2,1)}, u32[]{:S(2)}, u32[]{:S(2)}) collective-permute-start(bf16[1024,512]{1,0:T(8,128)(2,1)} %collective-permute-done.27.refs_16_), channel_id=1, source_target_pairs={{2,1},{1,0},{6,5},{5,4},{10,9},{9,8},{14,13},{13,12},{18,17},{17,1... | collective-permute-start | bytes 3145736 | tf_op jit(solution)/shard_map/ppermute | solution.py:58
  237.7 30.8 %collective-permute-start.20 = (bf16[512,512]{1,0:T(8,128)(2,1)S(1)}, bf16[512,512]{1,0:T(8,128)(2,1)S(1)}, u32[]{:S(2)}, u32[]{:S(2)}) collective-permute-start(bf16[512,512]{1,0:T(8,128)(2,1)S(1)} %get-tuple-element.157.refs_3_), channel_id=1, source_target_pairs={{0,1},{1,2},{2,3},{4,5},{5,6},{6,7},{8,9},{9,10},{10,11},{12,13},{... | collective-permute-start | bytes 1572872 | tf_op jit(solution)/shard_map/ppermute | solution.py:57
  246.3 25.9 %collective-permute-start.22 = (bf16[512,512]{1,0:T(8,128)(2,1)S(1)}, bf16[512,512]{1,0:T(8,128)(2,1)S(1)}, u32[]{:S(2)}, u32[]{:S(2)}) collective-permute-start(bf16[512,512]{1,0:T(8,128)(2,1)S(1)} %get-tuple-element.157.refs_3_), channel_id=1, source_target_pairs={{3,2},{2,1},{1,0},{7,6},{6,5},{5,4},{11,10},{10,9},{9,8},{15,14},{... | collective-permute-start | bytes 1572872 | tf_op jit(solution)/shard_map/ppermute | solution.py:58
  249.2 34.2 %collective-permute-start.41 = (bf16[512,512]{1,0:T(8,128)(2,1)S(1)}, bf16[512,512]{1,0:T(8,128)(2,1)S(1)}, u32[]{:S(2)}, u32[]{:S(2)}) collective-permute-start(bf16[512,512]{1,0:T(8,128)(2,1)S(1)} %get-tuple-element.177), channel_id=1, source_target_pairs={{3,2},{2,1},{1,0},{7,6},{6,5},{5,4},{11,10},{10,9},{9,8},{15,14},{... | collective-permute-start | bytes 1572872 | tf_op jit(solution)/shard_map/ppermute | solution.py:103
  250.5 32.9 %collective-permute-start.39 = (bf16[512,512]{1,0:T(8,128)(2,1)S(1)}, bf16[512,512]{1,0:T(8,128)(2,1)S(1)}, u32[]{:S(2)}, u32[]{:S(2)}) collective-permute-start(bf16[512,512]{1,0:T(8,128)(2,1)S(1)} %get-tuple-element.176), channel_id=1, source_target_pairs={{0,1},{1,2},{2,3},{4,5},{5,6},{6,7},{8,9},{9,10},{10,11},{12,13},{... | collective-permute-start | bytes 1572872 | tf_op jit(solution)/shard_map/ppermute | solution.py:102
  267.2 62.6 %collective-permute-start.29 = (bf16[1024,512]{1,0:T(8,128)(2,1)S(1)}, bf16[1024,512]{1,0:T(8,128)(2,1)S(1)}, u32[]{:S(2)}, u32[]{:S(2)}) collective-permute-start(bf16[1024,512]{1,0:T(8,128)(2,1)S(1)} %broadcast_select_fusion), channel_id=1, source_target_pairs={{2,3},{1,0},{6,7},{5,4},{10,11},{9,8},{14,15},{13,12},{18,19},{17,... | collective-permute-start | bytes 3145736 | tf_op jit(solution)/shard_map/ppermute | solution.py:53
  272.2 44.9 %collective-permute-start.23 = (bf16[512,512]{1,0:T(8,128)(2,1)S(1)}, bf16[512,512]{1,0:T(8,128)(2,1)S(1)}, u32[]{:S(2)}, u32[]{:S(2)}) collective-permute-start(bf16[512,512]{1,0:T(8,128)(2,1)S(1)} %collective-permute-done.22.refs_9_), channel_id=1, source_target_pairs={{2,1},{1,0},{6,5},{5,4},{10,9},{9,8},{14,13},{13,12},{18,17},{17,1... | collective-permute-start | bytes 1572872 | tf_op jit(solution)/shard_map/ppermute | solution.py:58
  284.0 34.5 %collective-permute-start.42 = (bf16[512,512]{1,0:T(8,128)(2,1)S(1)}, bf16[512,512]{1,0:T(8,128)(2,1)}, u32[]{:S(2)}, u32[]{:S(2)}) collective-permute-start(bf16[512,512]{1,0:T(8,128)(2,1)S(1)} %get-tuple-element.155.refs_3_), channel_id=1, source_target_pairs={{0,1},{1,2},{2,3},{4,5},{5,6},{6,7},{8,9},{9,10},{10,11},{12,13},{... | collective-permute-start | bytes 1572872 | tf_op jit(solution)/shard_map/ppermute | solution.py:57
  289.2 39.3 %collective-permute-start.44 = (bf16[512,512]{1,0:T(8,128)(2,1)S(1)}, bf16[512,512]{1,0:T(8,128)(2,1)}, u32[]{:S(2)}, u32[]{:S(2)}) collective-permute-start(bf16[512,512]{1,0:T(8,128)(2,1)S(1)} %get-tuple-element.155.refs_3_), channel_id=1, source_target_pairs={{3,2},{2,1},{1,0},{7,6},{6,5},{5,4},{11,10},{10,9},{9,8},{15,14},{... | collective-permute-start | bytes 1572872 | tf_op jit(solution)/shard_map/ppermute | solution.py:58
  318.5 45.8 %collective-permute-start.43 = (bf16[512,512]{1,0:T(8,128)(2,1)}, bf16[512,512]{1,0:T(8,128)(2,1)}, u32[]{:S(2)}, u32[]{:S(2)}) collective-permute-start(bf16[512,512]{1,0:T(8,128)(2,1)} %collective-permute-done.42.refs_4_), channel_id=1, source_target_pairs={{1,2},{2,3},{5,6},{6,7},{9,10},{10,11},{13,14},{14,15},{17,18},{18... | collective-permute-start | bytes 1572872 | tf_op jit(solution)/shard_map/ppermute | solution.py:57
  328.5 35.8 %collective-permute-start.45 = (bf16[512,512]{1,0:T(8,128)(2,1)}, bf16[512,512]{1,0:T(8,128)(2,1)}, u32[]{:S(2)}, u32[]{:S(2)}) collective-permute-start(bf16[512,512]{1,0:T(8,128)(2,1)} %collective-permute-done.44.refs_9_), channel_id=1, source_target_pairs={{2,1},{1,0},{6,5},{5,4},{10,9},{9,8},{14,13},{13,12},{18,17},{17,1... | collective-permute-start | bytes 1572872 | tf_op jit(solution)/shard_map/ppermute | solution.py:58
  376.4 28.9 %collective-permute-start.31 = (bf16[512,512]{1,0:T(8,128)(2,1)}, bf16[512,512]{1,0:T(8,128)(2,1)}, u32[]{:S(2)}, u32[]{:S(2)}) collective-permute-start(bf16[512,512]{1,0:T(8,128)(2,1)} %add_convert_fusion.17), channel_id=1, source_target_pairs={{0,1},{1,2},{4,5},{5,6},{8,9},{9,10},{12,13},{13,14},{16,17},{17,1... | collective-permute-start | bytes 1572872 | tf_op jit(solution)/shard_map/ppermute | solution.py:95
  381.6 23.7 %collective-permute-start.33 = (bf16[512,512]{1,0:T(8,128)(2,1)}, bf16[512,512]{1,0:T(8,128)(2,1)}, u32[]{:S(2)}, u32[]{:S(2)}) collective-permute-start(bf16[512,512]{1,0:T(8,128)(2,1)} %add_convert_fusion.17), channel_id=1, source_target_pairs={{3,2},{2,1},{7,6},{6,5},{11,10},{10,9},{15,14},{14,13},{19,18},{18... | collective-permute-start | bytes 1572872 | tf_op jit(solution)/shard_map/ppermute | solution.py:96
  407.1 26.2 %collective-permute-start.52 = (bf16[512,512]{1,0:T(8,128)(2,1)}, bf16[512,512]{1,0:T(8,128)(2,1)}, u32[]{:S(2)}, u32[]{:S(2)}) collective-permute-start(bf16[512,512]{1,0:T(8,128)(2,1)} %constant_dynamic-slice_fusion.5), channel_id=1, source_target_pairs={{0,1},{3,2},{4,5},{7,6},{8,9},{11,10},{12,13},{15,14},{16,17},{19,... | collective-permute-start | bytes 1572872 | tf_op jit(solution)/shard_map/ppermute | solution.py:88
  418.8 29.2 %collective-permute-start.36 = (f32[4,128]{1,0:T(4,128)S(1)}, f32[4,128]{1,0:T(4,128)S(1)}, u32[]{:S(2)}, u32[]{:S(2)}) collective-permute-start(f32[4,128]{1,0:T(4,128)S(1)} %bitcast_add_fusion.1), channel_id=1, source_target_pairs={{0,2},{1,3},{2,0},{3,1},{4,6},{5,7},{6,4},{7,5},{8,10},{9,11},{10,... | collective-permute-start | bytes 6152 | tf_op jit(solution)/shard_map/ppermute | solution.py:132
  427.5 38.5 %collective-permute-start.34 = (bf16[512,512]{1,0:T(8,128)(2,1)}, bf16[512,512]{1,0:T(8,128)(2,1)S(1)}, u32[]{:S(2)}, u32[]{:S(2)}) collective-permute-start(bf16[512,512]{1,0:T(8,128)(2,1)} %get-tuple-element.171), channel_id=1, source_target_pairs={{3,2},{2,1},{1,0},{7,6},{6,5},{5,4},{11,10},{10,9},{9,8},{15,14},{... | collective-permute-start | bytes 1572872 | tf_op jit(solution)/shard_map/ppermute | solution.py:103
  428.8 37.2 %collective-permute-start.32 = (bf16[512,512]{1,0:T(8,128)(2,1)}, bf16[512,512]{1,0:T(8,128)(2,1)S(1)}, u32[]{:S(2)}, u32[]{:S(2)}) collective-permute-start(bf16[512,512]{1,0:T(8,128)(2,1)} %get-tuple-element.170), channel_id=1, source_target_pairs={{0,1},{1,2},{2,3},{4,5},{5,6},{6,7},{8,9},{9,10},{10,11},{12,13},{... | collective-permute-start | bytes 1572872 | tf_op jit(solution)/shard_map/ppermute | solution.py:102
  448.0 321.1 %reduce-scatter.9.cloned.1.call-start = ((), (), s32[]{:S(2)}) async-start(), calls=%async_computation.9 | async-start | bytes 4718592 | tf_op jit(solution)/shard_map/reduce_scatter | solution.py:887
  448.0 24.8 %collective-permute-start.57 = (f32[4,128]{1,0:T(4,128)S(1)}, f32[4,128]{1,0:T(4,128)S(1)}, u32[]{:S(2)}, u32[]{:S(2)}) collective-permute-start(f32[4,128]{1,0:T(4,128)S(1)} %bitcast.47), channel_id=1, source_target_pairs={{0,1},{1,0},{2,3},{3,2},{4,5},{5,4},{6,7},{7,6},{8,9},{9,8},{10,11... | collective-permute-start | bytes 6152 | tf_op jit(solution)/shard_map/ppermute | solution.py:132
  458.9 25.7 %collective-permute-start.56 = (bf16[512,512]{1,0:T(8,128)(2,1)}, bf16[512,512]{1,0:T(8,128)(2,1)}, u32[]{:S(2)}, u32[]{:S(2)}) collective-permute-start(bf16[512,512]{1,0:T(8,128)(2,1)} %get-tuple-element.173), channel_id=1, source_target_pairs={{3,2},{2,1},{1,0},{7,6},{6,5},{5,4},{11,10},{10,9},{9,8},{15,14},{... | collective-permute-start | bytes 1572872 | tf_op jit(solution)/shard_map/ppermute | solution.py:103
  460.1 24.5 %collective-permute-start.54 = (bf16[512,512]{1,0:T(8,128)(2,1)}, bf16[512,512]{1,0:T(8,128)(2,1)}, u32[]{:S(2)}, u32[]{:S(2)}) collective-permute-start(bf16[512,512]{1,0:T(8,128)(2,1)} %get-tuple-element.172), channel_id=1, source_target_pairs={{0,1},{1,2},{2,3},{4,5},{5,6},{6,7},{8,9},{9,10},{10,11},{12,13},{... | collective-permute-start | bytes 1572872 | tf_op jit(solution)/shard_map/ppermute | solution.py:102
  483.3 22.6 %collective-permute-start.49 = (bf16[512,512]{1,0:T(8,128)(2,1)}, bf16[512,512]{1,0:T(8,128)(2,1)S(1)}, u32[]{:S(2)}, u32[]{:S(2)}) collective-permute-start(bf16[512,512]{1,0:T(8,128)(2,1)} %get-tuple-element.114.refs_6_), channel_id=1, source_target_pairs={{3,2},{2,1},{1,0},{7,6},{6,5},{5,4},{11,10},{10,9},{9,8},{15,14},{... | collective-permute-start | bytes 1572872 | tf_op jit(solution)/shard_map/ppermute | solution.py:58
  529.4 23.7 %collective-permute-start.63 = (bf16[512,512]{1,0:T(8,128)(2,1)}, bf16[512,512]{1,0:T(8,128)(2,1)}, u32[]{:S(2)}, u32[]{:S(2)}) collective-permute-start(bf16[512,512]{1,0:T(8,128)(2,1)} %broadcast_select_fusion.3), channel_id=1, source_target_pairs={{2,3},{1,0},{6,7},{5,4},{10,11},{9,8},{14,15},{13,12},{18,19},{17,... | collective-permute-start | bytes 1572872 | tf_op jit(solution)/shard_map/ppermute | solution.py:53
  576.3 194.9 %reduce-scatter.7.cloned.1.call-start = ((), (), s32[]{:S(2)}) async-start(), calls=%async_computation.8 | async-start | bytes 9437184 | tf_op jit(solution)/shard_map/reduce_scatter | solution.py:887
  576.8 236.7 %reduce-scatter.11.cloned.1.call-start = ((), (), s32[]{:S(2)}) async-start(), calls=%async_computation.10 | async-start | bytes 14155776 | tf_op jit(solution)/shard_map/reduce_scatter | solution.py:887
  654.5 104.1 %collective-permute-start.68 = (bf16[1024,512]{1,0:T(8,128)(2,1)}, bf16[1024,512]{1,0:T(8,128)(2,1)}, u32[]{:S(2)}, u32[]{:S(2)}) collective-permute-start(bf16[1024,512]{1,0:T(8,128)(2,1)} %get-tuple-element.162), channel_id=1, source_target_pairs={{0,3},{1,0},{2,1},{3,2},{4,7},{5,4},{6,5},{7,6},{8,11},{9,8},{10,9... | collective-permute-start | bytes 3145736 | tf_op jit(solution)/shard_map/ppermute | solution.py:118
  654.5 104.1 %collective-permute-start.67 = (bf16[1024,512]{1,0:T(8,128)(2,1)}, bf16[1024,512]{1,0:T(8,128)(2,1)}, u32[]{:S(2)}, u32[]{:S(2)}) collective-permute-start(bf16[1024,512]{1,0:T(8,128)(2,1)} %get-tuple-element.163), channel_id=1, source_target_pairs={{0,2},{1,3},{2,0},{3,1},{4,6},{5,7},{6,4},{7,5},{8,10},{9,11},{10,... | collective-permute-start | bytes 3145736 | tf_op jit(solution)/shard_map/ppermute | solution.py:118
  659.8 98.8 %collective-permute-start.66 = (bf16[1024,512]{1,0:T(8,128)(2,1)}, bf16[1024,512]{1,0:T(8,128)(2,1)}, u32[]{:S(2)}, u32[]{:S(2)}) collective-permute-start(bf16[1024,512]{1,0:T(8,128)(2,1)} %get-tuple-element.161), channel_id=1, source_target_pairs={{0,1},{1,2},{2,3},{3,0},{4,5},{5,6},{6,7},{7,4},{8,9},{9,10},{10,1... | collective-permute-start | bytes 3145736 | tf_op jit(solution)/shard_map/ppermute | solution.py:118
  659.9 73.2 %collective-permute-start.69 = (bf16[512,512]{1,0:T(8,128)(2,1)S(1)}, bf16[512,512]{1,0:T(8,128)(2,1)S(1)}, u32[]{:S(2)}, u32[]{:S(2)}) collective-permute-start(bf16[512,512]{1,0:T(8,128)(2,1)S(1)} %constant_dynamic-slice_fusion.1), channel_id=1, source_target_pairs={{0,1},{3,2},{4,5},{7,6},{8,9},{11,10},{12,13},{15,14},{16,17},{19,... | collective-permute-start | bytes 1572872 | tf_op jit(solution)/shard_map/ppermute | solution.py:88
  752.1 25.2 %collective-permute-start.77 = (bf16[512,512]{1,0:T(8,128)(2,1)}, bf16[512,512]{1,0:T(8,128)(2,1)}, u32[]{:S(2)}, u32[]{:S(2)}) collective-permute-start(bf16[512,512]{1,0:T(8,128)(2,1)} %add_convert_fusion.3), channel_id=1, source_target_pairs={{0,1},{1,2},{4,5},{5,6},{8,9},{9,10},{12,13},{13,14},{16,17},{17,1... | collective-permute-start | bytes 1572872 | tf_op jit(solution)/shard_map/ppermute | solution.py:95
  764.0 23.6 %collective-permute-start.70 = (bf16[512,512]{1,0:T(8,128)(2,1)}, bf16[512,512]{1,0:T(8,128)(2,1)S(1)}, u32[]{:S(2)}, u32[]{:S(2)}) collective-permute-start(bf16[512,512]{1,0:T(8,128)(2,1)} %add_convert_fusion.7), channel_id=1, source_target_pairs={{0,1},{1,2},{4,5},{5,6},{8,9},{9,10},{12,13},{13,14},{16,17},{17,1... | collective-permute-start | bytes 1572872 | tf_op jit(solution)/shard_map/ppermute | solution.py:95
  (102 other events, 1709.5 us)
Sparse Core Ops, SparseCore 0:
  11.1 74.7 all-gather.3
  87.8 36.5 all-gather.5
  140.0 70.1 all-gather.7
  448.1 49.0 reduce-scatter.4
  576.4 50.3 reduce-scatter.8
  630.1 71.5 reduce-scatter.6
  705.1 92.2 reduce-scatter.10

commit v7 on v6

--- a/solution.py
+++ b/solution.py
@@ -11,6 +11,7 @@
 HK = 256
 HV = 512
 EPSILON = 1e-06
+EXTRA = 16
 BLOCK = 512
 TP, CTX, DP = "tp", "ctx", "dp"
 F32 = jnp.float32
@@ -350,7 +351,7 @@
 
 def mlp_kernel(units, count, at_ref, gain_ref, w_ref, *refs):
     blocks, grads = refs[:count], refs[count : 2 * count]
-    full_ref, hidden_ref, acts_ref, grad_ref, scale_ref, inner_ref, back_ref, kept_ref, sems = refs[-9:]
+    full_ref, hidden_ref, acts_ref, grad_ref, scale_ref, back_ref, kept_ref, sems = refs[-8:]
     at, n = at_ref[0], count // 2 + 1
     first = pl.program_id(0) == 0
 
@@ -384,8 +385,18 @@
     g_up = (grad * gelu).astype(BF16)
     acts_ref[:, :units] = g_gate
     acts_ref[:, units:] = g_up
-    inner_ref[...] = jnp.sum(g_gate.astype(F32) * gate + g_up.astype(F32) * up, axis=1, keepdims=True)
-    back_ref[...] = (nt(g_gate, kept_ref[:, :units]) + nt(g_up, kept_ref[:, units : 2 * units])).astype(BF16)
+    back = (nt(g_gate, kept_ref[:, :units]) + nt(g_up, kept_ref[:, units : 2 * units])).astype(BF16)
+    step, rows = pl.program_id(0), back.shape[0]
+    back_ref[pl.ds(pl.multiple_of(step * rows, rows), rows), :] = back
+    inner = jnp.sum(g_gate.astype(F32) * gate + g_up.astype(F32) * up, axis=1, keepdims=True)
+    turned = jnp.transpose(jnp.broadcast_to(inner, (rows, 128)))[:EXTRA]
+    first_row = lax.broadcasted_iota(jnp.int32, turned.shape, 0) == 0
+    turned = jnp.where(first_row, turned, 0.0).astype(BF16)
+    width = blocks[0].shape[1]
+    total = pl.num_programs(0) * rows
+    for k in range(n):
+        where = pl.ds(pl.multiple_of(k * width + step * rows, rows), rows)
+        back_ref[total:, where] = turned
 
 
 def mlp(at, gain, w, part, grads, x, pairs, shared):
@@ -420,8 +431,7 @@
             own_rows(2 * units),
             own_rows(features),
             by_rows(1),
-            by_rows(1),
-            by_rows(features),
+            pl.BlockSpec((rows + EXTRA, features), lambda r: (0, 0)),
         ],
         out_shape=[
             jax.ShapeDtypeStruct((total, features), BF16),
@@ -429,8 +439,7 @@
             jax.ShapeDtypeStruct((total, 2 * units), BF16),
             jax.ShapeDtypeStruct((total, features), BF16),
             jax.ShapeDtypeStruct((rows, 1), F32),
-            jax.ShapeDtypeStruct((rows, 1), F32),
-            jax.ShapeDtypeStruct((rows, features), BF16),
+            jax.ShapeDtypeStruct((rows + EXTRA, features), BF16),
         ],
         input_output_aliases={3 + 2 * len(blocks) + i: i for i in range(len(shared))},
         scratch_shapes=[pltpu.VMEM((features, 3 * units), BF16), pltpu.SemaphoreType.DMA((3,))],
@@ -801,7 +810,7 @@
     gated, retained = heads_out
 
     x_own = layer_input.astype(F32)
-    middle, mid_pairs, scale_mlp, inner_mlp, back, grad_middle, grad_own, grad_pairs = ([] for _ in range(8))
+    middle, mid_pairs, scale_mlp, back, grad_middle, grad_own, grad_pairs = ([] for _ in range(7))
     gain_mlp_sum = 0.0
 
     def norm_back(own_rows, scale, gain, inner, grad_normed):
@@ -823,22 +832,20 @@
         mid_pairs.append(line_gather(middle[c].astype(BF16), TP))
     shared = []
     for c in range(parts):
-        *results, scale, inner, out = mlp(
+        *results, scale, out = mlp(
             here, gains[1:2], mlp_full, c, cot_blocks, middle[c].astype(BF16), mid_pairs[c], shared
         )
         shared = results
         scale_mlp.append(scale)
-        inner_mlp.append(inner[:, 0])
         back.append(out)
     normed_mlp, hidden, grad_acts, grad_full = shared
     early = ()
     for c in range(parts):
-        inner = row_total(inner_mlp[c])
         total, steps = line_scatter(after(back[c], *early), TP)
         early = steps[-1]
         if c:
             total = after(total, grad_pairs[c - 1][0][0])
-        grad_mid, gain_sum = norm_back(middle[c], scale_mlp[c], gain_mlp, inner, total)
+        grad_mid, gain_sum = norm_back(middle[c], scale_mlp[c], gain_mlp, total[own], total[:own])
         gain_mlp_sum = gain_mlp_sum + gain_sum
         grad_middle.append(cotangent[cuts[c]].astype(F32) + grad_mid)
         grad_own.append(grad_middle[c].astype(BF16))
@@ -848,7 +855,7 @@
     mlp_parts = nt(hidden, mlp_full[:, 2 * units :]).astype(BF16)
 
     grad_own[0] = after(grad_own[0], grad_gate_up, grad_down)
-    mlp_out = routed_scatter(after(mlp_parts, grad_pairs[-1][-1][0]), TP)
+    mlp_out = routed_scatter(after(mlp_parts, grad_pairs[-1][0][0]), TP)
     layer_output = (jnp.concatenate(middle) + mlp_out).astype(BF16)
     shared = []
     partial_state = None
@@ -891,9 +898,7 @@
     s_gate, s_up = s_gate_up[:, :units], s_gate_up[:, units:]
     s_out = shard(grad_out)
     s_in = shard(grad_in_w)
-    inner_attn, s_down, s_gate, s_up, s_out, layer_output = lax.optimization_barrier(
-        (inner_attn, s_down, s_gate, s_up, s_out, layer_output)
-    )
+    inner_attn, s_down, s_gate, s_up = lax.optimization_barrier((inner_attn, s_down, s_gate, s_up))
     inner_attn = row_total(inner_attn)
     grad_input, gain_attn_sum = [], 0.0
     early = ()

time: 830 us -> 880 us (1.060)
  waiting for transfers between devices: 297 us -> 337 us
    ppermute x6, waiting for transfers between devices: 93.3 us -> 30 us  [line_scatter(): from_left = from_right = lax.ppermute(data, axis, r_pairs + l_pairs)]
    ppermute x9 -> x5, waiting for transfers between devices: 28.1 us -> 88.5 us  [swap_sum(): x = x + lax.ppermute(x, axis, [(j, j ^ g) for j in range(n)])]
    ppermute x14, waiting for transfers between devices: 85.4 us -> 111 us  [line_gather(): lefts.append(lax.ppermute(lefts[-1], axis, l_pairs))]
    ppermute x14, starting transfers between devices: 40.2 us -> 63.1 us  [line_gather(): rights.append(lax.ppermute(rights[-1], axis, r_pairs))]
    ppermute x6, starting transfers between devices: 40.2 us -> 27.7 us  [line_scatter(): from_left = lax.ppermute(r_data, axis, r_pairs)]
    ppermute x6, waiting for transfers between devices: 3.49 us -> 15.4 us  [line_scatter(): from_left = lax.ppermute(r_data, axis, r_pairs)]
    ppermute x6, waiting for transfers between devices: 12 us -> 22.3 us  [line_scatter(): from_left = lax.ppermute(data, axis, r_pairs)]
  transfers between devices with their start and end apart: 91 -> 87, of which waited for: 34 -> 32; matrix products, arithmetic and copies ran while one was open for 18% -> 17% of each run, Pallas kernels for 18% -> 14%
where the time goes in v7:
time: 880 us; the launch traced here: 874 us
  waiting for transfers between devices  337 us (38%)
  starting transfers between devices  204 us (23%)
  Pallas kernels  150 us (17%)
  matrix products  78.6 us (9%)
  other arithmetic  67.3 us (8%)
  local copies, waits for them, and re-layouts  21.1 us (2%)
  between operations  16.1 us (2%)
    ppermute x14, waiting for transfers between devices, line_gather(): lefts.append(lax.ppermute(lefts[-1], axis, l_pairs))  111 us
    ppermute x5, waiting for transfers between devices, swap_sum(): x = x + lax.ppermute(x, axis, [(j, j ^ g) for j in range(n)])  88.5 us
    ppermute x14, starting transfers between devices, line_gather(): rights.append(lax.ppermute(rights[-1], axis, r_pairs))  63.1 us
    dot_general x4, matrix products, tn(): lax.dot_general(a, b, (((0,), (0,)), ((), ())), preferred_element_type=F32)  47.8 us
    pallas_call x2, Pallas kernels, mlp(): pl.pallas_call(lambda *refs: mlp_kernel(units, len(blocks), *refs), grid=...  43.3 us
    dot_general x3, matrix products, nt(): lax.dot_general(a, b, (((1,), (1,)), ((), ())), preferred_element_type=F32)  30.8 us
    ppermute x6, waiting for transfers between devices, line_scatter(): from_left = from_right = lax.ppermute(data, axis, r_pairs + l_pairs)  30 us
    ppermute x6, starting transfers between devices, line_scatter(): from_left = lax.ppermute(data, axis, r_pairs)  28.2 us
  transfers between devices with their start and end apart: 87, of which 32 were waited for; matrix products, arithmetic and copies ran while one was open for 17% of the time, Pallas kernels for 14%

profile of v7, /device:TPU:0, one launch (start us, length us, event | category | flops | bytes accessed | tf_op | source)
XLA Modules:
  0.0 874.2 jit_solution(16113196676127934193)
XLA Ops:
  25.9 5.5 fusion.16
  41.6 9.0 %collective-permute-done.2 = f32[2,512]{1,0:T(2,128)S(1)} collective-permute-done((f32[2,512]{1,0:T(2,128)S(1)}, f32[2,512]{1,0:T(2,128)S(1)}, u32[]{:S(2)}, u32[]{:S(2)}) %collective-permute-start.2) | collective-permute-done | bytes 4128 | tf_op jit(solution)/shard_map/ppermute | solution.py:125
  55.5 12.6 %collective-permute-done.11.refs_10_ = bf16[512,512]{1,0:T(8,128)(2,1)S(1)} collective-permute-done((bf16[512,512]{1,0:T(8,128)(2,1)S(1)}, bf16[512,512]{1,0:T(8,128)(2,1)S(1)}, u32[]{:S(2)}, u32[]{:S(2)}) %collective-permute-start.11) | collective-permute-done | bytes 524320 | tf_op jit(solution)/shard_map/ppermute | solution.py:59
  69.5 9.8 %collective-permute-done.6.refs_10_ = bf16[512,512]{1,0:T(8,128)(2,1)S(1)} collective-permute-done((bf16[512,512]{1,0:T(8,128)(2,1)S(1)}, bf16[512,512]{1,0:T(8,128)(2,1)S(1)}, u32[]{:S(2)}, u32[]{:S(2)}) %collective-permute-start.6) | collective-permute-done | bytes 524320 | tf_op jit(solution)/shard_map/ppermute | solution.py:59
  82.4 8.2 collective-permute-done.12.refs_8_.refs_11_
  91.4 12.6 %proj.2 = (bf16[1024,2048]{1,0:T(8,128)(2,1)}, bf16[1024,512]{1,0:T(8,128)(2,1)}, bf16[1024,512]{1,0:T(8,128)(2,1)}, bf16[1024,1024]{1,0:T(8,128)(2,1)}, f32[512...) custom-call(s32[1]{0:T(128)} %bitcast.refs_0_, f32[2]{0:T(128)} %negate_log-plus-one_fusion.1.refs_1_.refs_0_, ...), custom_call_target="tpu_custom_call" | custom-call | flops 4294967296 | bytes 20971520 | tf_op jit(solution)/shard_map/proj/pallas_call | solution.py:289
  104.9 13.7 %proj.3 = (bf16[1024,2048]{1,0:T(8,128)(2,1)}, bf16[1024,512]{1,0:T(8,128)(2,1)}, bf16[1024,512]{1,0:T(8,128)(2,1)}, bf16[1024,1024]{1,0:T(8,128)(2,1)}, f32[512...) custom-call(s32[1]{0:T(128)} %bitcast.refs_0_, ...), custom_call_target="tpu_custom_call", output_to_operand_aliasing={{0}: (14, {}), {1}: (15, {}), {2}: (16, {}), {3}: (17, {})} | custom-call | flops 4294967296 | bytes 20971520 | tf_op jit(solution)/shard_map/proj/pallas_call | solution.py:289
  124.2 12.5 %collective-permute-done.14.refs_8_.refs_9_ = bf16[2,256,512]{2,1,0:T(8,128)(2,1)S(1)} collective-permute-done((bf16[2,256,512]{2,1,0:T(8,128)(2,1)S(1)}, bf16[2,256,512]{2,1,0:T(8,128)(2,1)S(1)}, u32[]{:S(2)}, u32[]{:S(2)}) %collective-permute-start.14) | collective-permute-done | bytes 524320 | tf_op jit(solution)/shard_map/ppermute | solution.py:153
  137.0 8.8 %prod.1.refs_5_.refs_4_ = f32[1024,1024]{1,0:T(8,128)} custom-call(bf16[1024,2048]{1,0:T(8,128)(2,1)} %get-tuple-element.87.x_ref, bf16[2048,3072]{1,0:T(8,128)(2,1)} %all-gather.4.cloned.1.call-done.refs_3_.w_ref), custom_call_target="tpu_custom_call" | custom-call | flops 4294967296 | bytes 12582912 | tf_op jit(solution)/shard_map/prod/pallas_call | solution.py:336
  145.8 10.0 %fwd.2 = (bf16[1024,1024]{1,0:T(8,128)(2,1)}, f32[1024,1024]{1,0:T(8,128)}, bf16[512,2048]{1,0:T(8,128)(2,1)}) custom-call(f32[2]{0:T(128)} %negate_log-plus-one_fusion.1.refs_1_.refs_0_, f32[2,2]{1,0:T(2,128)} %pad_maximum_fusion.3.refs_1_, bf16[1024,512]{1,0:T(8,128)(2,1)} %get-tuple-element.82.refs_2_.refs_3_, ...), custom_call_target="tpu_custom_call" | custom-call | flops 3221225472 | bytes 10485760 | tf_op jit(solution)/shard_map/fwd/pallas_call | solution.py:517
  158.3 11.0 %collective-permute-done.15 = bf16[512,512]{1,0:T(8,128)(2,1)S(1)} collective-permute-done((bf16[512,512]{1,0:T(8,128)(2,1)S(1)}, bf16[512,512]{1,0:T(8,128)(2,1)S(1)}, u32[]{:S(2)}, u32[]{:S(2)}) %collective-permute-start.15) | collective-permute-done | bytes 524320 | tf_op jit(solution)/shard_map/ppermute | solution.py:89
  171.2 5.8 collective-permute-start.16
  177.0 10.5 %fwd.3 = (bf16[1024,1024]{1,0:T(8,128)(2,1)}, f32[1024,1024]{1,0:T(8,128)}, bf16[512,2048]{1,0:T(8,128)(2,1)}) custom-call(f32[2]{0:T(128)} %negate_log-plus-one_fusion.1.refs_1_.refs_0_, f32[2,2]{1,0:T(2,128)} %pad_maximum_fusion.3.refs_1_, bf16[1024,512]{1,0:T(8,128)(2,1)} %get-tuple-element.82.refs_2_.refs_3_, ...), custom_call_target="tpu_custom_call", output_to_operand_aliasing={{0}: (9, {}), {1}: (10, {})} | custom-call | flops 4026531840 | bytes 10485760 | tf_op jit(solution)/shard_map/fwd/pallas_call | solution.py:517
  189.5 6.0 collective-permute-start.20
  202.6 6.2 collective-permute-start.31
  212.4 6.6 collective-permute-done.17
  228.4 25.0 %collective-permute-start.25 = (bf16[512,512]{1,0:T(8,128)(2,1)S(1)}, bf16[512,512]{1,0:T(8,128)(2,1)S(1)}, u32[]{:S(2)}, u32[]{:S(2)}) collective-permute-start(bf16[512,512]{1,0:T(8,128)(2,1)S(1)} %get-tuple-element.147.refs_3_), channel_id=1, source_target_pairs={{0,1},{1,2},{2,3},{4,5},{5,6},{6,7},{8,9},{9,10},{10,11},{12,13},{... | collective-permute-start | bytes 1572872 | tf_op jit(solution)/shard_map/ppermute | solution.py:58
  255.0 6.6 collective-permute-start.22
  266.9 5.5 collective-permute-done.22
  281.1 19.7 %collective-permute-done.34.refs_14_ = bf16[1024,512]{1,0:T(8,128)(2,1)S(1)} collective-permute-done((bf16[1024,512]{1,0:T(8,128)(2,1)}, bf16[1024,512]{1,0:T(8,128)(2,1)S(1)}, u32[]{:S(2)}, u32[]{:S(2)}) %collective-permute-start.34) | collective-permute-done | bytes 1048608 | tf_op jit(solution)/shard_map/ppermute | solution.py:59
  304.6 18.6 %collective-permute-done.28.refs_9_ = bf16[512,512]{1,0:T(8,128)(2,1)S(1)} collective-permute-done((bf16[512,512]{1,0:T(8,128)(2,1)S(1)}, bf16[512,512]{1,0:T(8,128)(2,1)S(1)}, u32[]{:S(2)}, u32[]{:S(2)}) %collective-permute-start.28) | collective-permute-done | bytes 524320 | tf_op jit(solution)/shard_map/ppermute | solution.py:59
  326.7 30.3 %collective-permute-done.29.refs_7_ = bf16[512,512]{1,0:T(8,128)(2,1)S(1)} collective-permute-done((bf16[512,512]{1,0:T(8,128)(2,1)S(1)}, bf16[512,512]{1,0:T(8,128)(2,1)S(1)}, u32[]{:S(2)}, u32[]{:S(2)}) %collective-permute-start.29) | collective-permute-done | bytes 524320 | tf_op jit(solution)/shard_map/ppermute | solution.py:59
  359.3 6.5 collective-permute-done.39.refs_5_.refs_8_
  365.9 21.7 %mlp.2 = (bf16[1024,2048]{1,0:T(8,128)(2,1)}, bf16[1024,1024]{1,0:T(8,128)(2,1)}, bf16[1024,2048]{1,0:T(8,128)(2,1)}, bf16[1024,2048]{1,0:T(8,128)(2,1)}, f32[512,1]{1,0:T(8,128)}, /*index=5*/bf16[528,2048]{1,0:T(8,128)(2,1)}) custom-call(s32[1]{0:T(128)} %bitcast.refs_0_, f32[1,2048]{1,0:T(1,128)} %get-tuple-element.176.refs_1_, ...), custom_call_target="tpu_custom_call" | custom-call | flops 10737418240 | bytes 27262976 | tf_op jit(solution)/shard_map/mlp/pallas_call | solution.py:417
  387.6 21.6 %mlp.3 = (bf16[1024,2048]{1,0:T(8,128)(2,1)}, bf16[1024,1024]{1,0:T(8,128)(2,1)}, bf16[1024,2048]{1,0:T(8,128)(2,1)}, bf16[1024,2048]{1,0:T(8,128)(2,1)}, f32[512,1]{1,0:T(8,128)}, /*index=5*/bf16[528,2048]{1,0:T(8,128)(2,1)}) custom-call(s32[1]{0:T(128)} %bitcast.refs_0_, ...), custom_call_target="tpu_custom_call", output_to_operand_aliasing={{0}: (17, {}), {1}: (18, {}), {2}: (19, {}), {3}: (20, {})} | custom-call | flops 10737418240 | bytes 27262976 | tf_op jit(solution)/shard_map/mlp/pallas_call | solution.py:417
  409.3 9.4 %convolution_convert_fusion.3 = bf16[2048,1024]{1,0:T(8,128)(2,1)} fusion(bf16[1024,2048]{1,0:T(8,128)(2,1)} %get-tuple-element.112, bf16[1024,1024]{1,0:T(8,128)(2,1)} %get-tuple-element.101), kind=kOutput, calls=%fused_computation.6 | convolution fusion | flops 4297064448 | bytes 10485760 | tf_op jit(solution)/shard_map/dot_general | solution.py:26
  418.7 14.0 %convolution_convert_fusion.1 = bf16[2048,2048]{1,0:T(8,128)(2,1)} fusion(bf16[1024,2048]{1,0:T(8,128)(2,1)} %get-tuple-element.113, bf16[1024,2048]{1,0:T(8,128)(2,1)} %get-tuple-element.114), kind=kOutput, calls=%fused_computation.1 | convolution fusion | flops 8594128896 | bytes 16777216 | tf_op jit(solution)/shard_map/dot_general | solution.py:26
  435.5 10.9 %collective-permute-done.40 = bf16[528,512]{1,0:T(8,128)(2,1)S(1)} collective-permute-done((bf16[528,512]{1,0:T(8,128)(2,1)S(1)}, bf16[528,512]{1,0:T(8,128)(2,1)S(1)}, u32[]{:S(2)}, u32[]{:S(2)}) %collective-permute-start.40) | collective-permute-done | bytes 540704 | tf_op jit(solution)/shard_map/ppermute | solution.py:89
  453.4 12.6 %collective-permute-done.41 = bf16[528,512]{1,0:T(8,128)(2,1)S(1)} collective-permute-done((bf16[528,512]{1,0:T(8,128)(2,1)S(1)}, bf16[528,512]{1,0:T(8,128)(2,1)S(1)}, u32[]{:S(2)}, u32[]{:S(2)}) %collective-permute-start.41) | collective-permute-done | bytes 540704 | tf_op jit(solution)/shard_map/ppermute | solution.py:96
  490.0 9.7 %collective-permute-done.44 = bf16[528,512]{1,0:T(8,128)(2,1)} collective-permute-done((bf16[528,512]{1,0:T(8,128)(2,1)}, bf16[528,512]{1,0:T(8,128)(2,1)}, u32[]{:S(2)}, u32[]{:S(2)}) %collective-permute-start.44) | collective-permute-done | bytes 540704 | tf_op jit(solution)/shard_map/ppermute | solution.py:96
  518.4 7.0 collective-permute-done.47
  530.2 9.6 %collective-permute-start.51 = (bf16[512,512]{1,0:T(8,128)(2,1)S(1)}, bf16[512,512]{1,0:T(8,128)(2,1)S(1)}, u32[]{:S(2)}, u32[]{:S(2)}) collective-permute-start(bf16[512,512]{1,0:T(8,128)(2,1)S(1)} %get-tuple-element.157.refs_6_), channel_id=1, source_target_pairs={{0,1},{1,2},{2,3},{4,5},{5,6},{6,7},{8,9},{9,10},{10,11},{12,13},{... | collective-permute-start | bytes 1572872 | tf_op jit(solution)/shard_map/ppermute | solution.py:58
  541.8 8.8 %collective-permute-done.56.refs_12_ = bf16[512,512]{1,0:T(8,128)(2,1)S(1)} collective-permute-done((bf16[512,512]{1,0:T(8,128)(2,1)S(1)}, bf16[512,512]{1,0:T(8,128)(2,1)S(1)}, u32[]{:S(2)}, u32[]{:S(2)}) %collective-permute-start.56) | collective-permute-done | bytes 524320 | tf_op jit(solution)/shard_map/ppermute | solution.py:59
  552.6 6.5 collective-permute-done.61.refs_10_
  571.1 10.8 %gate.2 = (bf16[1024,1024]{1,0:T(8,128)(2,1)}, bf16[1024,1024]{1,0:T(8,128)(2,1)}, bf16[1024,2048]{1,0:T(8,128)(2,1)}, f32[2,256,512]{2,1,0:T(8,128)}, bf16[2,25...) custom-call(s32[1]{0:T(128)} %bitcast.refs_0_, f32[2]{0:T(128)} %negate_log-plus-one_fusion.1.refs_1_.refs_0_, ...), custom_call_target="tpu_custom_call" | custom-call | flops 2415919104 | bytes 8388608 | tf_op jit(solution)/shard_map/gate/pallas_call | solution.py:590
  582.8 11.5 %gate.3 = (bf16[1024,1024]{1,0:T(8,128)(2,1)}, bf16[1024,1024]{1,0:T(8,128)(2,1)}, bf16[1024,2048]{1,0:T(8,128)(2,1)}, f32[2,256,512]{2,1,0:T(8,128)}, bf16[2,25...) custom-call(s32[1]{0:T(128)} %bitcast.refs_0_, ...), custom_call_target="tpu_custom_call", output_to_operand_aliasing={{0}: (14, {}), {1}: (15, {}), {2}: (16, {})} | custom-call | flops 2415919104 | bytes 8388608 | tf_op jit(solution)/shard_map/gate/pallas_call | solution.py:590
  596.7 8.4 convolution_convert_fusion.2
  609.1 12.5 %collective-permute-done.64.refs_11_ = bf16[2,256,512]{2,1,0:T(8,128)(2,1)S(1)} collective-permute-done((bf16[2,256,512]{2,1,0:T(8,128)(2,1)S(1)}, bf16[2,256,512]{2,1,0:T(8,128)(2,1)S(1)}, u32[]{:S(2)}, u32[]{:S(2)}) %collective-permute-start.64) | collective-permute-done | bytes 524320 | tf_op jit(solution)/shard_map/ppermute | solution.py:167
  622.4 21.1 %bwd.1 = (bf16[1024,3072]{1,0:T(8,128)(2,1)}, f32[2,1024,1]{2,1,0:T(8,128)}) custom-call(f32[2]{0:T(128)} %negate_log-plus-one_fusion.1.refs_1_.refs_0_, f32[2,2]{1,0:T(2,128)} %pad_maximum_fusion.3.refs_1_, f32[2,2]{1,0:T(2,128)} %pad_maximum_fusion.4.refs_2_, bf16[1024,512]{1,0:T(8,128)(2,1)} %get-tuple-element.82.refs_2_.refs_3_, ...), custom_call_target="tpu_custom_call" | custom-call | flops 7247757312 | bytes 12582912 | tf_op jit(solution)/shard_map/bwd/pallas_call | solution.py:700
  643.6 10.8 %fusion.12 = bf16[512,2048]{1,0:T(8,128)(2,1)S(1)} fusion(bf16[2048,3072]{1,0:T(8,128)(2,1)} %all-gather.4.cloned.1.call-done.refs_3_.w_ref, bf16[1024,3072]{1,0:T(8,128)(2,1)} %get-tuple-element.135), kind=kOutput, calls=%fused_computation.12 | convolution fusion | flops 6443499520 | bytes 17825792 | tf_op jit(solution)/shard_map/dot_general | solution.py:30
  654.4 15.9 %convolution_convert_fusion = bf16[2048,3072]{1,0:T(8,128)(2,1)} fusion(bf16[1024,2048]{1,0:T(8,128)(2,1)S(1)} %copy-done.2, bf16[1024,3072]{1,0:T(8,128)(2,1)S(1)} %copy-done.69), kind=kOutput, calls=%fused_computation | convolution fusion | flops 12891193344 | bytes 23068672 | tf_op jit(solution)/shard_map/dot_general | solution.py:26
  672.3 10.6 %fusion.9 = bf16[512,2048]{1,0:T(8,128)(2,1)S(1)} fusion(bf16[2048,3072]{1,0:T(8,128)(2,1)} %all-gather.4.cloned.1.call-done.refs_3_.w_ref, bf16[1024,3072]{1,0:T(8,128)(2,1)} %get-tuple-element.135), kind=kOutput, calls=%fused_computation.11 | convolution fusion | flops 6443499520 | bytes 17825792 | tf_op jit(solution)/shard_map/dot_general | solution.py:30
  694.9 6.9 collective-permute-done.72
  710.5 9.4 %fusion.2 = bf16[1024,2048]{1,0:T(8,128)(2,1)} fusion(bf16[1024,1024]{1,0:T(8,128)(2,1)} %get-tuple-element.101, bf16[2048,3072]{1,0:T(8,128)(2,1)} %all-gather.8.cloned.1.call-done.refs_2_), kind=kOutput, calls=%fused_computation.4 | convolution fusion | flops 4297064448 | bytes 10485760 | tf_op jit(solution)/shard_map/dot_general | solution.py:30
  728.7 6.2 collective-permute-start.67
  738.8 5.4 collective-permute-start.74
  751.4 6.6 collective-permute-done.70
  767.3 80.5 %collective-permute-done.71 = f32[8,128]{1,0:T(8,128)S(1)} collective-permute-done((f32[8,128]{1,0:T(8,128)S(1)}, f32[8,128]{1,0:T(8,128)S(1)}, u32[]{:S(2)}, u32[]{:S(2)}) %collective-permute-start.71) | collective-permute-done | bytes 4128 | tf_op jit(solution)/shard_map/ppermute | solution.py:133
  (378 shorter events, 248.3 us)
Async XLA Ops:
  7.2 83.4 %all-gather.4.cloned.1.call-start = ((), (), s32[]{:S(2)}) async-start(), calls=%async_computation.4 | async-start | bytes 14155776 | tf_op jit(solution)/shard_map/all_gather | solution.py:760
  11.0 134.8 %all-gather.6.cloned.1.call-start = ((), (), s32[]{:S(2)}) async-start(), calls=%async_computation.5 | async-start | bytes 4718592 | tf_op jit(solution)/shard_map/all_gather | solution.py:761
  11.7 354.2 %all-gather.8.cloned.1.call-start = ((), (), s32[]{:S(2)}) async-start(), calls=%async_computation.6 | async-start | bytes 14155776 | tf_op jit(solution)/shard_map/all_gather | solution.py:803
  11.9 29.7 %collective-permute-start.1 = (f32[2,512]{1,0:T(2,128)S(1)}, f32[2,512]{1,0:T(2,128)S(1)}, u32[]{:S(2)}, u32[]{:S(2)}) collective-permute-start(f32[2,512]{1,0:T(2,128)S(1)} %get-tuple-element.184), channel_id=1, source_target_pairs={{0,2},{1,3},{2,0},{3,1},{4,6},{5,7},{6,4},{7,5},{8,10},{9,11},{10,... | collective-permute-start | bytes 12296 | tf_op jit(solution)/shard_map/ppermute | solution.py:125
  17.7 33.8 %collective-permute-start.10 = (bf16[512,512]{1,0:T(8,128)(2,1)S(1)}, bf16[512,512]{1,0:T(8,128)(2,1)S(1)}, u32[]{:S(2)}, u32[]{:S(2)}) collective-permute-start(bf16[512,512]{1,0:T(8,128)(2,1)S(1)} %get-tuple-element.174.refs_6_), channel_id=1, source_target_pairs={{3,2},{2,1},{1,0},{7,6},{6,5},{5,4},{11,10},{10,9},{9,8},{15,14},{... | collective-permute-start | bytes 1572872 | tf_op jit(solution)/shard_map/ppermute | solution.py:59
  19.0 31.7 %collective-permute-start.8 = (bf16[512,512]{1,0:T(8,128)(2,1)S(1)}, bf16[512,512]{1,0:T(8,128)(2,1)S(1)}, u32[]{:S(2)}, u32[]{:S(2)}) collective-permute-start(bf16[512,512]{1,0:T(8,128)(2,1)S(1)} %get-tuple-element.174.refs_6_), channel_id=1, source_target_pairs={{0,1},{1,2},{2,3},{4,5},{5,6},{6,7},{8,9},{9,10},{10,11},{12,13},{... | collective-permute-start | bytes 1572872 | tf_op jit(solution)/shard_map/ppermute | solution.py:58
  23.6 29.9 %collective-permute-start.5 = (bf16[512,512]{1,0:T(8,128)(2,1)S(1)}, bf16[512,512]{1,0:T(8,128)(2,1)S(1)}, u32[]{:S(2)}, u32[]{:S(2)}) collective-permute-start(bf16[512,512]{1,0:T(8,128)(2,1)S(1)} %get-tuple-element.175.refs_6_), channel_id=1, source_target_pairs={{3,2},{2,1},{1,0},{7,6},{6,5},{5,4},{11,10},{10,9},{9,8},{15,14},{... | collective-permute-start | bytes 1572872 | tf_op jit(solution)/shard_map/ppermute | solution.py:59
  53.5 25.9 %collective-permute-start.6 = (bf16[512,512]{1,0:T(8,128)(2,1)S(1)}, bf16[512,512]{1,0:T(8,128)(2,1)S(1)}, u32[]{:S(2)}, u32[]{:S(2)}) collective-permute-start(bf16[512,512]{1,0:T(8,128)(2,1)S(1)} %collective-permute-done.5.refs_12_), channel_id=1, source_target_pairs={{2,1},{1,0},{6,5},{5,4},{10,9},{9,8},{14,13},{13,12},{18,17},{17,1... | collective-permute-start | bytes 1572872 | tf_op jit(solution)/shard_map/ppermute | solution.py:59
  54.8 24.6 %collective-permute-start.4 = (bf16[512,512]{1,0:T(8,128)(2,1)}, bf16[512,512]{1,0:T(8,128)(2,1)S(1)}, u32[]{:S(2)}, u32[]{:S(2)}) collective-permute-start(bf16[512,512]{1,0:T(8,128)(2,1)} %collective-permute-done.3.refs_7_), channel_id=1, source_target_pairs={{1,2},{2,3},{5,6},{6,7},{9,10},{10,11},{13,14},{14,15},{17,18},{18... | collective-permute-start | bytes 1572872 | tf_op jit(solution)/shard_map/ppermute | solution.py:58
  68.2 22.4 %collective-permute-start.12 = (bf16[512,512]{1,0:T(8,128)(2,1)S(1)}, bf16[512,512]{1,0:T(8,128)(2,1)S(1)}, u32[]{:S(2)}, u32[]{:S(2)}) collective-permute-start(bf16[512,512]{1,0:T(8,128)(2,1)S(1)} %broadcast_select_fusion.7), channel_id=1, source_target_pairs={{2,3},{1,0},{6,7},{5,4},{10,11},{9,8},{14,15},{13,12},{18,19},{17,... | collective-permute-start | bytes 1572872 | tf_op jit(solution)/shard_map/ppermute | solution.py:54
  80.4 23.7 %collective-permute-start.7 = (bf16[512,512]{1,0:T(8,128)(2,1)}, bf16[512,512]{1,0:T(8,128)(2,1)S(1)}, u32[]{:S(2)}, u32[]{:S(2)}) collective-permute-start(bf16[512,512]{1,0:T(8,128)(2,1)} %broadcast_select_fusion.8), channel_id=1, source_target_pairs={{2,3},{1,0},{6,7},{5,4},{10,11},{9,8},{14,15},{13,12},{18,19},{17,... | collective-permute-start | bytes 1572872 | tf_op jit(solution)/shard_map/ppermute | solution.py:54
  136.7 587.1 %reduce-scatter.5.cloned.1.call-start = ((), (), s32[]{:S(2)}) async-start(), calls=%async_computation.7 | async-start | bytes 4718592 | tf_op jit(solution)/shard_map/reduce_scatter | solution.py:894
  197.9 21.1 %collective-permute-start.17 = (bf16[512,512]{1,0:T(8,128)(2,1)S(1)}, bf16[512,512]{1,0:T(8,128)(2,1)}, u32[]{:S(2)}, u32[]{:S(2)}) collective-permute-start(bf16[512,512]{1,0:T(8,128)(2,1)S(1)} %get-tuple-element.164), channel_id=1, source_target_pairs={{0,1},{1,2},{2,3},{4,5},{5,6},{6,7},{8,9},{9,10},{10,11},{12,13},{... | collective-permute-start | bytes 1572872 | tf_op jit(solution)/shard_map/ppermute | solution.py:103
  200.0 24.6 %collective-permute-start.19 = (bf16[512,512]{1,0:T(8,128)(2,1)}, bf16[512,512]{1,0:T(8,128)(2,1)}, u32[]{:S(2)}, u32[]{:S(2)}) collective-permute-start(bf16[512,512]{1,0:T(8,128)(2,1)} %get-tuple-element.165), channel_id=1, source_target_pairs={{3,2},{2,1},{1,0},{7,6},{6,5},{5,4},{11,10},{10,9},{9,8},{15,14},{... | collective-permute-start | bytes 1572872 | tf_op jit(solution)/shard_map/ppermute | solution.py:104
  201.3 60.3 %collective-permute-start.33 = (bf16[1024,512]{1,0:T(8,128)(2,1)}, bf16[1024,512]{1,0:T(8,128)(2,1)}, u32[]{:S(2)}, u32[]{:S(2)}) collective-permute-start(bf16[1024,512]{1,0:T(8,128)(2,1)} %refs_10_.1), channel_id=1, source_target_pairs={{3,2},{2,1},{1,0},{7,6},{6,5},{5,4},{11,10},{10,9},{9,8},{15,14},{... | collective-permute-start | bytes 3145736 | tf_op jit(solution)/shard_map/ppermute | solution.py:59
  202.6 60.3 %collective-permute-start.31 = (bf16[1024,512]{1,0:T(8,128)(2,1)}, bf16[1024,512]{1,0:T(8,128)(2,1)}, u32[]{:S(2)}, u32[]{:S(2)}) collective-permute-start(bf16[1024,512]{1,0:T(8,128)(2,1)} %refs_10_.1), channel_id=1, source_target_pairs={{0,1},{1,2},{2,3},{4,5},{5,6},{6,7},{8,9},{9,10},{10,11},{12,13},{... | collective-permute-start | bytes 3145736 | tf_op jit(solution)/shard_map/ppermute | solution.py:58
  219.0 34.4 %collective-permute-start.21 = (bf16[512,512]{1,0:T(8,128)(2,1)}, bf16[512,512]{1,0:T(8,128)(2,1)}, u32[]{:S(2)}, u32[]{:S(2)}) collective-permute-start(bf16[512,512]{1,0:T(8,128)(2,1)} %add_convert_fusion.17), channel_id=1, source_target_pairs={{0,1},{1,2},{4,5},{5,6},{8,9},{9,10},{12,13},{13,14},{16,17},{17,1... | collective-permute-start | bytes 1572872 | tf_op jit(solution)/shard_map/ppermute | solution.py:96
  227.1 37.1 %collective-permute-start.37 = (bf16[512,512]{1,0:T(8,128)(2,1)S(1)}, bf16[512,512]{1,0:T(8,128)(2,1)S(1)}, u32[]{:S(2)}, u32[]{:S(2)}) collective-permute-start(bf16[512,512]{1,0:T(8,128)(2,1)S(1)} %get-tuple-element.147.refs_3_), channel_id=1, source_target_pairs={{3,2},{2,1},{1,0},{7,6},{6,5},{5,4},{11,10},{10,9},{9,8},{15,14},{... | collective-permute-start | bytes 1572872 | tf_op jit(solution)/shard_map/ppermute | solution.py:59
  228.4 37.2 %collective-permute-start.25 = (bf16[512,512]{1,0:T(8,128)(2,1)S(1)}, bf16[512,512]{1,0:T(8,128)(2,1)S(1)}, u32[]{:S(2)}, u32[]{:S(2)}) collective-permute-start(bf16[512,512]{1,0:T(8,128)(2,1)S(1)} %get-tuple-element.147.refs_3_), channel_id=1, source_target_pairs={{0,1},{1,2},{2,3},{4,5},{5,6},{6,7},{8,9},{9,10},{10,11},{12,13},{... | collective-permute-start | bytes 1572872 | tf_op jit(solution)/shard_map/ppermute | solution.py:58
  262.9 37.8 %collective-permute-start.34 = (bf16[1024,512]{1,0:T(8,128)(2,1)}, bf16[1024,512]{1,0:T(8,128)(2,1)S(1)}, u32[]{:S(2)}, u32[]{:S(2)}) collective-permute-start(bf16[1024,512]{1,0:T(8,128)(2,1)} %collective-permute-done.33.refs_16_), channel_id=1, source_target_pairs={{2,1},{1,0},{6,5},{5,4},{10,9},{9,8},{14,13},{13,12},{18,17},{17,1... | collective-permute-start | bytes 3145736 | tf_op jit(solution)/shard_map/ppermute | solution.py:59
  264.3 38.9 %collective-permute-start.32 = (bf16[1024,512]{1,0:T(8,128)(2,1)}, bf16[1024,512]{1,0:T(8,128)(2,1)S(1)}, u32[]{:S(2)}, u32[]{:S(2)}) collective-permute-start(bf16[1024,512]{1,0:T(8,128)(2,1)} %collective-permute-done.31.refs_11_), channel_id=1, source_target_pairs={{1,2},{2,3},{5,6},{6,7},{9,10},{10,11},{13,14},{14,15},{17,18},{18... | collective-permute-start | bytes 3145736 | tf_op jit(solution)/shard_map/ppermute | solution.py:58
  265.7 59.6 %collective-permute-start.38 = (bf16[512,512]{1,0:T(8,128)(2,1)S(1)}, bf16[512,512]{1,0:T(8,128)(2,1)S(1)}, u32[]{:S(2)}, u32[]{:S(2)}) collective-permute-start(bf16[512,512]{1,0:T(8,128)(2,1)S(1)} %collective-permute-done.37.refs_9_), channel_id=1, source_target_pairs={{2,1},{1,0},{6,5},{5,4},{10,9},{9,8},{14,13},{13,12},{18,17},{17,1... | collective-permute-start | bytes 1572872 | tf_op jit(solution)/shard_map/ppermute | solution.py:59
  272.4 52.9 %collective-permute-start.36 = (bf16[512,512]{1,0:T(8,128)(2,1)S(1)}, bf16[512,512]{1,0:T(8,128)(2,1)S(1)}, u32[]{:S(2)}, u32[]{:S(2)}) collective-permute-start(bf16[512,512]{1,0:T(8,128)(2,1)S(1)} %collective-permute-done.25.refs_4_), channel_id=1, source_target_pairs={{1,2},{2,3},{5,6},{6,7},{9,10},{10,11},{13,14},{14,15},{17,18},{18... | collective-permute-start | bytes 1572872 | tf_op jit(solution)/shard_map/ppermute | solution.py:58
  279.8 43.5 %collective-permute-start.28 = (bf16[512,512]{1,0:T(8,128)(2,1)S(1)}, bf16[512,512]{1,0:T(8,128)(2,1)S(1)}, u32[]{:S(2)}, u32[]{:S(2)}) collective-permute-start(bf16[512,512]{1,0:T(8,128)(2,1)S(1)} %get-tuple-element.145.refs_3_), channel_id=1, source_target_pairs={{3,2},{2,1},{1,0},{7,6},{6,5},{5,4},{11,10},{10,9},{9,8},{15,14},{... | collective-permute-start | bytes 1572872 | tf_op jit(solution)/shard_map/ppermute | solution.py:59
  300.8 23.8 %collective-permute-start.26 = (bf16[512,512]{1,0:T(8,128)(2,1)S(1)}, bf16[512,512]{1,0:T(8,128)(2,1)S(1)}, u32[]{:S(2)}, u32[]{:S(2)}) collective-permute-start(bf16[512,512]{1,0:T(8,128)(2,1)S(1)} %get-tuple-element.145.refs_3_), channel_id=1, source_target_pairs={{0,1},{1,2},{2,3},{4,5},{5,6},{6,7},{8,9},{9,10},{10,11},{12,13},{... | collective-permute-start | bytes 1572872 | tf_op jit(solution)/shard_map/ppermute | solution.py:58
  303.3 55.0 %collective-permute-start.35 = (bf16[1024,512]{1,0:T(8,128)(2,1)S(1)}, bf16[1024,512]{1,0:T(8,128)(2,1)S(1)}, u32[]{:S(2)}, u32[]{:S(2)}) collective-permute-start(bf16[1024,512]{1,0:T(8,128)(2,1)S(1)} %broadcast_select_fusion), channel_id=1, source_target_pairs={{2,3},{1,0},{6,7},{5,4},{10,11},{9,8},{14,15},{13,12},{18,19},{17,... | collective-permute-start | bytes 3145736 | tf_op jit(solution)/shard_map/ppermute | solution.py:54
  323.3 33.7 %collective-permute-start.29 = (bf16[512,512]{1,0:T(8,128)(2,1)S(1)}, bf16[512,512]{1,0:T(8,128)(2,1)S(1)}, u32[]{:S(2)}, u32[]{:S(2)}) collective-permute-start(bf16[512,512]{1,0:T(8,128)(2,1)S(1)} %collective-permute-done.28.refs_9_), channel_id=1, source_target_pairs={{2,1},{1,0},{6,5},{5,4},{10,9},{9,8},{14,13},{13,12},{18,17},{17,1... | collective-permute-start | bytes 1572872 | tf_op jit(solution)/shard_map/ppermute | solution.py:59
  324.6 32.4 %collective-permute-start.27 = (bf16[512,512]{1,0:T(8,128)(2,1)S(1)}, bf16[512,512]{1,0:T(8,128)(2,1)S(1)}, u32[]{:S(2)}, u32[]{:S(2)}) collective-permute-start(bf16[512,512]{1,0:T(8,128)(2,1)S(1)} %collective-permute-done.26.refs_4_), channel_id=1, source_target_pairs={{1,2},{2,3},{5,6},{6,7},{9,10},{10,11},{13,14},{14,15},{17,18},{18... | collective-permute-start | bytes 1572872 | tf_op jit(solution)/shard_map/ppermute | solution.py:58
  325.4 40.5 %collective-permute-start.39 = (bf16[512,512]{1,0:T(8,128)(2,1)S(1)}, bf16[512,512]{1,0:T(8,128)(2,1)}, u32[]{:S(2)}, u32[]{:S(2)}) collective-permute-start(bf16[512,512]{1,0:T(8,128)(2,1)S(1)} %broadcast_select_fusion.5), channel_id=1, source_target_pairs={{2,3},{1,0},{6,7},{5,4},{10,11},{9,8},{14,15},{13,12},{18,19},{17,... | collective-permute-start | bytes 1572872 | tf_op jit(solution)/shard_map/ppermute | solution.py:54
  357.0 30.6 %collective-permute-start.30 = (bf16[512,512]{1,0:T(8,128)(2,1)S(1)}, bf16[512,512]{1,0:T(8,128)(2,1)}, u32[]{:S(2)}, u32[]{:S(2)}) collective-permute-start(bf16[512,512]{1,0:T(8,128)(2,1)S(1)} %broadcast_select_fusion.6), channel_id=1, source_target_pairs={{2,3},{1,0},{6,7},{5,4},{10,11},{9,8},{14,15},{13,12},{18,19},{17,... | collective-permute-start | bytes 1572872 | tf_op jit(solution)/shard_map/ppermute | solution.py:54
  418.7 326.8 %reduce-scatter.7.cloned.1.call-start = ((), (), s32[]{:S(2)}) async-start(), calls=%async_computation.8 | async-start | bytes 9437184 | tf_op jit(solution)/shard_map/reduce_scatter | solution.py:894
  432.8 420.0 %reduce-scatter.11.cloned.1.call-start = ((), (), s32[]{:S(2)}) async-start(), calls=%async_computation.10 | async-start | bytes 4718592 | tf_op jit(solution)/shard_map/reduce_scatter | solution.py:894
  515.8 23.9 %collective-permute-start.60 = (bf16[512,512]{1,0:T(8,128)(2,1)S(1)}, bf16[512,512]{1,0:T(8,128)(2,1)S(1)}, u32[]{:S(2)}, u32[]{:S(2)}) collective-permute-start(bf16[512,512]{1,0:T(8,128)(2,1)S(1)} %fusion.19.refs_6_), channel_id=1, source_target_pairs={{3,2},{2,1},{1,0},{7,6},{6,5},{5,4},{11,10},{10,9},{9,8},{15,14},{... | collective-permute-start | bytes 1572872 | tf_op jit(solution)/shard_map/ppermute | solution.py:59
  528.9 21.7 %collective-permute-start.56 = (bf16[512,512]{1,0:T(8,128)(2,1)S(1)}, bf16[512,512]{1,0:T(8,128)(2,1)S(1)}, u32[]{:S(2)}, u32[]{:S(2)}) collective-permute-start(bf16[512,512]{1,0:T(8,128)(2,1)S(1)} %get-tuple-element.157.refs_6_), channel_id=1, source_target_pairs={{3,2},{2,1},{1,0},{7,6},{6,5},{5,4},{11,10},{10,9},{9,8},{15,14},{... | collective-permute-start | bytes 1572872 | tf_op jit(solution)/shard_map/ppermute | solution.py:59
  530.2 21.7 %collective-permute-start.51 = (bf16[512,512]{1,0:T(8,128)(2,1)S(1)}, bf16[512,512]{1,0:T(8,128)(2,1)S(1)}, u32[]{:S(2)}, u32[]{:S(2)}) collective-permute-start(bf16[512,512]{1,0:T(8,128)(2,1)S(1)} %get-tuple-element.157.refs_6_), channel_id=1, source_target_pairs={{0,1},{1,2},{2,3},{4,5},{5,6},{6,7},{8,9},{9,10},{10,11},{12,13},{... | collective-permute-start | bytes 1572872 | tf_op jit(solution)/shard_map/ppermute | solution.py:58
  605.1 258.2 %reduce-scatter.9.cloned.1.call-start = ((), (), s32[]{:S(2)}) async-start(), calls=%async_computation.9 | async-start | bytes 14155776 | tf_op jit(solution)/shard_map/reduce_scatter | solution.py:894
  691.3 34.8 %collective-permute-start.68 = (bf16[512,512]{1,0:T(8,128)(2,1)}, bf16[512,512]{1,0:T(8,128)(2,1)}, u32[]{:S(2)}, u32[]{:S(2)}) collective-permute-start(bf16[512,512]{1,0:T(8,128)(2,1)} %add_convert_fusion.13), channel_id=1, source_target_pairs={{3,2},{2,1},{7,6},{6,5},{11,10},{10,9},{15,14},{14,13},{19,18},{18... | collective-permute-start | bytes 1572872 | tf_op jit(solution)/shard_map/ppermute | solution.py:97
  692.8 33.3 %collective-permute-start.66 = (bf16[512,512]{1,0:T(8,128)(2,1)}, bf16[512,512]{1,0:T(8,128)(2,1)}, u32[]{:S(2)}, u32[]{:S(2)}) collective-permute-start(bf16[512,512]{1,0:T(8,128)(2,1)} %add_convert_fusion.13), channel_id=1, source_target_pairs={{0,1},{1,2},{4,5},{5,6},{8,9},{9,10},{12,13},{13,14},{16,17},{17,1... | collective-permute-start | bytes 1572872 | tf_op jit(solution)/shard_map/ppermute | solution.py:96
  704.1 32.1 %collective-permute-start.75 = (bf16[512,512]{1,0:T(8,128)(2,1)}, bf16[512,512]{1,0:T(8,128)(2,1)}, u32[]{:S(2)}, u32[]{:S(2)}) collective-permute-start(bf16[512,512]{1,0:T(8,128)(2,1)} %add_convert_fusion.9), channel_id=1, source_target_pairs={{3,2},{2,1},{7,6},{6,5},{11,10},{10,9},{15,14},{14,13},{19,18},{18... | collective-permute-start | bytes 1572872 | tf_op jit(solution)/shard_map/ppermute | solution.py:97
  705.6 30.6 %collective-permute-start.73 = (bf16[512,512]{1,0:T(8,128)(2,1)}, bf16[512,512]{1,0:T(8,128)(2,1)}, u32[]{:S(2)}, u32[]{:S(2)}) collective-permute-start(bf16[512,512]{1,0:T(8,128)(2,1)} %add_convert_fusion.9), channel_id=1, source_target_pairs={{0,1},{1,2},{4,5},{5,6},{8,9},{9,10},{12,13},{13,14},{16,17},{17,1... | collective-permute-start | bytes 1572872 | tf_op jit(solution)/shard_map/ppermute | solution.py:96
  728.7 29.4 %collective-permute-start.67 = (bf16[512,512]{1,0:T(8,128)(2,1)}, bf16[512,512]{1,0:T(8,128)(2,1)}, u32[]{:S(2)}, u32[]{:S(2)}) collective-permute-start(bf16[512,512]{1,0:T(8,128)(2,1)} %get-tuple-element.160), channel_id=1, source_target_pairs={{0,1},{1,2},{2,3},{4,5},{5,6},{6,7},{8,9},{9,10},{10,11},{12,13},{... | collective-permute-start | bytes 1572872 | tf_op jit(solution)/shard_map/ppermute | solution.py:103
  734.9 27.2 %collective-permute-start.69 = (bf16[512,512]{1,0:T(8,128)(2,1)}, bf16[512,512]{1,0:T(8,128)(2,1)}, u32[]{:S(2)}, u32[]{:S(2)}) collective-permute-start(bf16[512,512]{1,0:T(8,128)(2,1)} %get-tuple-element.161), channel_id=1, source_target_pairs={{3,2},{2,1},{1,0},{7,6},{6,5},{5,4},{11,10},{10,9},{9,8},{15,14},{... | collective-permute-start | bytes 1572872 | tf_op jit(solution)/shard_map/ppermute | solution.py:104
  738.8 23.3 %collective-permute-start.74 = (bf16[512,512]{1,0:T(8,128)(2,1)}, bf16[512,512]{1,0:T(8,128)(2,1)}, u32[]{:S(2)}, u32[]{:S(2)}) collective-permute-start(bf16[512,512]{1,0:T(8,128)(2,1)} %get-tuple-element.162), channel_id=1, source_target_pairs={{0,1},{1,2},{2,3},{4,5},{5,6},{6,7},{8,9},{9,10},{10,11},{12,13},{... | collective-permute-start | bytes 1572872 | tf_op jit(solution)/shard_map/ppermute | solution.py:103
  744.1 20.9 %collective-permute-start.76 = (bf16[512,512]{1,0:T(8,128)(2,1)}, bf16[512,512]{1,0:T(8,128)(2,1)}, u32[]{:S(2)}, u32[]{:S(2)}) collective-permute-start(bf16[512,512]{1,0:T(8,128)(2,1)} %get-tuple-element.163), channel_id=1, source_target_pairs={{3,2},{2,1},{1,0},{7,6},{6,5},{5,4},{11,10},{10,9},{9,8},{15,14},{... | collective-permute-start | bytes 1572872 | tf_op jit(solution)/shard_map/ppermute | solution.py:104
  758.1 92.9 %collective-permute-start.52 = (bf16[1024,512]{1,0:T(8,128)(2,1)S(1)}, bf16[1024,512]{1,0:T(8,128)(2,1)S(1)}, u32[]{:S(2)}, u32[]{:S(2)}) collective-permute-start(bf16[1024,512]{1,0:T(8,128)(2,1)S(1)} %get-tuple-element.149), channel_id=1, source_target_pairs={{0,1},{1,2},{2,3},{3,0},{4,5},{5,6},{6,7},{7,4},{8,9},{9,10},{10,1... | collective-permute-start | bytes 3145736 | tf_op jit(solution)/shard_map/ppermute | solution.py:119
  758.1 92.9 %collective-permute-start.54 = (bf16[1024,512]{1,0:T(8,128)(2,1)S(1)}, bf16[1024,512]{1,0:T(8,128)(2,1)S(1)}, u32[]{:S(2)}, u32[]{:S(2)}) collective-permute-start(bf16[1024,512]{1,0:T(8,128)(2,1)S(1)} %get-tuple-element.150), channel_id=1, source_target_pairs={{0,3},{1,0},{2,1},{3,2},{4,7},{5,4},{6,5},{7,6},{8,11},{9,8},{10,9... | collective-permute-start | bytes 3145736 | tf_op jit(solution)/shard_map/ppermute | solution.py:119
  762.1 88.9 %collective-permute-start.53 = (bf16[1024,512]{1,0:T(8,128)(2,1)S(1)}, bf16[1024,512]{1,0:T(8,128)(2,1)S(1)}, u32[]{:S(2)}, u32[]{:S(2)}) collective-permute-start(bf16[1024,512]{1,0:T(8,128)(2,1)S(1)} %get-tuple-element.151), channel_id=1, source_target_pairs={{0,2},{1,3},{2,0},{3,1},{4,6},{5,7},{6,4},{7,5},{8,10},{9,11},{10,... | collective-permute-start | bytes 3145736 | tf_op jit(solution)/shard_map/ppermute | solution.py:119
  762.1 85.7 %collective-permute-start.71 = (f32[8,128]{1,0:T(8,128)S(1)}, f32[8,128]{1,0:T(8,128)S(1)}, u32[]{:S(2)}, u32[]{:S(2)}) collective-permute-start(f32[8,128]{1,0:T(8,128)S(1)} %bitcast_add_fusion), channel_id=1, source_target_pairs={{0,2},{1,3},{2,0},{3,1},{4,6},{5,7},{6,4},{7,5},{8,10},{9,11},{10,... | collective-permute-start | bytes 12296 | tf_op jit(solution)/shard_map/ppermute | solution.py:133
  (109 other events, 1959.5 us)
Sparse Core Ops, SparseCore 0:
  11.1 74.7 all-gather.3
  87.7 36.5 all-gather.5
  136.8 73.9 all-gather.7
  418.8 54.3 reduce-scatter.4
  476.5 71.5 reduce-scatter.6
  605.2 52.9 reduce-scatter.10
  670.5 94.0 reduce-scatter.8

commit v8 on v7

--- a/solution.py
+++ b/solution.py
@@ -855,7 +855,7 @@
     mlp_parts = nt(hidden, mlp_full[:, 2 * units :]).astype(BF16)
 
     grad_own[0] = after(grad_own[0], grad_gate_up, grad_down)
-    mlp_out = routed_scatter(after(mlp_parts, grad_pairs[-1][0][0]), TP)
+    mlp_out = routed_scatter(after(mlp_parts, grad_pairs[-1][-1][0]), TP)
     layer_output = (jnp.concatenate(middle) + mlp_out).astype(BF16)
     shared = []
     partial_state = None
@@ -898,7 +898,9 @@
     s_gate, s_up = s_gate_up[:, :units], s_gate_up[:, units:]
     s_out = shard(grad_out)
     s_in = shard(grad_in_w)
-    inner_attn, s_down, s_gate, s_up = lax.optimization_barrier((inner_attn, s_down, s_gate, s_up))
+    inner_attn, s_down, s_gate, s_up, s_out, layer_output = lax.optimization_barrier(
+        (inner_attn, s_down, s_gate, s_up, s_out, layer_output)
+    )
     inner_attn = row_total(inner_attn)
     grad_input, gain_attn_sum = [], 0.0
     early = ()

time: 880 us -> 816 us (0.927)
  waiting for transfers between devices: 337 us -> 278 us
    ppermute x5, waiting for transfers between devices: 88.5 us -> 3.78 us  [swap_sum(): x = x + lax.ppermute(x, axis, [(j, j ^ g) for j in range(n)])]
    ppermute x6, waiting for transfers between devices: 30 us -> 99 us  [line_scatter(): from_left = from_right = lax.ppermute(data, axis, r_pairs + l_pairs)]
    ppermute x14, starting transfers between devices: 63.1 us -> 39.1 us  [line_gather(): rights.append(lax.ppermute(rights[-1], axis, r_pairs))]
    ppermute x6, starting transfers between devices: 27.7 us -> 50.4 us  [line_scatter(): from_left = lax.ppermute(r_data, axis, r_pairs)]
    ppermute x14, waiting for transfers between devices: 111 us -> 90.4 us  [line_gather(): lefts.append(lax.ppermute(lefts[-1], axis, l_pairs))]
    ppermute x6, waiting for transfers between devices: 22.3 us -> 7.4 us  [line_scatter(): from_left = lax.ppermute(data, axis, r_pairs)]
  transfers between devices with their start and end apart: 87 -> 87, of which waited for: 32 -> 33; matrix products, arithmetic and copies ran while one was open for 17% -> 19% of each run, Pallas kernels for 14% -> 18%
where the time goes in v8:
time: 816 us; the launch traced here: 811 us
  waiting for transfers between devices  278 us (34%)
  starting transfers between devices  201 us (25%)
  Pallas kernels  149 us (18%)
  matrix products  76.7 us (9%)
  other arithmetic  63.3 us (8%)
  local copies, waits for them, and re-layouts  26 us (3%)
  between operations  16.2 us (2%)
    ppermute x6, waiting for transfers between devices, line_scatter(): from_left = from_right = lax.ppermute(data, axis, r_pairs + l_pairs)  99 us
    ppermute x14, waiting for transfers between devices, line_gather(): lefts.append(lax.ppermute(lefts[-1], axis, l_pairs))  90.4 us
    ppermute x6, starting transfers between devices, line_scatter(): from_left = lax.ppermute(r_data, axis, r_pairs)  50.4 us
    dot_general x4, matrix products, tn(): lax.dot_general(a, b, (((0,), (0,)), ((), ())), preferred_element_type=F32)  45.5 us
    pallas_call x2, Pallas kernels, mlp(): pl.pallas_call(lambda *refs: mlp_kernel(units, len(blocks), *refs), grid=...  43.3 us
    ppermute x14, starting transfers between devices, line_gather(): rights.append(lax.ppermute(rights[-1], axis, r_pairs))  39.1 us
    dot_general x3, matrix products, nt(): lax.dot_general(a, b, (((1,), (1,)), ((), ())), preferred_element_type=F32)  31.1 us
    pallas_call x2, Pallas kernels, project(): pl.pallas_call(lambda *refs: project_kernel(part, parts, heads, len(block...  26.3 us
  transfers between devices with their start and end apart: 87, of which 33 were waited for; matrix products, arithmetic and copies ran while one was open for 19% of the time, Pallas kernels for 18%

profile of v8, /device:TPU:0, one launch (start us, length us, event | category | flops | bytes accessed | tf_op | source)
XLA Modules:
  0.0 810.8 jit_solution(12649263460424837390)
XLA Ops:
  26.6 5.5 fusion.16
  38.2 5.4 collective-permute-start.2
  43.6 7.8 collective-permute-done.2
  55.6 15.6 %collective-permute-done.11.refs_10_ = bf16[512,512]{1,0:T(8,128)(2,1)S(1)} collective-permute-done((bf16[512,512]{1,0:T(8,128)(2,1)}, bf16[512,512]{1,0:T(8,128)(2,1)S(1)}, u32[]{:S(2)}, u32[]{:S(2)}) %collective-permute-start.11) | collective-permute-done | bytes 524320 | tf_op jit(solution)/shard_map/ppermute | solution.py:59
  72.6 9.8 %collective-permute-done.6.refs_10_ = bf16[512,512]{1,0:T(8,128)(2,1)S(1)} collective-permute-done((bf16[512,512]{1,0:T(8,128)(2,1)}, bf16[512,512]{1,0:T(8,128)(2,1)S(1)}, u32[]{:S(2)}, u32[]{:S(2)}) %collective-permute-start.6) | collective-permute-done | bytes 524320 | tf_op jit(solution)/shard_map/ppermute | solution.py:59
  85.4 8.3 %collective-permute-done.12.refs_8_.refs_11_ = bf16[512,512]{1,0:T(8,128)(2,1)S(1)} collective-permute-done((bf16[512,512]{1,0:T(8,128)(2,1)S(1)}, bf16[512,512]{1,0:T(8,128)(2,1)S(1)}, u32[]{:S(2)}, u32[]{:S(2)}) %collective-permute-start.12) | collective-permute-done | bytes 524320 | tf_op jit(solution)/shard_map/ppermute | solution.py:54
  94.5 12.6 %proj.2 = (bf16[1024,2048]{1,0:T(8,128)(2,1)}, bf16[1024,512]{1,0:T(8,128)(2,1)}, bf16[1024,512]{1,0:T(8,128)(2,1)}, bf16[1024,1024]{1,0:T(8,128)(2,1)}, f32[512...) custom-call(s32[1]{0:T(128)} %bitcast.refs_0_, f32[2]{0:T(128)} %negate_log-plus-one_fusion.1.refs_1_.refs_0_, ...), custom_call_target="tpu_custom_call" | custom-call | flops 4294967296 | bytes 20971520 | tf_op jit(solution)/shard_map/proj/pallas_call | solution.py:289
  107.9 13.8 %proj.3 = (bf16[1024,2048]{1,0:T(8,128)(2,1)}, bf16[1024,512]{1,0:T(8,128)(2,1)}, bf16[1024,512]{1,0:T(8,128)(2,1)}, bf16[1024,1024]{1,0:T(8,128)(2,1)}, f32[512...) custom-call(s32[1]{0:T(128)} %bitcast.refs_0_, ...), custom_call_target="tpu_custom_call", output_to_operand_aliasing={{0}: (14, {}), {1}: (15, {}), {2}: (16, {}), {3}: (17, {})} | custom-call | flops 4294967296 | bytes 20971520 | tf_op jit(solution)/shard_map/proj/pallas_call | solution.py:289
  127.3 12.5 %collective-permute-done.14.refs_8_.refs_9_ = bf16[2,256,512]{2,1,0:T(8,128)(2,1)S(1)} collective-permute-done((bf16[2,256,512]{2,1,0:T(8,128)(2,1)S(1)}, bf16[2,256,512]{2,1,0:T(8,128)(2,1)S(1)}, u32[]{:S(2)}, u32[]{:S(2)}) %collective-permute-start.14) | collective-permute-done | bytes 524320 | tf_op jit(solution)/shard_map/ppermute | solution.py:153
  140.1 8.9 %prod.1.refs_5_.refs_4_ = f32[1024,1024]{1,0:T(8,128)} custom-call(bf16[1024,2048]{1,0:T(8,128)(2,1)} %get-tuple-element.87.x_ref, bf16[2048,3072]{1,0:T(8,128)(2,1)} %all-gather.4.cloned.1.call-done.refs_3_.w_ref), custom_call_target="tpu_custom_call" | custom-call | flops 4294967296 | bytes 12582912 | tf_op jit(solution)/shard_map/prod/pallas_call | solution.py:336
  149.0 9.4 %fwd.2 = (bf16[1024,1024]{1,0:T(8,128)(2,1)}, f32[1024,1024]{1,0:T(8,128)}, bf16[512,2048]{1,0:T(8,128)(2,1)}) custom-call(f32[2]{0:T(128)} %negate_log-plus-one_fusion.1.refs_1_.refs_0_, f32[2,2]{1,0:T(2,128)} %pad_maximum_fusion.3.refs_1_, bf16[1024,512]{1,0:T(8,128)(2,1)} %get-tuple-element.84.refs_2_.refs_3_, ...), custom_call_target="tpu_custom_call" | custom-call | flops 3221225472 | bytes 10485760 | tf_op jit(solution)/shard_map/fwd/pallas_call | solution.py:517
  161.0 11.0 %collective-permute-done.15 = bf16[512,512]{1,0:T(8,128)(2,1)S(1)} collective-permute-done((bf16[512,512]{1,0:T(8,128)(2,1)S(1)}, bf16[512,512]{1,0:T(8,128)(2,1)S(1)}, u32[]{:S(2)}, u32[]{:S(2)}) %collective-permute-start.15) | collective-permute-done | bytes 524320 | tf_op jit(solution)/shard_map/ppermute | solution.py:89
  183.3 10.5 %fwd.3 = (bf16[1024,1024]{1,0:T(8,128)(2,1)}, f32[1024,1024]{1,0:T(8,128)}, bf16[512,2048]{1,0:T(8,128)(2,1)}) custom-call(f32[2]{0:T(128)} %negate_log-plus-one_fusion.1.refs_1_.refs_0_, f32[2,2]{1,0:T(2,128)} %pad_maximum_fusion.3.refs_1_, bf16[1024,512]{1,0:T(8,128)(2,1)} %get-tuple-element.84.refs_2_.refs_3_, ...), custom_call_target="tpu_custom_call", output_to_operand_aliasing={{0}: (9, {}), {1}: (10, {})} | custom-call | flops 4026531840 | bytes 10485760 | tf_op jit(solution)/shard_map/fwd/pallas_call | solution.py:517
  203.1 5.4 collective-permute-start.17
  215.5 8.3 %collective-permute-done.35 = bf16[512,512]{1,0:T(8,128)(2,1)S(1)} collective-permute-done((bf16[512,512]{1,0:T(8,128)(2,1)S(1)}, bf16[512,512]{1,0:T(8,128)(2,1)S(1)}, u32[]{:S(2)}, u32[]{:S(2)}) %collective-permute-start.35) | collective-permute-done | bytes 524320 | tf_op jit(solution)/shard_map/ppermute | solution.py:89
  225.9 5.2 collective-permute-start.36
  250.6 15.3 %collective-permute-start.37 = (bf16[512,512]{1,0:T(8,128)(2,1)S(1)}, bf16[512,512]{1,0:T(8,128)(2,1)S(1)}, u32[]{:S(2)}, u32[]{:S(2)}) collective-permute-start(bf16[512,512]{1,0:T(8,128)(2,1)S(1)} %get-tuple-element.170), channel_id=1, source_target_pairs={{0,1},{1,2},{2,3},{4,5},{5,6},{6,7},{8,9},{9,10},{10,11},{12,13},{... | collective-permute-start | bytes 1572872 | tf_op jit(solution)/shard_map/ppermute | solution.py:103
  273.6 9.9 %collective-permute-done.39 = bf16[512,512]{1,0:T(8,128)(2,1)S(1)} collective-permute-done((bf16[512,512]{1,0:T(8,128)(2,1)S(1)}, bf16[512,512]{1,0:T(8,128)(2,1)S(1)}, u32[]{:S(2)}, u32[]{:S(2)}) %collective-permute-start.39) | collective-permute-done | bytes 524320 | tf_op jit(solution)/shard_map/ppermute | solution.py:104
  285.0 5.2 collective-permute-start.40
  291.9 25.3 %collective-permute-done.23.refs_7_ = bf16[512,512]{1,0:T(8,128)(2,1)S(1)} collective-permute-done((bf16[512,512]{1,0:T(8,128)(2,1)S(1)}, bf16[512,512]{1,0:T(8,128)(2,1)S(1)}, u32[]{:S(2)}, u32[]{:S(2)}) %collective-permute-start.23) | collective-permute-done | bytes 524320 | tf_op jit(solution)/shard_map/ppermute | solution.py:59
  320.1 8.5 %collective-permute-done.42.refs_9_ = bf16[512,512]{1,0:T(8,128)(2,1)} collective-permute-done((bf16[512,512]{1,0:T(8,128)(2,1)S(1)}, bf16[512,512]{1,0:T(8,128)(2,1)}, u32[]{:S(2)}, u32[]{:S(2)}) %collective-permute-start.42) | collective-permute-done | bytes 524320 | tf_op jit(solution)/shard_map/ppermute | solution.py:59
  330.9 8.8 %collective-permute-done.24.refs_5_.refs_8_ = bf16[512,512]{1,0:T(8,128)(2,1)S(1)} collective-permute-done((bf16[512,512]{1,0:T(8,128)(2,1)S(1)}, bf16[512,512]{1,0:T(8,128)(2,1)S(1)}, u32[]{:S(2)}, u32[]{:S(2)}) %collective-permute-start.24) | collective-permute-done | bytes 524320 | tf_op jit(solution)/shard_map/ppermute | solution.py:54
  340.5 21.6 %mlp.2 = (bf16[1024,2048]{1,0:T(8,128)(2,1)}, bf16[1024,1024]{1,0:T(8,128)(2,1)}, bf16[1024,2048]{1,0:T(8,128)(2,1)}, bf16[1024,2048]{1,0:T(8,128)(2,1)}, f32[512,1]{1,0:T(8,128)}, /*index=5*/bf16[528,2048]{1,0:T(8,128)(2,1)}) custom-call(s32[1]{0:T(128)} %bitcast.refs_0_, f32[1,2048]{1,0:T(1,128)} %get-tuple-element.180.refs_1_, ...), custom_call_target="tpu_custom_call" | custom-call | flops 10737418240 | bytes 27262976 | tf_op jit(solution)/shard_map/mlp/pallas_call | solution.py:417
  367.3 8.6 %collective-permute-done.30 = bf16[528,512]{1,0:T(8,128)(2,1)S(1)} collective-permute-done((bf16[528,512]{1,0:T(8,128)(2,1)S(1)}, bf16[528,512]{1,0:T(8,128)(2,1)S(1)}, u32[]{:S(2)}, u32[]{:S(2)}) %collective-permute-start.30) | collective-permute-done | bytes 540704 | tf_op jit(solution)/shard_map/ppermute | solution.py:89
  377.0 5.2 collective-permute-start.31
  384.7 21.7 %mlp.3 = (bf16[1024,2048]{1,0:T(8,128)(2,1)}, bf16[1024,1024]{1,0:T(8,128)(2,1)}, bf16[1024,2048]{1,0:T(8,128)(2,1)}, bf16[1024,2048]{1,0:T(8,128)(2,1)}, f32[512,1]{1,0:T(8,128)}, /*index=5*/bf16[528,2048]{1,0:T(8,128)(2,1)}) custom-call(s32[1]{0:T(128)} %bitcast.refs_0_, ...), custom_call_target="tpu_custom_call", output_to_operand_aliasing={{0}: (17, {}), {1}: (18, {}), {2}: (19, {}), {3}: (20, {})} | custom-call | flops 10737418240 | bytes 27262976 | tf_op jit(solution)/shard_map/mlp/pallas_call | solution.py:417
  414.3 5.4 collective-permute-start.32
  437.0 5.4 collective-permute-start.45
  447.4 5.8 collective-permute-start.52
  453.2 6.2 convolution_convert_fusion.3
  464.4 7.4 collective-permute-start.55
  479.9 9.1 %collective-permute-done.57.refs_12_ = bf16[512,512]{1,0:T(8,128)(2,1)S(1)} collective-permute-done((bf16[512,512]{1,0:T(8,128)(2,1)S(1)}, bf16[512,512]{1,0:T(8,128)(2,1)S(1)}, u32[]{:S(2)}, u32[]{:S(2)}) %collective-permute-start.57) | collective-permute-done | bytes 524320 | tf_op jit(solution)/shard_map/ppermute | solution.py:59
  490.3 9.9 %collective-permute-done.48.refs_10_ = bf16[512,512]{1,0:T(8,128)(2,1)S(1)} collective-permute-done((bf16[512,512]{1,0:T(8,128)(2,1)S(1)}, bf16[512,512]{1,0:T(8,128)(2,1)S(1)}, u32[]{:S(2)}, u32[]{:S(2)}) %collective-permute-start.48) | collective-permute-done | bytes 524320 | tf_op jit(solution)/shard_map/ppermute | solution.py:59
  503.1 5.5 collective-permute-done.58.refs_10_
  511.0 13.5 %convolution_convert_fusion.1 = bf16[2048,2048]{1,0:T(8,128)(2,1)} fusion(bf16[1024,2048]{1,0:T(8,128)(2,1)S(1)} %copy-done.62, bf16[1024,2048]{1,0:T(8,128)(2,1)} %get-tuple-element.110), kind=kOutput, calls=%fused_computation.1 | convolution fusion | flops 8594128896 | bytes 16777216 | tf_op jit(solution)/shard_map/dot_general | solution.py:26
  525.3 10.9 %gate.2 = (bf16[1024,1024]{1,0:T(8,128)(2,1)}, bf16[1024,1024]{1,0:T(8,128)(2,1)}, bf16[1024,2048]{1,0:T(8,128)(2,1)}, f32[2,256,512]{2,1,0:T(8,128)}, bf16[2,25...) custom-call(s32[1]{0:T(128)} %bitcast.refs_0_, f32[2]{0:T(128)} %negate_log-plus-one_fusion.1.refs_1_.refs_0_, ...), custom_call_target="tpu_custom_call" | custom-call | flops 2415919104 | bytes 8388608 | tf_op jit(solution)/shard_map/gate/pallas_call | solution.py:590
  536.2 11.5 %gate.3 = (bf16[1024,1024]{1,0:T(8,128)(2,1)}, bf16[1024,1024]{1,0:T(8,128)(2,1)}, bf16[1024,2048]{1,0:T(8,128)(2,1)}, f32[2,256,512]{2,1,0:T(8,128)}, bf16[2,25...) custom-call(s32[1]{0:T(128)} %bitcast.refs_0_, ...), custom_call_target="tpu_custom_call", output_to_operand_aliasing={{0}: (14, {}), {1}: (15, {}), {2}: (16, {})} | custom-call | flops 2415919104 | bytes 8388608 | tf_op jit(solution)/shard_map/gate/pallas_call | solution.py:590
  550.0 9.5 %convolution_convert_fusion.2 = bf16[2048,1024]{1,0:T(8,128)(2,1)} fusion(bf16[1024,2048]{1,0:T(8,128)(2,1)} %get-tuple-element.124, bf16[1024,1024]{1,0:T(8,128)(2,1)} %get-tuple-element.125), kind=kOutput, calls=%fused_computation.5 | convolution fusion | flops 4297064448 | bytes 10485760 | tf_op jit(solution)/shard_map/dot_general | solution.py:26
  563.5 12.5 %collective-permute-done.61.refs_11_ = bf16[2,256,512]{2,1,0:T(8,128)(2,1)S(1)} collective-permute-done((bf16[2,256,512]{2,1,0:T(8,128)(2,1)S(1)}, bf16[2,256,512]{2,1,0:T(8,128)(2,1)S(1)}, u32[]{:S(2)}, u32[]{:S(2)}) %collective-permute-start.61) | collective-permute-done | bytes 524320 | tf_op jit(solution)/shard_map/ppermute | solution.py:167
  576.8 21.3 %bwd.1 = (bf16[1024,3072]{1,0:T(8,128)(2,1)}, f32[2,1024,1]{2,1,0:T(8,128)}) custom-call(f32[2]{0:T(128)} %negate_log-plus-one_fusion.1.refs_1_.refs_0_, f32[2,2]{1,0:T(2,128)} %pad_maximum_fusion.3.refs_1_, f32[2,2]{1,0:T(2,128)} %pad_maximum_fusion.4.refs_2_, bf16[1024,512]{1,0:T(8,128)(2,1)} %get-tuple-element.84.refs_2_.refs_3_, ...), custom_call_target="tpu_custom_call" | custom-call | flops 7247757312 | bytes 12582912 | tf_op jit(solution)/shard_map/bwd/pallas_call | solution.py:700
  598.2 11.9 %fusion.12 = bf16[512,2048]{1,0:T(8,128)(2,1)} fusion(bf16[2048,3072]{1,0:T(8,128)(2,1)} %all-gather.4.cloned.1.call-done.refs_3_.w_ref, bf16[1024,3072]{1,0:T(8,128)(2,1)} %get-tuple-element.138), kind=kOutput, calls=%fused_computation.12 | convolution fusion | flops 6443499520 | bytes 17825792 | tf_op jit(solution)/shard_map/dot_general | solution.py:30
  610.1 16.3 %convolution_convert_fusion = bf16[2048,3072]{1,0:T(8,128)(2,1)} fusion(bf16[1024,2048]{1,0:T(8,128)(2,1)S(1)} %copy-done.2, bf16[1024,3072]{1,0:T(8,128)(2,1)S(1)} %copy-done.65), kind=kOutput, calls=%fused_computation | convolution fusion | flops 12891193344 | bytes 23068672 | tf_op jit(solution)/shard_map/dot_general | solution.py:26
  626.4 8.6 %fusion.2 = bf16[1024,2048]{1,0:T(8,128)(2,1)S(1)} fusion(bf16[1024,1024]{1,0:T(8,128)(2,1)} %get-tuple-element.108, bf16[2048,3072]{1,0:T(8,128)(2,1)} %all-gather.8.cloned.1.call-done.refs_2_), kind=kOutput, calls=%fused_computation.4 | convolution fusion | flops 4297064448 | bytes 10485760 | tf_op jit(solution)/shard_map/dot_general | solution.py:30
  645.4 10.7 %fusion.9 = bf16[512,2048]{1,0:T(8,128)(2,1)S(1)} fusion(bf16[2048,3072]{1,0:T(8,128)(2,1)} %all-gather.4.cloned.1.call-done.refs_3_.w_ref, bf16[1024,3072]{1,0:T(8,128)(2,1)} %get-tuple-element.138), kind=kOutput, calls=%fused_computation.11 | convolution fusion | flops 6443499520 | bytes 17825792 | tf_op jit(solution)/shard_map/dot_general | solution.py:30
  656.1 60.5 %collective-permute-done.65 = bf16[512,512]{1,0:T(8,128)(2,1)S(1)} collective-permute-done((bf16[512,512]{1,0:T(8,128)(2,1)S(1)}, bf16[512,512]{1,0:T(8,128)(2,1)S(1)}, u32[]{:S(2)}, u32[]{:S(2)}) %collective-permute-start.65) | collective-permute-done | bytes 524320 | tf_op jit(solution)/shard_map/ppermute | solution.py:89
  727.6 7.9 collective-permute-done.72
  750.0 9.7 %collective-permute-start.67 = (bf16[512,512]{1,0:T(8,128)(2,1)}, bf16[512,512]{1,0:T(8,128)(2,1)}, u32[]{:S(2)}, u32[]{:S(2)}) collective-permute-start(bf16[512,512]{1,0:T(8,128)(2,1)} %get-tuple-element.164), channel_id=1, source_target_pairs={{0,1},{1,2},{2,3},{4,5},{5,6},{6,7},{8,9},{9,10},{10,11},{12,13},{... | collective-permute-start | bytes 1572872 | tf_op jit(solution)/shard_map/ppermute | solution.py:103
  762.4 8.8 %collective-permute-start.74 = (bf16[512,512]{1,0:T(8,128)(2,1)}, bf16[512,512]{1,0:T(8,128)(2,1)}, u32[]{:S(2)}, u32[]{:S(2)}) collective-permute-start(bf16[512,512]{1,0:T(8,128)(2,1)} %get-tuple-element.166), channel_id=1, source_target_pairs={{0,1},{1,2},{2,3},{4,5},{5,6},{6,7},{8,9},{9,10},{10,11},{12,13},{... | collective-permute-start | bytes 1572872 | tf_op jit(solution)/shard_map/ppermute | solution.py:103
  (370 shorter events, 246.2 us)
Async XLA Ops:
  7.2 86.4 %all-gather.4.cloned.1.call-start = ((), (), s32[]{:S(2)}) async-start(), calls=%async_computation.4 | async-start | bytes 14155776 | tf_op jit(solution)/shard_map/all_gather | solution.py:760
  11.0 138.0 %all-gather.6.cloned.1.call-start = ((), (), s32[]{:S(2)}) async-start(), calls=%async_computation.5 | async-start | bytes 4718592 | tf_op jit(solution)/shard_map/all_gather | solution.py:761
  11.8 328.0 %all-gather.8.cloned.1.call-start = ((), (), s32[]{:S(2)}) async-start(), calls=%async_computation.6 | async-start | bytes 14155776 | tf_op jit(solution)/shard_map/all_gather | solution.py:803
  11.9 25.0 %collective-permute-start = (f32[2,512]{1,0:T(2,128)S(1)}, f32[2,512]{1,0:T(2,128)S(1)}, u32[]{:S(2)}, u32[]{:S(2)}) collective-permute-start(f32[2,512]{1,0:T(2,128)S(1)} %get-tuple-element.188), channel_id=1, source_target_pairs={{0,1},{1,2},{2,3},{3,0},{4,5},{5,6},{6,7},{7,4},{8,9},{9,10},{10,1... | collective-permute-start | bytes 12296 | tf_op jit(solution)/shard_map/ppermute | solution.py:125
  15.0 23.2 %collective-permute-start.1 = (f32[2,512]{1,0:T(2,128)S(1)}, f32[2,512]{1,0:T(2,128)S(1)}, u32[]{:S(2)}, u32[]{:S(2)}) collective-permute-start(f32[2,512]{1,0:T(2,128)S(1)} %get-tuple-element.188), channel_id=1, source_target_pairs={{0,2},{1,3},{2,0},{3,1},{4,6},{5,7},{6,4},{7,5},{8,10},{9,11},{10,... | collective-permute-start | bytes 12296 | tf_op jit(solution)/shard_map/ppermute | solution.py:125
  17.7 33.8 %collective-permute-start.8 = (bf16[512,512]{1,0:T(8,128)(2,1)S(1)}, bf16[512,512]{1,0:T(8,128)(2,1)S(1)}, u32[]{:S(2)}, u32[]{:S(2)}) collective-permute-start(bf16[512,512]{1,0:T(8,128)(2,1)S(1)} %get-tuple-element.178.refs_6_), channel_id=1, source_target_pairs={{0,1},{1,2},{2,3},{4,5},{5,6},{6,7},{8,9},{9,10},{10,11},{12,13},{... | collective-permute-start | bytes 1572872 | tf_op jit(solution)/shard_map/ppermute | solution.py:58
  19.7 32.5 %collective-permute-start.10 = (bf16[512,512]{1,0:T(8,128)(2,1)S(1)}, bf16[512,512]{1,0:T(8,128)(2,1)}, u32[]{:S(2)}, u32[]{:S(2)}) collective-permute-start(bf16[512,512]{1,0:T(8,128)(2,1)S(1)} %get-tuple-element.178.refs_6_), channel_id=1, source_target_pairs={{3,2},{2,1},{1,0},{7,6},{6,5},{5,4},{11,10},{10,9},{9,8},{15,14},{... | collective-permute-start | bytes 1572872 | tf_op jit(solution)/shard_map/ppermute | solution.py:59
  21.0 32.5 %collective-permute-start.3 = (bf16[512,512]{1,0:T(8,128)(2,1)S(1)}, bf16[512,512]{1,0:T(8,128)(2,1)S(1)}, u32[]{:S(2)}, u32[]{:S(2)}) collective-permute-start(bf16[512,512]{1,0:T(8,128)(2,1)S(1)} %get-tuple-element.179.refs_6_), channel_id=1, source_target_pairs={{0,1},{1,2},{2,3},{4,5},{5,6},{6,7},{8,9},{9,10},{10,11},{12,13},{... | collective-permute-start | bytes 1572872 | tf_op jit(solution)/shard_map/ppermute | solution.py:58
  54.2 28.2 %collective-permute-start.6 = (bf16[512,512]{1,0:T(8,128)(2,1)}, bf16[512,512]{1,0:T(8,128)(2,1)S(1)}, u32[]{:S(2)}, u32[]{:S(2)}) collective-permute-start(bf16[512,512]{1,0:T(8,128)(2,1)} %collective-permute-done.5.refs_12_), channel_id=1, source_target_pairs={{2,1},{1,0},{6,5},{5,4},{10,9},{9,8},{14,13},{13,12},{18,17},{17,1... | collective-permute-start | bytes 1572872 | tf_op jit(solution)/shard_map/ppermute | solution.py:59
  71.2 22.4 %collective-permute-start.12 = (bf16[512,512]{1,0:T(8,128)(2,1)S(1)}, bf16[512,512]{1,0:T(8,128)(2,1)S(1)}, u32[]{:S(2)}, u32[]{:S(2)}) collective-permute-start(bf16[512,512]{1,0:T(8,128)(2,1)S(1)} %broadcast_select_fusion.7), channel_id=1, source_target_pairs={{2,3},{1,0},{6,7},{5,4},{10,11},{9,8},{14,15},{13,12},{18,19},{17,... | collective-permute-start | bytes 1572872 | tf_op jit(solution)/shard_map/ppermute | solution.py:54
  83.3 23.8 %collective-permute-start.7 = (bf16[512,512]{1,0:T(8,128)(2,1)}, bf16[512,512]{1,0:T(8,128)(2,1)S(1)}, u32[]{:S(2)}, u32[]{:S(2)}) collective-permute-start(bf16[512,512]{1,0:T(8,128)(2,1)} %broadcast_select_fusion.8), channel_id=1, source_target_pairs={{2,3},{1,0},{6,7},{5,4},{10,11},{9,8},{14,15},{13,12},{18,19},{17,... | collective-permute-start | bytes 1572872 | tf_op jit(solution)/shard_map/ppermute | solution.py:54
  139.9 631.4 %reduce-scatter.5.cloned.1.call-start = ((), (), s32[]{:S(2)}) async-start(), calls=%async_computation.7 | async-start | bytes 4718592 | tf_op jit(solution)/shard_map/reduce_scatter | solution.py:894
  178.6 34.0 %collective-permute-start.25 = (bf16[1024,512]{1,0:T(8,128)(2,1)S(1)}, bf16[1024,512]{1,0:T(8,128)(2,1)}, u32[]{:S(2)}, u32[]{:S(2)}) collective-permute-start(bf16[1024,512]{1,0:T(8,128)(2,1)S(1)} %copy-done.18), channel_id=1, source_target_pairs={{0,1},{1,2},{2,3},{4,5},{5,6},{6,7},{8,9},{9,10},{10,11},{12,13},{... | collective-permute-start | bytes 3145736 | tf_op jit(solution)/shard_map/ppermute | solution.py:58
  182.0 32.2 %collective-permute-start.27 = (bf16[1024,512]{1,0:T(8,128)(2,1)S(1)}, bf16[1024,512]{1,0:T(8,128)(2,1)}, u32[]{:S(2)}, u32[]{:S(2)}) collective-permute-start(bf16[1024,512]{1,0:T(8,128)(2,1)S(1)} %copy-done.18), channel_id=1, source_target_pairs={{3,2},{2,1},{1,0},{7,6},{6,5},{5,4},{11,10},{10,9},{9,8},{15,14},{... | collective-permute-start | bytes 3145736 | tf_op jit(solution)/shard_map/ppermute | solution.py:59
  195.0 28.8 %collective-permute-start.35 = (bf16[512,512]{1,0:T(8,128)(2,1)S(1)}, bf16[512,512]{1,0:T(8,128)(2,1)S(1)}, u32[]{:S(2)}, u32[]{:S(2)}) collective-permute-start(bf16[512,512]{1,0:T(8,128)(2,1)S(1)} %constant_dynamic-slice_fusion.6), channel_id=1, source_target_pairs={{0,1},{3,2},{4,5},{7,6},{8,9},{11,10},{12,13},{15,14},{16,17},{19,... | collective-permute-start | bytes 1572872 | tf_op jit(solution)/shard_map/ppermute | solution.py:89
  201.8 29.2 %collective-permute-start.19 = (bf16[512,512]{1,0:T(8,128)(2,1)S(1)}, bf16[512,512]{1,0:T(8,128)(2,1)}, u32[]{:S(2)}, u32[]{:S(2)}) collective-permute-start(bf16[512,512]{1,0:T(8,128)(2,1)S(1)} %get-tuple-element.169), channel_id=1, source_target_pairs={{3,2},{2,1},{1,0},{7,6},{6,5},{5,4},{11,10},{10,9},{9,8},{15,14},{... | collective-permute-start | bytes 1572872 | tf_op jit(solution)/shard_map/ppermute | solution.py:104
  203.1 32.0 %collective-permute-start.17 = (bf16[512,512]{1,0:T(8,128)(2,1)}, bf16[512,512]{1,0:T(8,128)(2,1)}, u32[]{:S(2)}, u32[]{:S(2)}) collective-permute-start(bf16[512,512]{1,0:T(8,128)(2,1)} %get-tuple-element.168), channel_id=1, source_target_pairs={{0,1},{1,2},{2,3},{4,5},{5,6},{6,7},{8,9},{9,10},{10,11},{12,13},{... | collective-permute-start | bytes 1572872 | tf_op jit(solution)/shard_map/ppermute | solution.py:103
  212.6 38.0 %collective-permute-start.26 = (bf16[1024,512]{1,0:T(8,128)(2,1)}, bf16[1024,512]{1,0:T(8,128)(2,1)}, u32[]{:S(2)}, u32[]{:S(2)}) collective-permute-start(bf16[1024,512]{1,0:T(8,128)(2,1)} %collective-permute-done.25.refs_11_), channel_id=1, source_target_pairs={{1,2},{2,3},{5,6},{6,7},{9,10},{10,11},{13,14},{14,15},{17,18},{18... | collective-permute-start | bytes 3145736 | tf_op jit(solution)/shard_map/ppermute | solution.py:58
  214.3 51.7 %collective-permute-start.28 = (bf16[1024,512]{1,0:T(8,128)(2,1)}, bf16[1024,512]{1,0:T(8,128)(2,1)}, u32[]{:S(2)}, u32[]{:S(2)}) collective-permute-start(bf16[1024,512]{1,0:T(8,128)(2,1)} %collective-permute-done.27.refs_16_), channel_id=1, source_target_pairs={{2,1},{1,0},{6,5},{5,4},{10,9},{9,8},{14,13},{13,12},{18,17},{17,1... | collective-permute-start | bytes 3145736 | tf_op jit(solution)/shard_map/ppermute | solution.py:59
  236.8 31.8 %collective-permute-start.20 = (bf16[512,512]{1,0:T(8,128)(2,1)S(1)}, bf16[512,512]{1,0:T(8,128)(2,1)S(1)}, u32[]{:S(2)}, u32[]{:S(2)}) collective-permute-start(bf16[512,512]{1,0:T(8,128)(2,1)S(1)} %get-tuple-element.151.refs_3_), channel_id=1, source_target_pairs={{0,1},{1,2},{2,3},{4,5},{5,6},{6,7},{8,9},{9,10},{10,11},{12,13},{... | collective-permute-start | bytes 1572872 | tf_op jit(solution)/shard_map/ppermute | solution.py:58
  246.4 25.9 %collective-permute-start.22 = (bf16[512,512]{1,0:T(8,128)(2,1)S(1)}, bf16[512,512]{1,0:T(8,128)(2,1)S(1)}, u32[]{:S(2)}, u32[]{:S(2)}) collective-permute-start(bf16[512,512]{1,0:T(8,128)(2,1)S(1)} %get-tuple-element.151.refs_3_), channel_id=1, source_target_pairs={{3,2},{2,1},{1,0},{7,6},{6,5},{5,4},{11,10},{10,9},{9,8},{15,14},{... | collective-permute-start | bytes 1572872 | tf_op jit(solution)/shard_map/ppermute | solution.py:59
  249.3 34.2 %collective-permute-start.39 = (bf16[512,512]{1,0:T(8,128)(2,1)S(1)}, bf16[512,512]{1,0:T(8,128)(2,1)S(1)}, u32[]{:S(2)}, u32[]{:S(2)}) collective-permute-start(bf16[512,512]{1,0:T(8,128)(2,1)S(1)} %get-tuple-element.171), channel_id=1, source_target_pairs={{3,2},{2,1},{1,0},{7,6},{6,5},{5,4},{11,10},{10,9},{9,8},{15,14},{... | collective-permute-start | bytes 1572872 | tf_op jit(solution)/shard_map/ppermute | solution.py:104
  250.6 32.9 %collective-permute-start.37 = (bf16[512,512]{1,0:T(8,128)(2,1)S(1)}, bf16[512,512]{1,0:T(8,128)(2,1)S(1)}, u32[]{:S(2)}, u32[]{:S(2)}) collective-permute-start(bf16[512,512]{1,0:T(8,128)(2,1)S(1)} %get-tuple-element.170), channel_id=1, source_target_pairs={{0,1},{1,2},{2,3},{4,5},{5,6},{6,7},{8,9},{9,10},{10,11},{12,13},{... | collective-permute-start | bytes 1572872 | tf_op jit(solution)/shard_map/ppermute | solution.py:103
  267.3 62.6 %collective-permute-start.29 = (bf16[1024,512]{1,0:T(8,128)(2,1)S(1)}, bf16[1024,512]{1,0:T(8,128)(2,1)S(1)}, u32[]{:S(2)}, u32[]{:S(2)}) collective-permute-start(bf16[1024,512]{1,0:T(8,128)(2,1)S(1)} %broadcast_select_fusion), channel_id=1, source_target_pairs={{2,3},{1,0},{6,7},{5,4},{10,11},{9,8},{14,15},{13,12},{18,19},{17,... | collective-permute-start | bytes 3145736 | tf_op jit(solution)/shard_map/ppermute | solution.py:54
  268.6 23.3 %collective-permute-start.21 = (bf16[512,512]{1,0:T(8,128)(2,1)S(1)}, bf16[512,512]{1,0:T(8,128)(2,1)S(1)}, u32[]{:S(2)}, u32[]{:S(2)}) collective-permute-start(bf16[512,512]{1,0:T(8,128)(2,1)S(1)} %collective-permute-done.20.refs_4_), channel_id=1, source_target_pairs={{1,2},{2,3},{5,6},{6,7},{9,10},{10,11},{13,14},{14,15},{17,18},{18... | collective-permute-start | bytes 1572872 | tf_op jit(solution)/shard_map/ppermute | solution.py:58
  272.3 44.9 %collective-permute-start.23 = (bf16[512,512]{1,0:T(8,128)(2,1)S(1)}, bf16[512,512]{1,0:T(8,128)(2,1)S(1)}, u32[]{:S(2)}, u32[]{:S(2)}) collective-permute-start(bf16[512,512]{1,0:T(8,128)(2,1)S(1)} %collective-permute-done.22.refs_9_), channel_id=1, source_target_pairs={{2,1},{1,0},{6,5},{5,4},{10,9},{9,8},{14,13},{13,12},{18,17},{17,1... | collective-permute-start | bytes 1572872 | tf_op jit(solution)/shard_map/ppermute | solution.py:59
  285.0 33.6 %collective-permute-start.40 = (bf16[512,512]{1,0:T(8,128)(2,1)S(1)}, bf16[512,512]{1,0:T(8,128)(2,1)}, u32[]{:S(2)}, u32[]{:S(2)}) collective-permute-start(bf16[512,512]{1,0:T(8,128)(2,1)S(1)} %get-tuple-element.149.refs_3_), channel_id=1, source_target_pairs={{0,1},{1,2},{2,3},{4,5},{5,6},{6,7},{8,9},{9,10},{10,11},{12,13},{... | collective-permute-start | bytes 1572872 | tf_op jit(solution)/shard_map/ppermute | solution.py:58
  290.2 38.4 %collective-permute-start.42 = (bf16[512,512]{1,0:T(8,128)(2,1)S(1)}, bf16[512,512]{1,0:T(8,128)(2,1)}, u32[]{:S(2)}, u32[]{:S(2)}) collective-permute-start(bf16[512,512]{1,0:T(8,128)(2,1)S(1)} %get-tuple-element.149.refs_3_), channel_id=1, source_target_pairs={{3,2},{2,1},{1,0},{7,6},{6,5},{5,4},{11,10},{10,9},{9,8},{15,14},{... | collective-permute-start | bytes 1572872 | tf_op jit(solution)/shard_map/ppermute | solution.py:59
  317.3 22.4 %collective-permute-start.24 = (bf16[512,512]{1,0:T(8,128)(2,1)S(1)}, bf16[512,512]{1,0:T(8,128)(2,1)S(1)}, u32[]{:S(2)}, u32[]{:S(2)}) collective-permute-start(bf16[512,512]{1,0:T(8,128)(2,1)S(1)} %broadcast_select_fusion.6), channel_id=1, source_target_pairs={{2,3},{1,0},{6,7},{5,4},{10,11},{9,8},{14,15},{13,12},{18,19},{17,... | collective-permute-start | bytes 1572872 | tf_op jit(solution)/shard_map/ppermute | solution.py:54
  318.6 46.3 %collective-permute-start.41 = (bf16[512,512]{1,0:T(8,128)(2,1)}, bf16[512,512]{1,0:T(8,128)(2,1)}, u32[]{:S(2)}, u32[]{:S(2)}) collective-permute-start(bf16[512,512]{1,0:T(8,128)(2,1)} %collective-permute-done.40.refs_4_), channel_id=1, source_target_pairs={{1,2},{2,3},{5,6},{6,7},{9,10},{10,11},{13,14},{14,15},{17,18},{18... | collective-permute-start | bytes 1572872 | tf_op jit(solution)/shard_map/ppermute | solution.py:58
  328.6 36.3 %collective-permute-start.43 = (bf16[512,512]{1,0:T(8,128)(2,1)}, bf16[512,512]{1,0:T(8,128)(2,1)}, u32[]{:S(2)}, u32[]{:S(2)}) collective-permute-start(bf16[512,512]{1,0:T(8,128)(2,1)} %collective-permute-done.42.refs_9_), channel_id=1, source_target_pairs={{2,1},{1,0},{6,5},{5,4},{10,9},{9,8},{14,13},{13,12},{18,17},{17,1... | collective-permute-start | bytes 1572872 | tf_op jit(solution)/shard_map/ppermute | solution.py:59
  377.0 29.3 %collective-permute-start.31 = (bf16[528,512]{1,0:T(8,128)(2,1)}, bf16[528,512]{1,0:T(8,128)(2,1)}, u32[]{:S(2)}, u32[]{:S(2)}) collective-permute-start(bf16[528,512]{1,0:T(8,128)(2,1)} %add_convert_fusion.5), channel_id=1, source_target_pairs={{0,1},{1,2},{4,5},{5,6},{8,9},{9,10},{12,13},{13,14},{16,17},{17,1... | collective-permute-start | bytes 1622024 | tf_op jit(solution)/shard_map/ppermute | solution.py:96
  382.2 24.1 %collective-permute-start.33 = (bf16[528,512]{1,0:T(8,128)(2,1)}, bf16[528,512]{1,0:T(8,128)(2,1)}, u32[]{:S(2)}, u32[]{:S(2)}) collective-permute-start(bf16[528,512]{1,0:T(8,128)(2,1)} %add_convert_fusion.5), channel_id=1, source_target_pairs={{3,2},{2,1},{7,6},{6,5},{11,10},{10,9},{15,14},{14,13},{19,18},{18... | collective-permute-start | bytes 1622024 | tf_op jit(solution)/shard_map/ppermute | solution.py:97
  437.0 26.9 %collective-permute-start.45 = (bf16[512,512]{1,0:T(8,128)(2,1)}, bf16[512,512]{1,0:T(8,128)(2,1)}, u32[]{:S(2)}, u32[]{:S(2)}) collective-permute-start(bf16[512,512]{1,0:T(8,128)(2,1)} %fusion.19.refs_6_), channel_id=1, source_target_pairs={{0,1},{1,2},{2,3},{4,5},{5,6},{6,7},{8,9},{9,10},{10,11},{12,13},{... | collective-permute-start | bytes 1572872 | tf_op jit(solution)/shard_map/ppermute | solution.py:58
  459.5 313.9 %reduce-scatter.9.cloned.1.call-start = ((), (), s32[]{:S(2)}) async-start(), calls=%async_computation.9 | async-start | bytes 4718592 | tf_op jit(solution)/shard_map/reduce_scatter | solution.py:894
  477.5 22.7 %collective-permute-start.48 = (bf16[512,512]{1,0:T(8,128)(2,1)S(1)}, bf16[512,512]{1,0:T(8,128)(2,1)S(1)}, u32[]{:S(2)}, u32[]{:S(2)}) collective-permute-start(bf16[512,512]{1,0:T(8,128)(2,1)S(1)} %collective-permute-done.47.refs_12_), channel_id=1, source_target_pairs={{2,1},{1,0},{6,5},{5,4},{10,9},{9,8},{14,13},{13,12},{18,17},{17,1... | collective-permute-start | bytes 1572872 | tf_op jit(solution)/shard_map/ppermute | solution.py:59
  479.2 23.9 %collective-permute-start.56 = (bf16[512,512]{1,0:T(8,128)(2,1)S(1)}, bf16[512,512]{1,0:T(8,128)(2,1)S(1)}, u32[]{:S(2)}, u32[]{:S(2)}) collective-permute-start(bf16[512,512]{1,0:T(8,128)(2,1)S(1)} %collective-permute-done.55.refs_7_), channel_id=1, source_target_pairs={{1,2},{2,3},{5,6},{6,7},{9,10},{10,11},{13,14},{14,15},{17,18},{18... | collective-permute-start | bytes 1572872 | tf_op jit(solution)/shard_map/ppermute | solution.py:58
  501.8 22.6 %collective-permute-start.49 = (bf16[512,512]{1,0:T(8,128)(2,1)}, bf16[512,512]{1,0:T(8,128)(2,1)S(1)}, u32[]{:S(2)}, u32[]{:S(2)}) collective-permute-start(bf16[512,512]{1,0:T(8,128)(2,1)} %broadcast_select_fusion.4), channel_id=1, source_target_pairs={{2,3},{1,0},{6,7},{5,4},{10,11},{9,8},{14,15},{13,12},{18,19},{17,... | collective-permute-start | bytes 1572872 | tf_op jit(solution)/shard_map/ppermute | solution.py:54
  509.6 26.5 %collective-permute-start.59 = (bf16[512,512]{1,0:T(8,128)(2,1)}, bf16[512,512]{1,0:T(8,128)(2,1)}, u32[]{:S(2)}, u32[]{:S(2)}) collective-permute-start(bf16[512,512]{1,0:T(8,128)(2,1)} %broadcast_select_fusion.3), channel_id=1, source_target_pairs={{2,3},{1,0},{6,7},{5,4},{10,11},{9,8},{14,15},{13,12},{18,19},{17,... | collective-permute-start | bytes 1572872 | tf_op jit(solution)/shard_map/ppermute | solution.py:54
  559.5 216.1 %reduce-scatter.7.cloned.1.call-start = ((), (), s32[]{:S(2)}) async-start(), calls=%async_computation.8 | async-start | bytes 9437184 | tf_op jit(solution)/shard_map/reduce_scatter | solution.py:894
  560.1 239.8 %reduce-scatter.11.cloned.1.call-start = ((), (), s32[]{:S(2)}) async-start(), calls=%async_computation.10 | async-start | bytes 14155776 | tf_op jit(solution)/shard_map/reduce_scatter | solution.py:894
  638.1 99.5 %collective-permute-start.64 = (bf16[1024,512]{1,0:T(8,128)(2,1)}, bf16[1024,512]{1,0:T(8,128)(2,1)}, u32[]{:S(2)}, u32[]{:S(2)}) collective-permute-start(bf16[1024,512]{1,0:T(8,128)(2,1)} %get-tuple-element.154), channel_id=1, source_target_pairs={{0,3},{1,0},{2,1},{3,2},{4,7},{5,4},{6,5},{7,6},{8,11},{9,8},{10,9... | collective-permute-start | bytes 3145736 | tf_op jit(solution)/shard_map/ppermute | solution.py:119
  638.1 104.6 %collective-permute-start.63 = (bf16[1024,512]{1,0:T(8,128)(2,1)}, bf16[1024,512]{1,0:T(8,128)(2,1)}, u32[]{:S(2)}, u32[]{:S(2)}) collective-permute-start(bf16[1024,512]{1,0:T(8,128)(2,1)} %get-tuple-element.155), channel_id=1, source_target_pairs={{0,2},{1,3},{2,0},{3,1},{4,6},{5,7},{6,4},{7,5},{8,10},{9,11},{10,... | collective-permute-start | bytes 3145736 | tf_op jit(solution)/shard_map/ppermute | solution.py:119
  642.8 100.7 %collective-permute-start.62 = (bf16[1024,512]{1,0:T(8,128)(2,1)}, bf16[1024,512]{1,0:T(8,128)(2,1)}, u32[]{:S(2)}, u32[]{:S(2)}) collective-permute-start(bf16[1024,512]{1,0:T(8,128)(2,1)} %get-tuple-element.153), channel_id=1, source_target_pairs={{0,1},{1,2},{2,3},{3,0},{4,5},{5,6},{6,7},{7,4},{8,9},{9,10},{10,1... | collective-permute-start | bytes 3145736 | tf_op jit(solution)/shard_map/ppermute | solution.py:119
  642.9 73.8 %collective-permute-start.65 = (bf16[512,512]{1,0:T(8,128)(2,1)S(1)}, bf16[512,512]{1,0:T(8,128)(2,1)S(1)}, u32[]{:S(2)}, u32[]{:S(2)}) collective-permute-start(bf16[512,512]{1,0:T(8,128)(2,1)S(1)} %constant_dynamic-slice_fusion.1), channel_id=1, source_target_pairs={{0,1},{3,2},{4,5},{7,6},{8,9},{11,10},{12,13},{15,14},{16,17},{19,... | collective-permute-start | bytes 1572872 | tf_op jit(solution)/shard_map/ppermute | solution.py:89
  737.7 22.1 %collective-permute-start.73 = (bf16[512,512]{1,0:T(8,128)(2,1)S(1)}, bf16[512,512]{1,0:T(8,128)(2,1)S(1)}, u32[]{:S(2)}, u32[]{:S(2)}) collective-permute-start(bf16[512,512]{1,0:T(8,128)(2,1)S(1)} %add_convert_fusion.9), channel_id=1, source_target_pairs={{0,1},{1,2},{4,5},{5,6},{8,9},{9,10},{12,13},{13,14},{16,17},{17,1... | collective-permute-start | bytes 1572872 | tf_op jit(solution)/shard_map/ppermute | solution.py:96
  748.7 34.4 %collective-permute-start.69 = (bf16[512,512]{1,0:T(8,128)(2,1)}, bf16[512,512]{1,0:T(8,128)(2,1)}, u32[]{:S(2)}, u32[]{:S(2)}) collective-permute-start(bf16[512,512]{1,0:T(8,128)(2,1)} %get-tuple-element.165), channel_id=1, source_target_pairs={{3,2},{2,1},{1,0},{7,6},{6,5},{5,4},{11,10},{10,9},{9,8},{15,14},{... | collective-permute-start | bytes 1572872 | tf_op jit(solution)/shard_map/ppermute | solution.py:104
  750.0 33.1 %collective-permute-start.67 = (bf16[512,512]{1,0:T(8,128)(2,1)}, bf16[512,512]{1,0:T(8,128)(2,1)}, u32[]{:S(2)}, u32[]{:S(2)}) collective-permute-start(bf16[512,512]{1,0:T(8,128)(2,1)} %get-tuple-element.164), channel_id=1, source_target_pairs={{0,1},{1,2},{2,3},{4,5},{5,6},{6,7},{8,9},{9,10},{10,11},{12,13},{... | collective-permute-start | bytes 1572872 | tf_op jit(solution)/shard_map/ppermute | solution.py:103
  (105 other events, 1692.4 us)
Sparse Core Ops, SparseCore 0:
  11.1 74.7 all-gather.3
  87.8 36.5 all-gather.5
  140.0 70.1 all-gather.7
  459.6 49.5 reduce-scatter.4
  559.6 53.8 reduce-scatter.8
  616.8 71.5 reduce-scatter.6
  691.9 92.2 reduce-scatter.10
